TPU v7x, 32 devices: a whole 2x2x4 slice. The times are simulated.
32 devices in a mesh: row: 8 (over z, y), col: 4 (over x, core).
Axes of the slice: x: 2, y: 2, z: 4, core: 2. Of those that a mesh axis runs over, the one named last changes fastest.
Arguments:
- tile_basis: bfloat16 [8, 4, 2304, 256], P('row', 'col'), may hold values from -6 to 6
- tile_coeffs: bfloat16 [8, 4, 2304, 256], P('row', 'col'), may hold values from -0.375 to 0.375
- panel_basis: bfloat16 [8, 256, 2304], P('row', 'col'), may hold values from -6 to 6
- panel_coeffs: bfloat16 [8, 256, 2304], P('row', 'col'), may hold values from -0.125 to 0.125
- tile_rank: int32 [8, 4], P('row', 'col'), may hold values from 64 to 256
- target_rank: int32 [8, 4], P('row', 'col'), may hold values from 64 to 256, as said below
- panel_rank: int32 [8], replicated, may hold values from 64 to 256
- owner_row: int32 [4], replicated, may hold values from 0 to 7, as said below
Outputs:
- fresh_basis: bfloat16 [8, 4, 2304, 256], P('row', 'col')
- fresh_coeffs: bfloat16 [8, 4, 2304, 256], P('row', 'col')
Inputs may be any that keep to these rules, and one draw needn't show every extreme that they name: `target_rank`: a tile's rank after recompression never exceeds its rank before. `owner_row`: distinct panel tile rows.
All inputs are finite; a program needn't handle non-finite values.
Results may differ from a plain program's by a relative error of at most 0.0068.
Values may be sent and summed in bfloat16 or wider, within the bound.
No kernel may reach another device: no remote copies, remote signals or barrier semaphores. Data moves between devices by JAX's collectives and lax.ppermute only.
A program may use at most 64 MiB of HBM per device.

v0:
```python
import math

import jax
import jax.numpy as jnp
from jax import lax
from jax.sharding import PartitionSpec as P

NB = 2304


def spread(value, axis, source):
    kept = jnp.where(lax.axis_index(axis) == source, value, 0).astype(value.dtype)
    return lax.psum(kept, axis)


def keep_columns(matrix, limit):
    flags = (jnp.arange(matrix.shape[1]) < limit).astype(matrix.dtype)
    return matrix * flags[None, :]


def keep_rows(matrix, limit):
    flags = (jnp.arange(matrix.shape[0]) < limit).astype(matrix.dtype)
    return matrix * flags[:, None]


def lead_product(first, second):
    return lax.dot_general(
        first, second, (((0,), (0,)), ((), ())), preferred_element_type=jnp.float32
    )


def tail_product(first, second):
    return lax.dot_general(
        first, second, (((1,), (1,)), ((), ())), preferred_element_type=jnp.float32
    )


def body(
    tile_basis,
    tile_coeffs,
    panel_basis,
    panel_coeffs,
    tile_rank,
    target_rank,
    panel_rank,
    owner_row,
):
    row_basis, row_coeffs = (
        lax.all_gather(panel_basis, "col", axis=1, tiled=True),
        lax.all_gather(panel_coeffs, "col", axis=1, tiled=True),
    )
    source = owner_row[lax.axis_index("col")]
    col_basis, col_coeffs = (spread(row_basis, "row", source), spread(row_coeffs, "row", source))
    here_rank = panel_rank[lax.axis_index("row")]
    there_rank = panel_rank[source]
    left_u = keep_rows(row_basis[0], here_rank)
    left_v = keep_rows(row_coeffs[0], here_rank)
    other_u = keep_rows(col_basis[0], there_rank)
    other_v = keep_rows(col_coeffs[0], there_rank)
    old_rank = tile_rank[0, 0]
    goal_rank = target_rank[0, 0]
    basis = keep_columns(tile_basis[0, 0], old_rank)
    coeffs = keep_columns(tile_coeffs[0, 0], old_rank)
    coupling = tail_product(left_v, other_v).astype(jnp.bfloat16)
    shifted = lead_product(left_u, coupling).astype(jnp.bfloat16)
    sketch = keep_columns(coeffs, goal_rank)
    core_upper = lead_product(coeffs, sketch).astype(jnp.bfloat16)
    core_lower = jnp.dot(other_u, sketch, preferred_element_type=jnp.float32).astype(jnp.bfloat16)
    sampled = jnp.dot(basis, core_upper, preferred_element_type=jnp.float32) - jnp.dot(
        shifted, core_lower, preferred_element_type=jnp.float32
    )
    extra = (jnp.arange(sampled.shape[1]) >= goal_rank).astype(jnp.float32)
    gram_matrix = lax.dot_general(
        sampled,
        sampled,
        (((0,), (0,)), ((), ())),
        precision=lax.Precision.HIGHEST,
        preferred_element_type=jnp.float32,
    )
    gram_matrix = gram_matrix + jnp.diag(extra)
    factor = jnp.linalg.cholesky(gram_matrix)
    orthonormal = jax.scipy.linalg.solve_triangular(factor, sampled.T, lower=True).T
    scaling = math.sqrt(NB)
    fresh_basis = (orthonormal * scaling).astype(jnp.bfloat16)
    reduced_upper = (lead_product(basis, fresh_basis) / scaling).astype(jnp.bfloat16)
    reduced_lower = (-lead_product(shifted, fresh_basis) / scaling).astype(jnp.bfloat16)
    fresh_coeffs = jnp.dot(
        coeffs, reduced_upper, preferred_element_type=jnp.float32
    ) + lead_product(other_u, reduced_lower)
    return (fresh_basis[None, None], fresh_coeffs.astype(jnp.bfloat16)[None, None])


def solution(mesh):
    return jax.shard_map(
        body,
        mesh=mesh,
        in_specs=(
            P("row", "col", None, None),
            P("row", "col", None, None),
            P("row", "col", None),
            P("row", "col", None),
            P("row", "col"),
            P("row", "col"),
            P(),
            P(),
        ),
        out_specs=(P("row", "col", None, None), P("row", "col", None, None)),
        check_vma=False,
    )
```

profile of v0, /device:TPU:0, one launch (start us, length us, event | category | flops | bytes accessed | tf_op | source)
XLA Modules:
  0.0 263.1 jit_solution(7175004458664713414)
XLA Ops:
  7.2 0.0 all-gather.3.cloned.1.call-start
  7.2 0.7 all-gather.3.cloned.1.call-update
  7.9 0.0 all-gather.5.cloned.1.call-start
  7.9 0.7 all-gather.5.cloned.1.call-update
  8.6 0.0 all-reduce.4.cloned.1.call-start
  8.7 1.3 dynamic_slice.10
  10.6 19.1 %all-gather.3.cloned.1.call-done = bf16[1,256,2304]{2,1,0:T(8,128)(2,1)} async-done(((bf16[1,64,2304]{2,1,0:T(8,128)(2,1)}), bf16[1,256,2304]{2,1,0:T(8,128)(2,1)}) %all-gather.3.cloned.1.call-update) | async-done | bytes 1179664 | tf_op jit(solution)/shard_map/all_gather | solution.py:49
  29.7 1.1 broadcast_select_fusion
  30.8 18.0 %all-gather.5.cloned.1.call-done = bf16[1,256,2304]{2,1,0:T(8,128)(2,1)} async-done(((bf16[1,64,2304]{2,1,0:T(8,128)(2,1)}), bf16[1,256,2304]{2,1,0:T(8,128)(2,1)}) %all-gather.5.cloned.1.call-update) | async-done | bytes 1179664 | tf_op jit(solution)/shard_map/all_gather | solution.py:50
  48.8 1.1 broadcast_select_fusion.1
  49.9 0.0 copy-start.8
  49.9 0.0 copy-start.2
  49.9 0.0 copy-start.6
  49.9 0.0 all-reduce.4.cloned.1.call-update
  53.3 0.0 copy-done.8
  53.3 0.6 fusion.93
  53.9 0.6 iota_multiply_fusion
  54.5 1.7 compare_convert_fusion.1
  56.2 0.0 copy-done.2
  56.2 0.0 copy-done.6
  56.2 0.0 copy-start.5
  56.2 2.9 %fusion.38 = f32[2304,256]{1,0:T(8,128)} fusion(bf16[1,1,2304,256]{3,2,1,0:T(8,128)(2,1)S(1)} %copy-done.6, bf16[1,1,2304,256]{3,2,1,0:T(8,128)(2,1)S(1)} %copy-done.2, bf16[256]{0:T(256)(128)(2,1)S(1)} %get-tuple-element.32, bf16[256]{0:T(256)(128)(2,1)S(1)} %get-tuple-element.33), kind=kOutput, calls=%fused_computation.39 | convolution fusion | flops 606404608 | bytes 4719616 | tf_op jit(solution)/shard_map/dot_general | solution.py:69
  59.1 102.9 %all-reduce.4.cloned.1.call-done = (bf16[1,256,2304]{2,1,0:T(8,128)(2,1)}, bf16[1,256,2304]{2,1,0:T(8,128)(2,1)}) async-done(((bf16[1,256,2304]{2,1,0:T(8,128)(2,1)}, bf16[1,256,2304]{2,1,0:T(8,128)(2,1)}), (bf16[1,256,2304]{2,1,0:T(8,128)(2,1)}, bf16[1,256,2304]{2,1,0:T(8,128)(2,1)})) %all-reduce.4.cloned.1.call-update) | async-done | bytes 2359312 | tf_op jit(solution)/shard_map/psum | solution.py:13
  162.1 0.0 copy-done.5
  162.1 0.0 copy-start
  162.1 4.3 %convolution_convert_fusion = bf16[2304,256]{1,0:T(8,128)(2,1)} fusion(bf16[1,256,2304]{2,1,0:T(8,128)(2,1)S(1)} %copy-done.5, bf16[1,256,2304]{2,1,0:T(8,128)(2,1)} %get-tuple-element.20, bf16[1,256,2304]{2,1,0:T(8,128)(2,1)} %all-gather.5.cloned.1.call-done, bf16[256]{0:T(256)(128)(2,1)S(1)} %get-tuple-element.34, bf16[256]{0:T(256)(128)(2,1)} %get-tuple-element.35), kind=kOutput, calls=%fused_computation.5 | convolution fusion | flops 606404608 | bytes 4719616 | tf_op jit(solution)/shard_map/dot_general | solution.py:27
  166.4 0.0 copy-done
  166.4 3.9 %convolution_subtract_fusion = f32[2304,256]{1,0:T(8,128)S(1)} fusion(f32[2304,256]{1,0:T(8,128)} %fusion.38, bf16[2304,256]{1,0:T(8,128)(2,1)} %convolution_convert_fusion, bf16[1,256,2304]{2,1,0:T(8,128)(2,1)S(1)} %copy-done, bf16[1,1,2304,256]{3,2,1,0:T(8,128)(2,1)} %param.9, bf16[256]{0:T(256)(128)(2,1)S(1)} %get-tuple-element.34, ...), kind=kOutput, calls=%fused_computation.3 | convolution fusion | flops 606404608 | bytes 8259072 | tf_op jit(solution)/shard_map/dot_general | solution.py:69
  170.4 3.9 %fusion.94 = f32[256,256]{1,0:T(8,128)S(1)} fusion(f32[2304,256]{1,0:T(8,128)S(1)} %convolution_subtract_fusion), kind=kOutput, calls=%fused_computation.92 | convolution fusion | flops 1811939328 | bytes 2621440 | tf_op jit(solution)/shard_map/dot_general | solution.py:73
  174.3 0.1 copy.10
  174.4 0.0 copy-start.9
  174.4 0.1 fusion.77
  174.5 11.7 %cholesky.49 = f32[128,128]{1,0:T(8,128)S(1)} custom-call(f32[128,128]{1,0:T(8,128)S(1)} %cholesky.115), custom_call_target="Cholesky" | custom-call | tf_op jit(solution)/shard_map/jit(cholesky)/cholesky | solution.py:81
  186.3 9.9 %custom-call.15 = f32[1,128,128]{1,2,0:T(8,128)S(1)} custom-call(f32[1,128,128]{2,1,0:T(8,128)S(1)} %get-tuple-element.27), custom_call_target="InvertDiagBlocksLowerTriangular" | custom-call | tf_op jit(solution)/shard_map/jit(cholesky)/cholesky | solution.py:81
  196.2 0.2 constant_dynamic-update-slice_fusion.1
  196.4 0.3 convolution_subtract_fusion.2
  196.7 11.7 %cholesky.103 = f32[128,128]{1,0:T(8,128)S(1)} custom-call(f32[128,128]{1,0:T(8,128)S(1)} %convolution_subtract_fusion.2), custom_call_target="Cholesky" | custom-call | tf_op jit(solution)/shard_map/jit(cholesky)/cholesky | solution.py:81
  208.4 0.7 compare_reduce_fusion
  209.1 0.6 compare_reduce_fusion.1
  211.1 0.0 copy-done.9
  211.1 0.1 triangular_solve.63
  211.1 5.2 %while.1 = (s32[]{:T(128)}, f32[256,256]{1,0:T(8,128)S(1)}, s32[2,2]{1,0:T(2,128)S(1)}, f32[2,128,128]{2,1,0:T(8,128)}, s32[]{:T(128)}) while((s32[]{:T(128)}, f32[256,256]{1,0:T(8,128)S(1)}, s32[2,2]{1,0:T(2,128)S(1)}, f32[2,128,128]{2,1,0:T(8,128)}, s32[]{:T(128)}) %tuple.30), condition=%wide.while_cond, body=%wide.while_body.sunk | while | flops 2 | bytes 132705 | solution.py:82
  211.1 0.6 fusion.104
  211.7 2.0 bitcast_dynamic-update-slice_fusion.2
  213.7 0.6 fusion.104
  214.3 2.0 bitcast_dynamic-update-slice_fusion.2
  216.3 0.0 copy-start.4
  216.3 21.2 %custom-call.16 = f32[2,128,128]{1,2,0:T(8,128)} custom-call(f32[2,128,128]{2,1,0:T(8,128)} %get-tuple-element.9), custom_call_target="InvertDiagBlocksLowerTriangular" | custom-call | tf_op jit(solution)/shard_map/jit(_solve_triangular)/triangular_solve | solution.py:82
  237.5 0.0 copy-done.4
  237.5 2.0 fusion.3
  239.5 0.0 copy-start.7
  239.5 2.9 %convolution_subtract_fusion.1 = f32[128,2304]{0,1:T(8,128)S(1)} fusion(f32[128,2304]{1,0:T(8,128)S(1)} %fusion.3, f32[256,2304]{0,1:T(8,128)S(1)} %bitcast.108, f32[256,256]{1,0:T(8,128)} %copy-done.4), kind=kOutput, calls=%fused_computation.6 | convolution fusion | flops 453279744 | bytes 3604480 | tf_op jit(solution)/shard_map/jit(_solve_triangular)/triangular_solve | solution.py:82
  242.4 0.0 copy-done.7
  242.4 0.0 copy-start.3
  242.4 1.2 fusion.81
  243.6 0.1 copy-done.3
  243.7 4.2 %fusion.5 = f32[2304,256]{1,0:T(8,128)} fusion(bf16[1,1,2304,256]{3,2,1,0:T(8,128)(2,1)S(1)} %copy-done.3, bf16[1,1,2304,256]{3,2,1,0:T(8,128)(2,1)} %param.8, bf16[256]{0:T(256)(128)(2,1)S(1)} %get-tuple-element.33, f32[128,2304]{1,0:T(8,128)S(1)} %fusion.81, f32[128,2304]{1,0:T(8,128)S(1)} %fusion.3), kind=kOutput, calls=%fused_computation.14 | convolution fusion | flops 607059968 | bytes 7078400 | tf_op jit(solution)/shard_map/dot_general | solution.py:87
  247.9 0.0 copy-start.1
  247.9 1.2 fusion.91
  249.1 0.5 copy-done.1
  249.6 4.6 %fusion.1 = bf16[1,1,2304,256]{3,2,1,0:T(8,128)(2,1)} fusion(f32[2304,256]{1,0:T(8,128)} %fusion.5, bf16[1,256,2304]{2,1,0:T(8,128)(2,1)S(1)} %copy-done.1, bf16[2304,256]{1,0:T(8,128)(2,1)} %convolution_convert_fusion, bf16[256]{0:T(256)(128)(2,1)S(1)} %get-tuple-element.34, f32[128,2304]{1,0:T(8,128)S(1)} %fusion.81, f32[128,2304]{1,0:T(8,128)S(1)} %fusion.3), kind=kOutput, calls=%fused_computation.7 | convolution fusion | flops 607715328 | bytes 8258048 | tf_op jit(solution)/shard_map/dot_general | solution.py:27
  254.2 2.4 copy.11
  (10 shorter events, 0.1 us)
Async XLA Ops:
  7.2 22.6 %all-gather.3.cloned.1.call-start = ((), (), s32[]{:S(2)}) async-start(), calls=%async_computation | async-start | bytes 1474560 | tf_op jit(solution)/shard_map/all_gather | solution.py:49
  7.9 40.9 %all-gather.5.cloned.1.call-start = ((), (), s32[]{:S(2)}) async-start(), calls=%async_computation.1 | async-start | bytes 1474560 | tf_op jit(solution)/shard_map/all_gather | solution.py:50
  8.6 153.4 %all-reduce.4.cloned.1.call-start = ((), (), s32[]{:S(2)}) async-start(), calls=%async_computation.2 | async-start | bytes 4718592 | tf_op jit(solution)/shard_map/psum | solution.py:13
  49.9 3.4 %copy-start.8 = (s32[8]{0:T(128)S(1)}, s32[8]{0:T(128)}, u32[]{:S(2)}) copy-start(s32[8]{0:T(128)} %param.14) | copy-start | bytes 100
  49.9 6.3 %copy-start.2 = (bf16[1,1,2304,256]{3,2,1,0:T(8,128)(2,1)S(1)}, bf16[1,1,2304,256]{3,2,1,0:T(8,128)(2,1)}, u32[]{:S(2)}) copy-start(bf16[1,1,2304,256]{3,2,1,0:T(8,128)(2,1)} %param.9) | copy-start | bytes 3538948
  49.9 6.3 %copy-start.6 = (bf16[1,1,2304,256]{3,2,1,0:T(8,128)(2,1)S(1)}, bf16[1,1,2304,256]{3,2,1,0:T(8,128)(2,1)}, u32[]{:S(2)}) copy-start(bf16[1,1,2304,256]{3,2,1,0:T(8,128)(2,1)} %param.8) | copy-start | bytes 3538948
  56.2 105.9 %copy-start.5 = (bf16[1,256,2304]{2,1,0:T(8,128)(2,1)S(1)}, bf16[1,256,2304]{2,1,0:T(8,128)(2,1)}, u32[]{:S(2)}) copy-start(bf16[1,256,2304]{2,1,0:T(8,128)(2,1)} %all-gather.3.cloned.1.call-done) | copy-start | bytes 3538948
  162.1 4.3 %copy-start = (bf16[1,256,2304]{2,1,0:T(8,128)(2,1)S(1)}, bf16[1,256,2304]{2,1,0:T(8,128)(2,1)}, u32[]{:S(2)}) copy-start(bf16[1,256,2304]{2,1,0:T(8,128)(2,1)} %get-tuple-element.21) | copy-start | bytes 3538948
  174.4 36.7 %copy-start.9 = (s32[2]{0:T(128)S(1)}, s32[2]{0:T(128)}, u32[]{:S(2)}) copy-start(s32[2]{0:T(128)} %iota_multiply_fusion) | copy-start | bytes 28
  216.3 21.2 %copy-start.4 = (f32[256,256]{1,0:T(8,128)}, f32[256,256]{1,0:T(8,128)S(1)}, u32[]{:S(2)}) copy-start(f32[256,256]{1,0:T(8,128)S(1)} %get-tuple-element.91) | copy-start | bytes 786436
  239.5 2.9 %copy-start.7 = (f32[2,128,128]{1,2,0:T(8,128)S(1)}, f32[2,128,128]{1,2,0:T(8,128)}, u32[]{:S(2)}) copy-start(f32[2,128,128]{1,2,0:T(8,128)} %custom-call.16) | copy-start | bytes 393220
  242.4 1.3 copy-start.3
  247.9 1.7 copy-start.1
Sparse Core Ops, SparseCore 0:
  9.6 20.1 all-gather.2
  31.3 17.4 all-gather.4
  53.0 109.0 all-reduce.3
where the time goes:
time: 264 us; the launch traced here: 263 us
  waiting for transfers between devices  141 us (53%)
  other arithmetic  61.6 us (23%)
  matrix products  30.4 us (12%)
  between operations  19.2 us (7%)
  local copies, waits for them, and re-layouts  10.3 us (4%)
    psum x1, waiting for transfers between devices, spread(): return lax.psum(kept, axis)  103 us
    another operation x7, other arithmetic, body(): factor = jnp.linalg.cholesky(gram_matrix)  34.7 us
    another operation x3, other arithmetic, body(): jax.scipy.linalg.solve_triangular(factor, sampled.T, lower=True)  21.8 us
    all_gather x1, waiting for transfers between devices, body(): lax.all_gather(panel_basis, 'col', axis=1, tiled=True)  19.1 us
    all_gather x1, waiting for transfers between devices, body(): lax.all_gather(panel_coeffs, 'col', axis=1, tiled=True)  18 us
    dot_general x2, matrix products, lead_product(): lax.dot_general(first, second, (((0,), (0,)), ((), ())), preferred_elemen...  8.91 us
    another operation x3, matrix products, body(): jax.scipy.linalg.solve_triangular(factor, sampled.T, lower=True)  6.08 us
  transfers between devices with their start and end apart: 3, of which 3 were waited for; matrix products, arithmetic and copies ran while one was open for 3% of the time, Pallas kernels for 0%

commit v1 on v0

v1 whole, which is shorter than its diff:
```python
import functools
import math

import jax
import jax.numpy as jnp
from jax import lax
from jax.experimental import pallas as pl
from jax.experimental.pallas import tpu as pltpu
from jax.sharding import PartitionSpec as P

F32 = jnp.float32
BF16 = jnp.bfloat16
HIGHEST = lax.Precision.HIGHEST
VMEM = pl.BlockSpec(memory_space=pltpu.VMEM)
SMEM = pl.BlockSpec(memory_space=pltpu.SMEM)
ANY = pl.BlockSpec(memory_space=pl.ANY)
ROUGH, FINE = 0.05, 2e-3
ROUGH_STEPS, FINE_STEPS = 8, 6


def nn(a, b, precision=None):
    return lax.dot_general(a, b, (((1,), (0,)), ((), ())), precision=precision, preferred_element_type=F32)


def nt(a, b, precision=None):
    return lax.dot_general(a, b, (((1,), (1,)), ((), ())), precision=precision, preferred_element_type=F32)


def tn(a, b, precision=None):
    return lax.dot_general(a, b, (((0,), (0,)), ((), ())), precision=precision, preferred_element_type=F32)


def halves(x):
    high = x.astype(BF16)
    return high, (x - high.astype(F32)).astype(BF16)


def ring_order(n):
    return list(range(0, n, 2)) + list(range(n - 1, 0, -2))


def ring_gather(x, axis, n):
    ring = ring_order(n)
    ahead = [(ring[i], ring[(i + 1) % n]) for i in range(n)]
    back = [(b, a) for a, b in ahead]
    out = [None] * n
    out[0] = right = left = x
    for s in range(1, n // 2):
        right = lax.ppermute(right, axis, ahead)
        left = lax.ppermute(left, axis, back)
        out[s], out[n - s] = right, left
    half = x.shape[0] // 2
    out[n // 2] = (lax.ppermute(right[:half], axis, ahead), lax.ppermute(left[half:], axis, back))
    return out


def swap(x, axis, n, m):
    return lax.ppermute(x, axis, [(i, i ^ m) for i in range(n)])


def xor_gather(x, axis, n):
    have = {0: x}
    bit = n // 2
    while bit:
        for m in list(have):
            have[m | bit] = swap(have[m], axis, n, bit)
        bit //= 2
    return [have[m] for m in range(n)]


def pick_and_multiply(n_row, n_col, count, index, *refs):
    pieces = refs[: n_row + 1]
    rights = refs[n_row + 1 : n_row + 1 + count]
    out_ref, picked, sem = refs[n_row + 1 + count :]
    half = n_row // 2
    low = picked.shape[1] // 2
    for m in range(n_col):
        for k in range(n_row):

            @pl.when(index[m] == k)
            def _():
                if k == half:
                    a = pltpu.make_async_copy(pieces[half], picked.at[m, pl.ds(0, low)], sem.at[m])
                    b = pltpu.make_async_copy(pieces[n_row], picked.at[m, pl.ds(low, low)], sem.at[m])
                    a.start()
                    a.wait()
                    b.start()
                    b.wait()
                else:
                    c = pltpu.make_async_copy(pieces[k], picked.at[m], sem.at[m])
                    c.start()
                    c.wait()
    for m in range(n_col):
        right = rights[m if count > 1 else 0]
        dot = nn if count > 1 else nt
        out_ref[m] = dot(picked[m], right[...]).astype(BF16)


def picked_products(pieces, rights, index, n_row, n_col, name):
    shard, width = pieces[0].shape
    half = n_row // 2
    flat = list(pieces)
    flat[half] = pieces[half][0]
    flat.append(pieces[half][1])
    rank = n_col * shard
    keep = len(rights) > 1
    outs = jax.ShapeDtypeStruct((n_col, shard, rank), BF16)
    sel = jax.ShapeDtypeStruct((n_col, shard, width), BF16)
    return pl.pallas_call(
        functools.partial(pick_and_multiply, n_row, n_col, len(rights)),
        out_shape=(outs, sel),
        in_specs=[SMEM] + [ANY] * len(flat) + [VMEM] * len(rights),
        out_specs=(VMEM, VMEM),
        scratch_shapes=[pltpu.SemaphoreType.DMA((n_col,))],
        compiler_params=pltpu.CompilerParams(vmem_limit_bytes=40 << 20),
        cost_estimate=pl.CostEstimate(
            flops=2 * rank * rank * width, bytes_accessed=6 << 20, transcendentals=0
        ),
        name=name,
    )(index, *flat, *rights)


def lower_half(e, eye, below):
    return jnp.where(below, e, jnp.where(eye, 0.5 * e, 0.0))


def finish(n_col, scalars, u_ref, v_ref, uit_ref, h_ref, cu_ref, *refs):
    ujt_in, kt_in, cl_in = refs[:n_col], refs[n_col : 2 * n_col], refs[2 * n_col : 3 * n_col]
    q_ref, w_ref, ujt, kt, cl, mf, hm, gn, y_ref, a_ref = refs[3 * n_col :]
    rows, rank = u_ref.shape
    shard = rank // n_col
    old, goal, here, there, me = (scalars[t] for t in range(5))
    sub = lax.broadcasted_iota(jnp.int32, (rank, rank), 0)
    lane = lax.broadcasted_iota(jnp.int32, (rank, rank), 1)
    eye, below = sub == lane, sub > lane
    one = jnp.where(eye, 1.0, 0.0).astype(F32)
    for m in range(n_col):
        at = pl.ds(pl.multiple_of((me ^ m) * shard, shard), shard)
        kt[at, :] = kt_in[m][...]
        cl[at, :] = cl_in[m][...]
        ujt[at, :] = ujt_in[m][...]
    zero = jnp.zeros((rank, rank), F32)
    kt[...] = jnp.where((sub < there) & (lane < here), kt[...].astype(F32), zero).astype(BF16)
    cl[...] = jnp.where(lane < goal, cl[...].astype(F32), zero).astype(BF16)
    cu = jnp.where((sub < old) & (lane < goal), cu_ref[...], zero).astype(BF16).astype(F32)
    mf[pl.ds(0, rank), :] = cu
    mf[pl.ds(rank, rank), :] = -tn(kt[...], cl[...])
    hm[...] = nn(h_ref[...], mf[...], HIGHEST)
    g = tn(mf[...], hm[...], HIGHEST) + jnp.where(eye & (lane >= goal), 1.0, 0.0)
    dg = jnp.where(eye, g, 0.0)
    d_row = lax.rsqrt(jnp.sum(dg, axis=0, keepdims=True))
    d_col = lax.rsqrt(jnp.sum(dg, axis=1, keepdims=True))
    gn[...] = g * d_col * d_row
    y_ref[...] = one - lower_half(gn[...] - one, eye, below)
    gb = gn[...].astype(BF16)

    def rough(carry):
        step, _ = carry
        y = y_ref[...]
        yb = y.astype(BF16)
        e = nt(nn(yb, gb).astype(BF16), yb) - one
        y_ref[...] = y - nn(lower_half(e, eye, below).astype(BF16), yb)
        return step + 1, jnp.max(jnp.abs(e))

    def fine(carry):
        step, _ = carry
        y = y_ref[...]
        e = nt(nn(y, gn[...], HIGHEST), y, HIGHEST) - one
        y_ref[...] = y - nn(lower_half(e, eye, below), y, HIGHEST)
        return step + 1, jnp.max(jnp.abs(e))

    lax.while_loop(lambda c: (c[0] < ROUGH_STEPS) & (c[1] > ROUGH), rough, (jnp.int32(0), F32(1.0)))
    _, err = lax.while_loop(lambda c: (c[0] < FINE_STEPS) & (c[1] > FINE), fine, (jnp.int32(0), F32(1.0)))

    lowest = jnp.min(jnp.where(eye, y_ref[...], 1.0))

    @pl.when(jnp.logical_not((err <= FINE) & (lowest > 0.0)))
    def _():
        a_ref[...] = gn[...]
        y_ref[...] = one

        def pivot(k, _):
            col = jnp.sum(jnp.where(lane == k, a_ref[...], 0.0), axis=1, keepdims=True)
            row = jnp.sum(jnp.where(sub == k, a_ref[...], 0.0), axis=0, keepdims=True)
            yrow = jnp.sum(jnp.where(sub == k, y_ref[...], 0.0), axis=0, keepdims=True)
            top = jnp.sum(jnp.where(lax.broadcasted_iota(jnp.int32, (1, rank), 1) == k, row, 0.0))
            inv = 1.0 / jnp.sqrt(jnp.full((1, rank), top))
            row, yrow = row * inv, yrow * inv
            col = jnp.where(lax.broadcasted_iota(jnp.int32, (rank, 1), 0) > k, col * inv[:, :1], 0.0)
            a_ref[...] = a_ref[...] - col * row
            y_ref[...] = jnp.where(sub == k, yrow, y_ref[...] - col * yrow)
            return 0

        lax.fori_loop(0, rank, pivot, 0)

    x = y_ref[...] * d_row
    root = math.sqrt(rows)
    c = nt(mf[...], x, HIGHEST) * root
    r = nt(hm[...], x, HIGHEST)
    r_up = jnp.where(sub < old, r[:rank], 0.0).astype(BF16)
    r_low = (-nn(kt[...].astype(F32), r[rank:], HIGHEST)).astype(BF16)
    ch, cl2 = halves(c)
    cu_h, cu_l, cl_h, cl_l = ch[:rank], cl2[:rank], ch[rank:], cl2[rank:]
    step = 256 if rows % 256 == 0 else rows
    for t in range(rows // step):
        at = pl.ds(t * step, step)
        u, v = u_ref[at, :], v_ref[at, :]
        ui, uj = uit_ref[:, at], ujt[:, at]
        q_ref[at, :] = (nn(u, cu_h) + nn(u, cu_l) + tn(ui, cl_h) + tn(ui, cl_l)).astype(BF16)
        w_ref[at, :] = (nn(v, r_up) + tn(uj, r_low)).astype(BF16)


def body(tile_basis, tile_coeffs, panel_basis, panel_coeffs, tile_rank, target_rank, panel_rank, owner_row):
    n_row, n_col = lax.axis_size("row"), lax.axis_size("col")
    row, col = lax.axis_index("row"), lax.axis_index("col")
    u, v = tile_basis[0, 0], tile_coeffs[0, 0]
    pu, pv = panel_basis[0], panel_coeffs[0]
    rows, rank = u.shape
    shard = rank // n_col

    us = ring_gather(pu, "row", n_row)
    vs = ring_gather(pv, "row", n_row)
    ui_parts = xor_gather(pu, "col", n_col)
    vi_parts = xor_gather(pv, "col", n_col)
    v_tiles = xor_gather(v, "col", n_col)

    place = [0] * n_row
    for at, r in enumerate(ring_order(n_row)):
        place[r] = at
    place = jnp.array(place, jnp.int32)
    columns = col ^ jnp.arange(n_col, dtype=jnp.int32)
    owners = owner_row[columns]
    index = (place[row] - place[owners] + n_row) % n_row

    uit = jnp.zeros((rank, rows), BF16)
    vit = jnp.zeros((rank, rows), BF16)
    for m in range(n_col):
        uit = lax.dynamic_update_slice(uit, ui_parts[m], ((col ^ m) * shard, 0))
        vit = lax.dynamic_update_slice(vit, vi_parts[m], ((col ^ m) * shard, 0))

    h11 = tn(u, u)
    h21 = nn(uit, u)
    h22 = nt(uit, uit)
    h = jnp.concatenate([jnp.concatenate([h11, h21.T], 1), jnp.concatenate([h21, h22], 1)], 0)
    core_up = tn(v, v)

    low, u_sel = picked_products(us, v_tiles, index, n_row, n_col, "core_low")
    kt, _ = picked_products(vs, [vit], index, n_row, n_col, "coupling")
    low = [low[0]] + [swap(low[m], "col", n_col, m) for m in range(1, n_col)]
    kts = [kt[0]] + [swap(kt[m], "col", n_col, m) for m in range(1, n_col)]
    ujs = [u_sel[0]] + [swap(u_sel[m], "col", n_col, m) for m in range(1, n_col)]

    scalars = jnp.stack([tile_rank[0, 0], target_rank[0, 0], panel_rank[row], panel_rank[owners[0]], col])
    out = jax.ShapeDtypeStruct((rows, rank), BF16)
    square = pltpu.VMEM((rank, rank), F32)
    fresh_basis, fresh_coeffs = pl.pallas_call(
        functools.partial(finish, n_col),
        out_shape=(out, out),
        in_specs=[SMEM] + [VMEM] * (5 + 3 * n_col),
        out_specs=(VMEM, VMEM),
        scratch_shapes=[
            pltpu.VMEM((rank, rows), BF16),
            pltpu.VMEM((rank, rank), BF16),
            pltpu.VMEM((rank, rank), BF16),
            pltpu.VMEM((2 * rank, rank), F32),
            pltpu.VMEM((2 * rank, rank), F32),
            square,
            square,
            square,
        ],
        compiler_params=pltpu.CompilerParams(vmem_limit_bytes=48 << 20),
        cost_estimate=pl.CostEstimate(flops=8 << 30, bytes_accessed=12 << 20, transcendentals=0),
        name="finish",
    )(scalars, u, v, uit, h, core_up, *ujs, *kts, *low)
    return fresh_basis[None, None], fresh_coeffs[None, None]


def solution(mesh):
    tiles, panels = P("row", "col", None, None), P("row", "col", None)
    return jax.shard_map(
        body,
        mesh=mesh,
        in_specs=(tiles, tiles, panels, panels, P("row", "col"), P("row", "col"), P(), P()),
        out_specs=(tiles, tiles),
        check_vma=False,
    )
```

time: 264 us -> 180 us (0.68)
  waiting for transfers between devices: 141 us -> 37.4 us
  Pallas kernels: 0 us -> 81.7 us
  other arithmetic: 61.6 us -> 4.37 us
  starting transfers between devices: 0.11 us -> 27.5 us
  matrix products: 30.4 us -> 9.61 us
  between operations: 19.2 us -> 3.78 us
  local copies, waits for them, and re-layouts: 10.3 us -> 16.1 us
    psum x1 -> x0, waiting for transfers between devices: 103 us -> none  [spread(): return lax.psum(kept, axis)]
    pallas_call x0 -> x3, Pallas kernels: none -> 81.7 us  [the longest x1 73.9 us: body(): pl.pallas_call(functools.partial(finish, n_col), out_shape=(out, out), in...]
    another operation x10 -> x0, other arithmetic: 56.5 us -> none  [the longest x7 34.7 us: body(): factor = jnp.linalg.cholesky(gram_matrix)]
    ppermute x0 -> x34, waiting for transfers between devices: none -> 37.4 us  [the longest x6 19.9 us: ring_gather(): left = lax.ppermute(left, axis, back)]
    all_gather x2 -> x0, waiting for transfers between devices: 37.1 us -> none  [the longest x1 19.1 us: body(): lax.all_gather(panel_basis, 'col', axis=1, tiled=True)]
    ppermute x0 -> x34, starting transfers between devices: none -> 27.5 us  [the longest x18 10.7 us: swap(): return lax.ppermute(x, axis, [(i, i ^ m) for i in range(n)])]
    dot_general x6 -> x4, matrix products: 23.9 us -> 9.61 us  [the longest x2 4.26 us: tn(): lax.dot_general(a, b, (((0,), (0,)), ((), ())), precision=precision, pref...]
    another operation x5 -> x0, matrix products: 6.55 us -> none  [the longest x3 6.08 us: body(): jax.scipy.linalg.solve_triangular(factor, sampled.T, lower=True)]
  transfers between devices with their start and end apart: 3 -> 34, of which waited for: 3 -> 11; matrix products, arithmetic and copies ran while one was open for 3% -> 17% of each run, Pallas kernels for 0% -> 4%
where the time goes in v1:
time: 180 us
  Pallas kernels  81.7 us (45%)
  waiting for transfers between devices  37.4 us (21%)
  starting transfers between devices  27.5 us (15%)
  local copies, waits for them, and re-layouts  16.1 us (9%)
  matrix products  9.61 us (5%)
  other arithmetic  4.37 us (2%)
  between operations  3.78 us (2%)
    pallas_call x1, Pallas kernels, body(): pl.pallas_call(functools.partial(finish, n_col), out_shape=(out, out), in...  73.9 us
    ppermute x6, waiting for transfers between devices, ring_gather(): left = lax.ppermute(left, axis, back)  19.9 us
    ppermute x18, starting transfers between devices, swap(): return lax.ppermute(x, axis, [(i, i ^ m) for i in range(n)])  10.7 us
    ppermute x6, waiting for transfers between devices, ring_gather(): right = lax.ppermute(right, axis, ahead)  9.27 us
    ppermute x6, starting transfers between devices, ring_gather(): right = lax.ppermute(right, axis, ahead)  8.67 us
    pallas_call x2, Pallas kernels, picked_products(): pl.pallas_call(functools.partial(pick_and_multiply, n_row, n_col, len(rig...  7.73 us
    ppermute x18, waiting for transfers between devices, swap(): return lax.ppermute(x, axis, [(i, i ^ m) for i in range(n)])  6.62 us
    dot_general x2, matrix products, tn(): lax.dot_general(a, b, (((0,), (0,)), ((), ())), precision=precision, pref...  4.26 us
  transfers between devices with their start and end apart: 34, of which 11 were waited for; matrix products, arithmetic and copies ran while one was open for 17% of the time, Pallas kernels for 4%

profile of v1, /device:TPU:0, one launch (start us, length us, event | category | flops | bytes accessed | tf_op | source)
XLA Modules:
  0.0 180.4 jit_solution(4579680358672580939)
XLA Ops:
  0.6 0.5 collective-permute-start
  1.2 2.6 %collective-permute-start.1 = (bf16[64,2304]{1,0:T(8,128)(2,1)}, bf16[64,2304]{1,0:T(8,128)(2,1)S(1)}, u32[]{:S(2)}, u32[]{:S(2)}) collective-permute-start(bf16[64,2304]{1,0:T(8,128)(2,1)} %bitcast.7.refs_0_), channel_id=1, source_target_pairs={{0,2},{1,3},{2,0},{3,1},{4,6},{5,7},{6,4},{7,5},{8,10},{9,11},{10,... | collective-permute-start | bytes 884744 | tf_op jit(solution)/shard_map/ppermute | solution.py:58
  4.2 1.8 %collective-permute-start.17 = (bf16[64,2304]{1,0:T(8,128)(2,1)}, bf16[64,2304]{1,0:T(8,128)(2,1)}, u32[]{:S(2)}, u32[]{:S(2)}) collective-permute-start(bf16[64,2304]{1,0:T(8,128)(2,1)} %bitcast.16.refs_0_), channel_id=1, source_target_pairs={{0,8},{8,16},{16,24},{24,28},{28,20},{20,12},{12,4},{4,0},{1,9},{9... | collective-permute-start | bytes 884744 | tf_op jit(solution)/shard_map/ppermute | solution.py:49
  6.0 0.5 fusion.1
  6.5 3.0 %fusion.7 = f32[256,256]{1,0:T(8,128)} fusion(bf16[1,1,2304,256]{3,2,1,0:T(8,128)(2,1)} %param.9), kind=kOutput, calls=%fused_computation.37 | convolution fusion | flops 301989888 | bytes 1441792 | tf_op jit(solution)/shard_map/dot_general | solution.py:30
  9.6 1.1 broadcast.57.clone
  10.7 1.7 constant_dynamic-update-slice_fusion.7
  12.5 1.1 constant_dynamic-update-slice_fusion.3
  13.5 0.7 pad_clamp_fusion.1
  14.2 1.1 gather_fusion
  15.3 0.6 fusion.2
  15.9 0.6 dynamic_slice.11
  16.5 1.1 gather_fusion.1
  17.6 1.3 and_select_fusion.index
  21.9 0.6 fusion.9
  22.5 1.3 stack.7.scalars
  23.8 1.2 fusion.3.cu_ref
  25.0 1.5 collective-permute-start.12
  26.5 0.7 constant_dynamic-update-slice_fusion.6
  27.2 0.5 collective-permute-start.21
  27.7 1.6 collective-permute-start.7
  29.3 0.5 collective-permute-start.3
  30.0 0.7 constant_dynamic-update-slice_fusion.5
  30.8 6.6 %collective-permute-done.21.refs_7_ = bf16[64,2304]{1,0:T(8,128)(2,1)S(1)} collective-permute-done((bf16[64,2304]{1,0:T(8,128)(2,1)}, bf16[64,2304]{1,0:T(8,128)(2,1)S(1)}, u32[]{:S(2)}, u32[]{:S(2)}) %collective-permute-start.21) | collective-permute-done | bytes 294944 | tf_op jit(solution)/shard_map/ppermute | solution.py:50
  37.4 4.8 %collective-permute-done.7.refs_7_ = bf16[64,2304]{1,0:T(8,128)(2,1)S(1)} collective-permute-done((bf16[64,2304]{1,0:T(8,128)(2,1)}, bf16[64,2304]{1,0:T(8,128)(2,1)S(1)}, u32[]{:S(2)}, u32[]{:S(2)}) %collective-permute-start.7) | collective-permute-done | bytes 294944 | tf_op jit(solution)/shard_map/ppermute | solution.py:50
  42.2 1.6 collective-permute-start.18
  43.8 0.5 collective-permute-start.22
  44.2 1.0 constant_dynamic-update-slice_fusion.1
  45.3 0.5 collective-permute-start.8
  45.8 4.1 %collective-permute-done.18.refs_2_ = bf16[64,2304]{1,0:T(8,128)(2,1)S(1)} collective-permute-done((bf16[64,2304]{1,0:T(8,128)(2,1)}, bf16[64,2304]{1,0:T(8,128)(2,1)S(1)}, u32[]{:S(2)}, u32[]{:S(2)}) %collective-permute-start.18) | collective-permute-done | bytes 294944 | tf_op jit(solution)/shard_map/ppermute | solution.py:49
  49.9 1.6 collective-permute-start.4
  51.5 2.1 %collective-permute-done.22.refs_6_ = bf16[64,2304]{1,0:T(8,128)(2,1)S(1)} collective-permute-done((bf16[64,2304]{1,0:T(8,128)(2,1)S(1)}, bf16[64,2304]{1,0:T(8,128)(2,1)S(1)}, u32[]{:S(2)}, u32[]{:S(2)}) %collective-permute-start.22) | collective-permute-done | bytes 294944 | tf_op jit(solution)/shard_map/ppermute | solution.py:50
  53.6 1.6 collective-permute-start.19
  55.2 0.7 constant_dynamic-update-slice_fusion.4.uit_ref
  55.9 1.4 collective-permute-done.8.refs_6_
  57.3 0.4 collective-permute-start.23
  57.8 1.9 %collective-permute-done.4.refs_2_ = bf16[64,2304]{1,0:T(8,128)(2,1)S(1)} collective-permute-done((bf16[64,2304]{1,0:T(8,128)(2,1)S(1)}, bf16[64,2304]{1,0:T(8,128)(2,1)S(1)}, u32[]{:S(2)}, u32[]{:S(2)}) %collective-permute-start.4) | collective-permute-done | bytes 294944 | tf_op jit(solution)/shard_map/ppermute | solution.py:49
  59.6 0.5 collective-permute-start.9
  60.1 3.3 %collective-permute-done.19.refs_3_ = bf16[64,2304]{1,0:T(8,128)(2,1)S(1)} collective-permute-done((bf16[64,2304]{1,0:T(8,128)(2,1)S(1)}, bf16[64,2304]{1,0:T(8,128)(2,1)S(1)}, u32[]{:S(2)}, u32[]{:S(2)}) %collective-permute-start.19) | collective-permute-done | bytes 294944 | tf_op jit(solution)/shard_map/ppermute | solution.py:49
  63.4 1.6 collective-permute-start.5
  65.0 2.2 %collective-permute-done.23.refs_5_ = bf16[64,2304]{1,0:T(8,128)(2,1)S(1)} collective-permute-done((bf16[64,2304]{1,0:T(8,128)(2,1)S(1)}, bf16[64,2304]{1,0:T(8,128)(2,1)S(1)}, u32[]{:S(2)}, u32[]{:S(2)}) %collective-permute-start.23) | collective-permute-done | bytes 294944 | tf_op jit(solution)/shard_map/ppermute | solution.py:50
  67.3 1.6 collective-permute-start.20
  68.9 2.8 %collective-permute-done.9.refs_5_ = bf16[64,2304]{1,0:T(8,128)(2,1)S(1)} collective-permute-done((bf16[64,2304]{1,0:T(8,128)(2,1)S(1)}, bf16[64,2304]{1,0:T(8,128)(2,1)S(1)}, u32[]{:S(2)}, u32[]{:S(2)}) %collective-permute-start.9) | collective-permute-done | bytes 294944 | tf_op jit(solution)/shard_map/ppermute | solution.py:50
  72.1 2.5 %fusion.5 = f32[256,256]{1,0:T(8,128)} fusion(bf16[256,2304]{1,0:T(8,128)(2,1)} %constant_dynamic-update-slice_fusion.4.uit_ref, bf16[1,1,2304,256]{3,2,1,0:T(8,128)(2,1)S(1)} %copy-done.2), kind=kOutput, calls=%fused_computation.35 | convolution fusion | flops 301989888 | bytes 2621440 | tf_op jit(solution)/shard_map/dot_general | solution.py:22
  74.6 0.5 collective-permute-start.10
  75.1 1.6 collective-permute-start.6
  76.7 1.5 collective-permute-done.24.refs_8_
  78.3 4.5 %coupling.1 = (bf16[4,64,256]{2,1,0:T(8,128)(2,1)S(1)}, bf16[4,64,2304]{2,1,0:T(8,128)(2,1)}) custom-call(s32[4]{0:T(128)S(1)} %and_select_fusion.index, bf16[64,2304]{1,0:T(8,128)(2,1)} %bitcast.16.refs_0_, bf16[64,2304]{1,0:T(8,128)(2,1)} %collective-permute-done.17.refs_1_, bf16[64,2304]{1,0:T(8,128)(2,1)S(1)} %collective-permute-done.18.refs_2_, ...), custom_call_target="tpu_custom_call" | custom-call | flops 301989888 | bytes 6291456 | tf_op jit(solution)/shard_map/coupling/pallas_call | solution.py:109
  82.7 0.6 slice_bitcast_fusion.8
  83.3 0.6 collective-permute-start.29
  83.9 1.3 collective-permute-start.30
  85.2 3.3 %core_low.1 = (bf16[4,64,256]{2,1,0:T(8,128)(2,1)S(1)}, bf16[4,64,2304]{2,1,0:T(8,128)(2,1)S(1)}) custom-call(s32[4]{0:T(128)S(1)} %and_select_fusion.index, bf16[64,2304]{1,0:T(8,128)(2,1)} %bitcast.7.refs_0_, bf16[64,2304]{1,0:T(8,128)(2,1)S(1)} %collective-permute-done.3.refs_1_, bf16[64,2304]{1,0:T(8,128)(2,1)S(1)} %collective-permute-done.4.refs_2_, ...), custom_call_target="tpu_custom_call" | custom-call | flops 301989888 | bytes 6291456 | tf_op jit(solution)/shard_map/core_low/pallas_call | solution.py:109
  88.5 0.9 slice_bitcast_fusion
  89.7 0.5 collective-permute-start.15
  90.2 0.6 slice_bitcast_fusion.4
  90.8 1.1 collective-permute-start.16
  91.9 0.6 collective-permute-start.31
  92.5 2.9 %fusion.10 = f32[256,256]{1,0:T(8,128)} fusion(bf16[256,2304]{1,0:T(8,128)(2,1)} %constant_dynamic-update-slice_fusion.4.uit_ref), kind=kOutput, calls=%fused_computation.40 | convolution fusion | flops 301989888 | bytes 1441792 | tf_op jit(solution)/shard_map/dot_general | solution.py:26
  95.4 1.8 copy.14
  97.2 0.5 collective-permute-start.32
  97.7 0.9 collective-permute-start.33
  98.6 1.3 maximum_maximum_fusion.h_ref
  99.9 6.6 %collective-permute-done.32.refs_10_ = bf16[64,256]{1,0:T(8,128)(2,1)S(1)} collective-permute-done((bf16[64,256]{1,0:T(8,128)(2,1)}, bf16[64,256]{1,0:T(8,128)(2,1)S(1)}, u32[]{:S(2)}, u32[]{:S(2)}) %collective-permute-start.32) | collective-permute-done | bytes 32800 | tf_op jit(solution)/shard_map/ppermute | solution.py:58
  106.5 73.9 %finish.1 = (bf16[2304,256]{1,0:T(8,128)(2,1)}, bf16[2304,256]{1,0:T(8,128)(2,1)}) custom-call(s32[5]{0:T(128)S(1)} %stack.7.scalars, bf16[2304,256]{1,0:T(8,128)(2,1)S(1)} %bitcast.60, bf16[2304,256]{1,0:T(8,128)(2,1)S(1)} %bitcast.59, bf16[256,2304]{1,0:T(8,128)(2,1)} %constant_dynamic-update-slice_fusion.4.uit_ref, ...), custom_call_target="tpu_custom_call" | custom-call | flops 8589934592 | bytes 12582912 | tf_op jit(solution)/shard_map/finish/pallas_call | solution.py:256
  (58 shorter events, 1.7 us)
Async XLA Ops:
  0.6 13.6 %copy-start = (s32[4]{0:T(128)S(1)}, s32[4]{0:T(128)}, u32[]{:S(2)}) copy-start(s32[4]{0:T(128)} %param.16) | copy-start | bytes 52
  0.6 24.4 %collective-permute-start = (bf16[64,2304]{1,0:T(8,128)(2,1)}, bf16[64,2304]{1,0:T(8,128)(2,1)S(1)}, u32[]{:S(2)}, u32[]{:S(2)}) collective-permute-start(bf16[64,2304]{1,0:T(8,128)(2,1)} %bitcast.7.refs_0_), channel_id=1, source_target_pairs={{0,1},{1,0},{2,3},{3,2},{4,5},{5,4},{6,7},{7,6},{8,9},{9,8},{10,11... | collective-permute-start | bytes 884744 | tf_op jit(solution)/shard_map/ppermute | solution.py:58
  1.2 26.6 %collective-permute-start.1 = (bf16[64,2304]{1,0:T(8,128)(2,1)}, bf16[64,2304]{1,0:T(8,128)(2,1)S(1)}, u32[]{:S(2)}, u32[]{:S(2)}) collective-permute-start(bf16[64,2304]{1,0:T(8,128)(2,1)} %bitcast.7.refs_0_), channel_id=1, source_target_pairs={{0,2},{1,3},{2,0},{3,1},{4,6},{5,7},{6,4},{7,5},{8,10},{9,11},{10,... | collective-permute-start | bytes 884744 | tf_op jit(solution)/shard_map/ppermute | solution.py:58
  3.7 23.5 %collective-permute-start.25 = (bf16[64,2304]{1,0:T(8,128)(2,1)}, bf16[64,2304]{1,0:T(8,128)(2,1)S(1)}, u32[]{:S(2)}, u32[]{:S(2)}) collective-permute-start(bf16[64,2304]{1,0:T(8,128)(2,1)} %bitcast.16.refs_0_), channel_id=1, source_target_pairs={{0,1},{1,0},{2,3},{3,2},{4,5},{5,4},{6,7},{7,6},{8,9},{9,8},{10,11... | collective-permute-start | bytes 884744 | tf_op jit(solution)/shard_map/ppermute | solution.py:58
  3.9 25.4 %collective-permute-start.26 = (bf16[64,2304]{1,0:T(8,128)(2,1)}, bf16[64,2304]{1,0:T(8,128)(2,1)S(1)}, u32[]{:S(2)}, u32[]{:S(2)}) collective-permute-start(bf16[64,2304]{1,0:T(8,128)(2,1)} %bitcast.16.refs_0_), channel_id=1, source_target_pairs={{0,2},{1,3},{2,0},{3,1},{4,6},{5,7},{6,4},{7,5},{8,10},{9,11},{10,... | collective-permute-start | bytes 884744 | tf_op jit(solution)/shard_map/ppermute | solution.py:58
  4.2 26.6 %collective-permute-start.17 = (bf16[64,2304]{1,0:T(8,128)(2,1)}, bf16[64,2304]{1,0:T(8,128)(2,1)}, u32[]{:S(2)}, u32[]{:S(2)}) collective-permute-start(bf16[64,2304]{1,0:T(8,128)(2,1)} %bitcast.16.refs_0_), channel_id=1, source_target_pairs={{0,8},{8,16},{16,24},{24,28},{28,20},{20,12},{12,4},{4,0},{1,9},{9... | collective-permute-start | bytes 884744 | tf_op jit(solution)/shard_map/ppermute | solution.py:49
  12.4 3.5 %copy-start.4 = (s32[8]{0:T(128)S(1)}, s32[8]{0:T(128)}, u32[]{:S(2)}) copy-start(s32[8]{0:T(128)} %constant.43.clone) | copy-start | bytes 100
  12.4 9.5 %copy-start.8 = (s32[8]{0:T(128)S(1)}, s32[8]{0:T(128)}, u32[]{:S(2)}) copy-start(s32[8]{0:T(128)} %param.15) | copy-start | bytes 100
  12.4 11.4 %copy-start.1 = (bf16[1,1,2304,256]{3,2,1,0:T(8,128)(2,1)S(1)}, bf16[1,1,2304,256]{3,2,1,0:T(8,128)(2,1)}, u32[]{:S(2)}) copy-start(bf16[1,1,2304,256]{3,2,1,0:T(8,128)(2,1)} %param.10) | copy-start | bytes 3538948
  25.0 30.2 %collective-permute-start.12 = (bf16[2304,256]{1,0:T(8,128)(2,1)S(1)}, bf16[2304,256]{1,0:T(8,128)(2,1)S(1)}, u32[]{:S(2)}, u32[]{:S(2)}) collective-permute-start(bf16[2304,256]{1,0:T(8,128)(2,1)S(1)} %bitcast.56), channel_id=1, source_target_pairs={{0,2},{1,3},{2,0},{3,1},{4,6},{5,7},{6,4},{7,5},{8,10},{9,11},{10,... | collective-permute-start | bytes 3538952 | tf_op jit(solution)/shard_map/ppermute | solution.py:58
  27.2 10.2 %collective-permute-start.21 = (bf16[64,2304]{1,0:T(8,128)(2,1)}, bf16[64,2304]{1,0:T(8,128)(2,1)S(1)}, u32[]{:S(2)}, u32[]{:S(2)}) collective-permute-start(bf16[64,2304]{1,0:T(8,128)(2,1)} %bitcast.16.refs_0_), channel_id=1, source_target_pairs={{8,0},{16,8},{24,16},{28,24},{20,28},{12,20},{4,12},{0,4},{9,1},{1... | collective-permute-start | bytes 884744 | tf_op jit(solution)/shard_map/ppermute | solution.py:50
  27.7 2.1 %copy-start.5 = (bf16[64,2304]{1,0:T(8,128)(2,1)}, bf16[64,2304]{1,0:T(8,128)(2,1)S(1)}, u32[]{:S(2)}) copy-start(bf16[64,2304]{1,0:T(8,128)(2,1)S(1)} %collective-permute-done.1) | copy-start | bytes 884740
  27.7 14.4 %collective-permute-start.7 = (bf16[64,2304]{1,0:T(8,128)(2,1)}, bf16[64,2304]{1,0:T(8,128)(2,1)S(1)}, u32[]{:S(2)}, u32[]{:S(2)}) collective-permute-start(bf16[64,2304]{1,0:T(8,128)(2,1)} %bitcast.7.refs_0_), channel_id=1, source_target_pairs={{8,0},{16,8},{24,16},{28,24},{20,28},{12,20},{4,12},{0,4},{9,1},{1... | collective-permute-start | bytes 884744 | tf_op jit(solution)/shard_map/ppermute | solution.py:50
  29.3 0.7 copy-start.6
  29.3 14.4 %collective-permute-start.3 = (bf16[64,2304]{1,0:T(8,128)(2,1)}, bf16[64,2304]{1,0:T(8,128)(2,1)S(1)}, u32[]{:S(2)}, u32[]{:S(2)}) collective-permute-start(bf16[64,2304]{1,0:T(8,128)(2,1)} %bitcast.7.refs_0_), channel_id=1, source_target_pairs={{0,8},{8,16},{16,24},{24,28},{28,20},{20,12},{12,4},{4,0},{1,9},{9... | collective-permute-start | bytes 884744 | tf_op jit(solution)/shard_map/ppermute | solution.py:49
  30.8 41.3 %copy-start.2 = (bf16[1,1,2304,256]{3,2,1,0:T(8,128)(2,1)S(1)}, bf16[1,1,2304,256]{3,2,1,0:T(8,128)(2,1)}, u32[]{:S(2)}) copy-start(bf16[1,1,2304,256]{3,2,1,0:T(8,128)(2,1)} %param.9) | copy-start | bytes 3538948
  30.8 14.4 %collective-permute-start.2 = (bf16[64,2304]{1,0:T(8,128)(2,1)}, bf16[64,2304]{1,0:T(8,128)(2,1)S(1)}, u32[]{:S(2)}, u32[]{:S(2)}) collective-permute-start(bf16[64,2304]{1,0:T(8,128)(2,1)} %copy-done.5), channel_id=1, source_target_pairs={{0,1},{1,0},{2,3},{3,2},{4,5},{5,4},{6,7},{7,6},{8,9},{9,8},{10,11... | collective-permute-start | bytes 884744 | tf_op jit(solution)/shard_map/ppermute | solution.py:58
  37.4 7.9 %collective-permute-start.27 = (bf16[64,2304]{1,0:T(8,128)(2,1)}, bf16[64,2304]{1,0:T(8,128)(2,1)S(1)}, u32[]{:S(2)}, u32[]{:S(2)}) collective-permute-start(bf16[64,2304]{1,0:T(8,128)(2,1)} %copy-done.6), channel_id=1, source_target_pairs={{0,1},{1,0},{2,3},{3,2},{4,5},{5,4},{6,7},{7,6},{8,9},{9,8},{10,11... | collective-permute-start | bytes 884744 | tf_op jit(solution)/shard_map/ppermute | solution.py:58
  42.2 7.7 %collective-permute-start.18 = (bf16[64,2304]{1,0:T(8,128)(2,1)}, bf16[64,2304]{1,0:T(8,128)(2,1)S(1)}, u32[]{:S(2)}, u32[]{:S(2)}) collective-permute-start(bf16[64,2304]{1,0:T(8,128)(2,1)} %collective-permute-done.17.refs_1_), channel_id=1, source_target_pairs={{0,8},{8,16},{16,24},{24,28},{28,20},{20,12},{12,4},{4,0},{1,9},{9... | collective-permute-start | bytes 884744 | tf_op jit(solution)/shard_map/ppermute | solution.py:49
  43.8 9.8 %collective-permute-start.22 = (bf16[64,2304]{1,0:T(8,128)(2,1)S(1)}, bf16[64,2304]{1,0:T(8,128)(2,1)S(1)}, u32[]{:S(2)}, u32[]{:S(2)}) collective-permute-start(bf16[64,2304]{1,0:T(8,128)(2,1)S(1)} %collective-permute-done.21.refs_7_), channel_id=1, source_target_pairs={{8,0},{16,8},{24,16},{28,24},{20,28},{12,20},{4,12},{0,4},{9,1},{1... | collective-permute-start | bytes 884744 | tf_op jit(solution)/shard_map/ppermute | solution.py:50
  45.2 40.0 %collective-permute-start.11 = (bf16[2304,256]{1,0:T(8,128)(2,1)S(1)}, bf16[2304,256]{1,0:T(8,128)(2,1)S(1)}, u32[]{:S(2)}, u32[]{:S(2)}) collective-permute-start(bf16[2304,256]{1,0:T(8,128)(2,1)S(1)} %bitcast.57), channel_id=1, source_target_pairs={{0,1},{1,0},{2,3},{3,2},{4,5},{5,4},{6,7},{7,6},{8,9},{9,8},{10,11... | collective-permute-start | bytes 3538952 | tf_op jit(solution)/shard_map/ppermute | solution.py:58
  45.3 12.0 %collective-permute-start.8 = (bf16[64,2304]{1,0:T(8,128)(2,1)S(1)}, bf16[64,2304]{1,0:T(8,128)(2,1)S(1)}, u32[]{:S(2)}, u32[]{:S(2)}) collective-permute-start(bf16[64,2304]{1,0:T(8,128)(2,1)S(1)} %collective-permute-done.7.refs_7_), channel_id=1, source_target_pairs={{8,0},{16,8},{24,16},{28,24},{20,28},{12,20},{4,12},{0,4},{9,1},{1... | collective-permute-start | bytes 884744 | tf_op jit(solution)/shard_map/ppermute | solution.py:50
  49.9 9.7 %collective-permute-start.4 = (bf16[64,2304]{1,0:T(8,128)(2,1)S(1)}, bf16[64,2304]{1,0:T(8,128)(2,1)S(1)}, u32[]{:S(2)}, u32[]{:S(2)}) collective-permute-start(bf16[64,2304]{1,0:T(8,128)(2,1)S(1)} %collective-permute-done.3.refs_1_), channel_id=1, source_target_pairs={{0,8},{8,16},{16,24},{24,28},{28,20},{20,12},{12,4},{4,0},{1,9},{9... | collective-permute-start | bytes 884744 | tf_op jit(solution)/shard_map/ppermute | solution.py:49
  53.6 9.8 %collective-permute-start.19 = (bf16[64,2304]{1,0:T(8,128)(2,1)S(1)}, bf16[64,2304]{1,0:T(8,128)(2,1)S(1)}, u32[]{:S(2)}, u32[]{:S(2)}) collective-permute-start(bf16[64,2304]{1,0:T(8,128)(2,1)S(1)} %collective-permute-done.18.refs_2_), channel_id=1, source_target_pairs={{0,8},{8,16},{16,24},{24,28},{28,20},{20,12},{12,4},{4,0},{1,9},{9... | collective-permute-start | bytes 884744 | tf_op jit(solution)/shard_map/ppermute | solution.py:49
  55.2 30.0 %collective-permute-start.13 = (bf16[2304,256]{1,0:T(8,128)(2,1)S(1)}, bf16[2304,256]{1,0:T(8,128)(2,1)S(1)}, u32[]{:S(2)}, u32[]{:S(2)}) collective-permute-start(bf16[2304,256]{1,0:T(8,128)(2,1)S(1)} %collective-permute-done.12.refs_11_), channel_id=1, source_target_pairs={{0,1},{1,0},{2,3},{3,2},{4,5},{5,4},{6,7},{7,6},{8,9},{9,8},{10,11... | collective-permute-start | bytes 3538952 | tf_op jit(solution)/shard_map/ppermute | solution.py:58
  57.3 9.9 %collective-permute-start.23 = (bf16[64,2304]{1,0:T(8,128)(2,1)S(1)}, bf16[64,2304]{1,0:T(8,128)(2,1)S(1)}, u32[]{:S(2)}, u32[]{:S(2)}) collective-permute-start(bf16[64,2304]{1,0:T(8,128)(2,1)S(1)} %collective-permute-done.22.refs_6_), channel_id=1, source_target_pairs={{8,0},{16,8},{24,16},{28,24},{20,28},{12,20},{4,12},{0,4},{9,1},{1... | collective-permute-start | bytes 884744 | tf_op jit(solution)/shard_map/ppermute | solution.py:50
  59.6 12.0 %collective-permute-start.9 = (bf16[64,2304]{1,0:T(8,128)(2,1)S(1)}, bf16[64,2304]{1,0:T(8,128)(2,1)S(1)}, u32[]{:S(2)}, u32[]{:S(2)}) collective-permute-start(bf16[64,2304]{1,0:T(8,128)(2,1)S(1)} %collective-permute-done.8.refs_6_), channel_id=1, source_target_pairs={{8,0},{16,8},{24,16},{28,24},{20,28},{12,20},{4,12},{0,4},{9,1},{1... | collective-permute-start | bytes 884744 | tf_op jit(solution)/shard_map/ppermute | solution.py:50
  63.4 11.2 %collective-permute-start.5 = (bf16[64,2304]{1,0:T(8,128)(2,1)S(1)}, bf16[64,2304]{1,0:T(8,128)(2,1)S(1)}, u32[]{:S(2)}, u32[]{:S(2)}) collective-permute-start(bf16[64,2304]{1,0:T(8,128)(2,1)S(1)} %collective-permute-done.4.refs_2_), channel_id=1, source_target_pairs={{0,8},{8,16},{16,24},{24,28},{28,20},{20,12},{12,4},{4,0},{1,9},{9... | collective-permute-start | bytes 884744 | tf_op jit(solution)/shard_map/ppermute | solution.py:49
  67.3 7.8 %collective-permute-start.20 = (bf16[32,2304]{1,0:T(8,128)(2,1)S(1)}, bf16[32,2304]{1,0:T(8,128)(2,1)S(1)}, u32[]{:S(2)}, u32[]{:S(2)}) collective-permute-start(bf16[32,2304]{1,0:T(8,128)(2,1)S(1)} %slice.74), channel_id=1, source_target_pairs={{0,8},{8,16},{16,24},{24,28},{28,20},{20,12},{12,4},{4,0},{1,9},{9... | collective-permute-start | bytes 442376 | tf_op jit(solution)/shard_map/ppermute | solution.py:53
  71.7 6.6 %collective-permute-start.24 = (bf16[32,2304]{1,0:T(8,128)(2,1)S(1)}, bf16[32,2304]{1,0:T(8,128)(2,1)S(1)}, u32[]{:S(2)}, u32[]{:S(2)}) collective-permute-start(bf16[32,2304]{1,0:T(8,128)(2,1)S(1)} %slice.75), channel_id=1, source_target_pairs={{8,0},{16,8},{24,16},{28,24},{20,28},{12,20},{4,12},{0,4},{9,1},{1... | collective-permute-start | bytes 442376 | tf_op jit(solution)/shard_map/ppermute | solution.py:53
  74.6 8.8 %collective-permute-start.10 = (bf16[32,2304]{1,0:T(8,128)(2,1)S(1)}, bf16[32,2304]{1,0:T(8,128)(2,1)S(1)}, u32[]{:S(2)}, u32[]{:S(2)}) collective-permute-start(bf16[32,2304]{1,0:T(8,128)(2,1)S(1)} %slice.73), channel_id=1, source_target_pairs={{8,0},{16,8},{24,16},{28,24},{20,28},{12,20},{4,12},{0,4},{9,1},{1... | collective-permute-start | bytes 442376 | tf_op jit(solution)/shard_map/ppermute | solution.py:53
  75.1 8.8 %collective-permute-start.6 = (bf16[32,2304]{1,0:T(8,128)(2,1)S(1)}, bf16[32,2304]{1,0:T(8,128)(2,1)S(1)}, u32[]{:S(2)}, u32[]{:S(2)}) collective-permute-start(bf16[32,2304]{1,0:T(8,128)(2,1)S(1)} %slice.72), channel_id=1, source_target_pairs={{0,8},{8,16},{16,24},{24,28},{28,20},{20,12},{12,4},{4,0},{1,9},{9... | collective-permute-start | bytes 442376 | tf_op jit(solution)/shard_map/ppermute | solution.py:53
  83.3 7.5 %collective-permute-start.28 = (bf16[64,256]{1,0:T(8,128)(2,1)S(1)}, bf16[64,256]{1,0:T(8,128)(2,1)S(1)}, u32[]{:S(2)}, u32[]{:S(2)}) collective-permute-start(bf16[64,256]{1,0:T(8,128)(2,1)S(1)} %get-tuple-element.22), channel_id=1, source_target_pairs={{0,1},{1,0},{2,3},{3,2},{4,5},{5,4},{6,7},{7,6},{8,9},{9,8},{10,11... | collective-permute-start | bytes 98312 | tf_op jit(solution)/shard_map/ppermute | solution.py:58
  83.3 8.6 %collective-permute-start.29 = (bf16[64,256]{1,0:T(8,128)(2,1)S(1)}, bf16[64,256]{1,0:T(8,128)(2,1)S(1)}, u32[]{:S(2)}, u32[]{:S(2)}) collective-permute-start(bf16[64,256]{1,0:T(8,128)(2,1)S(1)} %get-tuple-element.21), channel_id=1, source_target_pairs={{0,2},{1,3},{2,0},{3,1},{4,6},{5,7},{6,4},{7,5},{8,10},{9,11},{10,... | collective-permute-start | bytes 98312 | tf_op jit(solution)/shard_map/ppermute | solution.py:58
  83.9 13.3 %collective-permute-start.30 = (bf16[64,256]{1,0:T(8,128)(2,1)}, bf16[64,256]{1,0:T(8,128)(2,1)S(1)}, u32[]{:S(2)}, u32[]{:S(2)}) collective-permute-start(bf16[64,256]{1,0:T(8,128)(2,1)} %get-tuple-element.20), channel_id=1, source_target_pairs={{0,3},{1,2},{2,1},{3,0},{4,7},{5,6},{6,5},{7,4},{8,11},{9,10},{10,... | collective-permute-start | bytes 98312 | tf_op jit(solution)/shard_map/ppermute | solution.py:58
  89.4 17.0 %collective-permute-start.14 = (bf16[64,2304]{1,0:T(8,128)(2,1)}, bf16[64,2304]{1,0:T(8,128)(2,1)S(1)}, u32[]{:S(2)}, u32[]{:S(2)}) collective-permute-start(bf16[64,2304]{1,0:T(8,128)(2,1)} %get-tuple-element.14), channel_id=1, source_target_pairs={{0,1},{1,0},{2,3},{3,2},{4,5},{5,4},{6,7},{7,6},{8,9},{9,8},{10,11... | collective-permute-start | bytes 884744 | tf_op jit(solution)/shard_map/ppermute | solution.py:58
  89.7 16.7 %collective-permute-start.15 = (bf16[64,2304]{1,0:T(8,128)(2,1)}, bf16[64,2304]{1,0:T(8,128)(2,1)S(1)}, u32[]{:S(2)}, u32[]{:S(2)}) collective-permute-start(bf16[64,2304]{1,0:T(8,128)(2,1)} %get-tuple-element.13), channel_id=1, source_target_pairs={{0,2},{1,3},{2,0},{3,1},{4,6},{5,7},{6,4},{7,5},{8,10},{9,11},{10,... | collective-permute-start | bytes 884744 | tf_op jit(solution)/shard_map/ppermute | solution.py:58
  90.8 15.6 %collective-permute-start.16 = (bf16[64,2304]{1,0:T(8,128)(2,1)}, bf16[64,2304]{1,0:T(8,128)(2,1)}, u32[]{:S(2)}, u32[]{:S(2)}) collective-permute-start(bf16[64,2304]{1,0:T(8,128)(2,1)} %get-tuple-element.12), channel_id=1, source_target_pairs={{0,3},{1,2},{2,1},{3,0},{4,7},{5,6},{6,5},{7,4},{8,11},{9,10},{10,... | collective-permute-start | bytes 884744 | tf_op jit(solution)/shard_map/ppermute | solution.py:58
  91.9 5.7 %copy-start.7 = (bf16[64,256]{1,0:T(8,128)(2,1)S(1)}, bf16[64,256]{1,0:T(8,128)(2,1)}, u32[]{:S(2)}) copy-start(bf16[64,256]{1,0:T(8,128)(2,1)} %get-tuple-element.16) | copy-start | bytes 98308
  91.9 5.7 %collective-permute-start.31 = (bf16[64,256]{1,0:T(8,128)(2,1)}, bf16[64,256]{1,0:T(8,128)(2,1)S(1)}, u32[]{:S(2)}, u32[]{:S(2)}) collective-permute-start(bf16[64,256]{1,0:T(8,128)(2,1)} %get-tuple-element.18), channel_id=1, source_target_pairs={{0,1},{1,0},{2,3},{3,2},{4,5},{5,4},{6,7},{7,6},{8,9},{9,8},{10,11... | collective-permute-start | bytes 98312 | tf_op jit(solution)/shard_map/ppermute | solution.py:58
  97.2 9.3 %copy-start.3 = (f32[256,256]{1,0:T(8,128)S(1)}, f32[256,256]{1,0:T(8,128)}, u32[]{:S(2)}) copy-start(f32[256,256]{1,0:T(8,128)} %fusion.3.cu_ref) | copy-start | bytes 786436
  97.2 9.3 %collective-permute-start.32 = (bf16[64,256]{1,0:T(8,128)(2,1)}, bf16[64,256]{1,0:T(8,128)(2,1)S(1)}, u32[]{:S(2)}, u32[]{:S(2)}) collective-permute-start(bf16[64,256]{1,0:T(8,128)(2,1)} %get-tuple-element.17), channel_id=1, source_target_pairs={{0,2},{1,3},{2,0},{3,1},{4,6},{5,7},{6,4},{7,5},{8,10},{9,11},{10,... | collective-permute-start | bytes 98312 | tf_op jit(solution)/shard_map/ppermute | solution.py:58
  97.7 8.8 %collective-permute-start.33 = (bf16[64,256]{1,0:T(8,128)(2,1)S(1)}, bf16[64,256]{1,0:T(8,128)(2,1)S(1)}, u32[]{:S(2)}, u32[]{:S(2)}) collective-permute-start(bf16[64,256]{1,0:T(8,128)(2,1)S(1)} %copy-done.7), channel_id=1, source_target_pairs={{0,3},{1,2},{2,1},{3,0},{4,7},{5,6},{6,5},{7,4},{8,11},{9,10},{10,... | collective-permute-start | bytes 98312 | tf_op jit(solution)/shard_map/ppermute | solution.py:58

commit v2 on v1

v2 whole, which is shorter than its diff:
```python
import functools
import math

import jax
import jax.numpy as jnp
from jax import lax
from jax.experimental import pallas as pl
from jax.experimental.pallas import tpu as pltpu
from jax.sharding import PartitionSpec as P

F32 = jnp.float32
BF16 = jnp.bfloat16
HIGHEST = lax.Precision.HIGHEST
VMEM = pl.BlockSpec(memory_space=pltpu.VMEM)
SMEM = pl.BlockSpec(memory_space=pltpu.SMEM)
ANY = pl.BlockSpec(memory_space=pl.ANY)
ROUGH, FINE = 0.05, 0.015
ROUGH_STEPS, FINE_STEPS = 12, 6


def nn(a, b, precision=None):
    return lax.dot_general(a, b, (((1,), (0,)), ((), ())), precision=precision, preferred_element_type=F32)


def nt(a, b, precision=None):
    return lax.dot_general(a, b, (((1,), (1,)), ((), ())), precision=precision, preferred_element_type=F32)


def tn(a, b, precision=None):
    return lax.dot_general(a, b, (((0,), (0,)), ((), ())), precision=precision, preferred_element_type=F32)


def halves(x):
    high = x.astype(BF16)
    return high, (x - high.astype(F32)).astype(BF16)


def after(x, *others):
    return lax.optimization_barrier((x, *others))[0]


def ring_place(r, n):
    return jnp.where(r % 2 == 0, r // 2, n - 1 - r // 2)


def ring_steps(n):
    ring = list(range(0, n, 2)) + list(range(n - 1, 0, -2))
    ahead = [(ring[i], ring[(i + 1) % n]) for i in range(n)]
    return ahead, [(b, a) for a, b in ahead]


def ring_gathers(left, right, axis, n, early):
    ahead, back = ring_steps(n)
    send = lambda x, way: lax.ppermute(x, axis, way)
    low = left.shape[0] // 2
    lefts, rights = [left] + [None] * (n - 1), []
    for h in range(2):
        rights.append([right[h * low : (h + 1) * low]] + [None] * (n - 1))

    def right_step(h, s, gate):
        r = rights[h]
        if s < n // 2:
            r[s] = send(after(r[s - 1], *gate), ahead)
            r[n - s] = send(after(r[(n - s + 1) % n], *gate), back)
            return (r[s], r[n - s])
        r[s] = send(after(r[s + 1], *gate), back)
        return (r[s],)

    turns = [(h, s) for s in range(1, n // 2 + 1) for h in range(2)]
    before, beside = (), ()
    for s in range(1, n // 2 + 1):
        gate = beside
        if s >= 3 and early:
            gate = (*gate, *early[0]())
            early = early[1:]
        lefts[s] = send(after(lefts[s - 1], *gate), ahead)
        if s < n // 2:
            lefts[n - s] = send(after(lefts[(n - s + 1) % n], *gate), back)
        if s >= 2:
            beside = right_step(*turns.pop(0), before)
        before = (lefts[s],) if s == n // 2 else (lefts[s], lefts[n - s])
    return lefts, rights, lambda gate: right_rest(turns, right_step, gate)


def right_rest(turns, right_step, gate):
    for at, turn in enumerate(turns):
        right_step(*turn, gate if at else ())


def swap(x, axis, n, m):
    return lax.ppermute(x, axis, [(i, i ^ m) for i in range(n)])


def xor_gather(x, axis, n):
    have = {0: x}
    bit = n // 2
    while bit:
        for m in list(have):
            have[m | bit] = swap(have[m], axis, n, bit)
        bit //= 2
    return [have[m] for m in range(n)]


def owner_steps(n_row, n_col, owner):
    row, col = lax.axis_index("row"), lax.axis_index("col")
    here = ring_place(row, n_row)
    return [lax.rem(here - ring_place(owner[col ^ m], n_row) + n_row, n_row) for m in range(n_col)]


def pick_left(n_row, n_col, owner, *refs):
    pieces, outs, sem = refs[:n_row], refs[n_row:-1], refs[-1]
    steps = owner_steps(n_row, n_col, owner)
    for m in range(n_col):
        for k in range(n_row):

            @pl.when(steps[m] == k)
            def _():
                pltpu.make_async_copy(pieces[k], outs[m], sem.at[m]).start()

    for m in range(n_col):
        pltpu.make_async_copy(pieces[0], outs[m], sem.at[m]).wait()


def picked_left(pieces, owner, n_row, n_col):
    shard, width = pieces[0].shape
    return pl.pallas_call(
        functools.partial(pick_left, n_row, n_col),
        out_shape=[jax.ShapeDtypeStruct((shard, width), BF16)] * n_col,
        in_specs=[SMEM] + [ANY] * n_row,
        out_specs=[VMEM] * n_col,
        scratch_shapes=[pltpu.SemaphoreType.DMA((n_col,))],
        cost_estimate=pl.CostEstimate(flops=0, bytes_accessed=3 << 20, transcendentals=0),
        name="pick_left",
    )(owner, *pieces)


def couple(n_row, n_col, owner, *refs):
    pieces = refs[: 2 * n_row]
    parts = refs[2 * n_row : 2 * n_row + n_col]
    outs = refs[2 * n_row + n_col : 2 * n_row + 2 * n_col]
    picked, mine, sem, sem2 = refs[2 * n_row + 2 * n_col :]
    shard = outs[0].shape[0]
    low = shard // 2
    col = lax.axis_index("col")
    steps = owner_steps(n_row, n_col, owner)

    def copies(m, k):
        return (
            pltpu.make_async_copy(pieces[k], picked.at[pl.ds(m * shard, low)], sem.at[m]),
            pltpu.make_async_copy(pieces[n_row + k], picked.at[pl.ds(m * shard + low, low)], sem2.at[m]),
        )

    for m in range(n_col):
        for k in range(n_row):

            @pl.when(steps[m] == k)
            def _():
                a, b = copies(m, k)
                a.start()
                b.start()

    for m in range(n_col):
        at = pl.ds(pl.multiple_of((col ^ m) * shard, shard), shard)
        mine[at, :] = parts[m][...]
    for m in range(n_col):
        a, b = copies(m, 0)
        a.wait()
        b.wait()
    product = nt(picked[...], mine[...]).astype(BF16)
    for m in range(n_col):
        outs[m][...] = product[m * shard : (m + 1) * shard]


def coupled(halves_, parts, owner, n_row, n_col):
    shard, width = parts[0].shape
    rank = n_col * shard
    return pl.pallas_call(
        functools.partial(couple, n_row, n_col),
        out_shape=[jax.ShapeDtypeStruct((shard, rank), BF16)] * n_col,
        in_specs=[SMEM] + [ANY] * (2 * n_row) + [VMEM] * n_col,
        out_specs=[VMEM] * n_col,
        scratch_shapes=[
            pltpu.VMEM((rank, width), BF16),
            pltpu.VMEM((rank, width), BF16),
            pltpu.SemaphoreType.DMA((n_col,)),
            pltpu.SemaphoreType.DMA((n_col,)),
        ],
        compiler_params=pltpu.CompilerParams(vmem_limit_bytes=32 << 20),
        cost_estimate=pl.CostEstimate(flops=2 * rank * rank * width, bytes_accessed=3 << 20, transcendentals=0),
        name="coupling",
    )(owner, *halves_[0], *halves_[1], *parts)


def grams(n_col, u_ref, v_ref, *refs):
    parts, (uit, h_ref, cu_ref) = refs[:n_col], refs[n_col:]
    rank = cu_ref.shape[0]
    shard = rank // n_col
    col = lax.axis_index("col")
    for m in range(n_col):
        at = pl.ds(pl.multiple_of((col ^ m) * shard, shard), shard)
        uit[at, :] = parts[m][...]
    top, bottom = pl.ds(0, rank), pl.ds(rank, rank)
    cu_ref[...] = tn(v_ref[...], v_ref[...])
    h_ref[top, :rank] = tn(u_ref[...], u_ref[...])
    cross = nn(uit[...], u_ref[...])
    h_ref[bottom, :rank] = cross
    h_ref[top, rank:] = cross.T
    h_ref[bottom, rank:] = nt(uit[...], uit[...])


def gram_products(u, v, parts, n_col):
    rows, rank = u.shape
    return pl.pallas_call(
        functools.partial(grams, n_col),
        out_shape=[
            jax.ShapeDtypeStruct((rank, rows), BF16),
            jax.ShapeDtypeStruct((2 * rank, 2 * rank), F32),
            jax.ShapeDtypeStruct((rank, rank), F32),
        ],
        in_specs=[VMEM] * (2 + n_col),
        out_specs=[VMEM] * 3,
        compiler_params=pltpu.CompilerParams(vmem_limit_bytes=40 << 20),
        cost_estimate=pl.CostEstimate(flops=8 * rank * rank * rows, bytes_accessed=6 << 20, transcendentals=0),
        name="grams",
    )(u, v, *parts)


def lower_half(e, eye, below):
    return jnp.where(below, e, jnp.where(eye, 0.5 * e, 0.0))


def finish(n_col, old_ref, goal_ref, panel, owner, u_ref, v_ref, uit_ref, h_ref, cu_ref, *refs):
    ujt_in, kt_in = refs[:n_col], refs[n_col : 2 * n_col]
    q_ref, w_ref, ujt, kt, mf, hm, gn, y_ref, a_ref = refs[2 * n_col :]
    rows, rank = u_ref.shape
    shard = rank // n_col
    row, col = lax.axis_index("row"), lax.axis_index("col")
    old, goal, here, there = old_ref[0, 0], goal_ref[0, 0], panel[row], panel[owner[col]]
    sub = lax.broadcasted_iota(jnp.int32, (rank, rank), 0)
    lane = lax.broadcasted_iota(jnp.int32, (rank, rank), 1)
    eye, below = sub == lane, sub > lane
    one = jnp.where(eye, 1.0, 0.0).astype(F32)
    for m in range(n_col):
        at = pl.ds(pl.multiple_of((col ^ m) * shard, shard), shard)
        kt[at, :] = kt_in[m][...]
        ujt[at, :] = ujt_in[m][...]
    zero = jnp.zeros((rank, rank), F32)
    kt[...] = jnp.where((sub < there) & (lane < here), kt[...].astype(F32), zero).astype(BF16)
    cl = jnp.where(lane < goal, nn(ujt[...], v_ref[...]), zero).astype(BF16)
    cu = jnp.where((sub < old) & (lane < goal), cu_ref[...], zero).astype(BF16).astype(F32)
    mf[pl.ds(0, rank), :] = cu
    mf[pl.ds(rank, rank), :] = -tn(kt[...], cl)
    hm[...] = nn(h_ref[...], mf[...], HIGHEST)
    g = tn(mf[...], hm[...], HIGHEST) + jnp.where(eye & (lane >= goal), 1.0, 0.0)
    dg = jnp.where(eye, g, 0.0)
    d_row = lax.rsqrt(jnp.sum(dg, axis=0, keepdims=True))
    d_col = lax.rsqrt(jnp.sum(dg, axis=1, keepdims=True))
    gn[...] = g * d_col * d_row
    scale = rank / jnp.sum(gn[...] * gn[...], keepdims=True)
    y_ref[...] = (one - lower_half(gn[...] * scale - one, eye, below)) * jnp.sqrt(scale)
    gb = gn[...].astype(BF16)

    def rough(carry):
        step, _ = carry
        y = y_ref[...]
        yb = y.astype(BF16)
        e = nt(nn(yb, gb).astype(BF16), yb) - one
        y_ref[...] = y - nn(lower_half(e, eye, below).astype(BF16), yb)
        return step + 1, jnp.max(jnp.abs(e))

    def fine(carry):
        step, _ = carry
        y = y_ref[...]
        e = nt(nn(y, gn[...], HIGHEST), y, HIGHEST) - one
        y_ref[...] = y - nn(lower_half(e, eye, below), y, HIGHEST)
        return step + 1, jnp.max(jnp.abs(e))

    lax.while_loop(lambda c: (c[0] < ROUGH_STEPS) & (c[1] > ROUGH), rough, (jnp.int32(0), F32(1.0)))
    _, err = lax.while_loop(lambda c: (c[0] < FINE_STEPS) & (c[1] > FINE), fine, (jnp.int32(0), F32(1.0)))

    lowest = jnp.min(jnp.where(eye, y_ref[...], 1.0))

    @pl.when(jnp.logical_not((err <= FINE) & (lowest > 0.0)))
    def _():
        a_ref[...] = gn[...]
        y_ref[...] = one

        def pivot(k, _):
            col = jnp.sum(jnp.where(lane == k, a_ref[...], 0.0), axis=1, keepdims=True)
            row = jnp.sum(jnp.where(sub == k, a_ref[...], 0.0), axis=0, keepdims=True)
            yrow = jnp.sum(jnp.where(sub == k, y_ref[...], 0.0), axis=0, keepdims=True)
            top = jnp.sum(jnp.where(lax.broadcasted_iota(jnp.int32, (1, rank), 1) == k, row, 0.0))
            inv = 1.0 / jnp.sqrt(jnp.full((1, rank), top))
            row, yrow = row * inv, yrow * inv
            col = jnp.where(lax.broadcasted_iota(jnp.int32, (rank, 1), 0) > k, col * inv[:, :1], 0.0)
            a_ref[...] = a_ref[...] - col * row
            y_ref[...] = jnp.where(sub == k, yrow, y_ref[...] - col * yrow)
            return 0

        lax.fori_loop(0, rank, pivot, 0)

    x = y_ref[...] * d_row
    root = math.sqrt(rows)
    c = nt(mf[...], x, HIGHEST) * root
    r = nt(hm[...], x, HIGHEST)
    r_up = jnp.where(sub < old, r[:rank], 0.0).astype(BF16)
    r_low = (-nn(kt[...].astype(F32), r[rank:], HIGHEST)).astype(BF16)
    ch, cl2 = halves(c)
    cu_h, cu_l, cl_h, cl_l = ch[:rank], cl2[:rank], ch[rank:], cl2[rank:]
    step = 256 if rows % 256 == 0 else rows
    for t in range(rows // step):
        at = pl.ds(t * step, step)
        u, v = u_ref[at, :], v_ref[at, :]
        ui, uj = uit_ref[:, at], ujt[:, at]
        q_ref[at, :] = (nn(u, cu_h) + nn(u, cu_l) + tn(ui, cl_h) + tn(ui, cl_l)).astype(BF16)
        w_ref[at, :] = (nn(v, r_up) + tn(uj, r_low)).astype(BF16)


def body(tile_basis, tile_coeffs, panel_basis, panel_coeffs, tile_rank, target_rank, panel_rank, owner_row):
    n_row, n_col = lax.axis_size("row"), lax.axis_size("col")
    u, v = tile_basis[0, 0], tile_coeffs[0, 0]
    pu, pv = panel_basis[0], panel_coeffs[0]
    rows, rank = u.shape

    parts = {}

    def left_parts():
        parts["left"] = xor_gather(pu, "col", n_col)
        return parts["left"]

    def right_parts():
        parts["right"] = xor_gather(after(pv, *parts["left"]), "col", n_col)
        return parts["right"]

    us, vs, rest = ring_gathers(pu, pv, "row", n_row, [left_parts, right_parts])
    ui_parts, vi_parts = parts["left"], parts["right"]
    uit, h, core_up = gram_products(u, v, ui_parts, n_col)
    rest((core_up,))

    ujs = picked_left(us, owner_row, n_row, n_col)
    ujs = [ujs[0]] + [swap(ujs[m], "col", n_col, m) for m in range(1, n_col)]
    kts = coupled(vs, vi_parts, owner_row, n_row, n_col)
    kts = [kts[0]] + [swap(kts[m], "col", n_col, m) for m in range(1, n_col)]

    out = jax.ShapeDtypeStruct((rows, rank), BF16)
    square = pltpu.VMEM((rank, rank), F32)
    fresh_basis, fresh_coeffs = pl.pallas_call(
        functools.partial(finish, n_col),
        out_shape=(out, out),
        in_specs=[SMEM] * 4 + [VMEM] * (5 + 2 * n_col),
        out_specs=(VMEM, VMEM),
        scratch_shapes=[
            pltpu.VMEM((rank, rows), BF16),
            pltpu.VMEM((rank, rank), BF16),
            pltpu.VMEM((2 * rank, rank), F32),
            pltpu.VMEM((2 * rank, rank), F32),
            square,
            square,
            square,
        ],
        compiler_params=pltpu.CompilerParams(vmem_limit_bytes=48 << 20),
        cost_estimate=pl.CostEstimate(flops=8 << 30, bytes_accessed=12 << 20, transcendentals=0),
        name="finish",
    )(tile_rank, target_rank, panel_rank, owner_row, u, v, uit, h, core_up, *ujs, *kts)
    return fresh_basis[None, None], fresh_coeffs[None, None]


def solution(mesh):
    tiles, panels = P("row", "col", None, None), P("row", "col", None)
    return jax.shard_map(
        body,
        mesh=mesh,
        in_specs=(tiles, tiles, panels, panels, P("row", "col"), P("row", "col"), P(), P()),
        out_specs=(tiles, tiles),
        check_vma=False,
    )
```

time: 180 us -> 153 us (0.85)
  waiting for transfers between devices: 37.4 us -> 27.3 us
  matrix products: 9.61 us -> 0 us
  local copies, waits for them, and re-layouts: 16.1 us -> 9.01 us
  other arithmetic: 4.37 us -> 0 us
  starting transfers between devices: 27.5 us -> 31.5 us
    ppermute x16 -> x21, waiting for transfers between devices: 30.8 us -> 21 us  [ring_gathers(): send = lambda x, way: lax.ppermute(x, axis, way)]
    dot_general x4 -> x0, matrix products: 9.61 us -> none  [the longest x2 4.26 us: tn(): lax.dot_general(a, b, (((0,), (0,)), ((), ())), precision=precision, pref...]
    unnamed x18 -> x38, local copies, waits for them, and re-layouts: 0.25 us -> 8.01 us
    ppermute x16 -> x21, starting transfers between devices: 16.7 us -> 23 us  [ring_gathers(): send = lambda x, way: lax.ppermute(x, axis, way)]
    dynamic_update_slice x8 -> x0, local copies, waits for them, and re-layouts: 5.96 us -> none  [the longest x4 3.86 us: body(): uit = lax.dynamic_update_slice(uit, ui_parts[m], ((col ^ m) * shard, 0))]
    another operation x3 -> x0, local copies, waits for them, and re-layouts: 2.47 us -> none  [the longest x1 1.26 us: body(): jnp.stack([tile_rank[0, 0], target_rank[0, 0], panel_rank[row], panel_ran...]
    select_n x3 -> x0, other arithmetic: 2.4 us -> none  [the longest x2 1.89 us: body(): index = (place[row] - place[owners] + n_row) % n_row]
    ppermute x18 -> x12, starting transfers between devices: 10.7 us -> 8.48 us  [swap(): return lax.ppermute(x, axis, [(i, i ^ m) for i in range(n)])]
  transfers between devices with their start and end apart: 34 -> 33, of which waited for: 11 -> 10; matrix products, arithmetic and copies ran while one was open for 17% -> 1% of each run, Pallas kernels for 4% -> 5%
where the time goes in v2:
time: 153 us; the launch traced here: 152 us
  Pallas kernels  82 us (54%)
  starting transfers between devices  31.5 us (21%)
  waiting for transfers between devices  27.3 us (18%)
  local copies, waits for them, and re-layouts  9.01 us (6%)
  between operations  2.12 us (1%)
    pallas_call x1, Pallas kernels, body(): pl.pallas_call(functools.partial(finish, n_col), out_shape=(out, out), in...  74.4 us
    ppermute x21, starting transfers between devices, ring_gathers(): send = lambda x, way: lax.ppermute(x, axis, way)  23 us
    ppermute x21, waiting for transfers between devices, ring_gathers(): send = lambda x, way: lax.ppermute(x, axis, way)  21 us
    ppermute x12, starting transfers between devices, swap(): return lax.ppermute(x, axis, [(i, i ^ m) for i in range(n)])  8.48 us
    unnamed x38, local copies, waits for them, and re-layouts  8.01 us
    ppermute x12, waiting for transfers between devices, swap(): return lax.ppermute(x, axis, [(i, i ^ m) for i in range(n)])  6.36 us
    pallas_call x1, Pallas kernels, coupled(): pl.pallas_call(functools.partial(couple, n_row, n_col), out_shape=[jax.Sh...  3.09 us
  transfers between devices with their start and end apart: 33, of which 10 were waited for; matrix products, arithmetic and copies ran while one was open for 1% of the time, Pallas kernels for 5%

profile of v2, /device:TPU:0, one launch (start us, length us, event | category | flops | bytes accessed | tf_op | source)
XLA Modules:
  0.0 151.9 jit_solution(9428131504931031439)
XLA Ops:
  0.6 3.0 %collective-permute-start.1 = (bf16[64,2304]{1,0:T(8,128)(2,1)}, bf16[64,2304]{1,0:T(8,128)(2,1)S(1)}, u32[]{:S(2)}, u32[]{:S(2)}) collective-permute-start(bf16[64,2304]{1,0:T(8,128)(2,1)} %bitcast.13), channel_id=1, source_target_pairs={{0,2},{1,3},{2,0},{3,1},{4,6},{5,7},{6,4},{7,5},{8,10},{9,11},{10,... | collective-permute-start | bytes 884744 | tf_op jit(solution)/shard_map/ppermute | solution.py:91
  3.6 1.5 %collective-permute-start.5 = (bf16[64,2304]{1,0:T(8,128)(2,1)}, bf16[64,2304]{1,0:T(8,128)(2,1)S(1)}, u32[]{:S(2)}, u32[]{:S(2)}) collective-permute-start(bf16[64,2304]{1,0:T(8,128)(2,1)} %bitcast.14), channel_id=1, source_target_pairs={{8,0},{16,8},{24,16},{28,24},{20,28},{12,20},{4,12},{0,4},{9,1},{1... | collective-permute-start | bytes 884744 | tf_op jit(solution)/shard_map/ppermute | solution.py:54
  5.2 0.5 collective-permute-start.3
  5.7 0.0 collective-permute-start
  5.7 5.2 %collective-permute-done.1.refs_2_ = bf16[64,2304]{1,0:T(8,128)(2,1)S(1)} collective-permute-done((bf16[64,2304]{1,0:T(8,128)(2,1)}, bf16[64,2304]{1,0:T(8,128)(2,1)S(1)}, u32[]{:S(2)}, u32[]{:S(2)}) %collective-permute-start.1) | collective-permute-done | bytes 294944 | tf_op jit(solution)/shard_map/ppermute | solution.py:91
  10.9 0.0 collective-permute-start.2
  10.9 1.5 collective-permute-done.5.refs_7_
  12.3 1.5 %collective-permute-start.9 = (bf16[64,2304]{1,0:T(8,128)(2,1)S(1)}, bf16[64,2304]{1,0:T(8,128)(2,1)S(1)}, u32[]{:S(2)}, u32[]{:S(2)}) collective-permute-start(bf16[64,2304]{1,0:T(8,128)(2,1)S(1)} %collective-permute-done.5.refs_7_), channel_id=1, source_target_pairs={{8,0},{16,8},{24,16},{28,24},{20,28},{12,20},{4,12},{0,4},{9,1},{1... | collective-permute-start | bytes 884744 | tf_op jit(solution)/shard_map/ppermute | solution.py:54
  13.8 0.0 collective-permute-done.3.refs_1_
  13.8 0.5 collective-permute-start.4
  14.3 0.0 collective-permute-done.refs_1_
  14.3 0.0 collective-permute-done.2.refs_3_
  14.4 0.4 collective-permute-start.13
  14.8 1.0 slice_bitcast_fusion
  15.8 1.7 %collective-permute-start.7 = (bf16[32,2304]{1,0:T(8,128)(2,1)S(1)}, bf16[32,2304]{1,0:T(8,128)(2,1)S(1)}, u32[]{:S(2)}, u32[]{:S(2)}) collective-permute-start(bf16[32,2304]{1,0:T(8,128)(2,1)S(1)} %get-tuple-element.32.refs_0_), channel_id=1, source_target_pairs={{8,0},{16,8},{24,16},{28,24},{20,28},{12,20},{4,12},{0,4},{9,1},{1... | collective-permute-start | bytes 442376 | tf_op jit(solution)/shard_map/ppermute | solution.py:54
  17.5 0.4 collective-permute-start.6
  17.9 4.1 %collective-permute-done.9.refs_6_ = bf16[64,2304]{1,0:T(8,128)(2,1)S(1)} collective-permute-done((bf16[64,2304]{1,0:T(8,128)(2,1)S(1)}, bf16[64,2304]{1,0:T(8,128)(2,1)S(1)}, u32[]{:S(2)}, u32[]{:S(2)}) %collective-permute-start.9) | collective-permute-done | bytes 294944 | tf_op jit(solution)/shard_map/ppermute | solution.py:54
  21.9 1.4 collective-permute-done.4.refs_2_
  23.4 1.6 %collective-permute-start.11 = (bf16[32,2304]{1,0:T(8,128)(2,1)S(1)}, bf16[32,2304]{1,0:T(8,128)(2,1)S(1)}, u32[]{:S(2)}, u32[]{:S(2)}) collective-permute-start(bf16[32,2304]{1,0:T(8,128)(2,1)S(1)} %get-tuple-element.34.refs_8_), channel_id=1, source_target_pairs={{8,0},{16,8},{24,16},{28,24},{20,28},{12,20},{4,12},{0,4},{9,1},{1... | collective-permute-start | bytes 442376 | tf_op jit(solution)/shard_map/ppermute | solution.py:54
  24.9 0.0 collective-permute-done.7.refs_7_
  24.9 0.0 collective-permute-done.6.refs_1_
  24.9 0.5 collective-permute-start.8
  25.4 0.0 collective-permute-done.13.refs_18_
  25.4 0.0 collective-permute-start.14
  25.4 1.6 %collective-permute-start.16 = (bf16[64,2304]{1,0:T(8,128)(2,1)S(1)}, bf16[64,2304]{1,0:T(8,128)(2,1)S(1)}, u32[]{:S(2)}, u32[]{:S(2)}) collective-permute-start(bf16[64,2304]{1,0:T(8,128)(2,1)S(1)} %collective-permute-done.9.refs_6_), channel_id=1, source_target_pairs={{8,0},{16,8},{24,16},{28,24},{20,28},{12,20},{4,12},{0,4},{9,1},{1... | collective-permute-start | bytes 884744 | tf_op jit(solution)/shard_map/ppermute | solution.py:54
  27.0 1.5 collective-permute-done.11.refs_15_
  28.5 1.5 collective-permute-start.10
  30.0 6.0 %collective-permute-done.10.refs_9_ = bf16[32,2304]{1,0:T(8,128)(2,1)S(1)} collective-permute-done((bf16[32,2304]{1,0:T(8,128)(2,1)S(1)}, bf16[32,2304]{1,0:T(8,128)(2,1)S(1)}, u32[]{:S(2)}, u32[]{:S(2)}) %collective-permute-start.10) | collective-permute-done | bytes 147488 | tf_op jit(solution)/shard_map/ppermute | solution.py:54
  36.0 1.6 %collective-permute-start.27 = (bf16[32,2304]{1,0:T(8,128)(2,1)S(1)}, bf16[32,2304]{1,0:T(8,128)(2,1)S(1)}, u32[]{:S(2)}, u32[]{:S(2)}) collective-permute-start(bf16[32,2304]{1,0:T(8,128)(2,1)S(1)} %collective-permute-done.11.refs_15_), channel_id=1, source_target_pairs={{8,0},{16,8},{24,16},{28,24},{20,28},{12,20},{4,12},{0,4},{9,1},{1... | collective-permute-start | bytes 442376 | tf_op jit(solution)/shard_map/ppermute | solution.py:54
  37.5 0.0 collective-permute-done.8.refs_3_
  37.5 0.5 collective-permute-start.15
  38.1 1.6 %collective-permute-start.22 = (bf16[32,2304]{1,0:T(8,128)(2,1)S(1)}, bf16[32,2304]{1,0:T(8,128)(2,1)S(1)}, u32[]{:S(2)}, u32[]{:S(2)}) collective-permute-start(bf16[32,2304]{1,0:T(8,128)(2,1)S(1)} %collective-permute-done.7.refs_7_), channel_id=1, source_target_pairs={{8,0},{16,8},{24,16},{28,24},{20,28},{12,20},{4,12},{0,4},{9,1},{1... | collective-permute-start | bytes 442376 | tf_op jit(solution)/shard_map/ppermute | solution.py:54
  39.6 0.4 collective-permute-start.25
  40.1 0.4 collective-permute-start.20
  40.5 1.0 copy-done.1
  41.5 1.3 copy-done.3
  42.8 1.3 copy-done.5
  44.0 1.5 grams.1
  45.5 0.0 copy-start.9
  45.5 1.0 copy-done.9
  46.5 1.0 copy-done.11
  47.5 1.6 %collective-permute-start.28 = (bf16[32,2304]{1,0:T(8,128)(2,1)S(1)}, bf16[32,2304]{1,0:T(8,128)(2,1)S(1)}, u32[]{:S(2)}, u32[]{:S(2)}) collective-permute-start(bf16[32,2304]{1,0:T(8,128)(2,1)S(1)} %collective-permute-done.27.refs_14_), channel_id=1, source_target_pairs={{8,0},{16,8},{24,16},{28,24},{20,28},{12,20},{4,12},{0,4},{9,1},{1... | collective-permute-start | bytes 442376 | tf_op jit(solution)/shard_map/ppermute | solution.py:54
  49.1 1.6 %collective-permute-start.23 = (bf16[32,2304]{1,0:T(8,128)(2,1)S(1)}, bf16[32,2304]{1,0:T(8,128)(2,1)S(1)}, u32[]{:S(2)}, u32[]{:S(2)}) collective-permute-start(bf16[32,2304]{1,0:T(8,128)(2,1)S(1)} %collective-permute-done.22.refs_6_), channel_id=1, source_target_pairs={{8,0},{16,8},{24,16},{28,24},{20,28},{12,20},{4,12},{0,4},{9,1},{1... | collective-permute-start | bytes 442376 | tf_op jit(solution)/shard_map/ppermute | solution.py:54
  50.7 0.5 collective-permute-start.26
  51.1 0.6 collective-permute-done.20.refs_2_
  51.7 0.4 collective-permute-start.21
  52.2 3.0 %pick_left.1 = (bf16[64,2304]{1,0:T(8,128)(2,1)}, bf16[64,2304]{1,0:T(8,128)(2,1)}, bf16[64,2304]{1,0:T(8,128)(2,1)}, bf16[64,2304]{1,0:T(8,128)(2,1)}) custom-call(s32[4]{0:T(128)} %owner.5, bf16[64,2304]{1,0:T(8,128)(2,1)} %bitcast.17, bf16[64,2304]{1,0:T(8,128)(2,1)} %copy-done.14, bf16[64,2304]{1,0:T(8,128)(2,1)} %copy-done.16, ...), custom_call_target="tpu_custom_call" | custom-call | bytes 3145728 | tf_op jit(solution)/shard_map/pick_left/pallas_call | solution.py:126
  55.2 0.1 collective-permute-start.17
  55.3 1.9 %collective-permute-start.18 = (bf16[64,2304]{1,0:T(8,128)(2,1)}, bf16[64,2304]{1,0:T(8,128)(2,1)S(1)}, u32[]{:S(2)}, u32[]{:S(2)}) collective-permute-start(bf16[64,2304]{1,0:T(8,128)(2,1)} %get-tuple-element.40), channel_id=1, source_target_pairs={{0,2},{1,3},{2,0},{3,1},{4,6},{5,7},{6,4},{7,5},{8,10},{9,11},{10,... | collective-permute-start | bytes 884744 | tf_op jit(solution)/shard_map/ppermute | solution.py:91
  57.2 0.0 copy-start.8
  57.2 0.1 collective-permute-start.19
  57.4 1.6 %collective-permute-start.29 = (bf16[32,2304]{1,0:T(8,128)(2,1)S(1)}, bf16[32,2304]{1,0:T(8,128)(2,1)S(1)}, u32[]{:S(2)}, u32[]{:S(2)}) collective-permute-start(bf16[32,2304]{1,0:T(8,128)(2,1)S(1)} %collective-permute-done.28.refs_13_), channel_id=1, source_target_pairs={{8,0},{16,8},{24,16},{28,24},{20,28},{12,20},{4,12},{0,4},{9,1},{1... | collective-permute-start | bytes 442376 | tf_op jit(solution)/shard_map/ppermute | solution.py:54
  59.0 1.6 %collective-permute-start.24 = (bf16[32,2304]{1,0:T(8,128)(2,1)S(1)}, bf16[32,2304]{1,0:T(8,128)(2,1)S(1)}, u32[]{:S(2)}, u32[]{:S(2)}) collective-permute-start(bf16[32,2304]{1,0:T(8,128)(2,1)S(1)} %collective-permute-done.23.refs_5_), channel_id=1, source_target_pairs={{8,0},{16,8},{24,16},{28,24},{20,28},{12,20},{4,12},{0,4},{9,1},{1... | collective-permute-start | bytes 442376 | tf_op jit(solution)/shard_map/ppermute | solution.py:54
  60.5 3.5 %collective-permute-done.29.refs_12_ = bf16[32,2304]{1,0:T(8,128)(2,1)S(1)} collective-permute-done((bf16[32,2304]{1,0:T(8,128)(2,1)S(1)}, bf16[32,2304]{1,0:T(8,128)(2,1)S(1)}, u32[]{:S(2)}, u32[]{:S(2)}) %collective-permute-start.29) | collective-permute-done | bytes 147488 | tf_op jit(solution)/shard_map/ppermute | solution.py:54
  64.0 2.4 %collective-permute-done.24.refs_4_ = bf16[32,2304]{1,0:T(8,128)(2,1)S(1)} collective-permute-done((bf16[32,2304]{1,0:T(8,128)(2,1)S(1)}, bf16[32,2304]{1,0:T(8,128)(2,1)S(1)}, u32[]{:S(2)}, u32[]{:S(2)}) %collective-permute-start.24) | collective-permute-done | bytes 147488 | tf_op jit(solution)/shard_map/ppermute | solution.py:54
  66.5 3.1 %coupling.1 = (bf16[64,256]{1,0:T(8,128)(2,1)S(1)}, bf16[64,256]{1,0:T(8,128)(2,1)S(1)}, bf16[64,256]{1,0:T(8,128)(2,1)S(1)}, bf16[64,256]{1,0:T(8,128)(2,1)S(1)}) custom-call(s32[4]{0:T(128)S(1)} %copy-done.2, bf16[32,2304]{1,0:T(8,128)(2,1)S(1)} %get-tuple-element.32.refs_0_, bf16[32,2304]{1,0:T(8,128)(2,1)S(1)} %collective-permute-done.6.refs_1_, ...), custom_call_target="tpu_custom_call" | custom-call | flops 301989888 | bytes 3145728 | tf_op jit(solution)/shard_map/coupling/pallas_call | solution.py:177
  69.6 0.1 collective-permute-start.30
  69.7 1.9 %collective-permute-start.31 = (bf16[64,256]{1,0:T(8,128)(2,1)S(1)}, bf16[64,256]{1,0:T(8,128)(2,1)S(1)}, u32[]{:S(2)}, u32[]{:S(2)}) collective-permute-start(bf16[64,256]{1,0:T(8,128)(2,1)S(1)} %get-tuple-element.52), channel_id=1, source_target_pairs={{0,2},{1,3},{2,0},{3,1},{4,6},{5,7},{6,4},{7,5},{8,10},{9,11},{10,... | collective-permute-start | bytes 98312 | tf_op jit(solution)/shard_map/ppermute | solution.py:91
  71.6 0.9 collective-permute-start.32
  73.8 1.1 collective-permute-done.32.refs_7_
  75.0 0.0 copy-start.10
  75.0 1.3 copy-done.10
  76.3 1.2 copy-done.12
  77.5 74.4 %finish.1 = (bf16[2304,256]{1,0:T(8,128)(2,1)}, bf16[2304,256]{1,0:T(8,128)(2,1)}) custom-call(s32[1,1]{1,0:T(1,128)S(6)} %copy.10.old_ref, s32[1,1]{1,0:T(1,128)S(6)} %copy.11.goal_ref, s32[8]{0:T(128)S(1)} %copy-done.8, s32[4]{0:T(128)S(1)} %copy-done.2, bf16[2304,256]{1,0:T(8,128)(2,1)S(1)} %bitcast.20, bf16[2304,256]{1,0:T(8,128)(2,1)S(1)} %bitcast.22, ...), custom_call_target="tpu_custom_call" | custom-call | flops 8589934592 | bytes 12582912 | tf_op jit(solution)/shard_map/finish/pallas_call | solution.py:347
  (45 shorter events, 0.1 us)
Async XLA Ops:
  0.6 10.2 %collective-permute-start.1 = (bf16[64,2304]{1,0:T(8,128)(2,1)}, bf16[64,2304]{1,0:T(8,128)(2,1)S(1)}, u32[]{:S(2)}, u32[]{:S(2)}) collective-permute-start(bf16[64,2304]{1,0:T(8,128)(2,1)} %bitcast.13), channel_id=1, source_target_pairs={{0,2},{1,3},{2,0},{3,1},{4,6},{5,7},{6,4},{7,5},{8,10},{9,11},{10,... | collective-permute-start | bytes 884744 | tf_op jit(solution)/shard_map/ppermute | solution.py:91
  3.6 8.7 %collective-permute-start.5 = (bf16[64,2304]{1,0:T(8,128)(2,1)}, bf16[64,2304]{1,0:T(8,128)(2,1)S(1)}, u32[]{:S(2)}, u32[]{:S(2)}) collective-permute-start(bf16[64,2304]{1,0:T(8,128)(2,1)} %bitcast.14), channel_id=1, source_target_pairs={{8,0},{16,8},{24,16},{28,24},{20,28},{12,20},{4,12},{0,4},{9,1},{1... | collective-permute-start | bytes 884744 | tf_op jit(solution)/shard_map/ppermute | solution.py:54
  5.2 8.7 %collective-permute-start.3 = (bf16[64,2304]{1,0:T(8,128)(2,1)}, bf16[64,2304]{1,0:T(8,128)(2,1)S(1)}, u32[]{:S(2)}, u32[]{:S(2)}) collective-permute-start(bf16[64,2304]{1,0:T(8,128)(2,1)} %bitcast.15), channel_id=1, source_target_pairs={{0,8},{8,16},{16,24},{24,28},{28,20},{20,12},{12,4},{4,0},{1,9},{9... | collective-permute-start | bytes 884744 | tf_op jit(solution)/shard_map/ppermute | solution.py:54
  5.7 8.7 %collective-permute-start = (bf16[64,2304]{1,0:T(8,128)(2,1)}, bf16[64,2304]{1,0:T(8,128)(2,1)S(1)}, u32[]{:S(2)}, u32[]{:S(2)}) collective-permute-start(bf16[64,2304]{1,0:T(8,128)(2,1)} %bitcast.16), channel_id=1, source_target_pairs={{0,1},{1,0},{2,3},{3,2},{4,5},{5,4},{6,7},{7,6},{8,9},{9,8},{10,11... | collective-permute-start | bytes 884744 | tf_op jit(solution)/shard_map/ppermute | solution.py:91
  10.9 3.5 %collective-permute-start.2 = (bf16[64,2304]{1,0:T(8,128)(2,1)S(1)}, bf16[64,2304]{1,0:T(8,128)(2,1)S(1)}, u32[]{:S(2)}, u32[]{:S(2)}) collective-permute-start(bf16[64,2304]{1,0:T(8,128)(2,1)S(1)} %collective-permute-done.1.refs_2_), channel_id=1, source_target_pairs={{0,1},{1,0},{2,3},{3,2},{4,5},{5,4},{6,7},{7,6},{8,9},{9,8},{10,11... | collective-permute-start | bytes 884744 | tf_op jit(solution)/shard_map/ppermute | solution.py:91
  12.3 5.6 %copy-start.13 = (bf16[64,2304]{1,0:T(8,128)(2,1)}, bf16[64,2304]{1,0:T(8,128)(2,1)S(1)}, u32[]{:S(2)}) copy-start(bf16[64,2304]{1,0:T(8,128)(2,1)S(1)} %collective-permute-done.5.refs_7_) | copy-start | bytes 884740
  12.3 9.6 %collective-permute-start.9 = (bf16[64,2304]{1,0:T(8,128)(2,1)S(1)}, bf16[64,2304]{1,0:T(8,128)(2,1)S(1)}, u32[]{:S(2)}, u32[]{:S(2)}) collective-permute-start(bf16[64,2304]{1,0:T(8,128)(2,1)S(1)} %collective-permute-done.5.refs_7_), channel_id=1, source_target_pairs={{8,0},{16,8},{24,16},{28,24},{20,28},{12,20},{4,12},{0,4},{9,1},{1... | collective-permute-start | bytes 884744 | tf_op jit(solution)/shard_map/ppermute | solution.py:54
  13.8 11.6 %copy-start.14 = (bf16[64,2304]{1,0:T(8,128)(2,1)}, bf16[64,2304]{1,0:T(8,128)(2,1)S(1)}, u32[]{:S(2)}) copy-start(bf16[64,2304]{1,0:T(8,128)(2,1)S(1)} %collective-permute-done.3.refs_1_) | copy-start | bytes 884740
  13.8 9.5 %collective-permute-start.4 = (bf16[64,2304]{1,0:T(8,128)(2,1)S(1)}, bf16[64,2304]{1,0:T(8,128)(2,1)S(1)}, u32[]{:S(2)}, u32[]{:S(2)}) collective-permute-start(bf16[64,2304]{1,0:T(8,128)(2,1)S(1)} %collective-permute-done.3.refs_1_), channel_id=1, source_target_pairs={{0,8},{8,16},{16,24},{24,28},{28,20},{20,12},{12,4},{4,0},{1,9},{9... | collective-permute-start | bytes 884744 | tf_op jit(solution)/shard_map/ppermute | solution.py:54
  14.4 11.0 %collective-permute-start.13 = (bf16[64,2304]{1,0:T(8,128)(2,1)}, bf16[64,2304]{1,0:T(8,128)(2,1)S(1)}, u32[]{:S(2)}, u32[]{:S(2)}) collective-permute-start(bf16[64,2304]{1,0:T(8,128)(2,1)} %bitcast.10), channel_id=1, source_target_pairs={{0,2},{1,3},{2,0},{3,1},{4,6},{5,7},{6,4},{7,5},{8,10},{9,11},{10,... | collective-permute-start | bytes 884744 | tf_op jit(solution)/shard_map/ppermute | solution.py:91
  15.8 9.1 %collective-permute-start.7 = (bf16[32,2304]{1,0:T(8,128)(2,1)S(1)}, bf16[32,2304]{1,0:T(8,128)(2,1)S(1)}, u32[]{:S(2)}, u32[]{:S(2)}) collective-permute-start(bf16[32,2304]{1,0:T(8,128)(2,1)S(1)} %get-tuple-element.32.refs_0_), channel_id=1, source_target_pairs={{8,0},{16,8},{24,16},{28,24},{20,28},{12,20},{4,12},{0,4},{9,1},{1... | collective-permute-start | bytes 442376 | tf_op jit(solution)/shard_map/ppermute | solution.py:54
  17.5 7.5 %collective-permute-start.6 = (bf16[32,2304]{1,0:T(8,128)(2,1)S(1)}, bf16[32,2304]{1,0:T(8,128)(2,1)S(1)}, u32[]{:S(2)}, u32[]{:S(2)}) collective-permute-start(bf16[32,2304]{1,0:T(8,128)(2,1)S(1)} %get-tuple-element.32.refs_0_), channel_id=1, source_target_pairs={{0,8},{8,16},{16,24},{24,28},{28,20},{20,12},{12,4},{4,0},{1,9},{9... | collective-permute-start | bytes 442376 | tf_op jit(solution)/shard_map/ppermute | solution.py:54
  21.9 18.6 %copy-start.15 = (bf16[64,2304]{1,0:T(8,128)(2,1)}, bf16[64,2304]{1,0:T(8,128)(2,1)S(1)}, u32[]{:S(2)}) copy-start(bf16[64,2304]{1,0:T(8,128)(2,1)S(1)} %collective-permute-done.9.refs_6_) | copy-start | bytes 884740
  21.9 15.6 %collective-permute-start.12 = (bf16[64,2304]{1,0:T(8,128)(2,1)}, bf16[64,2304]{1,0:T(8,128)(2,1)S(1)}, u32[]{:S(2)}, u32[]{:S(2)}) collective-permute-start(bf16[64,2304]{1,0:T(8,128)(2,1)} %bitcast.11), channel_id=1, source_target_pairs={{0,1},{1,0},{2,3},{3,2},{4,5},{5,4},{6,7},{7,6},{8,9},{9,8},{10,11... | collective-permute-start | bytes 884744 | tf_op jit(solution)/shard_map/ppermute | solution.py:91
  23.4 17.2 %copy-start.16 = (bf16[64,2304]{1,0:T(8,128)(2,1)}, bf16[64,2304]{1,0:T(8,128)(2,1)S(1)}, u32[]{:S(2)}) copy-start(bf16[64,2304]{1,0:T(8,128)(2,1)S(1)} %collective-permute-done.4.refs_2_) | copy-start | bytes 884740
  23.4 5.1 %collective-permute-start.11 = (bf16[32,2304]{1,0:T(8,128)(2,1)S(1)}, bf16[32,2304]{1,0:T(8,128)(2,1)S(1)}, u32[]{:S(2)}, u32[]{:S(2)}) collective-permute-start(bf16[32,2304]{1,0:T(8,128)(2,1)S(1)} %get-tuple-element.34.refs_8_), channel_id=1, source_target_pairs={{8,0},{16,8},{24,16},{28,24},{20,28},{12,20},{4,12},{0,4},{9,1},{1... | collective-permute-start | bytes 442376 | tf_op jit(solution)/shard_map/ppermute | solution.py:54
  24.9 12.6 %collective-permute-start.8 = (bf16[64,2304]{1,0:T(8,128)(2,1)S(1)}, bf16[64,2304]{1,0:T(8,128)(2,1)S(1)}, u32[]{:S(2)}, u32[]{:S(2)}) collective-permute-start(bf16[64,2304]{1,0:T(8,128)(2,1)S(1)} %collective-permute-done.4.refs_2_), channel_id=1, source_target_pairs={{0,8},{8,16},{16,24},{24,28},{28,20},{20,12},{12,4},{4,0},{1,9},{9... | collective-permute-start | bytes 884744 | tf_op jit(solution)/shard_map/ppermute | solution.py:54
  25.4 12.1 %collective-permute-start.14 = (bf16[64,2304]{1,0:T(8,128)(2,1)S(1)}, bf16[64,2304]{1,0:T(8,128)(2,1)S(1)}, u32[]{:S(2)}, u32[]{:S(2)}) collective-permute-start(bf16[64,2304]{1,0:T(8,128)(2,1)S(1)} %collective-permute-done.13.refs_18_), channel_id=1, source_target_pairs={{0,1},{1,0},{2,3},{3,2},{4,5},{5,4},{6,7},{7,6},{8,9},{9,8},{10,11... | collective-permute-start | bytes 884744 | tf_op jit(solution)/shard_map/ppermute | solution.py:91
  25.4 12.6 %collective-permute-start.16 = (bf16[64,2304]{1,0:T(8,128)(2,1)S(1)}, bf16[64,2304]{1,0:T(8,128)(2,1)S(1)}, u32[]{:S(2)}, u32[]{:S(2)}) collective-permute-start(bf16[64,2304]{1,0:T(8,128)(2,1)S(1)} %collective-permute-done.9.refs_6_), channel_id=1, source_target_pairs={{8,0},{16,8},{24,16},{28,24},{20,28},{12,20},{4,12},{0,4},{9,1},{1... | collective-permute-start | bytes 884744 | tf_op jit(solution)/shard_map/ppermute | solution.py:54
  28.5 7.4 %collective-permute-start.10 = (bf16[32,2304]{1,0:T(8,128)(2,1)S(1)}, bf16[32,2304]{1,0:T(8,128)(2,1)S(1)}, u32[]{:S(2)}, u32[]{:S(2)}) collective-permute-start(bf16[32,2304]{1,0:T(8,128)(2,1)S(1)} %get-tuple-element.34.refs_8_), channel_id=1, source_target_pairs={{0,8},{8,16},{16,24},{24,28},{28,20},{20,12},{12,4},{4,0},{1,9},{9... | collective-permute-start | bytes 442376 | tf_op jit(solution)/shard_map/ppermute | solution.py:54
  36.0 11.5 %collective-permute-start.27 = (bf16[32,2304]{1,0:T(8,128)(2,1)S(1)}, bf16[32,2304]{1,0:T(8,128)(2,1)S(1)}, u32[]{:S(2)}, u32[]{:S(2)}) collective-permute-start(bf16[32,2304]{1,0:T(8,128)(2,1)S(1)} %collective-permute-done.11.refs_15_), channel_id=1, source_target_pairs={{8,0},{16,8},{24,16},{28,24},{20,28},{12,20},{4,12},{0,4},{9,1},{1... | collective-permute-start | bytes 442376 | tf_op jit(solution)/shard_map/ppermute | solution.py:54
  37.5 8.0 %copy-start.17 = (bf16[64,2304]{1,0:T(8,128)(2,1)}, bf16[64,2304]{1,0:T(8,128)(2,1)S(1)}, u32[]{:S(2)}) copy-start(bf16[64,2304]{1,0:T(8,128)(2,1)S(1)} %collective-permute-done.8.refs_3_) | copy-start | bytes 884740
  37.5 14.6 %collective-permute-start.15 = (bf16[64,2304]{1,0:T(8,128)(2,1)S(1)}, bf16[64,2304]{1,0:T(8,128)(2,1)}, u32[]{:S(2)}, u32[]{:S(2)}) collective-permute-start(bf16[64,2304]{1,0:T(8,128)(2,1)S(1)} %collective-permute-done.8.refs_3_), channel_id=1, source_target_pairs={{0,8},{8,16},{16,24},{24,28},{28,20},{20,12},{12,4},{4,0},{1,9},{9... | collective-permute-start | bytes 884744 | tf_op jit(solution)/shard_map/ppermute | solution.py:54
  38.1 2.5 %copy-start.18 = (bf16[64,2304]{1,0:T(8,128)(2,1)}, bf16[64,2304]{1,0:T(8,128)(2,1)S(1)}, u32[]{:S(2)}) copy-start(bf16[64,2304]{1,0:T(8,128)(2,1)S(1)} %collective-permute-done.16.refs_5_) | copy-start | bytes 884740
  38.1 11.1 %collective-permute-start.22 = (bf16[32,2304]{1,0:T(8,128)(2,1)S(1)}, bf16[32,2304]{1,0:T(8,128)(2,1)S(1)}, u32[]{:S(2)}, u32[]{:S(2)}) collective-permute-start(bf16[32,2304]{1,0:T(8,128)(2,1)S(1)} %collective-permute-done.7.refs_7_), channel_id=1, source_target_pairs={{8,0},{16,8},{24,16},{28,24},{20,28},{12,20},{4,12},{0,4},{9,1},{1... | collective-permute-start | bytes 442376 | tf_op jit(solution)/shard_map/ppermute | solution.py:54
  39.6 11.1 %collective-permute-start.25 = (bf16[32,2304]{1,0:T(8,128)(2,1)S(1)}, bf16[32,2304]{1,0:T(8,128)(2,1)S(1)}, u32[]{:S(2)}, u32[]{:S(2)}) collective-permute-start(bf16[32,2304]{1,0:T(8,128)(2,1)S(1)} %collective-permute-done.10.refs_9_), channel_id=1, source_target_pairs={{0,8},{8,16},{16,24},{24,28},{28,20},{20,12},{12,4},{4,0},{1,9},{9... | collective-permute-start | bytes 442376 | tf_op jit(solution)/shard_map/ppermute | solution.py:54
  40.1 11.6 %collective-permute-start.20 = (bf16[32,2304]{1,0:T(8,128)(2,1)S(1)}, bf16[32,2304]{1,0:T(8,128)(2,1)S(1)}, u32[]{:S(2)}, u32[]{:S(2)}) collective-permute-start(bf16[32,2304]{1,0:T(8,128)(2,1)S(1)} %collective-permute-done.6.refs_1_), channel_id=1, source_target_pairs={{0,8},{8,16},{16,24},{24,28},{28,20},{20,12},{12,4},{4,0},{1,9},{9... | collective-permute-start | bytes 442376 | tf_op jit(solution)/shard_map/ppermute | solution.py:54
  40.5 1.0 copy-start.1
  41.5 1.3 copy-start.3
  42.7 1.3 copy-start.5
  45.5 1.0 copy-start.9
  46.5 1.0 copy-start.11
  47.5 19.0 %copy-start = (bf16[1,64,2304]{2,1,0:T(8,128)(2,1)S(1)}, bf16[1,64,2304]{2,1,0:T(8,128)(2,1)}, u32[]{:S(2)}) copy-start(bf16[1,64,2304]{2,1,0:T(8,128)(2,1)} %param.11) | copy-start | bytes 884740
  47.5 19.0 %copy-start.2 = (s32[4]{0:T(128)S(1)}, s32[4]{0:T(128)}, u32[]{:S(2)}) copy-start(s32[4]{0:T(128)} %owner.5) | copy-start | bytes 52
  47.5 7.8 %collective-permute-start.28 = (bf16[32,2304]{1,0:T(8,128)(2,1)S(1)}, bf16[32,2304]{1,0:T(8,128)(2,1)S(1)}, u32[]{:S(2)}, u32[]{:S(2)}) collective-permute-start(bf16[32,2304]{1,0:T(8,128)(2,1)S(1)} %collective-permute-done.27.refs_14_), channel_id=1, source_target_pairs={{8,0},{16,8},{24,16},{28,24},{20,28},{12,20},{4,12},{0,4},{9,1},{1... | collective-permute-start | bytes 442376 | tf_op jit(solution)/shard_map/ppermute | solution.py:54
  49.1 8.1 %collective-permute-start.23 = (bf16[32,2304]{1,0:T(8,128)(2,1)S(1)}, bf16[32,2304]{1,0:T(8,128)(2,1)S(1)}, u32[]{:S(2)}, u32[]{:S(2)}) collective-permute-start(bf16[32,2304]{1,0:T(8,128)(2,1)S(1)} %collective-permute-done.22.refs_6_), channel_id=1, source_target_pairs={{8,0},{16,8},{24,16},{28,24},{20,28},{12,20},{4,12},{0,4},{9,1},{1... | collective-permute-start | bytes 442376 | tf_op jit(solution)/shard_map/ppermute | solution.py:54
  50.7 6.7 %collective-permute-start.26 = (bf16[32,2304]{1,0:T(8,128)(2,1)S(1)}, bf16[32,2304]{1,0:T(8,128)(2,1)S(1)}, u32[]{:S(2)}, u32[]{:S(2)}) collective-permute-start(bf16[32,2304]{1,0:T(8,128)(2,1)S(1)} %collective-permute-done.25.refs_10_), channel_id=1, source_target_pairs={{0,8},{8,16},{16,24},{24,28},{28,20},{20,12},{12,4},{4,0},{1,9},{9... | collective-permute-start | bytes 442376 | tf_op jit(solution)/shard_map/ppermute | solution.py:54
  51.7 7.2 %collective-permute-start.21 = (bf16[32,2304]{1,0:T(8,128)(2,1)S(1)}, bf16[32,2304]{1,0:T(8,128)(2,1)S(1)}, u32[]{:S(2)}, u32[]{:S(2)}) collective-permute-start(bf16[32,2304]{1,0:T(8,128)(2,1)S(1)} %collective-permute-done.20.refs_2_), channel_id=1, source_target_pairs={{0,8},{8,16},{16,24},{24,28},{28,20},{20,12},{12,4},{4,0},{1,9},{9... | collective-permute-start | bytes 442376 | tf_op jit(solution)/shard_map/ppermute | solution.py:54
  55.2 19.8 %collective-permute-start.17 = (bf16[64,2304]{1,0:T(8,128)(2,1)}, bf16[64,2304]{1,0:T(8,128)(2,1)S(1)}, u32[]{:S(2)}, u32[]{:S(2)}) collective-permute-start(bf16[64,2304]{1,0:T(8,128)(2,1)} %get-tuple-element.39), channel_id=1, source_target_pairs={{0,1},{1,0},{2,3},{3,2},{4,5},{5,4},{6,7},{7,6},{8,9},{9,8},{10,11... | collective-permute-start | bytes 884744 | tf_op jit(solution)/shard_map/ppermute | solution.py:91
  55.3 19.7 %collective-permute-start.18 = (bf16[64,2304]{1,0:T(8,128)(2,1)}, bf16[64,2304]{1,0:T(8,128)(2,1)S(1)}, u32[]{:S(2)}, u32[]{:S(2)}) collective-permute-start(bf16[64,2304]{1,0:T(8,128)(2,1)} %get-tuple-element.40), channel_id=1, source_target_pairs={{0,2},{1,3},{2,0},{3,1},{4,6},{5,7},{6,4},{7,5},{8,10},{9,11},{10,... | collective-permute-start | bytes 884744 | tf_op jit(solution)/shard_map/ppermute | solution.py:91
  57.2 17.8 %copy-start.4 = (bf16[1,1,2304,256]{3,2,1,0:T(8,128)(2,1)S(1)}, bf16[1,1,2304,256]{3,2,1,0:T(8,128)(2,1)}, u32[]{:S(2)}) copy-start(bf16[1,1,2304,256]{3,2,1,0:T(8,128)(2,1)} %param.8) | copy-start | bytes 3538948
  57.2 17.8 %copy-start.6 = (bf16[1,1,2304,256]{3,2,1,0:T(8,128)(2,1)S(1)}, bf16[1,1,2304,256]{3,2,1,0:T(8,128)(2,1)}, u32[]{:S(2)}) copy-start(bf16[1,1,2304,256]{3,2,1,0:T(8,128)(2,1)} %param.9) | copy-start | bytes 3538948
  57.2 17.8 %copy-start.7 = (bf16[64,2304]{1,0:T(8,128)(2,1)S(1)}, bf16[64,2304]{1,0:T(8,128)(2,1)}, u32[]{:S(2)}) copy-start(bf16[64,2304]{1,0:T(8,128)(2,1)} %get-tuple-element.38.refs_0_) | copy-start | bytes 884740
  57.2 17.8 %copy-start.8 = (s32[8]{0:T(128)S(1)}, s32[8]{0:T(128)}, u32[]{:S(2)}) copy-start(s32[8]{0:T(128)} %panel.1) | copy-start | bytes 100
  57.2 17.7 %collective-permute-start.19 = (bf16[64,2304]{1,0:T(8,128)(2,1)}, bf16[64,2304]{1,0:T(8,128)(2,1)S(1)}, u32[]{:S(2)}, u32[]{:S(2)}) collective-permute-start(bf16[64,2304]{1,0:T(8,128)(2,1)} %get-tuple-element.41), channel_id=1, source_target_pairs={{0,3},{1,2},{2,1},{3,0},{4,7},{5,6},{6,5},{7,4},{8,11},{9,10},{10,... | collective-permute-start | bytes 884744 | tf_op jit(solution)/shard_map/ppermute | solution.py:91
  57.4 6.7 %collective-permute-start.29 = (bf16[32,2304]{1,0:T(8,128)(2,1)S(1)}, bf16[32,2304]{1,0:T(8,128)(2,1)S(1)}, u32[]{:S(2)}, u32[]{:S(2)}) collective-permute-start(bf16[32,2304]{1,0:T(8,128)(2,1)S(1)} %collective-permute-done.28.refs_13_), channel_id=1, source_target_pairs={{8,0},{16,8},{24,16},{28,24},{20,28},{12,20},{4,12},{0,4},{9,1},{1... | collective-permute-start | bytes 442376 | tf_op jit(solution)/shard_map/ppermute | solution.py:54
  59.0 7.5 %collective-permute-start.24 = (bf16[32,2304]{1,0:T(8,128)(2,1)S(1)}, bf16[32,2304]{1,0:T(8,128)(2,1)S(1)}, u32[]{:S(2)}, u32[]{:S(2)}) collective-permute-start(bf16[32,2304]{1,0:T(8,128)(2,1)S(1)} %collective-permute-done.23.refs_5_), channel_id=1, source_target_pairs={{8,0},{16,8},{24,16},{28,24},{20,28},{12,20},{4,12},{0,4},{9,1},{1... | collective-permute-start | bytes 442376 | tf_op jit(solution)/shard_map/ppermute | solution.py:54
  69.6 2.0 %collective-permute-start.30 = (bf16[64,256]{1,0:T(8,128)(2,1)S(1)}, bf16[64,256]{1,0:T(8,128)(2,1)S(1)}, u32[]{:S(2)}, u32[]{:S(2)}) collective-permute-start(bf16[64,256]{1,0:T(8,128)(2,1)S(1)} %get-tuple-element.51), channel_id=1, source_target_pairs={{0,1},{1,0},{2,3},{3,2},{4,5},{5,4},{6,7},{7,6},{8,9},{9,8},{10,11... | collective-permute-start | bytes 98312 | tf_op jit(solution)/shard_map/ppermute | solution.py:91
  69.7 4.1 %collective-permute-start.31 = (bf16[64,256]{1,0:T(8,128)(2,1)S(1)}, bf16[64,256]{1,0:T(8,128)(2,1)S(1)}, u32[]{:S(2)}, u32[]{:S(2)}) collective-permute-start(bf16[64,256]{1,0:T(8,128)(2,1)S(1)} %get-tuple-element.52), channel_id=1, source_target_pairs={{0,2},{1,3},{2,0},{3,1},{4,6},{5,7},{6,4},{7,5},{8,10},{9,11},{10,... | collective-permute-start | bytes 98312 | tf_op jit(solution)/shard_map/ppermute | solution.py:91
  71.6 3.3 %collective-permute-start.32 = (bf16[64,256]{1,0:T(8,128)(2,1)S(1)}, bf16[64,256]{1,0:T(8,128)(2,1)S(1)}, u32[]{:S(2)}, u32[]{:S(2)}) collective-permute-start(bf16[64,256]{1,0:T(8,128)(2,1)S(1)} %get-tuple-element.53), channel_id=1, source_target_pairs={{0,3},{1,2},{2,1},{3,0},{4,7},{5,6},{6,5},{7,4},{8,11},{9,10},{10,... | collective-permute-start | bytes 98312 | tf_op jit(solution)/shard_map/ppermute | solution.py:91
  75.0 1.3 copy-start.10
  76.3 1.2 copy-start.12

commit v3 on v2

v3 whole, which is shorter than its diff:
```python
import functools
import math

import jax
import jax.numpy as jnp
from jax import lax
from jax.experimental import pallas as pl
from jax.experimental.pallas import tpu as pltpu
from jax.sharding import PartitionSpec as P

F32 = jnp.float32
BF16 = jnp.bfloat16
HIGHEST = lax.Precision.HIGHEST
VMEM = pl.BlockSpec(memory_space=pltpu.VMEM)
SMEM = pl.BlockSpec(memory_space=pltpu.SMEM)
HBM = pl.BlockSpec(memory_space=pltpu.HBM)
ROUGH, FINE = 0.05, 0.015
ROUGH_STEPS, FINE_STEPS = 12, 6


def nn(a, b, precision=None):
    return lax.dot_general(a, b, (((1,), (0,)), ((), ())), precision=precision, preferred_element_type=F32)


def nt(a, b, precision=None):
    return lax.dot_general(a, b, (((1,), (1,)), ((), ())), precision=precision, preferred_element_type=F32)


def tn(a, b, precision=None):
    return lax.dot_general(a, b, (((0,), (0,)), ((), ())), precision=precision, preferred_element_type=F32)


def halves(x):
    high = x.astype(BF16)
    return high, (x - high.astype(F32)).astype(BF16)


def after(x, *others):
    return lax.optimization_barrier((x, *others))[0]


def ring_place(r, n):
    return jnp.where(r % 2 == 0, r // 2, n - 1 - r // 2)


def ring_steps(n):
    ring = list(range(0, n, 2)) + list(range(n - 1, 0, -2))
    ahead = [(ring[i], ring[(i + 1) % n]) for i in range(n)]
    return ahead, [(b, a) for a, b in ahead]


def farther(n_row, n_col, d):
    ring = [a for a, _ in ring_steps(n_row)[0]]
    pairs = []
    for at, r in enumerate(ring):
        for c in range(n_col):
            to = ring[(at + (d if c % 2 == 0 else -d)) % n_row]
            pairs.append((r * n_col + c, to * n_col + c))
    return pairs


def rings(left, right, n_row, n_col, gates):
    ahead, back = ring_steps(n_row)
    half = n_row // 2
    lefts, rights = [left] + [None] * (n_row - 1), [right]
    fwd = bwd = left
    step = lambda d: rights.append(lax.ppermute(rights[-1], ("row", "col"), farther(n_row, n_col, 1)))
    step(1)
    for s in range(1, half):
        if s > 1:
            lag = rights[s - 2 : s - 1] if s > 2 else ()
            fwd, bwd, *_ = lax.optimization_barrier((fwd, bwd, *lag, *(gates[s]() if s in gates else ())))
            step(s)
        fwd, bwd = lax.ppermute(fwd, "row", ahead), lax.ppermute(bwd, "row", back)
        lefts[s], lefts[n_row - s] = fwd, bwd
    gate = gates[half]() if half in gates else ()
    fwd, bwd, *_ = lax.optimization_barrier((fwd, bwd, rights[half - 2], *gate))
    low = left.shape[0] // 2
    lefts[half] = lax.ppermute(fwd[:low], "row", ahead)
    lefts.append(lax.ppermute(bwd[low:], "row", back))
    step(half)
    return lefts, rights


def swap(x, axis, n, m):
    return lax.ppermute(x, axis, [(i, i ^ m) for i in range(n)])


def part_copies(parts, target, sem):
    shard = target.shape[0] // len(parts)
    col = lax.axis_index("col")
    spots = [pl.ds(pl.multiple_of((col ^ m) * shard, shard), shard) for m in range(len(parts))]
    return [pltpu.make_async_copy(part, target.at[spots[m]], sem.at[m]) for m, part in enumerate(parts)]


def owner_steps(n_row, n_col, owner):
    row, col = lax.axis_index("row"), lax.axis_index("col")
    here = ring_place(row, n_row)
    return [lax.rem(here - ring_place(owner[col ^ m], n_row) + n_row, n_row) for m in range(n_col)]


def start_picks(pieces, n_row, steps, place, sems):
    low = pieces[0].shape[0] // 2

    def copy(m, k, h):
        if k == n_row // 2:
            source = pieces[n_row if h else k]
        else:
            source = pieces[k].at[pl.ds(h * low, low)]
        return pltpu.make_async_copy(source, place(m, h), sems[h].at[m])

    for m, step in enumerate(steps):
        for k in range(n_row):

            @pl.when(step == k)
            def _():
                copy(m, k, 0).start()
                copy(m, k, 1).start()

    return [copy(m, 0, h) for m in range(len(steps)) for h in range(2)]


def pick_left(n_row, n_col, owner, *refs):
    pieces, outs, sems = refs[: n_row + 1], refs[n_row + 1 : -2], refs[-2:]
    shard = pieces[0].shape[0]
    place = lambda m, h: outs[m].at[pl.ds(h * shard // 2, shard // 2)]
    for copy in start_picks(pieces, n_row, owner_steps(n_row, n_col, owner), place, sems):
        copy.wait()


def picked_left(pieces, owner, n_row, n_col):
    shard, width = pieces[0].shape
    return pl.pallas_call(
        functools.partial(pick_left, n_row, n_col),
        out_shape=[jax.ShapeDtypeStruct((shard, width), BF16)] * n_col,
        in_specs=[SMEM] + [HBM] * (n_row + 1),
        out_specs=[VMEM] * n_col,
        scratch_shapes=[pltpu.SemaphoreType.DMA((n_col,))] * 2,
        cost_estimate=pl.CostEstimate(flops=0, bytes_accessed=3 << 20, transcendentals=0),
        name="pick_left",
    )(owner, *pieces)


def couple(n_rights, *refs):
    rights, mates = refs[:n_rights], refs[n_rights : -n_rights - 4]
    outs = refs[-n_rights - 4 : -4]
    theirs, mine, sem, part_sem = refs[-4:]
    pair, half = rights[0].shape
    shard = pair // 2
    col = lax.axis_index("col")
    loads = [
        pltpu.make_async_copy(right, theirs.at[pl.ds(d * pair, pair)], sem.at[d]) for d, right in enumerate(rights)
    ]
    parts = []
    for m, mate in enumerate([rights[0], *mates]):
        for t in range(2):
            spot = pl.ds(pl.multiple_of((col ^ (2 * m) ^ t) * shard, shard), shard)
            parts.append(
                pltpu.make_async_copy(mate.at[pl.ds(t * shard, shard)], mine.at[spot], part_sem.at[2 * m + t])
            )
    for copy in [*loads, *parts]:
        copy.start()
    for copy in [*loads, *parts]:
        copy.wait()
    product = nt(theirs[...], mine[...]).astype(BF16)
    for d in range(n_rights):
        outs[d][...] = product[d * pair : (d + 1) * pair]


def coupled(rights, mates, n_col):
    pair, half = rights[0].shape
    rank = n_col * pair // 2
    count = len(rights)
    return pl.pallas_call(
        functools.partial(couple, count),
        out_shape=[jax.ShapeDtypeStruct((pair, rank), BF16)] * count,
        in_specs=[HBM] * (count + len(mates)),
        out_specs=[VMEM] * count,
        scratch_shapes=[
            pltpu.VMEM((count * pair, half), BF16),
            pltpu.VMEM((rank, half), BF16),
            pltpu.SemaphoreType.DMA((count,)),
            pltpu.SemaphoreType.DMA((n_col,)),
        ],
        compiler_params=pltpu.CompilerParams(vmem_limit_bytes=32 << 20),
        cost_estimate=pl.CostEstimate(
            flops=2 * count * pair * rank * half, bytes_accessed=3 << 20, transcendentals=0
        ),
        name="coupling",
    )(*rights, *mates)


def pick_products(n_row, n_col, owner, *refs):
    pieces, outs = refs[:n_row], refs[n_row:]
    odd = lax.rem(lax.axis_index("col"), 2) == 1
    for m, step in enumerate(owner_steps(n_row, n_col, owner)):
        at = jnp.where(odd, lax.rem(n_row - step, n_row), step)
        for k in range(n_row):

            @pl.when(at == k)
            def _():
                outs[m][...] = pieces[k][...]


def picked_products(pieces, owner, n_row, n_col):
    return pl.pallas_call(
        functools.partial(pick_products, n_row, n_col),
        out_shape=[jax.ShapeDtypeStruct(pieces[0].shape, BF16)] * n_col,
        in_specs=[SMEM] + [VMEM] * n_row,
        out_specs=[VMEM] * n_col,
        cost_estimate=pl.CostEstimate(flops=0, bytes_accessed=1 << 20, transcendentals=0),
        name="pick_products",
    )(owner, *pieces)


def grams(n_col, u_hbm, v_hbm, *refs):
    h_ref, cu_ref, u_ref, v_ref, uit, sem, part_sem = refs[n_col:]
    rank = cu_ref.shape[0]
    loads = [pltpu.make_async_copy(v_hbm, v_ref, sem.at[0]), pltpu.make_async_copy(u_hbm, u_ref, sem.at[1])]
    parts = part_copies(refs[:n_col], uit, part_sem)
    for copy in [*loads, *parts]:
        copy.start()
    top, bottom = pl.ds(0, rank), pl.ds(rank, rank)
    loads[0].wait()
    cu_ref[...] = tn(v_ref[...], v_ref[...])
    loads[1].wait()
    h_ref[top, :rank] = tn(u_ref[...], u_ref[...])
    for copy in parts:
        copy.wait()
    cross = nn(uit[...], u_ref[...])
    h_ref[bottom, :rank] = cross
    h_ref[top, rank:] = cross.T
    h_ref[bottom, rank:] = nt(uit[...], uit[...])


def gram_products(u, v, parts):
    rows, rank = u.shape
    tall = pltpu.VMEM((rows, rank), BF16)
    return pl.pallas_call(
        functools.partial(grams, len(parts)),
        out_shape=[jax.ShapeDtypeStruct((2 * rank, 2 * rank), F32), jax.ShapeDtypeStruct((rank, rank), F32)],
        in_specs=[HBM] * (2 + len(parts)),
        out_specs=[VMEM] * 2,
        scratch_shapes=[
            tall,
            tall,
            pltpu.VMEM((rank, rows), BF16),
            pltpu.SemaphoreType.DMA((2,)),
            pltpu.SemaphoreType.DMA((len(parts),)),
        ],
        compiler_params=pltpu.CompilerParams(vmem_limit_bytes=40 << 20),
        cost_estimate=pl.CostEstimate(flops=8 * rank * rank * rows, bytes_accessed=6 << 20, transcendentals=0),
        name="grams",
    )(u, v, *parts)


def lower_half(e, eye, below):
    return jnp.where(below, e, jnp.where(eye, 0.5 * e, 0.0))


def finish(n_row, n_col, old_ref, goal_ref, panel, owner, u_hbm, v_hbm, h_hbm, cu_hbm, *refs):
    ui_hbm, ujt_hbm, kt_in = refs[:n_col], refs[n_col : 2 * n_col], refs[2 * n_col : 3 * n_col]
    (q_hbm, w_hbm, u_ref, v_ref, uit_ref, h_ref, cu_ref, ujt, q_ref, w_ref, sides, kt, mf, hm, gn, y_ref, a_ref) = refs[
        3 * n_col : -5
    ]
    in_sem, ui_sem, uj_sem, q_sem, w_sem = refs[-5:]
    rows, rank = u_ref.shape
    shard = rank // n_col
    row, col = lax.axis_index("row"), lax.axis_index("col")
    loads = [
        pltpu.make_async_copy(src, dst, in_sem.at[t])
        for t, (src, dst) in enumerate(
            [(v_hbm, v_ref), (h_hbm, h_ref), (cu_hbm, cu_ref), (u_hbm, u_ref)]
        )
    ]
    ui_loads = part_copies(ui_hbm, uit_ref, ui_sem)
    uj_loads = part_copies(ujt_hbm, ujt, uj_sem)
    for copy in [*uj_loads, *loads, *ui_loads]:
        copy.start()
    old, goal, here, there = old_ref[0, 0], goal_ref[0, 0], panel[row], panel[owner[col]]
    sub = lax.broadcasted_iota(jnp.int32, (rank, rank), 0)
    lane = lax.broadcasted_iota(jnp.int32, (rank, rank), 1)
    eye, below = sub == lane, sub > lane
    one = jnp.where(eye, 1.0, 0.0).astype(F32)
    for m in range(n_col):
        other = col ^ m
        for t in range(2):
            spot = pl.ds(pl.multiple_of((other ^ t) * shard, shard), shard)
            sides[lax.rem(other, 2), spot, :] = kt_in[m][t * shard : (t + 1) * shard].astype(F32)
    step = owner_steps(n_row, 1, owner)[0]
    for side, at in enumerate((step, lax.rem(n_row - step, n_row))):

        @pl.when(at > n_row // 2)
        def _():
            sides[side] = sides[side].T

    zero = jnp.zeros((rank, rank), F32)
    kt[...] = jnp.where((sub < there) & (lane < here), sides[0] + sides[1], zero).astype(BF16)
    for copy in [*uj_loads, *loads[:1]]:
        copy.wait()
    cl = jnp.where(lane < goal, nn(ujt[...], v_ref[...]), zero).astype(BF16)
    for copy in loads[1:3]:
        copy.wait()
    cu = jnp.where((sub < old) & (lane < goal), cu_ref[...], zero).astype(BF16).astype(F32)
    mf[pl.ds(0, rank), :] = cu
    mf[pl.ds(rank, rank), :] = -tn(kt[...], cl)
    hm[...] = nn(h_ref[...], mf[...], HIGHEST)
    g = tn(mf[...], hm[...], HIGHEST) + jnp.where(eye & (lane >= goal), 1.0, 0.0)
    dg = jnp.where(eye, g, 0.0)
    d_row = lax.rsqrt(jnp.sum(dg, axis=0, keepdims=True))
    d_col = lax.rsqrt(jnp.sum(dg, axis=1, keepdims=True))
    gn[...] = g * d_col * d_row
    scale = rank / jnp.sum(gn[...] * gn[...], keepdims=True)
    y_ref[...] = (one - lower_half(gn[...] * scale - one, eye, below)) * jnp.sqrt(scale)
    gb = gn[...].astype(BF16)

    def rough(carry):
        step, _ = carry
        y = y_ref[...]
        yb = y.astype(BF16)
        e = nt(nn(yb, gb).astype(BF16), yb) - one
        y_ref[...] = y - nn(lower_half(e, eye, below).astype(BF16), yb)
        return step + 1, jnp.max(jnp.abs(e))

    def fine(carry):
        step, _ = carry
        y = y_ref[...]
        e = nt(nn(y, gn[...], HIGHEST), y, HIGHEST) - one
        y_ref[...] = y - nn(lower_half(e, eye, below), y, HIGHEST)
        return step + 1, jnp.max(jnp.abs(e))

    lax.while_loop(lambda c: (c[0] < ROUGH_STEPS) & (c[1] > ROUGH), rough, (jnp.int32(0), F32(1.0)))
    _, err = lax.while_loop(lambda c: (c[0] < FINE_STEPS) & (c[1] > FINE), fine, (jnp.int32(0), F32(1.0)))

    lowest = jnp.min(jnp.where(eye, y_ref[...], 1.0))

    @pl.when(jnp.logical_not((err <= FINE) & (lowest > 0.0)))
    def _():
        a_ref[...] = gn[...]
        y_ref[...] = one

        def pivot(k, _):
            col = jnp.sum(jnp.where(lane == k, a_ref[...], 0.0), axis=1, keepdims=True)
            row = jnp.sum(jnp.where(sub == k, a_ref[...], 0.0), axis=0, keepdims=True)
            yrow = jnp.sum(jnp.where(sub == k, y_ref[...], 0.0), axis=0, keepdims=True)
            top = jnp.sum(jnp.where(lax.broadcasted_iota(jnp.int32, (1, rank), 1) == k, row, 0.0))
            inv = 1.0 / jnp.sqrt(jnp.full((1, rank), top))
            row, yrow = row * inv, yrow * inv
            col = jnp.where(lax.broadcasted_iota(jnp.int32, (rank, 1), 0) > k, col * inv[:, :1], 0.0)
            a_ref[...] = a_ref[...] - col * row
            y_ref[...] = jnp.where(sub == k, yrow, y_ref[...] - col * yrow)
            return 0

        lax.fori_loop(0, rank, pivot, 0)

    x = y_ref[...] * d_row
    root = math.sqrt(rows)
    c = nt(mf[...], x, HIGHEST) * root
    r = nt(hm[...], x, HIGHEST)
    r_up = jnp.where(sub < old, r[:rank], 0.0).astype(BF16)
    r_low = (-nn(kt[...].astype(F32), r[rank:], HIGHEST)).astype(BF16)
    ch, cl2 = halves(c)
    cu_h, cu_l, cl_h, cl_l = ch[:rank], cl2[:rank], ch[rank:], cl2[rank:]
    for copy in [*loads[3:], *ui_loads]:
        copy.wait()
    step = rows // q_sem.shape[0]
    stores = []
    for t in range(rows // step):
        at = pl.ds(t * step, step)
        u, v = u_ref[at, :], v_ref[at, :]
        ui, uj = uit_ref[:, at], ujt[:, at]
        q_ref[at, :] = (nn(u, cu_h) + nn(u, cu_l) + tn(ui, cl_h) + tn(ui, cl_l)).astype(BF16)
        stores.append(pltpu.make_async_copy(q_ref.at[at], q_hbm.at[at], q_sem.at[t]))
        stores[-1].start()
        w_ref[at, :] = (nn(v, r_up) + tn(uj, r_low)).astype(BF16)
        stores.append(pltpu.make_async_copy(w_ref.at[at], w_hbm.at[at], w_sem.at[t]))
        stores[-1].start()
    for copy in stores:
        copy.wait()


def body(tile_basis, tile_coeffs, panel_basis, panel_coeffs, tile_rank, target_rank, panel_rank, owner_row):
    n_row, n_col = lax.axis_size("row"), lax.axis_size("col")
    u, v = tile_basis[0, 0], tile_coeffs[0, 0]
    pu, pv = panel_basis[0], panel_coeffs[0]
    rows, rank = u.shape

    odd = lax.axis_index("col") % 2
    cut = rows // 2
    own = lax.dynamic_slice_in_dim(pv, odd * cut, cut, 1)
    mate = swap(lax.dynamic_slice_in_dim(pv, (1 - odd) * cut, cut, 1), "col", n_col, 1)
    pair = jnp.concatenate([own, mate], 0)

    lefts, pairs = {0: pu}, {0: pair}

    def grow(have, gate, bits):
        for bit in bits:
            for m in list(have):
                have[m | bit] = swap(after(have[m], *gate), "col", n_col, bit)
        return tuple(have.values())

    high = [n_col >> t for t in range(1, n_col.bit_length() - 1)]
    half = n_row // 2
    gates = {half - 1: lambda: grow(lefts, (), high), half: lambda: grow(pairs, lefts.values(), high)}
    us, vs = rings(pu, pair, n_row, n_col, gates)
    grow(lefts, us[:3], [1])
    ui_parts = [lefts[m] for m in range(n_col)]

    ujs = picked_left(us, owner_row, n_row, n_col)
    ujs = [ujs[0]] + [swap(ujs[m], "col", n_col, m) for m in range(1, n_col)]
    near = coupled(vs, [pairs[m] for m in range(2, n_col, 2)], n_col)
    far = [lax.ppermute(near[d], ("row", "col"), farther(n_row, n_col, -d)) for d in range(half - 1, 0, -1)]
    kts = picked_products([*near, *far], owner_row, n_row, n_col)
    h, core_up = gram_products(u, v, [after(ui_parts[0], near[0]), *ui_parts[1:]])
    kts = [kts[0]] + [swap(kts[m], "col", n_col, m) for m in range(1, n_col)]

    out = jax.ShapeDtypeStruct((rows, rank), BF16)
    square = pltpu.VMEM((rank, rank), F32)
    tall, wide = pltpu.VMEM((rows, rank), BF16), pltpu.VMEM((rank, rows), BF16)
    tiles = rows // 256 if rows % 256 == 0 else 1
    fresh_basis, fresh_coeffs = pl.pallas_call(
        functools.partial(finish, n_row, n_col),
        out_shape=(out, out),
        in_specs=[SMEM] * 4 + [HBM] * (4 + 2 * n_col) + [VMEM] * n_col,
        out_specs=(HBM, HBM),
        scratch_shapes=[
            tall,
            tall,
            wide,
            pltpu.VMEM((2 * rank, 2 * rank), F32),
            square,
            wide,
            tall,
            tall,
            pltpu.VMEM((2, rank, rank), F32),
            pltpu.VMEM((rank, rank), BF16),
            pltpu.VMEM((2 * rank, rank), F32),
            pltpu.VMEM((2 * rank, rank), F32),
            square,
            square,
            square,
            pltpu.SemaphoreType.DMA((4,)),
            pltpu.SemaphoreType.DMA((n_col,)),
            pltpu.SemaphoreType.DMA((n_col,)),
            pltpu.SemaphoreType.DMA((tiles,)),
            pltpu.SemaphoreType.DMA((tiles,)),
        ],
        compiler_params=pltpu.CompilerParams(vmem_limit_bytes=40 << 20),
        cost_estimate=pl.CostEstimate(flops=8 << 30, bytes_accessed=12 << 20, transcendentals=0),
        name="finish",
    )(tile_rank, target_rank, panel_rank, owner_row, u, v, h, core_up, *ui_parts, *ujs, *kts)
    return fresh_basis[None, None], fresh_coeffs[None, None]


def solution(mesh):
    tiles, panels = P("row", "col", None, None), P("row", "col", None)
    return jax.shard_map(
        body,
        mesh=mesh,
        in_specs=(tiles, tiles, panels, panels, P("row", "col"), P("row", "col"), P(), P()),
        out_specs=(tiles, tiles),
        check_vma=False,
    )
```

time: 153 us -> 150 us (0.980)
  local copies, waits for them, and re-layouts: 9.01 us -> 2.39 us
  Pallas kernels: 82 us -> 86 us
    unnamed x38 -> x44, local copies, waits for them, and re-layouts: 8.01 us -> 1.31 us
    pallas_call x3 -> x4, Pallas kernels: 79 us -> 82.8 us  [the longest x1 76 us: body(): pl.pallas_call(functools.partial(finish, n_row, n_col), out_shape=(out, o...]
    ppermute x21 -> x15, waiting for transfers between devices: 21 us -> 19.9 us  [the longest x6 11.1 us: rings(): fwd, bwd = (lax.ppermute(fwd, 'row', ahead), lax.ppermute(bwd, 'row', back))]
    ppermute x12 -> x11, starting transfers between devices: 8.48 us -> 9.35 us  [swap(): return lax.ppermute(x, axis, [(i, i ^ m) for i in range(n)])]
    ppermute x21 -> x15, starting transfers between devices: 23 us -> 23.7 us  [the longest x4 10 us: rings(): lax.ppermute(rights[-1], ('row', 'col'), farther(n_row, n_col, 1))]
    ppermute x12 -> x11, waiting for transfers between devices: 6.36 us -> 5.9 us  [swap(): return lax.ppermute(x, axis, [(i, i ^ m) for i in range(n)])]
  transfers between devices with their start and end apart: 33 -> 26, of which waited for: 10 -> 13; matrix products, arithmetic and copies ran while one was open for 1% -> 0% of each run, Pallas kernels for 5% -> 7%
where the time goes in v3:
time: 150 us
  Pallas kernels  86 us (57%)
  starting transfers between devices  33 us (22%)
  waiting for transfers between devices  25.8 us (17%)
  local copies, waits for them, and re-layouts  2.39 us (2%)
  between operations  2.36 us (2%)
    pallas_call x1, Pallas kernels, body(): pl.pallas_call(functools.partial(finish, n_row, n_col), out_shape=(out, o...  76 us
    ppermute x6, waiting for transfers between devices, rings(): fwd, bwd = (lax.ppermute(fwd, 'row', ahead), lax.ppermute(bwd, 'row', back))  11.1 us
    ppermute x4, starting transfers between devices, rings(): lax.ppermute(rights[-1], ('row', 'col'), farther(n_row, n_col, 1))  10 us
    ppermute x11, starting transfers between devices, swap(): return lax.ppermute(x, axis, [(i, i ^ m) for i in range(n)])  9.35 us
    ppermute x4, waiting for transfers between devices, rings(): lax.ppermute(rights[-1], ('row', 'col'), farther(n_row, n_col, 1))  6.74 us
    ppermute x6, starting transfers between devices, rings(): fwd, bwd = (lax.ppermute(fwd, 'row', ahead), lax.ppermute(bwd, 'row', back))  6.13 us
    ppermute x11, waiting for transfers between devices, swap(): return lax.ppermute(x, axis, [(i, i ^ m) for i in range(n)])  5.9 us
    ppermute x3, starting transfers between devices, body(): lax.ppermute(near[d], ('row', 'col'), farther(n_row, n_col, -d))  5.44 us
  transfers between devices with their start and end apart: 26, of which 13 were waited for; matrix products, arithmetic and copies ran while one was open for 0% of the time, Pallas kernels for 7%

profile of v3, /device:TPU:0, one launch (start us, length us, event | category | flops | bytes accessed | tf_op | source)
XLA Modules:
  0.0 149.5 jit_solution(10053310400259528197)
XLA Ops:
  0.6 0.0 copy-start
  0.7 1.0 dynamic-slice_bitcast_fusion.1
  1.7 0.5 collective-permute-start
  2.2 1.0 collective-permute-done
  3.3 3.0 %collective-permute-start.1 = (bf16[128,1152]{1,0:T(8,128)(2,1)S(1)}, bf16[128,1152]{1,0:T(8,128)(2,1)S(1)}, u32[]{:S(2)}, u32[]{:S(2)}) collective-permute-start(bf16[128,1152]{1,0:T(8,128)(2,1)S(1)} %pad_maximum_fusion.refs_0_), channel_id=1, source_target_pairs={{0,8},{1,5},{2,10},{3,7},{8,16},{9,1},{10,18},{11,3},{16,24},{17,9... | collective-permute-start | bytes 884744 | tf_op jit(solution)/shard_map/ppermute | solution.py:67
  6.3 0.0 collective-permute-start.8
  6.3 2.0 %collective-permute-start.7 = (bf16[64,2304]{1,0:T(8,128)(2,1)S(1)}, bf16[64,2304]{1,0:T(8,128)(2,1)S(1)}, u32[]{:S(2)}, u32[]{:S(2)}) collective-permute-start(bf16[64,2304]{1,0:T(8,128)(2,1)S(1)} %bitcast.11), channel_id=1, source_target_pairs={{0,8},{8,16},{16,24},{24,28},{28,20},{20,12},{12,4},{4,0},{1,9},{9... | collective-permute-start | bytes 884744 | tf_op jit(solution)/shard_map/ppermute | solution.py:74
  8.3 4.8 %collective-permute-done.1.refs_1_ = bf16[128,1152]{1,0:T(8,128)(2,1)S(1)} collective-permute-done((bf16[128,1152]{1,0:T(8,128)(2,1)S(1)}, bf16[128,1152]{1,0:T(8,128)(2,1)S(1)}, u32[]{:S(2)}, u32[]{:S(2)}) %collective-permute-start.1) | collective-permute-done | bytes 294944 | tf_op jit(solution)/shard_map/ppermute | solution.py:67
  13.1 2.5 %collective-permute-start.2 = (bf16[128,1152]{1,0:T(8,128)(2,1)S(1)}, bf16[128,1152]{1,0:T(8,128)(2,1)S(1)}, u32[]{:S(2)}, u32[]{:S(2)}) collective-permute-start(bf16[128,1152]{1,0:T(8,128)(2,1)S(1)} %collective-permute-done.1.refs_1_), channel_id=1, source_target_pairs={{0,8},{1,5},{2,10},{3,7},{8,16},{9,1},{10,18},{11,3},{16,24},{17,9... | collective-permute-start | bytes 884744 | tf_op jit(solution)/shard_map/ppermute | solution.py:67
  15.6 1.5 collective-permute-start.5
  17.1 0.0 collective-permute-done.8.refs_7_
  17.1 0.1 collective-permute-done.7.refs_1_
  17.2 2.1 %collective-permute-start.9 = (bf16[64,2304]{1,0:T(8,128)(2,1)S(1)}, bf16[64,2304]{1,0:T(8,128)(2,1)S(1)}, u32[]{:S(2)}, u32[]{:S(2)}) collective-permute-start(bf16[64,2304]{1,0:T(8,128)(2,1)S(1)} %collective-permute-done.7.refs_1_), channel_id=1, source_target_pairs={{0,8},{8,16},{16,24},{24,28},{28,20},{20,12},{12,4},{4,0},{1,9},{9... | collective-permute-start | bytes 884744 | tf_op jit(solution)/shard_map/ppermute | solution.py:74
  19.3 0.0 collective-permute-start.12
  19.3 1.9 %collective-permute-done.2.refs_2_ = bf16[128,1152]{1,0:T(8,128)(2,1)S(1)} collective-permute-done((bf16[128,1152]{1,0:T(8,128)(2,1)S(1)}, bf16[128,1152]{1,0:T(8,128)(2,1)S(1)}, u32[]{:S(2)}, u32[]{:S(2)}) %collective-permute-start.2) | collective-permute-done | bytes 294944 | tf_op jit(solution)/shard_map/ppermute | solution.py:67
  21.2 2.4 %collective-permute-start.3 = (bf16[128,1152]{1,0:T(8,128)(2,1)S(1)}, bf16[128,1152]{1,0:T(8,128)(2,1)S(1)}, u32[]{:S(2)}, u32[]{:S(2)}) collective-permute-start(bf16[128,1152]{1,0:T(8,128)(2,1)S(1)} %collective-permute-done.2.refs_2_), channel_id=1, source_target_pairs={{0,8},{1,5},{2,10},{3,7},{8,16},{9,1},{10,18},{11,3},{16,24},{17,9... | collective-permute-start | bytes 884744 | tf_op jit(solution)/shard_map/ppermute | solution.py:67
  23.6 0.0 collective-permute-done.5.refs_2_
  23.6 1.5 collective-permute-start.6
  25.1 1.6 %collective-permute-done.9.refs_2_ = bf16[64,2304]{1,0:T(8,128)(2,1)S(1)} collective-permute-done((bf16[64,2304]{1,0:T(8,128)(2,1)S(1)}, bf16[64,2304]{1,0:T(8,128)(2,1)S(1)}, u32[]{:S(2)}, u32[]{:S(2)}) %collective-permute-start.9) | collective-permute-done | bytes 294944 | tf_op jit(solution)/shard_map/ppermute | solution.py:74
  26.7 2.5 %collective-permute-done.12.refs_6_ = bf16[64,2304]{1,0:T(8,128)(2,1)S(1)} collective-permute-done((bf16[64,2304]{1,0:T(8,128)(2,1)S(1)}, bf16[64,2304]{1,0:T(8,128)(2,1)S(1)}, u32[]{:S(2)}, u32[]{:S(2)}) %collective-permute-start.12) | collective-permute-done | bytes 294944 | tf_op jit(solution)/shard_map/ppermute | solution.py:74
  29.2 1.1 collective-permute-start.13
  30.3 1.0 collective-permute-start.14
  31.3 0.0 collective-permute-done.3.refs_3_
  31.3 2.1 %collective-permute-start.4 = (bf16[128,1152]{1,0:T(8,128)(2,1)S(1)}, bf16[128,1152]{1,0:T(8,128)(2,1)S(1)}, u32[]{:S(2)}, u32[]{:S(2)}) collective-permute-start(bf16[128,1152]{1,0:T(8,128)(2,1)S(1)} %collective-permute-done.3.refs_3_), channel_id=1, source_target_pairs={{0,8},{1,5},{2,10},{3,7},{8,16},{9,1},{10,18},{11,3},{16,24},{17,9... | collective-permute-start | bytes 884744 | tf_op jit(solution)/shard_map/ppermute | solution.py:67
  33.4 0.0 collective-permute-done.6.refs_5_
  33.4 2.8 %collective-permute-done.13.refs_3_ = bf16[64,2304]{1,0:T(8,128)(2,1)S(1)} collective-permute-done((bf16[64,2304]{1,0:T(8,128)(2,1)S(1)}, bf16[64,2304]{1,0:T(8,128)(2,1)S(1)}, u32[]{:S(2)}, u32[]{:S(2)}) %collective-permute-start.13) | collective-permute-done | bytes 294944 | tf_op jit(solution)/shard_map/ppermute | solution.py:74
  36.2 4.1 %collective-permute-done.14.refs_5_ = bf16[64,2304]{1,0:T(8,128)(2,1)S(1)} collective-permute-done((bf16[64,2304]{1,0:T(8,128)(2,1)S(1)}, bf16[64,2304]{1,0:T(8,128)(2,1)S(1)}, u32[]{:S(2)}, u32[]{:S(2)}) %collective-permute-start.14) | collective-permute-done | bytes 294944 | tf_op jit(solution)/shard_map/ppermute | solution.py:74
  40.3 1.0 collective-permute-start.16
  41.3 1.1 collective-permute-start.15
  42.4 0.0 collective-permute-done.4.refs_4_
  42.4 1.8 %coupling.1 = (bf16[128,256]{1,0:T(8,128)(2,1)S(1)}, bf16[128,256]{1,0:T(8,128)(2,1)S(1)}, bf16[128,256]{1,0:T(8,128)(2,1)S(1)}, bf16[128,256]{1,0:T(8,128)(2,1)S(1)}, bf16[128,256]{1,0:T(8,128)(2,1)S(1)}) custom-call(bf16[128,1152]{1,0:T(8,128)(2,1)S(1)} %pad_maximum_fusion.refs_0_, bf16[128,1152]{1,0:T(8,128)(2,1)S(1)} %collective-permute-done.1.refs_1_, ...), custom_call_target="tpu_custom_call" | custom-call | flops 377487360 | bytes 3145728 | tf_op jit(solution)/shard_map/coupling/pallas_call | solution.py:174
  44.2 0.6 copy-done.2
  44.8 0.6 copy-done.6
  45.5 0.0 copy-start.1
  45.5 0.0 copy-start.8
  45.5 0.0 copy-start.9
  45.5 1.0 collective-permute-start.22
  46.5 0.0 collective-permute-start.10
  46.5 0.5 collective-permute-start.11
  47.0 0.0 collective-permute-done.16.refs_8_
  47.0 0.3 collective-permute-done.15.refs_4_
  47.3 3.1 %pick_left.1 = (bf16[64,2304]{1,0:T(8,128)(2,1)}, bf16[64,2304]{1,0:T(8,128)(2,1)}, bf16[64,2304]{1,0:T(8,128)(2,1)}, bf16[64,2304]{1,0:T(8,128)(2,1)}) custom-call(s32[4]{0:T(128)} %owner.5, bf16[64,2304]{1,0:T(8,128)(2,1)} %bitcast.9, bf16[64,2304]{1,0:T(8,128)(2,1)} %copy-done.16, bf16[64,2304]{1,0:T(8,128)(2,1)} %copy-done.17, ...), custom_call_target="tpu_custom_call" | custom-call | bytes 3145728 | tf_op jit(solution)/shard_map/pick_left/pallas_call | solution.py:133
  50.4 0.1 collective-permute-start.17
  50.5 1.2 collective-permute-start.21
  51.7 0.0 collective-permute-done.22.refs_7_
  51.7 3.2 %collective-permute-start.20 = (bf16[128,256]{1,0:T(8,128)(2,1)S(1)}, bf16[128,256]{1,0:T(8,128)(2,1)S(1)}, u32[]{:S(2)}, u32[]{:S(2)}) collective-permute-start(bf16[128,256]{1,0:T(8,128)(2,1)S(1)} %get-tuple-element.48.refs_3_), channel_id=1, source_target_pairs={{0,20},{1,25},{2,22},{3,27},{8,12},{9,29},{10,14},{11,31},{16,4},{... | collective-permute-start | bytes 196616 | tf_op jit(solution)/shard_map/ppermute | solution.py:412
  55.0 1.5 collective-permute-done.21.refs_6_
  56.4 1.5 collective-permute-start.18
  57.9 0.3 collective-permute-done.20.refs_5_
  58.2 1.9 %collective-permute-start.19 = (bf16[64,2304]{1,0:T(8,128)(2,1)}, bf16[64,2304]{1,0:T(8,128)(2,1)}, u32[]{:S(2)}, u32[]{:S(2)}) collective-permute-start(bf16[64,2304]{1,0:T(8,128)(2,1)} %get-tuple-element.45), channel_id=1, source_target_pairs={{0,3},{1,2},{2,1},{3,0},{4,7},{5,6},{6,5},{7,4},{8,11},{9,10},{10,... | collective-permute-start | bytes 884744 | tf_op jit(solution)/shard_map/ppermute | solution.py:86
  61.4 2.0 %pick_products.1 = (bf16[128,256]{1,0:T(8,128)(2,1)}, bf16[128,256]{1,0:T(8,128)(2,1)}, bf16[128,256]{1,0:T(8,128)(2,1)}, bf16[128,256]{1,0:T(8,128)(2,1)}) custom-call(s32[4]{0:T(128)} %owner.5, bf16[128,256]{1,0:T(8,128)(2,1)} %copy-done.2, bf16[128,256]{1,0:T(8,128)(2,1)} %copy-done.3, bf16[128,256]{1,0:T(8,128)(2,1)} %copy-done.4, ...), custom_call_target="tpu_custom_call" | custom-call | bytes 1048576 | tf_op jit(solution)/shard_map/pick_products/pallas_call | solution.py:206
  63.4 0.0 collective-permute-done.10.refs_1_
  63.4 0.1 collective-permute-start.23
  63.4 0.0 collective-permute-done.11.refs_3_
  63.4 0.6 collective-permute-start.24
  64.0 0.0 collective-permute-done.17.refs_5_
  64.0 1.3 collective-permute-start.25
  65.3 0.0 copy-start.12
  65.4 3.1 %grams.1 = (f32[512,512]{1,0:T(8,128)S(1)}, f32[256,256]{1,0:T(8,128)S(1)}) custom-call(bf16[2304,256]{1,0:T(8,128)(2,1)S(1)} %bitcast.16, bf16[2304,256]{1,0:T(8,128)(2,1)S(1)} %bitcast.18, bf16[64,2304]{1,0:T(8,128)(2,1)S(1)} %bitcast.14, bf16[64,2304]{1,0:T(8,128)(2,1)} %collective-permute-done.10.refs_1_, ...), custom_call_target="tpu_custom_call" | custom-call | flops 1207959552 | bytes 6291456 | tf_op jit(solution)/shard_map/grams/pallas_call | solution.py:239
  68.4 0.0 collective-permute-done.18.refs_6_
  68.4 3.3 %collective-permute-done.19.refs_7_ = bf16[64,2304]{1,0:T(8,128)(2,1)} collective-permute-done((bf16[64,2304]{1,0:T(8,128)(2,1)}, bf16[64,2304]{1,0:T(8,128)(2,1)}, u32[]{:S(2)}, u32[]{:S(2)}) %collective-permute-start.19) | collective-permute-done | bytes 294944 | tf_op jit(solution)/shard_map/ppermute | solution.py:86
  71.7 0.0 collective-permute-done.23.refs_9_
  71.7 1.6 %collective-permute-done.24.refs_10_ = bf16[128,256]{1,0:T(8,128)(2,1)S(1)} collective-permute-done((bf16[128,256]{1,0:T(8,128)(2,1)}, bf16[128,256]{1,0:T(8,128)(2,1)S(1)}, u32[]{:S(2)}, u32[]{:S(2)}) %collective-permute-start.24) | collective-permute-done | bytes 65568 | tf_op jit(solution)/shard_map/ppermute | solution.py:86
  73.3 76.0 %finish.1 = (bf16[2304,256]{1,0:T(8,128)(2,1)}, bf16[2304,256]{1,0:T(8,128)(2,1)}) custom-call(s32[1,1]{1,0:T(1,128)S(6)} %copy.10.old_ref, s32[1,1]{1,0:T(1,128)S(6)} %copy.11.goal_ref, s32[8]{0:T(128)S(1)} %copy-done.12, s32[4]{0:T(128)S(1)} %copy-done.7, bf16[2304,256]{1,0:T(8,128)(2,1)S(1)} %bitcast.17, bf16[2304,256]{1,0:T(8,128)(2,1)S(1)} %bitcast.19, ...), custom_call_target="tpu_custom_call" | custom-call | flops 8589934592 | bytes 12582912 | tf_op jit(solution)/shard_map/finish/pallas_call | solution.py:421
  (41 shorter events, 0.1 us)
Async XLA Ops:
  0.6 5.6 %copy-start = (bf16[1,64,2304]{2,1,0:T(8,128)(2,1)S(1)}, bf16[1,64,2304]{2,1,0:T(8,128)(2,1)}, u32[]{:S(2)}) copy-start(bf16[1,64,2304]{2,1,0:T(8,128)(2,1)} %param.10) | copy-start | bytes 884740
  1.7 1.5 %collective-permute-start = (bf16[64,1152]{1,0:T(8,128)(2,1)S(1)}, bf16[64,1152]{1,0:T(8,128)(2,1)S(1)}, u32[]{:S(2)}, u32[]{:S(2)}) collective-permute-start(bf16[64,1152]{1,0:T(8,128)(2,1)S(1)} %get-tuple-element.57), channel_id=1, source_target_pairs={{0,1},{1,0},{2,3},{3,2},{4,5},{5,4},{6,7},{7,6},{8,9},{9,8},{10,11... | collective-permute-start | bytes 442376 | tf_op jit(solution)/shard_map/ppermute | solution.py:86
  3.3 9.9 %collective-permute-start.1 = (bf16[128,1152]{1,0:T(8,128)(2,1)S(1)}, bf16[128,1152]{1,0:T(8,128)(2,1)S(1)}, u32[]{:S(2)}, u32[]{:S(2)}) collective-permute-start(bf16[128,1152]{1,0:T(8,128)(2,1)S(1)} %pad_maximum_fusion.refs_0_), channel_id=1, source_target_pairs={{0,8},{1,5},{2,10},{3,7},{8,16},{9,1},{10,18},{11,3},{16,24},{17,9... | collective-permute-start | bytes 884744 | tf_op jit(solution)/shard_map/ppermute | solution.py:67
  6.3 10.8 %collective-permute-start.8 = (bf16[64,2304]{1,0:T(8,128)(2,1)S(1)}, bf16[64,2304]{1,0:T(8,128)(2,1)S(1)}, u32[]{:S(2)}, u32[]{:S(2)}) collective-permute-start(bf16[64,2304]{1,0:T(8,128)(2,1)S(1)} %bitcast.10), channel_id=1, source_target_pairs={{8,0},{16,8},{24,16},{28,24},{20,28},{12,20},{4,12},{0,4},{9,1},{1... | collective-permute-start | bytes 884744 | tf_op jit(solution)/shard_map/ppermute | solution.py:74
  6.3 10.9 %collective-permute-start.7 = (bf16[64,2304]{1,0:T(8,128)(2,1)S(1)}, bf16[64,2304]{1,0:T(8,128)(2,1)S(1)}, u32[]{:S(2)}, u32[]{:S(2)}) collective-permute-start(bf16[64,2304]{1,0:T(8,128)(2,1)S(1)} %bitcast.11), channel_id=1, source_target_pairs={{0,8},{8,16},{16,24},{24,28},{28,20},{20,12},{12,4},{4,0},{1,9},{9... | collective-permute-start | bytes 884744 | tf_op jit(solution)/shard_map/ppermute | solution.py:74
  13.1 8.1 %collective-permute-start.2 = (bf16[128,1152]{1,0:T(8,128)(2,1)S(1)}, bf16[128,1152]{1,0:T(8,128)(2,1)S(1)}, u32[]{:S(2)}, u32[]{:S(2)}) collective-permute-start(bf16[128,1152]{1,0:T(8,128)(2,1)S(1)} %collective-permute-done.1.refs_1_), channel_id=1, source_target_pairs={{0,8},{1,5},{2,10},{3,7},{8,16},{9,1},{10,18},{11,3},{16,24},{17,9... | collective-permute-start | bytes 884744 | tf_op jit(solution)/shard_map/ppermute | solution.py:67
  15.6 8.0 %collective-permute-start.5 = (bf16[64,2304]{1,0:T(8,128)(2,1)S(1)}, bf16[64,2304]{1,0:T(8,128)(2,1)S(1)}, u32[]{:S(2)}, u32[]{:S(2)}) collective-permute-start(bf16[64,2304]{1,0:T(8,128)(2,1)S(1)} %bitcast.12), channel_id=1, source_target_pairs={{0,2},{1,3},{2,0},{3,1},{4,6},{5,7},{6,4},{7,5},{8,10},{9,11},{10,... | collective-permute-start | bytes 884744 | tf_op jit(solution)/shard_map/ppermute | solution.py:86
  17.1 9.6 %copy-start.15 = (bf16[64,2304]{1,0:T(8,128)(2,1)}, bf16[64,2304]{1,0:T(8,128)(2,1)S(1)}, u32[]{:S(2)}) copy-start(bf16[64,2304]{1,0:T(8,128)(2,1)S(1)} %collective-permute-done.8.refs_7_) | copy-start | bytes 884740
  17.2 14.1 %copy-start.16 = (bf16[64,2304]{1,0:T(8,128)(2,1)}, bf16[64,2304]{1,0:T(8,128)(2,1)S(1)}, u32[]{:S(2)}) copy-start(bf16[64,2304]{1,0:T(8,128)(2,1)S(1)} %collective-permute-done.7.refs_1_) | copy-start | bytes 884740
  17.2 9.5 %collective-permute-start.9 = (bf16[64,2304]{1,0:T(8,128)(2,1)S(1)}, bf16[64,2304]{1,0:T(8,128)(2,1)S(1)}, u32[]{:S(2)}, u32[]{:S(2)}) collective-permute-start(bf16[64,2304]{1,0:T(8,128)(2,1)S(1)} %collective-permute-done.7.refs_1_), channel_id=1, source_target_pairs={{0,8},{8,16},{16,24},{24,28},{28,20},{20,12},{12,4},{4,0},{1,9},{9... | collective-permute-start | bytes 884744 | tf_op jit(solution)/shard_map/ppermute | solution.py:74
  19.3 9.9 %collective-permute-start.12 = (bf16[64,2304]{1,0:T(8,128)(2,1)S(1)}, bf16[64,2304]{1,0:T(8,128)(2,1)S(1)}, u32[]{:S(2)}, u32[]{:S(2)}) collective-permute-start(bf16[64,2304]{1,0:T(8,128)(2,1)S(1)} %collective-permute-done.8.refs_7_), channel_id=1, source_target_pairs={{8,0},{16,8},{24,16},{28,24},{20,28},{12,20},{4,12},{0,4},{9,1},{1... | collective-permute-start | bytes 884744 | tf_op jit(solution)/shard_map/ppermute | solution.py:74
  21.2 10.1 %collective-permute-start.3 = (bf16[128,1152]{1,0:T(8,128)(2,1)S(1)}, bf16[128,1152]{1,0:T(8,128)(2,1)S(1)}, u32[]{:S(2)}, u32[]{:S(2)}) collective-permute-start(bf16[128,1152]{1,0:T(8,128)(2,1)S(1)} %collective-permute-done.2.refs_2_), channel_id=1, source_target_pairs={{0,8},{1,5},{2,10},{3,7},{8,16},{9,1},{10,18},{11,3},{16,24},{17,9... | collective-permute-start | bytes 884744 | tf_op jit(solution)/shard_map/ppermute | solution.py:67
  23.6 9.8 %collective-permute-start.6 = (bf16[128,1152]{1,0:T(8,128)(2,1)S(1)}, bf16[128,1152]{1,0:T(8,128)(2,1)S(1)}, u32[]{:S(2)}, u32[]{:S(2)}) collective-permute-start(bf16[128,1152]{1,0:T(8,128)(2,1)S(1)} %pad_maximum_fusion.refs_0_), channel_id=1, source_target_pairs={{0,2},{1,3},{2,0},{3,1},{4,6},{5,7},{6,4},{7,5},{8,10},{9,11},{10,... | collective-permute-start | bytes 884744 | tf_op jit(solution)/shard_map/ppermute | solution.py:86
  26.7 17.5 %copy-start.17 = (bf16[64,2304]{1,0:T(8,128)(2,1)}, bf16[64,2304]{1,0:T(8,128)(2,1)S(1)}, u32[]{:S(2)}) copy-start(bf16[64,2304]{1,0:T(8,128)(2,1)S(1)} %collective-permute-done.9.refs_2_) | copy-start | bytes 884740
  29.2 13.1 %copy-start.18 = (bf16[64,2304]{1,0:T(8,128)(2,1)}, bf16[64,2304]{1,0:T(8,128)(2,1)S(1)}, u32[]{:S(2)}) copy-start(bf16[64,2304]{1,0:T(8,128)(2,1)S(1)} %collective-permute-done.12.refs_6_) | copy-start | bytes 884740
  29.2 6.9 %collective-permute-start.13 = (bf16[64,2304]{1,0:T(8,128)(2,1)S(1)}, bf16[64,2304]{1,0:T(8,128)(2,1)S(1)}, u32[]{:S(2)}, u32[]{:S(2)}) collective-permute-start(bf16[64,2304]{1,0:T(8,128)(2,1)S(1)} %collective-permute-done.9.refs_2_), channel_id=1, source_target_pairs={{0,8},{8,16},{16,24},{24,28},{28,20},{20,12},{12,4},{4,0},{1,9},{9... | collective-permute-start | bytes 884744 | tf_op jit(solution)/shard_map/ppermute | solution.py:74
  30.3 9.9 %collective-permute-start.14 = (bf16[64,2304]{1,0:T(8,128)(2,1)S(1)}, bf16[64,2304]{1,0:T(8,128)(2,1)S(1)}, u32[]{:S(2)}, u32[]{:S(2)}) collective-permute-start(bf16[64,2304]{1,0:T(8,128)(2,1)S(1)} %collective-permute-done.12.refs_6_), channel_id=1, source_target_pairs={{8,0},{16,8},{24,16},{28,24},{20,28},{12,20},{4,12},{0,4},{9,1},{1... | collective-permute-start | bytes 884744 | tf_op jit(solution)/shard_map/ppermute | solution.py:74
  31.3 11.1 %collective-permute-start.4 = (bf16[128,1152]{1,0:T(8,128)(2,1)S(1)}, bf16[128,1152]{1,0:T(8,128)(2,1)S(1)}, u32[]{:S(2)}, u32[]{:S(2)}) collective-permute-start(bf16[128,1152]{1,0:T(8,128)(2,1)S(1)} %collective-permute-done.3.refs_3_), channel_id=1, source_target_pairs={{0,8},{1,5},{2,10},{3,7},{8,16},{9,1},{10,18},{11,3},{16,24},{17,9... | collective-permute-start | bytes 884744 | tf_op jit(solution)/shard_map/ppermute | solution.py:67
  36.2 9.3 %copy-start.13 = (bf16[64,2304]{1,0:T(8,128)(2,1)}, bf16[64,2304]{1,0:T(8,128)(2,1)S(1)}, u32[]{:S(2)}) copy-start(bf16[64,2304]{1,0:T(8,128)(2,1)S(1)} %collective-permute-done.13.refs_3_) | copy-start | bytes 884740
  40.3 2.1 %copy-start.14 = (bf16[64,2304]{1,0:T(8,128)(2,1)}, bf16[64,2304]{1,0:T(8,128)(2,1)S(1)}, u32[]{:S(2)}) copy-start(bf16[64,2304]{1,0:T(8,128)(2,1)S(1)} %collective-permute-done.14.refs_5_) | copy-start | bytes 884740
  40.3 6.7 %collective-permute-start.16 = (bf16[32,2304]{1,0:T(8,128)(2,1)S(1)}, bf16[32,2304]{1,0:T(8,128)(2,1)}, u32[]{:S(2)}, u32[]{:S(2)}) collective-permute-start(bf16[32,2304]{1,0:T(8,128)(2,1)S(1)} %slice.7), channel_id=1, source_target_pairs={{8,0},{16,8},{24,16},{28,24},{20,28},{12,20},{4,12},{0,4},{9,1},{1... | collective-permute-start | bytes 442376 | tf_op jit(solution)/shard_map/ppermute | solution.py:80
  41.3 6.0 %collective-permute-start.15 = (bf16[32,2304]{1,0:T(8,128)(2,1)S(1)}, bf16[32,2304]{1,0:T(8,128)(2,1)}, u32[]{:S(2)}, u32[]{:S(2)}) collective-permute-start(bf16[32,2304]{1,0:T(8,128)(2,1)S(1)} %slice.6), channel_id=1, source_target_pairs={{0,8},{8,16},{16,24},{24,28},{28,20},{20,12},{12,4},{4,0},{1,9},{9... | collective-permute-start | bytes 442376 | tf_op jit(solution)/shard_map/ppermute | solution.py:79
  44.2 0.6 copy-start.2
  44.8 0.6 copy-start.6
  45.4 5.0 %copy-start.3 = (bf16[128,256]{1,0:T(8,128)(2,1)}, bf16[128,256]{1,0:T(8,128)(2,1)S(1)}, u32[]{:S(2)}) copy-start(bf16[128,256]{1,0:T(8,128)(2,1)S(1)} %get-tuple-element.46.refs_1_) | copy-start | bytes 196612
  45.4 5.1 %copy-start.4 = (bf16[128,256]{1,0:T(8,128)(2,1)}, bf16[128,256]{1,0:T(8,128)(2,1)S(1)}, u32[]{:S(2)}) copy-start(bf16[128,256]{1,0:T(8,128)(2,1)S(1)} %get-tuple-element.47.refs_2_) | copy-start | bytes 196612
  45.4 6.3 %copy-start.5 = (bf16[128,256]{1,0:T(8,128)(2,1)}, bf16[128,256]{1,0:T(8,128)(2,1)S(1)}, u32[]{:S(2)}) copy-start(bf16[128,256]{1,0:T(8,128)(2,1)S(1)} %get-tuple-element.48.refs_3_) | copy-start | bytes 196612
  45.5 19.9 %copy-start.1 = (bf16[1,64,2304]{2,1,0:T(8,128)(2,1)S(1)}, bf16[1,64,2304]{2,1,0:T(8,128)(2,1)}, u32[]{:S(2)}) copy-start(bf16[1,64,2304]{2,1,0:T(8,128)(2,1)} %param.10) | copy-start | bytes 884740
  45.5 19.8 %copy-start.8 = (bf16[1,1,2304,256]{3,2,1,0:T(8,128)(2,1)S(1)}, bf16[1,1,2304,256]{3,2,1,0:T(8,128)(2,1)}, u32[]{:S(2)}) copy-start(bf16[1,1,2304,256]{3,2,1,0:T(8,128)(2,1)} %param.8) | copy-start | bytes 3538948
  45.5 19.8 %copy-start.9 = (bf16[1,1,2304,256]{3,2,1,0:T(8,128)(2,1)S(1)}, bf16[1,1,2304,256]{3,2,1,0:T(8,128)(2,1)}, u32[]{:S(2)}) copy-start(bf16[1,1,2304,256]{3,2,1,0:T(8,128)(2,1)} %param.9) | copy-start | bytes 3538948
  45.5 6.2 %collective-permute-start.22 = (bf16[128,256]{1,0:T(8,128)(2,1)S(1)}, bf16[128,256]{1,0:T(8,128)(2,1)S(1)}, u32[]{:S(2)}, u32[]{:S(2)}) collective-permute-start(bf16[128,256]{1,0:T(8,128)(2,1)S(1)} %get-tuple-element.46.refs_1_), channel_id=1, source_target_pairs={{0,4},{1,9},{2,6},{3,11},{8,0},{9,17},{10,2},{11,19},{16,8},{17,25... | collective-permute-start | bytes 196616 | tf_op jit(solution)/shard_map/ppermute | solution.py:412
  46.5 16.9 %collective-permute-start.10 = (bf16[64,2304]{1,0:T(8,128)(2,1)S(1)}, bf16[64,2304]{1,0:T(8,128)(2,1)}, u32[]{:S(2)}, u32[]{:S(2)}) collective-permute-start(bf16[64,2304]{1,0:T(8,128)(2,1)S(1)} %bitcast.13), channel_id=1, source_target_pairs={{0,1},{1,0},{2,3},{3,2},{4,5},{5,4},{6,7},{7,6},{8,9},{9,8},{10,11... | collective-permute-start | bytes 884744 | tf_op jit(solution)/shard_map/ppermute | solution.py:86
  46.5 16.9 %collective-permute-start.11 = (bf16[64,2304]{1,0:T(8,128)(2,1)S(1)}, bf16[64,2304]{1,0:T(8,128)(2,1)}, u32[]{:S(2)}, u32[]{:S(2)}) collective-permute-start(bf16[64,2304]{1,0:T(8,128)(2,1)S(1)} %collective-permute-done.5.refs_2_), channel_id=1, source_target_pairs={{0,1},{1,0},{2,3},{3,2},{4,5},{5,4},{6,7},{7,6},{8,9},{9,8},{10,11... | collective-permute-start | bytes 884744 | tf_op jit(solution)/shard_map/ppermute | solution.py:86
  50.4 13.6 %collective-permute-start.17 = (bf16[64,2304]{1,0:T(8,128)(2,1)}, bf16[64,2304]{1,0:T(8,128)(2,1)}, u32[]{:S(2)}, u32[]{:S(2)}) collective-permute-start(bf16[64,2304]{1,0:T(8,128)(2,1)} %get-tuple-element.43), channel_id=1, source_target_pairs={{0,1},{1,0},{2,3},{3,2},{4,5},{5,4},{6,7},{7,6},{8,9},{9,8},{10,11... | collective-permute-start | bytes 884744 | tf_op jit(solution)/shard_map/ppermute | solution.py:86
  50.5 5.9 %collective-permute-start.21 = (bf16[128,256]{1,0:T(8,128)(2,1)S(1)}, bf16[128,256]{1,0:T(8,128)(2,1)S(1)}, u32[]{:S(2)}, u32[]{:S(2)}) collective-permute-start(bf16[128,256]{1,0:T(8,128)(2,1)S(1)} %get-tuple-element.47.refs_2_), channel_id=1, source_target_pairs={{0,12},{1,17},{2,14},{3,19},{8,4},{9,25},{10,6},{11,27},{16,0},{17... | collective-permute-start | bytes 196616 | tf_op jit(solution)/shard_map/ppermute | solution.py:412
  51.7 9.6 %copy-start.19 = (bf16[128,256]{1,0:T(8,128)(2,1)}, bf16[128,256]{1,0:T(8,128)(2,1)S(1)}, u32[]{:S(2)}) copy-start(bf16[128,256]{1,0:T(8,128)(2,1)S(1)} %collective-permute-done.22.refs_7_) | copy-start | bytes 196612
  51.7 6.5 %collective-permute-start.20 = (bf16[128,256]{1,0:T(8,128)(2,1)S(1)}, bf16[128,256]{1,0:T(8,128)(2,1)S(1)}, u32[]{:S(2)}, u32[]{:S(2)}) collective-permute-start(bf16[128,256]{1,0:T(8,128)(2,1)S(1)} %get-tuple-element.48.refs_3_), channel_id=1, source_target_pairs={{0,20},{1,25},{2,22},{3,27},{8,12},{9,29},{10,14},{11,31},{16,4},{... | collective-permute-start | bytes 196616 | tf_op jit(solution)/shard_map/ppermute | solution.py:412
  56.4 1.8 %copy-start.20 = (bf16[128,256]{1,0:T(8,128)(2,1)}, bf16[128,256]{1,0:T(8,128)(2,1)S(1)}, u32[]{:S(2)}) copy-start(bf16[128,256]{1,0:T(8,128)(2,1)S(1)} %collective-permute-done.21.refs_6_) | copy-start | bytes 196612
  56.4 12.0 %collective-permute-start.18 = (bf16[64,2304]{1,0:T(8,128)(2,1)}, bf16[64,2304]{1,0:T(8,128)(2,1)}, u32[]{:S(2)}, u32[]{:S(2)}) collective-permute-start(bf16[64,2304]{1,0:T(8,128)(2,1)} %get-tuple-element.44), channel_id=1, source_target_pairs={{0,2},{1,3},{2,0},{3,1},{4,6},{5,7},{6,4},{7,5},{8,10},{9,11},{10,... | collective-permute-start | bytes 884744 | tf_op jit(solution)/shard_map/ppermute | solution.py:86
  58.2 3.2 %copy-start.21 = (bf16[128,256]{1,0:T(8,128)(2,1)}, bf16[128,256]{1,0:T(8,128)(2,1)S(1)}, u32[]{:S(2)}) copy-start(bf16[128,256]{1,0:T(8,128)(2,1)S(1)} %collective-permute-done.20.refs_5_) | copy-start | bytes 196612
  58.2 13.5 %collective-permute-start.19 = (bf16[64,2304]{1,0:T(8,128)(2,1)}, bf16[64,2304]{1,0:T(8,128)(2,1)}, u32[]{:S(2)}, u32[]{:S(2)}) collective-permute-start(bf16[64,2304]{1,0:T(8,128)(2,1)} %get-tuple-element.45), channel_id=1, source_target_pairs={{0,3},{1,2},{2,1},{3,0},{4,7},{5,6},{6,5},{7,4},{8,11},{9,10},{10,... | collective-permute-start | bytes 884744 | tf_op jit(solution)/shard_map/ppermute | solution.py:86
  63.4 8.3 %collective-permute-start.23 = (bf16[128,256]{1,0:T(8,128)(2,1)}, bf16[128,256]{1,0:T(8,128)(2,1)S(1)}, u32[]{:S(2)}, u32[]{:S(2)}) collective-permute-start(bf16[128,256]{1,0:T(8,128)(2,1)} %get-tuple-element.51), channel_id=1, source_target_pairs={{0,1},{1,0},{2,3},{3,2},{4,5},{5,4},{6,7},{7,6},{8,9},{9,8},{10,11... | collective-permute-start | bytes 196616 | tf_op jit(solution)/shard_map/ppermute | solution.py:86
  63.4 9.9 %collective-permute-start.24 = (bf16[128,256]{1,0:T(8,128)(2,1)}, bf16[128,256]{1,0:T(8,128)(2,1)S(1)}, u32[]{:S(2)}, u32[]{:S(2)}) collective-permute-start(bf16[128,256]{1,0:T(8,128)(2,1)} %get-tuple-element.52), channel_id=1, source_target_pairs={{0,2},{1,3},{2,0},{3,1},{4,6},{5,7},{6,4},{7,5},{8,10},{9,11},{10,... | collective-permute-start | bytes 196616 | tf_op jit(solution)/shard_map/ppermute | solution.py:86
  64.0 9.3 %collective-permute-start.25 = (bf16[128,256]{1,0:T(8,128)(2,1)}, bf16[128,256]{1,0:T(8,128)(2,1)S(1)}, u32[]{:S(2)}, u32[]{:S(2)}) collective-permute-start(bf16[128,256]{1,0:T(8,128)(2,1)} %get-tuple-element.53), channel_id=1, source_target_pairs={{0,3},{1,2},{2,1},{3,0},{4,7},{5,6},{6,5},{7,4},{8,11},{9,10},{10,... | collective-permute-start | bytes 196616 | tf_op jit(solution)/shard_map/ppermute | solution.py:86
  65.3 8.0 %copy-start.7 = (s32[4]{0:T(128)S(1)}, s32[4]{0:T(128)}, u32[]{:S(2)}) copy-start(s32[4]{0:T(128)} %owner.5) | copy-start | bytes 52
  65.3 8.0 %copy-start.10 = (bf16[64,2304]{1,0:T(8,128)(2,1)S(1)}, bf16[64,2304]{1,0:T(8,128)(2,1)}, u32[]{:S(2)}) copy-start(bf16[64,2304]{1,0:T(8,128)(2,1)} %get-tuple-element.42.refs_4_) | copy-start | bytes 884740
  65.3 8.0 %copy-start.11 = (bf16[128,256]{1,0:T(8,128)(2,1)S(1)}, bf16[128,256]{1,0:T(8,128)(2,1)}, u32[]{:S(2)}) copy-start(bf16[128,256]{1,0:T(8,128)(2,1)} %get-tuple-element.50.refs_8_) | copy-start | bytes 196612
  65.3 8.0 %copy-start.12 = (s32[8]{0:T(128)S(1)}, s32[8]{0:T(128)}, u32[]{:S(2)}) copy-start(s32[8]{0:T(128)} %panel.1) | copy-start | bytes 100

commit v4 on v3

v4 whole, which is shorter than its diff:
```python
import functools
import math

import jax
import jax.numpy as jnp
from jax import lax
from jax.experimental import pallas as pl
from jax.experimental.pallas import tpu as pltpu
from jax.sharding import PartitionSpec as P

F32 = jnp.float32
BF16 = jnp.bfloat16
HIGHEST = lax.Precision.HIGHEST
VMEM = pl.BlockSpec(memory_space=pltpu.VMEM)
SMEM = pl.BlockSpec(memory_space=pltpu.SMEM)
HBM = pl.BlockSpec(memory_space=pltpu.HBM)
ROUGH, FINE = 0.05, 0.015
ROUGH_STEPS, FINE_STEPS = 12, 6


def nn(a, b, precision=None):
    return lax.dot_general(a, b, (((1,), (0,)), ((), ())), precision=precision, preferred_element_type=F32)


def nt(a, b, precision=None):
    return lax.dot_general(a, b, (((1,), (1,)), ((), ())), precision=precision, preferred_element_type=F32)


def tn(a, b, precision=None):
    return lax.dot_general(a, b, (((0,), (0,)), ((), ())), precision=precision, preferred_element_type=F32)


def halves(x):
    high = x.astype(BF16)
    return high, (x - high.astype(F32)).astype(BF16)


def after(x, *others):
    return lax.optimization_barrier((x, *others))[0]


def ring_place(r, n):
    return jnp.where(r % 2 == 0, r // 2, n - 1 - r // 2)


def ring_steps(n):
    ring = list(range(0, n, 2)) + list(range(n - 1, 0, -2))
    ahead = [(ring[i], ring[(i + 1) % n]) for i in range(n)]
    return ahead, [(b, a) for a, b in ahead]


def ring_gathers(left, right, axis, n, gates):
    ahead, back = ring_steps(n)
    half, low = n // 2, left.shape[0] // 2
    lists = [[panel] + [None] * (n - 1) for panel in (left, right)]
    now = [(left, left), (right, right)]

    def step(panel, s, *gate):
        fwd, bwd, *_ = lax.optimization_barrier((*now[panel], *gate))
        if s == half:
            fwd, bwd = fwd[:low], bwd[low:]
        fwd, bwd = lax.ppermute(fwd, axis, ahead), lax.ppermute(bwd, axis, back)
        now[panel] = fwd, bwd
        if s == half:
            lists[panel][half] = fwd
            lists[panel].append(bwd)
        else:
            lists[panel][s], lists[panel][n - s] = fwd, bwd
        return fwd, bwd

    for s in range(1, half - 1):
        done = step(0, s)
    for s in range(1, half + 1):
        if s < 3:
            early = step(0, half - 2 + s)
        gate = gates[s](lists) if s in gates else ()
        step(1, s, *gate, *(done if s < 3 else ()))
        done = early
    return lists


def swap(x, axis, n, m):
    return lax.ppermute(x, axis, [(i, i ^ m) for i in range(n)])


def part_copies(parts, target, sem):
    shard = target.shape[0] // len(parts)
    col = lax.axis_index("col")
    spots = [pl.ds(pl.multiple_of((col ^ m) * shard, shard), shard) for m in range(len(parts))]
    return [pltpu.make_async_copy(part, target.at[spots[m]], sem.at[m]) for m, part in enumerate(parts)]


def owner_steps(n_row, n_col, owner):
    row, col = lax.axis_index("row"), lax.axis_index("col")
    here = ring_place(row, n_row)
    return [lax.rem(here - ring_place(owner[col ^ m], n_row) + n_row, n_row) for m in range(n_col)]


def pick(pieces, n_row, n_col, owner, outs):
    low = pieces[0].shape[0] // 2
    for m, step in enumerate(owner_steps(n_row, n_col, owner)):
        for k in range(n_row):

            @pl.when(step == k)
            def _():
                if k == n_row // 2:
                    outs[m][:low] = pieces[k][...]
                    outs[m][low:] = pieces[n_row][...]
                else:
                    outs[m][...] = pieces[k][...]


def pick_left(n_row, n_col, owner, *refs):
    pick(refs[: n_row + 1], n_row, n_col, owner, refs[n_row + 1 :])


def picked_left(pieces, owner, n_row, n_col):
    shard, width = pieces[0].shape
    return pl.pallas_call(
        functools.partial(pick_left, n_row, n_col),
        out_shape=[jax.ShapeDtypeStruct((shard, width), BF16)] * n_col,
        in_specs=[SMEM] + [VMEM] * (n_row + 1),
        out_specs=[VMEM] * n_col,
        cost_estimate=pl.CostEstimate(flops=0, bytes_accessed=3 << 20, transcendentals=0),
        name="pick_left",
    )(owner, *pieces)


def couple(n_row, n_col, owner, *refs):
    pieces, parts = refs[: n_row + 1], refs[n_row + 1 : n_row + 1 + n_col]
    outs = refs[n_row + 1 + n_col : n_row + 1 + 2 * n_col]
    picked, mine = refs[n_row + 1 + 2 * n_col :]
    shard = pieces[0].shape[0]
    col = lax.axis_index("col")
    for m in range(n_col):
        mine[pl.ds(pl.multiple_of((col ^ m) * shard, shard), shard), :] = parts[m][...]
    pick(pieces, n_row, n_col, owner, [picked.at[pl.ds(m * shard, shard)] for m in range(n_col)])
    product = nt(picked[...], mine[...]).astype(BF16)
    for m in range(n_col):
        outs[m][...] = product[m * shard : (m + 1) * shard]


def coupled(pieces, parts, owner, n_row, n_col):
    shard, width = pieces[0].shape
    rank = n_col * shard
    return pl.pallas_call(
        functools.partial(couple, n_row, n_col),
        out_shape=[jax.ShapeDtypeStruct((shard, rank), BF16)] * n_col,
        in_specs=[SMEM] + [VMEM] * (n_row + 1 + n_col),
        out_specs=[VMEM] * n_col,
        scratch_shapes=[pltpu.VMEM((rank, width), BF16), pltpu.VMEM((rank, width), BF16)],
        compiler_params=pltpu.CompilerParams(vmem_limit_bytes=32 << 20),
        cost_estimate=pl.CostEstimate(flops=2 * rank * rank * width, bytes_accessed=3 << 20, transcendentals=0),
        name="coupling",
    )(owner, *pieces, *parts)


def grams(n_col, u_hbm, v_hbm, *refs):
    high, low, cu_ref, u_ref, v_ref, uit, sem, part_sem = refs[n_col:]
    rank = cu_ref.shape[0]
    loads = [pltpu.make_async_copy(v_hbm, v_ref, sem.at[0]), pltpu.make_async_copy(u_hbm, u_ref, sem.at[1])]
    parts = part_copies(refs[:n_col], uit, part_sem)
    for copy in [*loads, *parts]:
        copy.start()
    top, bottom = pl.ds(0, rank), pl.ds(rank, rank)

    def put(at, lanes, value):
        high[at, lanes], low[at, lanes] = halves(value)

    loads[0].wait()
    cu_ref[...] = tn(v_ref[...], v_ref[...])
    loads[1].wait()
    put(top, top, tn(u_ref[...], u_ref[...]))
    for copy in parts:
        copy.wait()
    cross = nn(uit[...], u_ref[...])
    put(bottom, top, cross)
    put(top, bottom, cross.T)
    put(bottom, bottom, nt(uit[...], uit[...]))


def gram_products(u, v, parts):
    rows, rank = u.shape
    tall = pltpu.VMEM((rows, rank), BF16)
    return pl.pallas_call(
        functools.partial(grams, len(parts)),
        out_shape=[jax.ShapeDtypeStruct((2 * rank, 2 * rank), BF16)] * 2 + [jax.ShapeDtypeStruct((rank, rank), F32)],
        in_specs=[HBM] * (2 + len(parts)),
        out_specs=[VMEM] * 3,
        scratch_shapes=[
            tall,
            tall,
            pltpu.VMEM((rank, rows), BF16),
            pltpu.SemaphoreType.DMA((2,)),
            pltpu.SemaphoreType.DMA((len(parts),)),
        ],
        compiler_params=pltpu.CompilerParams(vmem_limit_bytes=40 << 20),
        cost_estimate=pl.CostEstimate(flops=8 * rank * rank * rows, bytes_accessed=6 << 20, transcendentals=0),
        name="grams",
    )(u, v, *parts)


def lower_half(e, eye, below):
    return jnp.where(below, e, jnp.where(eye, 0.5 * e, 0.0))


def finish(n_col, old_ref, goal_ref, panel, owner, u_hbm, v_hbm, hh_hbm, hl_hbm, cu_hbm, *refs):
    ui_hbm, ujt_hbm, kt_in = refs[:n_col], refs[n_col : 2 * n_col], refs[2 * n_col : 3 * n_col]
    (q_hbm, w_hbm, u_ref, v_ref, uit_ref, hh, hl, cu_ref, ujt, q_ref, w_ref, kt, mh, gn, y_ref, a_ref) = refs[
        3 * n_col : -5
    ]
    in_sem, ui_sem, uj_sem, q_sem, w_sem = refs[-5:]
    rows, rank = u_ref.shape
    shard = rank // n_col
    row, col = lax.axis_index("row"), lax.axis_index("col")
    spots = [pl.ds(pl.multiple_of((col ^ m) * shard, shard), shard) for m in range(n_col)]
    loads = [
        pltpu.make_async_copy(src, dst, in_sem.at[t])
        for t, (src, dst) in enumerate(
            [(v_hbm, v_ref), (hh_hbm, hh), (hl_hbm, hl), (cu_hbm, cu_ref), (u_hbm, u_ref)]
        )
    ]
    ui_loads = part_copies(ui_hbm, uit_ref, ui_sem)
    uj_loads = [pltpu.make_async_copy(ujt_hbm[m], ujt.at[spots[m]], uj_sem.at[m]) for m in range(n_col)]
    for copy in [*uj_loads, *loads, *ui_loads]:
        copy.start()
    old, goal, here, there = old_ref[0, 0], goal_ref[0, 0], panel[row], panel[owner[col]]
    sub = lax.broadcasted_iota(jnp.int32, (rank, rank), 0)
    lane = lax.broadcasted_iota(jnp.int32, (rank, rank), 1)
    eye, below = sub == lane, sub > lane
    one = jnp.where(eye, 1.0, 0.0).astype(F32)
    for m in range(n_col):
        kt[spots[m], :] = kt_in[m][...]
    zero = jnp.zeros((rank, rank), F32)
    kt[...] = jnp.where((sub < there) & (lane < here), kt[...].astype(F32), zero).astype(BF16)
    for copy in [*uj_loads, *loads[:1]]:
        copy.wait()
    cl = jnp.where(lane < goal, nn(ujt[...], v_ref[...]), zero).astype(BF16)
    for copy in loads[1:4]:
        copy.wait()
    cu = jnp.where((sub < old) & (lane < goal), cu_ref[...], zero).astype(BF16)
    m_high, m_low = halves(-tn(kt[...], cl))
    mh[pl.ds(0, rank), :], mh[pl.ds(rank, rank), :] = cu, m_high
    hm = nn(hh[...], mh[...]) + nn(hl[...], mh[...]) + nn(hh[:, rank:], m_low)
    hm_high, hm_low = halves(hm)
    g = tn(mh[...], hm_high) + tn(mh[...], hm_low) + tn(m_low, hm_high[rank:])
    g = g + jnp.where(eye & (lane >= goal), 1.0, 0.0)
    dg = jnp.where(eye, g, 0.0)
    d_row = lax.rsqrt(jnp.sum(dg, axis=0, keepdims=True))
    d_col = lax.rsqrt(jnp.sum(dg, axis=1, keepdims=True))
    g = g * d_col * d_row
    gn[...] = g
    scale = rank / jnp.sum(g * g, keepdims=True)
    a_ref[...] = g * scale
    y_ref[...] = one * jnp.sqrt(scale)

    def rough(carry):
        step, _ = carry
        a = a_ref[...]
        e = a - one
        f = lower_half(e, eye, below).astype(BF16)
        y = y_ref[...]
        t = a - nn(f, a.astype(BF16))
        y_ref[...] = y - nn(f, y.astype(BF16))
        a_ref[...] = t - nt(t.astype(BF16), f)
        return step + 1, jnp.max(jnp.abs(e))

    def fine(carry):
        step, _ = carry
        y = y_ref[...]
        yh, yl = halves(y)
        gh, gl = halves(gn[...])
        th, tl = halves(nn(yh, gh) + nn(yh, gl) + nn(yl, gh))
        e = nt(th, yh) + nt(th, yl) + nt(tl, yh) - one
        y_ref[...] = y - nn(lower_half(e, eye, below).astype(BF16), yh)
        return step + 1, jnp.max(jnp.abs(e))

    lax.while_loop(lambda c: (c[0] < ROUGH_STEPS) & (c[1] > ROUGH), rough, (jnp.int32(0), F32(1.0)))
    _, err = lax.while_loop(lambda c: (c[0] < FINE_STEPS) & (c[1] > FINE), fine, (jnp.int32(0), F32(1.0)))
    lowest = jnp.min(jnp.where(eye, y_ref[...], 1.0))

    @pl.when(jnp.logical_not((err <= FINE) & (lowest > 0.0)))
    def _():
        a_ref[...] = gn[...]
        y_ref[...] = one

        def pivot(k, _):
            col = jnp.sum(jnp.where(lane == k, a_ref[...], 0.0), axis=1, keepdims=True)
            row = jnp.sum(jnp.where(sub == k, a_ref[...], 0.0), axis=0, keepdims=True)
            yrow = jnp.sum(jnp.where(sub == k, y_ref[...], 0.0), axis=0, keepdims=True)
            top = jnp.sum(jnp.where(lax.broadcasted_iota(jnp.int32, (1, rank), 1) == k, row, 0.0))
            inv = 1.0 / jnp.sqrt(jnp.full((1, rank), top))
            row, yrow = row * inv, yrow * inv
            col = jnp.where(lax.broadcasted_iota(jnp.int32, (rank, 1), 0) > k, col * inv[:, :1], 0.0)
            a_ref[...] = a_ref[...] - col * row
            y_ref[...] = jnp.where(sub == k, yrow, y_ref[...] - col * yrow)
            return 0

        lax.fori_loop(0, rank, pivot, 0)

    xh, xl = halves(y_ref[...] * d_row)
    root = math.sqrt(rows)
    c = nt(mh[...], xh) + nt(mh[...], xl)
    c_up = (c[:rank] * root).astype(BF16)
    c_low = ((c[rank:] + nt(m_low, xh)) * root).astype(BF16)
    r = nt(hm_high, xh) + nt(hm_high, xl) + nt(hm_low, xh)
    r_up = jnp.where(sub < old, r[:rank], 0.0).astype(BF16)
    w_high, w_low = halves(r[rank:])
    r_low = (-(nn(kt[...], w_high) + nn(kt[...], w_low))).astype(BF16)
    for copy in [*loads[4:], *ui_loads]:
        copy.wait()
    step = rows // q_sem.shape[0]
    stores = []
    for t in range(rows // step):
        at = pl.ds(t * step, step)
        u, v = u_ref[at, :], v_ref[at, :]
        ui, uj = uit_ref[:, at], ujt[:, at]
        q_ref[at, :] = (nn(u, c_up) + tn(ui, c_low)).astype(BF16)
        stores.append(pltpu.make_async_copy(q_ref.at[at], q_hbm.at[at], q_sem.at[t]))
        stores[-1].start()
        w_ref[at, :] = (nn(v, r_up) + tn(uj, r_low)).astype(BF16)
        stores.append(pltpu.make_async_copy(w_ref.at[at], w_hbm.at[at], w_sem.at[t]))
        stores[-1].start()
    for copy in stores:
        copy.wait()


def body(tile_basis, tile_coeffs, panel_basis, panel_coeffs, tile_rank, target_rank, panel_rank, owner_row):
    n_row, n_col = lax.axis_size("row"), lax.axis_size("col")
    u, v = tile_basis[0, 0], tile_coeffs[0, 0]
    pu, pv = panel_basis[0], panel_coeffs[0]
    rows, rank = u.shape

    lefts, rights, grammed = {0: pu}, {0: pv}, []

    def grow(have, bits):
        for bit in bits:
            for m in list(have):
                have[m | bit] = swap(have[m], "col", n_col, bit)
        return tuple(have.values())

    high = [n_col >> t for t in range(1, n_col.bit_length() - 1)]

    def columns_grams(lists):
        grow(lefts, [1])
        grow(rights, [1])
        grammed.extend(gram_products(u, v, [lefts[m] for m in range(n_col)]))
        return (grammed[2], *rights.values())

    gates = {1: lambda _: grow(lefts, high) + grow(rights, high), n_row // 2: columns_grams}
    us, vs = ring_gathers(pu, pv, "row", n_row, gates)
    h_high, h_low, core_up = grammed
    ui_parts = [lefts[m] for m in range(n_col)]

    ujs = picked_left(us, owner_row, n_row, n_col)
    ujs = [ujs[0]] + [swap(ujs[m], "col", n_col, m) for m in range(1, n_col)]
    kts = coupled(vs, [rights[m] for m in range(n_col)], owner_row, n_row, n_col)
    kts = [kts[0]] + [swap(kts[m], "col", n_col, m) for m in range(1, n_col)]

    out = jax.ShapeDtypeStruct((rows, rank), BF16)
    square = pltpu.VMEM((rank, rank), F32)
    tall, wide = pltpu.VMEM((rows, rank), BF16), pltpu.VMEM((rank, rows), BF16)
    tiles = rows // 256 if rows % 256 == 0 else 1
    fresh_basis, fresh_coeffs = pl.pallas_call(
        functools.partial(finish, n_col),
        out_shape=(out, out),
        in_specs=[SMEM] * 4 + [HBM] * (5 + 2 * n_col) + [VMEM] * n_col,
        out_specs=(HBM, HBM),
        scratch_shapes=[
            tall,
            tall,
            wide,
            pltpu.VMEM((2 * rank, 2 * rank), BF16),
            pltpu.VMEM((2 * rank, 2 * rank), BF16),
            square,
            wide,
            tall,
            tall,
            pltpu.VMEM((rank, rank), BF16),
            pltpu.VMEM((2 * rank, rank), BF16),
            square,
            square,
            square,
            pltpu.SemaphoreType.DMA((5,)),
            pltpu.SemaphoreType.DMA((n_col,)),
            pltpu.SemaphoreType.DMA((n_col,)),
            pltpu.SemaphoreType.DMA((tiles,)),
            pltpu.SemaphoreType.DMA((tiles,)),
        ],
        compiler_params=pltpu.CompilerParams(vmem_limit_bytes=40 << 20),
        cost_estimate=pl.CostEstimate(flops=8 << 30, bytes_accessed=12 << 20, transcendentals=0),
        name="finish",
    )(tile_rank, target_rank, panel_rank, owner_row, u, v, h_high, h_low, core_up, *ui_parts, *ujs, *kts)
    return fresh_basis[None, None], fresh_coeffs[None, None]


def solution(mesh):
    tiles, panels = P("row", "col", None, None), P("row", "col", None)
    return jax.shard_map(
        body,
        mesh=mesh,
        in_specs=(tiles, tiles, panels, panels, P("row", "col"), P("row", "col"), P(), P()),
        out_specs=(tiles, tiles),
        check_vma=False,
    )
```

time: 150 us -> 145 us (0.967)
  waiting for transfers between devices: 25.8 us -> 36.7 us
  starting transfers between devices: 33 us -> 23.4 us
  Pallas kernels: 86 us -> 79.4 us
    ppermute x15 -> x16, waiting for transfers between devices: 19.9 us -> 30.3 us  [step(): fwd, bwd = (lax.ppermute(fwd, axis, ahead), lax.ppermute(bwd, axis, back))]
    pallas_call x3 -> x2, Pallas kernels: 79.8 us -> 73.4 us  [the longest x1 72 us: body(): pl.pallas_call(functools.partial(finish, n_col), out_shape=(out, out), in...]
    ppermute x15 -> x16, starting transfers between devices: 23.7 us -> 17.6 us  [step(): fwd, bwd = (lax.ppermute(fwd, axis, ahead), lax.ppermute(bwd, axis, back))]
    ppermute x11 -> x12, starting transfers between devices: 9.35 us -> 5.87 us  [swap(): return lax.ppermute(x, axis, [(i, i ^ m) for i in range(n)])]
    ppermute x11 -> x12, waiting for transfers between devices: 5.9 us -> 6.41 us  [swap(): return lax.ppermute(x, axis, [(i, i ^ m) for i in range(n)])]
  transfers between devices with their start and end apart: 26 -> 28, of which waited for: 13 -> 14; matrix products, arithmetic and copies ran while one was open for 0% -> 0% of each run, Pallas kernels for 7% -> 5%
where the time goes in v4:
time: 145 us; the launch traced here: 144 us
  Pallas kernels  79.4 us (55%)
  waiting for transfers between devices  36.7 us (25%)
  starting transfers between devices  23.4 us (16%)
  local copies, waits for them, and re-layouts  2.64 us (2%)
  between operations  2.12 us (1%)
    pallas_call x1, Pallas kernels, body(): pl.pallas_call(functools.partial(finish, n_col), out_shape=(out, out), in...  72 us
    ppermute x16, waiting for transfers between devices, step(): fwd, bwd = (lax.ppermute(fwd, axis, ahead), lax.ppermute(bwd, axis, back))  30.3 us
    ppermute x16, starting transfers between devices, step(): fwd, bwd = (lax.ppermute(fwd, axis, ahead), lax.ppermute(bwd, axis, back))  17.6 us
    ppermute x12, waiting for transfers between devices, swap(): return lax.ppermute(x, axis, [(i, i ^ m) for i in range(n)])  6.41 us
    ppermute x12, starting transfers between devices, swap(): return lax.ppermute(x, axis, [(i, i ^ m) for i in range(n)])  5.87 us
    pallas_call x1, Pallas kernels, gram_products(): pl.pallas_call(functools.partial(grams, len(parts)), out_shape=[jax.Shape...  3.11 us
  transfers between devices with their start and end apart: 28, of which 14 were waited for; matrix products, arithmetic and copies ran while one was open for 0% of the time, Pallas kernels for 5%

profile of v4, /device:TPU:0, one launch (start us, length us, event | category | flops | bytes accessed | tf_op | source)
XLA Modules:
  0.0 144.3 jit_solution(3494513291390468492)
XLA Ops:
  0.6 3.1 %collective-permute-start.3 = (bf16[64,2304]{1,0:T(8,128)(2,1)}, bf16[64,2304]{1,0:T(8,128)(2,1)S(1)}, u32[]{:S(2)}, u32[]{:S(2)}) collective-permute-start(bf16[64,2304]{1,0:T(8,128)(2,1)} %bitcast.12), channel_id=1, source_target_pairs={{0,8},{8,16},{16,24},{24,28},{28,20},{20,12},{12,4},{4,0},{1,9},{9... | collective-permute-start | bytes 884744 | tf_op jit(solution)/shard_map/ppermute | solution.py:62
  3.7 0.0 collective-permute-start.4
  3.7 7.2 %collective-permute-done.3.refs_1_ = bf16[64,2304]{1,0:T(8,128)(2,1)S(1)} collective-permute-done((bf16[64,2304]{1,0:T(8,128)(2,1)}, bf16[64,2304]{1,0:T(8,128)(2,1)S(1)}, u32[]{:S(2)}, u32[]{:S(2)}) %collective-permute-start.3) | collective-permute-done | bytes 294944 | tf_op jit(solution)/shard_map/ppermute | solution.py:62
  10.9 1.5 %collective-permute-done.4.refs_7_ = bf16[64,2304]{1,0:T(8,128)(2,1)S(1)} collective-permute-done((bf16[64,2304]{1,0:T(8,128)(2,1)}, bf16[64,2304]{1,0:T(8,128)(2,1)S(1)}, u32[]{:S(2)}, u32[]{:S(2)}) %collective-permute-start.4) | collective-permute-done | bytes 294944 | tf_op jit(solution)/shard_map/ppermute | solution.py:62
  12.4 1.6 %collective-permute-start.5 = (bf16[64,2304]{1,0:T(8,128)(2,1)S(1)}, bf16[64,2304]{1,0:T(8,128)(2,1)S(1)}, u32[]{:S(2)}, u32[]{:S(2)}) collective-permute-start(bf16[64,2304]{1,0:T(8,128)(2,1)S(1)} %collective-permute-done.3.refs_1_), channel_id=1, source_target_pairs={{0,8},{8,16},{16,24},{24,28},{28,20},{20,12},{12,4},{4,0},{1,9},{9... | collective-permute-start | bytes 884744 | tf_op jit(solution)/shard_map/ppermute | solution.py:62
  14.0 0.4 collective-permute-start.6
  14.4 1.5 %collective-permute-start.1 = (bf16[64,2304]{1,0:T(8,128)(2,1)}, bf16[64,2304]{1,0:T(8,128)(2,1)S(1)}, u32[]{:S(2)}, u32[]{:S(2)}) collective-permute-start(bf16[64,2304]{1,0:T(8,128)(2,1)} %bitcast.14), channel_id=1, source_target_pairs={{0,2},{1,3},{2,0},{3,1},{4,6},{5,7},{6,4},{7,5},{8,10},{9,11},{10,... | collective-permute-start | bytes 884744 | tf_op jit(solution)/shard_map/ppermute | solution.py:83
  15.9 0.5 collective-permute-start.14
  16.4 3.5 %collective-permute-done.5.refs_2_ = bf16[64,2304]{1,0:T(8,128)(2,1)S(1)} collective-permute-done((bf16[64,2304]{1,0:T(8,128)(2,1)S(1)}, bf16[64,2304]{1,0:T(8,128)(2,1)S(1)}, u32[]{:S(2)}, u32[]{:S(2)}) %collective-permute-start.5) | collective-permute-done | bytes 294944 | tf_op jit(solution)/shard_map/ppermute | solution.py:62
  19.9 1.3 collective-permute-done.6.refs_6_
  21.2 1.6 %collective-permute-start.7 = (bf16[64,2304]{1,0:T(8,128)(2,1)S(1)}, bf16[64,2304]{1,0:T(8,128)(2,1)S(1)}, u32[]{:S(2)}, u32[]{:S(2)}) collective-permute-start(bf16[64,2304]{1,0:T(8,128)(2,1)S(1)} %collective-permute-done.5.refs_2_), channel_id=1, source_target_pairs={{0,8},{8,16},{16,24},{24,28},{28,20},{20,12},{12,4},{4,0},{1,9},{9... | collective-permute-start | bytes 884744 | tf_op jit(solution)/shard_map/ppermute | solution.py:62
  22.8 0.4 collective-permute-start.8
  23.3 1.3 collective-permute-done.1.refs_2_
  24.6 3.4 %collective-permute-done.14.refs_11_ = bf16[64,2304]{1,0:T(8,128)(2,1)S(1)} collective-permute-done((bf16[64,2304]{1,0:T(8,128)(2,1)}, bf16[64,2304]{1,0:T(8,128)(2,1)S(1)}, u32[]{:S(2)}, u32[]{:S(2)}) %collective-permute-start.14) | collective-permute-done | bytes 294944 | tf_op jit(solution)/shard_map/ppermute | solution.py:83
  27.9 1.6 %collective-permute-start.15 = (bf16[64,2304]{1,0:T(8,128)(2,1)}, bf16[64,2304]{1,0:T(8,128)(2,1)S(1)}, u32[]{:S(2)}, u32[]{:S(2)}) collective-permute-start(bf16[64,2304]{1,0:T(8,128)(2,1)} %bitcast.7), channel_id=1, source_target_pairs={{0,8},{8,16},{16,24},{24,28},{28,20},{20,12},{12,4},{4,0},{1,9},{9... | collective-permute-start | bytes 884744 | tf_op jit(solution)/shard_map/ppermute | solution.py:62
  29.5 0.4 collective-permute-start.16
  30.0 0.0 collective-permute-start
  30.0 0.0 collective-permute-done.7.refs_3_
  30.0 0.0 collective-permute-done.8.refs_5_
  30.0 4.9 %collective-permute-done.15.refs_1_ = bf16[64,2304]{1,0:T(8,128)(2,1)S(1)} collective-permute-done((bf16[64,2304]{1,0:T(8,128)(2,1)}, bf16[64,2304]{1,0:T(8,128)(2,1)S(1)}, u32[]{:S(2)}, u32[]{:S(2)}) %collective-permute-start.15) | collective-permute-done | bytes 294944 | tf_op jit(solution)/shard_map/ppermute | solution.py:62
  34.9 1.6 %collective-permute-done.16.refs_7_ = bf16[64,2304]{1,0:T(8,128)(2,1)S(1)} collective-permute-done((bf16[64,2304]{1,0:T(8,128)(2,1)}, bf16[64,2304]{1,0:T(8,128)(2,1)S(1)}, u32[]{:S(2)}, u32[]{:S(2)}) %collective-permute-start.16) | collective-permute-done | bytes 294944 | tf_op jit(solution)/shard_map/ppermute | solution.py:62
  36.5 1.6 %collective-permute-start.17 = (bf16[64,2304]{1,0:T(8,128)(2,1)S(1)}, bf16[64,2304]{1,0:T(8,128)(2,1)S(1)}, u32[]{:S(2)}, u32[]{:S(2)}) collective-permute-start(bf16[64,2304]{1,0:T(8,128)(2,1)S(1)} %collective-permute-done.15.refs_1_), channel_id=1, source_target_pairs={{0,8},{8,16},{16,24},{24,28},{28,20},{20,12},{12,4},{4,0},{1,9},{9... | collective-permute-start | bytes 884744 | tf_op jit(solution)/shard_map/ppermute | solution.py:62
  38.1 0.4 collective-permute-start.18
  38.5 0.5 collective-permute-start.10
  39.0 0.0 copy-start.1
  39.0 1.7 %collective-permute-start.9 = (bf16[32,2304]{1,0:T(8,128)(2,1)S(1)}, bf16[32,2304]{1,0:T(8,128)(2,1)}, u32[]{:S(2)}, u32[]{:S(2)}) collective-permute-start(bf16[32,2304]{1,0:T(8,128)(2,1)S(1)} %slice.12), channel_id=1, source_target_pairs={{0,8},{8,16},{16,24},{24,28},{28,20},{20,12},{12,4},{4,0},{1,9},{9... | collective-permute-start | bytes 442376 | tf_op jit(solution)/shard_map/ppermute | solution.py:62
  40.8 0.0 collective-permute-done.refs_1_
  40.8 0.0 collective-permute-start.21
  40.8 2.5 %collective-permute-done.17.refs_2_ = bf16[64,2304]{1,0:T(8,128)(2,1)S(1)} collective-permute-done((bf16[64,2304]{1,0:T(8,128)(2,1)S(1)}, bf16[64,2304]{1,0:T(8,128)(2,1)S(1)}, u32[]{:S(2)}, u32[]{:S(2)}) %collective-permute-start.17) | collective-permute-done | bytes 294944 | tf_op jit(solution)/shard_map/ppermute | solution.py:62
  43.3 0.0 collective-permute-start.2
  43.3 2.0 %collective-permute-done.18.refs_6_ = bf16[64,2304]{1,0:T(8,128)(2,1)S(1)} collective-permute-done((bf16[64,2304]{1,0:T(8,128)(2,1)S(1)}, bf16[64,2304]{1,0:T(8,128)(2,1)S(1)}, u32[]{:S(2)}, u32[]{:S(2)}) %collective-permute-start.18) | collective-permute-done | bytes 294944 | tf_op jit(solution)/shard_map/ppermute | solution.py:62
  45.3 0.0 collective-permute-start.22
  45.3 1.6 %collective-permute-done.10.refs_8_ = bf16[32,2304]{1,0:T(8,128)(2,1)S(1)} collective-permute-done((bf16[32,2304]{1,0:T(8,128)(2,1)S(1)}, bf16[32,2304]{1,0:T(8,128)(2,1)S(1)}, u32[]{:S(2)}, u32[]{:S(2)}) %collective-permute-start.10) | collective-permute-done | bytes 147488 | tf_op jit(solution)/shard_map/ppermute | solution.py:62
  46.9 2.0 %collective-permute-start.19 = (bf16[64,2304]{1,0:T(8,128)(2,1)S(1)}, bf16[64,2304]{1,0:T(8,128)(2,1)S(1)}, u32[]{:S(2)}, u32[]{:S(2)}) collective-permute-start(bf16[64,2304]{1,0:T(8,128)(2,1)S(1)} %collective-permute-done.17.refs_2_), channel_id=1, source_target_pairs={{0,8},{8,16},{16,24},{24,28},{28,20},{20,12},{12,4},{4,0},{1,9},{9... | collective-permute-start | bytes 884744 | tf_op jit(solution)/shard_map/ppermute | solution.py:62
  48.9 0.0 collective-permute-done.9.refs_4_
  48.9 0.0 collective-permute-start.20
  48.9 2.9 %pick_left.1 = (bf16[64,2304]{1,0:T(8,128)(2,1)}, bf16[64,2304]{1,0:T(8,128)(2,1)}, bf16[64,2304]{1,0:T(8,128)(2,1)}, bf16[64,2304]{1,0:T(8,128)(2,1)}) custom-call(s32[4]{0:T(128)} %owner.5, bf16[64,2304]{1,0:T(8,128)(2,1)} %bitcast.16, bf16[64,2304]{1,0:T(8,128)(2,1)} %copy-done.9, bf16[64,2304]{1,0:T(8,128)(2,1)} %copy-done.11, ...), custom_call_target="tpu_custom_call" | custom-call | bytes 3145728 | tf_op jit(solution)/shard_map/pick_left/pallas_call | solution.py:119
  51.8 0.0 collective-permute-done.21.refs_10_
  51.8 0.0 collective-permute-start.11
  51.8 0.0 collective-permute-done.2.refs_3_
  51.8 1.6 %collective-permute-start.12 = (bf16[64,2304]{1,0:T(8,128)(2,1)}, bf16[64,2304]{1,0:T(8,128)(2,1)S(1)}, u32[]{:S(2)}, u32[]{:S(2)}) collective-permute-start(bf16[64,2304]{1,0:T(8,128)(2,1)} %get-tuple-element.44), channel_id=1, source_target_pairs={{0,2},{1,3},{2,0},{3,1},{4,6},{5,7},{6,4},{7,5},{8,10},{9,11},{10,... | collective-permute-start | bytes 884744 | tf_op jit(solution)/shard_map/ppermute | solution.py:83
  53.4 0.0 collective-permute-done.22.refs_12_
  53.4 0.3 collective-permute-start.13
  53.7 1.3 copy-done.3
  55.0 1.3 copy-done.4
  56.2 3.1 %grams.1 = (bf16[512,512]{1,0:T(8,128)(2,1)S(1)}, bf16[512,512]{1,0:T(8,128)(2,1)S(1)}, f32[256,256]{1,0:T(8,128)S(1)}) custom-call(bf16[2304,256]{1,0:T(8,128)(2,1)S(1)} %bitcast.19, bf16[2304,256]{1,0:T(8,128)(2,1)S(1)} %bitcast.21, bf16[64,2304]{1,0:T(8,128)(2,1)S(1)} %bitcast.17, bf16[64,2304]{1,0:T(8,128)(2,1)S(1)} %collective-permute-done.refs_1_, ...), custom_call_target="tpu_custom_call" | custom-call | flops 1207959552 | bytes 6291456 | tf_op jit(solution)/shard_map/grams/pallas_call | solution.py:185
  59.4 0.0 collective-permute-done.19.refs_3_
  59.4 0.0 collective-permute-done.20.refs_5_
  59.4 0.0 copy-start.6
  59.4 0.1 collective-permute-start.24
  59.5 2.1 %collective-permute-start.23 = (bf16[32,2304]{1,0:T(8,128)(2,1)S(1)}, bf16[32,2304]{1,0:T(8,128)(2,1)S(1)}, u32[]{:S(2)}, u32[]{:S(2)}) collective-permute-start(bf16[32,2304]{1,0:T(8,128)(2,1)S(1)} %slice.14), channel_id=1, source_target_pairs={{0,8},{8,16},{16,24},{24,28},{28,20},{20,12},{12,4},{4,0},{1,9},{9... | collective-permute-start | bytes 442376 | tf_op jit(solution)/shard_map/ppermute | solution.py:62
  61.6 4.3 %collective-permute-done.24.refs_8_ = bf16[32,2304]{1,0:T(8,128)(2,1)S(1)} collective-permute-done((bf16[32,2304]{1,0:T(8,128)(2,1)S(1)}, bf16[32,2304]{1,0:T(8,128)(2,1)S(1)}, u32[]{:S(2)}, u32[]{:S(2)}) %collective-permute-start.24) | collective-permute-done | bytes 147488 | tf_op jit(solution)/shard_map/ppermute | solution.py:62
  65.9 0.0 collective-permute-done.23.refs_4_
  65.9 1.4 coupling.1
  67.3 0.1 collective-permute-start.25
  67.3 1.6 %collective-permute-start.26 = (bf16[64,256]{1,0:T(8,128)(2,1)S(1)}, bf16[64,256]{1,0:T(8,128)(2,1)S(1)}, u32[]{:S(2)}, u32[]{:S(2)}) collective-permute-start(bf16[64,256]{1,0:T(8,128)(2,1)S(1)} %get-tuple-element.56), channel_id=1, source_target_pairs={{0,2},{1,3},{2,0},{3,1},{4,6},{5,7},{6,4},{7,5},{8,10},{9,11},{10,... | collective-permute-start | bytes 98312 | tf_op jit(solution)/shard_map/ppermute | solution.py:83
  68.9 0.0 collective-permute-done.11.refs_5_
  68.9 0.3 collective-permute-start.27
  70.5 0.0 collective-permute-done.12.refs_6_
  70.5 0.0 collective-permute-done.13.refs_7_
  70.5 0.0 collective-permute-done.25.refs_9_
  70.5 0.8 collective-permute-done.26.refs_10_
  71.3 0.9 collective-permute-done.27.refs_11_
  72.3 72.0 %finish.1 = (bf16[2304,256]{1,0:T(8,128)(2,1)}, bf16[2304,256]{1,0:T(8,128)(2,1)}) custom-call(s32[1,1]{1,0:T(1,128)S(6)} %copy.10.old_ref, s32[1,1]{1,0:T(1,128)S(6)} %copy.11.goal_ref, s32[8]{0:T(128)S(1)} %copy-done.6, s32[4]{0:T(128)S(1)} %copy-done.2, bf16[2304,256]{1,0:T(8,128)(2,1)S(1)} %bitcast.20, bf16[2304,256]{1,0:T(8,128)(2,1)S(1)} %bitcast.22, ...), custom_call_target="tpu_custom_call" | custom-call | flops 8589934592 | bytes 12582912 | tf_op jit(solution)/shard_map/finish/pallas_call | solution.py:364
  (28 shorter events, 0.1 us)
Async XLA Ops:
  0.6 10.2 %collective-permute-start.3 = (bf16[64,2304]{1,0:T(8,128)(2,1)}, bf16[64,2304]{1,0:T(8,128)(2,1)S(1)}, u32[]{:S(2)}, u32[]{:S(2)}) collective-permute-start(bf16[64,2304]{1,0:T(8,128)(2,1)} %bitcast.12), channel_id=1, source_target_pairs={{0,8},{8,16},{16,24},{24,28},{28,20},{20,12},{12,4},{4,0},{1,9},{9... | collective-permute-start | bytes 884744 | tf_op jit(solution)/shard_map/ppermute | solution.py:62
  3.7 8.7 %collective-permute-start.4 = (bf16[64,2304]{1,0:T(8,128)(2,1)}, bf16[64,2304]{1,0:T(8,128)(2,1)S(1)}, u32[]{:S(2)}, u32[]{:S(2)}) collective-permute-start(bf16[64,2304]{1,0:T(8,128)(2,1)} %bitcast.13), channel_id=1, source_target_pairs={{8,0},{16,8},{24,16},{28,24},{20,28},{12,20},{4,12},{0,4},{9,1},{1... | collective-permute-start | bytes 884744 | tf_op jit(solution)/shard_map/ppermute | solution.py:62
  10.9 13.7 %copy-start.9 = (bf16[64,2304]{1,0:T(8,128)(2,1)}, bf16[64,2304]{1,0:T(8,128)(2,1)S(1)}, u32[]{:S(2)}) copy-start(bf16[64,2304]{1,0:T(8,128)(2,1)S(1)} %collective-permute-done.3.refs_1_) | copy-start | bytes 884740
  12.4 15.6 %copy-start.10 = (bf16[64,2304]{1,0:T(8,128)(2,1)}, bf16[64,2304]{1,0:T(8,128)(2,1)S(1)}, u32[]{:S(2)}) copy-start(bf16[64,2304]{1,0:T(8,128)(2,1)S(1)} %collective-permute-done.4.refs_7_) | copy-start | bytes 884740
  12.4 7.6 %collective-permute-start.5 = (bf16[64,2304]{1,0:T(8,128)(2,1)S(1)}, bf16[64,2304]{1,0:T(8,128)(2,1)S(1)}, u32[]{:S(2)}, u32[]{:S(2)}) collective-permute-start(bf16[64,2304]{1,0:T(8,128)(2,1)S(1)} %collective-permute-done.3.refs_1_), channel_id=1, source_target_pairs={{0,8},{8,16},{16,24},{24,28},{28,20},{20,12},{12,4},{4,0},{1,9},{9... | collective-permute-start | bytes 884744 | tf_op jit(solution)/shard_map/ppermute | solution.py:62
  14.0 7.3 %collective-permute-start.6 = (bf16[64,2304]{1,0:T(8,128)(2,1)S(1)}, bf16[64,2304]{1,0:T(8,128)(2,1)S(1)}, u32[]{:S(2)}, u32[]{:S(2)}) collective-permute-start(bf16[64,2304]{1,0:T(8,128)(2,1)S(1)} %collective-permute-done.4.refs_7_), channel_id=1, source_target_pairs={{8,0},{16,8},{24,16},{28,24},{20,28},{12,20},{4,12},{0,4},{9,1},{1... | collective-permute-start | bytes 884744 | tf_op jit(solution)/shard_map/ppermute | solution.py:62
  14.4 10.2 %collective-permute-start.1 = (bf16[64,2304]{1,0:T(8,128)(2,1)}, bf16[64,2304]{1,0:T(8,128)(2,1)S(1)}, u32[]{:S(2)}, u32[]{:S(2)}) collective-permute-start(bf16[64,2304]{1,0:T(8,128)(2,1)} %bitcast.14), channel_id=1, source_target_pairs={{0,2},{1,3},{2,0},{3,1},{4,6},{5,7},{6,4},{7,5},{8,10},{9,11},{10,... | collective-permute-start | bytes 884744 | tf_op jit(solution)/shard_map/ppermute | solution.py:83
  15.9 12.0 %collective-permute-start.14 = (bf16[64,2304]{1,0:T(8,128)(2,1)}, bf16[64,2304]{1,0:T(8,128)(2,1)S(1)}, u32[]{:S(2)}, u32[]{:S(2)}) collective-permute-start(bf16[64,2304]{1,0:T(8,128)(2,1)} %bitcast.6), channel_id=1, source_target_pairs={{0,2},{1,3},{2,0},{3,1},{4,6},{5,7},{6,4},{7,5},{8,10},{9,11},{10,... | collective-permute-start | bytes 884744 | tf_op jit(solution)/shard_map/ppermute | solution.py:83
  19.9 14.9 %copy-start.11 = (bf16[64,2304]{1,0:T(8,128)(2,1)}, bf16[64,2304]{1,0:T(8,128)(2,1)S(1)}, u32[]{:S(2)}) copy-start(bf16[64,2304]{1,0:T(8,128)(2,1)S(1)} %collective-permute-done.5.refs_2_) | copy-start | bytes 884740
  21.2 15.2 %copy-start.12 = (bf16[64,2304]{1,0:T(8,128)(2,1)}, bf16[64,2304]{1,0:T(8,128)(2,1)S(1)}, u32[]{:S(2)}) copy-start(bf16[64,2304]{1,0:T(8,128)(2,1)S(1)} %collective-permute-done.6.refs_6_) | copy-start | bytes 884740
  21.2 8.7 %collective-permute-start.7 = (bf16[64,2304]{1,0:T(8,128)(2,1)S(1)}, bf16[64,2304]{1,0:T(8,128)(2,1)S(1)}, u32[]{:S(2)}, u32[]{:S(2)}) collective-permute-start(bf16[64,2304]{1,0:T(8,128)(2,1)S(1)} %collective-permute-done.5.refs_2_), channel_id=1, source_target_pairs={{0,8},{8,16},{16,24},{24,28},{28,20},{20,12},{12,4},{4,0},{1,9},{9... | collective-permute-start | bytes 884744 | tf_op jit(solution)/shard_map/ppermute | solution.py:62
  22.8 7.2 %collective-permute-start.8 = (bf16[64,2304]{1,0:T(8,128)(2,1)S(1)}, bf16[64,2304]{1,0:T(8,128)(2,1)S(1)}, u32[]{:S(2)}, u32[]{:S(2)}) collective-permute-start(bf16[64,2304]{1,0:T(8,128)(2,1)S(1)} %collective-permute-done.6.refs_6_), channel_id=1, source_target_pairs={{8,0},{16,8},{24,16},{28,24},{20,28},{12,20},{4,12},{0,4},{9,1},{1... | collective-permute-start | bytes 884744 | tf_op jit(solution)/shard_map/ppermute | solution.py:62
  27.9 6.9 %collective-permute-start.15 = (bf16[64,2304]{1,0:T(8,128)(2,1)}, bf16[64,2304]{1,0:T(8,128)(2,1)S(1)}, u32[]{:S(2)}, u32[]{:S(2)}) collective-permute-start(bf16[64,2304]{1,0:T(8,128)(2,1)} %bitcast.7), channel_id=1, source_target_pairs={{0,8},{8,16},{16,24},{24,28},{28,20},{20,12},{12,4},{4,0},{1,9},{9... | collective-permute-start | bytes 884744 | tf_op jit(solution)/shard_map/ppermute | solution.py:62
  29.5 6.9 %collective-permute-start.16 = (bf16[64,2304]{1,0:T(8,128)(2,1)}, bf16[64,2304]{1,0:T(8,128)(2,1)S(1)}, u32[]{:S(2)}, u32[]{:S(2)}) collective-permute-start(bf16[64,2304]{1,0:T(8,128)(2,1)} %bitcast.8), channel_id=1, source_target_pairs={{8,0},{16,8},{24,16},{28,24},{20,28},{12,20},{4,12},{0,4},{9,1},{1... | collective-permute-start | bytes 884744 | tf_op jit(solution)/shard_map/ppermute | solution.py:62
  30.0 10.8 %collective-permute-start = (bf16[64,2304]{1,0:T(8,128)(2,1)}, bf16[64,2304]{1,0:T(8,128)(2,1)S(1)}, u32[]{:S(2)}, u32[]{:S(2)}) collective-permute-start(bf16[64,2304]{1,0:T(8,128)(2,1)} %bitcast.15), channel_id=1, source_target_pairs={{0,1},{1,0},{2,3},{3,2},{4,5},{5,4},{6,7},{7,6},{8,9},{9,8},{10,11... | collective-permute-start | bytes 884744 | tf_op jit(solution)/shard_map/ppermute | solution.py:83
  30.0 10.8 %copy-start.7 = (bf16[64,2304]{1,0:T(8,128)(2,1)}, bf16[64,2304]{1,0:T(8,128)(2,1)S(1)}, u32[]{:S(2)}) copy-start(bf16[64,2304]{1,0:T(8,128)(2,1)S(1)} %collective-permute-done.7.refs_3_) | copy-start | bytes 884740
  30.0 13.3 %copy-start.8 = (bf16[64,2304]{1,0:T(8,128)(2,1)}, bf16[64,2304]{1,0:T(8,128)(2,1)S(1)}, u32[]{:S(2)}) copy-start(bf16[64,2304]{1,0:T(8,128)(2,1)S(1)} %collective-permute-done.8.refs_5_) | copy-start | bytes 884740
  36.5 6.9 %collective-permute-start.17 = (bf16[64,2304]{1,0:T(8,128)(2,1)S(1)}, bf16[64,2304]{1,0:T(8,128)(2,1)S(1)}, u32[]{:S(2)}, u32[]{:S(2)}) collective-permute-start(bf16[64,2304]{1,0:T(8,128)(2,1)S(1)} %collective-permute-done.15.refs_1_), channel_id=1, source_target_pairs={{0,8},{8,16},{16,24},{24,28},{28,20},{20,12},{12,4},{4,0},{1,9},{9... | collective-permute-start | bytes 884744 | tf_op jit(solution)/shard_map/ppermute | solution.py:62
  38.1 7.2 %collective-permute-start.18 = (bf16[64,2304]{1,0:T(8,128)(2,1)S(1)}, bf16[64,2304]{1,0:T(8,128)(2,1)S(1)}, u32[]{:S(2)}, u32[]{:S(2)}) collective-permute-start(bf16[64,2304]{1,0:T(8,128)(2,1)S(1)} %collective-permute-done.16.refs_7_), channel_id=1, source_target_pairs={{8,0},{16,8},{24,16},{28,24},{20,28},{12,20},{4,12},{0,4},{9,1},{1... | collective-permute-start | bytes 884744 | tf_op jit(solution)/shard_map/ppermute | solution.py:62
  38.5 8.4 %collective-permute-start.10 = (bf16[32,2304]{1,0:T(8,128)(2,1)S(1)}, bf16[32,2304]{1,0:T(8,128)(2,1)S(1)}, u32[]{:S(2)}, u32[]{:S(2)}) collective-permute-start(bf16[32,2304]{1,0:T(8,128)(2,1)S(1)} %slice.13), channel_id=1, source_target_pairs={{8,0},{16,8},{24,16},{28,24},{20,28},{12,20},{4,12},{0,4},{9,1},{1... | collective-permute-start | bytes 442376 | tf_op jit(solution)/shard_map/ppermute | solution.py:62
  39.0 14.7 %copy-start.1 = (bf16[1,64,2304]{2,1,0:T(8,128)(2,1)S(1)}, bf16[1,64,2304]{2,1,0:T(8,128)(2,1)}, u32[]{:S(2)}) copy-start(bf16[1,64,2304]{2,1,0:T(8,128)(2,1)} %param.10) | copy-start | bytes 884740
  39.0 9.9 %collective-permute-start.9 = (bf16[32,2304]{1,0:T(8,128)(2,1)S(1)}, bf16[32,2304]{1,0:T(8,128)(2,1)}, u32[]{:S(2)}, u32[]{:S(2)}) collective-permute-start(bf16[32,2304]{1,0:T(8,128)(2,1)S(1)} %slice.12), channel_id=1, source_target_pairs={{0,8},{8,16},{16,24},{24,28},{28,20},{20,12},{12,4},{4,0},{1,9},{9... | collective-permute-start | bytes 442376 | tf_op jit(solution)/shard_map/ppermute | solution.py:62
  40.8 11.0 %collective-permute-start.21 = (bf16[64,2304]{1,0:T(8,128)(2,1)}, bf16[64,2304]{1,0:T(8,128)(2,1)S(1)}, u32[]{:S(2)}, u32[]{:S(2)}) collective-permute-start(bf16[64,2304]{1,0:T(8,128)(2,1)} %bitcast.9), channel_id=1, source_target_pairs={{0,1},{1,0},{2,3},{3,2},{4,5},{5,4},{6,7},{7,6},{8,9},{9,8},{10,11... | collective-permute-start | bytes 884744 | tf_op jit(solution)/shard_map/ppermute | solution.py:83
  43.3 8.5 %collective-permute-start.2 = (bf16[64,2304]{1,0:T(8,128)(2,1)S(1)}, bf16[64,2304]{1,0:T(8,128)(2,1)}, u32[]{:S(2)}, u32[]{:S(2)}) collective-permute-start(bf16[64,2304]{1,0:T(8,128)(2,1)S(1)} %collective-permute-done.1.refs_2_), channel_id=1, source_target_pairs={{0,1},{1,0},{2,3},{3,2},{4,5},{5,4},{6,7},{7,6},{8,9},{9,8},{10,11... | collective-permute-start | bytes 884744 | tf_op jit(solution)/shard_map/ppermute | solution.py:83
  45.3 8.1 %collective-permute-start.22 = (bf16[64,2304]{1,0:T(8,128)(2,1)S(1)}, bf16[64,2304]{1,0:T(8,128)(2,1)S(1)}, u32[]{:S(2)}, u32[]{:S(2)}) collective-permute-start(bf16[64,2304]{1,0:T(8,128)(2,1)S(1)} %collective-permute-done.14.refs_11_), channel_id=1, source_target_pairs={{0,1},{1,0},{2,3},{3,2},{4,5},{5,4},{6,7},{7,6},{8,9},{9,8},{10,11... | collective-permute-start | bytes 884744 | tf_op jit(solution)/shard_map/ppermute | solution.py:83
  46.9 2.0 %copy-start.13 = (bf16[32,2304]{1,0:T(8,128)(2,1)}, bf16[32,2304]{1,0:T(8,128)(2,1)S(1)}, u32[]{:S(2)}) copy-start(bf16[32,2304]{1,0:T(8,128)(2,1)S(1)} %collective-permute-done.10.refs_8_) | copy-start | bytes 442372
  46.9 12.5 %collective-permute-start.19 = (bf16[64,2304]{1,0:T(8,128)(2,1)S(1)}, bf16[64,2304]{1,0:T(8,128)(2,1)S(1)}, u32[]{:S(2)}, u32[]{:S(2)}) collective-permute-start(bf16[64,2304]{1,0:T(8,128)(2,1)S(1)} %collective-permute-done.17.refs_2_), channel_id=1, source_target_pairs={{0,8},{8,16},{16,24},{24,28},{28,20},{20,12},{12,4},{4,0},{1,9},{9... | collective-permute-start | bytes 884744 | tf_op jit(solution)/shard_map/ppermute | solution.py:62
  48.9 10.5 %collective-permute-start.20 = (bf16[64,2304]{1,0:T(8,128)(2,1)S(1)}, bf16[64,2304]{1,0:T(8,128)(2,1)S(1)}, u32[]{:S(2)}, u32[]{:S(2)}) collective-permute-start(bf16[64,2304]{1,0:T(8,128)(2,1)S(1)} %collective-permute-done.18.refs_6_), channel_id=1, source_target_pairs={{8,0},{16,8},{24,16},{28,24},{20,28},{12,20},{4,12},{0,4},{9,1},{1... | collective-permute-start | bytes 884744 | tf_op jit(solution)/shard_map/ppermute | solution.py:62
  51.8 17.1 %collective-permute-start.11 = (bf16[64,2304]{1,0:T(8,128)(2,1)}, bf16[64,2304]{1,0:T(8,128)(2,1)S(1)}, u32[]{:S(2)}, u32[]{:S(2)}) collective-permute-start(bf16[64,2304]{1,0:T(8,128)(2,1)} %get-tuple-element.43), channel_id=1, source_target_pairs={{0,1},{1,0},{2,3},{3,2},{4,5},{5,4},{6,7},{7,6},{8,9},{9,8},{10,11... | collective-permute-start | bytes 884744 | tf_op jit(solution)/shard_map/ppermute | solution.py:83
  51.8 18.7 %collective-permute-start.12 = (bf16[64,2304]{1,0:T(8,128)(2,1)}, bf16[64,2304]{1,0:T(8,128)(2,1)S(1)}, u32[]{:S(2)}, u32[]{:S(2)}) collective-permute-start(bf16[64,2304]{1,0:T(8,128)(2,1)} %get-tuple-element.44), channel_id=1, source_target_pairs={{0,2},{1,3},{2,0},{3,1},{4,6},{5,7},{6,4},{7,5},{8,10},{9,11},{10,... | collective-permute-start | bytes 884744 | tf_op jit(solution)/shard_map/ppermute | solution.py:83
  53.4 17.1 %collective-permute-start.13 = (bf16[64,2304]{1,0:T(8,128)(2,1)}, bf16[64,2304]{1,0:T(8,128)(2,1)S(1)}, u32[]{:S(2)}, u32[]{:S(2)}) collective-permute-start(bf16[64,2304]{1,0:T(8,128)(2,1)} %get-tuple-element.45), channel_id=1, source_target_pairs={{0,3},{1,2},{2,1},{3,0},{4,7},{5,6},{6,5},{7,4},{8,11},{9,10},{10,... | collective-permute-start | bytes 884744 | tf_op jit(solution)/shard_map/ppermute | solution.py:83
  53.7 1.3 copy-start.3
  55.0 1.3 copy-start.4
  56.2 9.6 %copy-start = (bf16[1,64,2304]{2,1,0:T(8,128)(2,1)S(1)}, bf16[1,64,2304]{2,1,0:T(8,128)(2,1)}, u32[]{:S(2)}) copy-start(bf16[1,64,2304]{2,1,0:T(8,128)(2,1)} %param.11) | copy-start | bytes 884740
  56.2 9.6 %copy-start.2 = (s32[4]{0:T(128)S(1)}, s32[4]{0:T(128)}, u32[]{:S(2)}) copy-start(s32[4]{0:T(128)} %owner.5) | copy-start | bytes 52
  59.4 12.8 %copy-start.5 = (bf16[64,2304]{1,0:T(8,128)(2,1)S(1)}, bf16[64,2304]{1,0:T(8,128)(2,1)}, u32[]{:S(2)}) copy-start(bf16[64,2304]{1,0:T(8,128)(2,1)} %get-tuple-element.42.refs_4_) | copy-start | bytes 884740
  59.4 12.8 %copy-start.6 = (s32[8]{0:T(128)S(1)}, s32[8]{0:T(128)}, u32[]{:S(2)}) copy-start(s32[8]{0:T(128)} %panel.1) | copy-start | bytes 100
  59.4 6.4 %collective-permute-start.24 = (bf16[32,2304]{1,0:T(8,128)(2,1)S(1)}, bf16[32,2304]{1,0:T(8,128)(2,1)S(1)}, u32[]{:S(2)}, u32[]{:S(2)}) collective-permute-start(bf16[32,2304]{1,0:T(8,128)(2,1)S(1)} %slice.15), channel_id=1, source_target_pairs={{8,0},{16,8},{24,16},{28,24},{20,28},{12,20},{4,12},{0,4},{9,1},{1... | collective-permute-start | bytes 442376 | tf_op jit(solution)/shard_map/ppermute | solution.py:62
  59.5 6.4 %collective-permute-start.23 = (bf16[32,2304]{1,0:T(8,128)(2,1)S(1)}, bf16[32,2304]{1,0:T(8,128)(2,1)S(1)}, u32[]{:S(2)}, u32[]{:S(2)}) collective-permute-start(bf16[32,2304]{1,0:T(8,128)(2,1)S(1)} %slice.14), channel_id=1, source_target_pairs={{0,8},{8,16},{16,24},{24,28},{28,20},{20,12},{12,4},{4,0},{1,9},{9... | collective-permute-start | bytes 442376 | tf_op jit(solution)/shard_map/ppermute | solution.py:62
  67.3 3.3 %collective-permute-start.25 = (bf16[64,256]{1,0:T(8,128)(2,1)S(1)}, bf16[64,256]{1,0:T(8,128)(2,1)S(1)}, u32[]{:S(2)}, u32[]{:S(2)}) collective-permute-start(bf16[64,256]{1,0:T(8,128)(2,1)S(1)} %get-tuple-element.55), channel_id=1, source_target_pairs={{0,1},{1,0},{2,3},{3,2},{4,5},{5,4},{6,7},{7,6},{8,9},{9,8},{10,11... | collective-permute-start | bytes 98312 | tf_op jit(solution)/shard_map/ppermute | solution.py:83
  67.3 4.0 %collective-permute-start.26 = (bf16[64,256]{1,0:T(8,128)(2,1)S(1)}, bf16[64,256]{1,0:T(8,128)(2,1)S(1)}, u32[]{:S(2)}, u32[]{:S(2)}) collective-permute-start(bf16[64,256]{1,0:T(8,128)(2,1)S(1)} %get-tuple-element.56), channel_id=1, source_target_pairs={{0,2},{1,3},{2,0},{3,1},{4,6},{5,7},{6,4},{7,5},{8,10},{9,11},{10,... | collective-permute-start | bytes 98312 | tf_op jit(solution)/shard_map/ppermute | solution.py:83
  68.9 3.3 %collective-permute-start.27 = (bf16[64,256]{1,0:T(8,128)(2,1)S(1)}, bf16[64,256]{1,0:T(8,128)(2,1)S(1)}, u32[]{:S(2)}, u32[]{:S(2)}) collective-permute-start(bf16[64,256]{1,0:T(8,128)(2,1)S(1)} %get-tuple-element.57), channel_id=1, source_target_pairs={{0,3},{1,2},{2,1},{3,0},{4,7},{5,6},{6,5},{7,4},{8,11},{9,10},{10,... | collective-permute-start | bytes 98312 | tf_op jit(solution)/shard_map/ppermute | solution.py:83

commit v5 on v4

--- a/solution.py
+++ b/solution.py
@@ -10,7 +10,6 @@
 
 F32 = jnp.float32
 BF16 = jnp.bfloat16
-HIGHEST = lax.Precision.HIGHEST
 VMEM = pl.BlockSpec(memory_space=pltpu.VMEM)
 SMEM = pl.BlockSpec(memory_space=pltpu.SMEM)
 HBM = pl.BlockSpec(memory_space=pltpu.HBM)
@@ -18,16 +17,16 @@
 ROUGH_STEPS, FINE_STEPS = 12, 6
 
 
-def nn(a, b, precision=None):
-    return lax.dot_general(a, b, (((1,), (0,)), ((), ())), precision=precision, preferred_element_type=F32)
-
-
-def nt(a, b, precision=None):
-    return lax.dot_general(a, b, (((1,), (1,)), ((), ())), precision=precision, preferred_element_type=F32)
-
-
-def tn(a, b, precision=None):
-    return lax.dot_general(a, b, (((0,), (0,)), ((), ())), precision=precision, preferred_element_type=F32)
+def nn(a, b):
+    return lax.dot_general(a, b, (((1,), (0,)), ((), ())), preferred_element_type=F32)
+
+
+def nt(a, b):
+    return lax.dot_general(a, b, (((1,), (1,)), ((), ())), preferred_element_type=F32)
+
+
+def tn(a, b):
+    return lax.dot_general(a, b, (((0,), (0,)), ((), ())), preferred_element_type=F32)
 
 
 def halves(x):
@@ -69,7 +68,7 @@
         return fwd, bwd
 
     for s in range(1, half - 1):
-        done = step(0, s)
+        done = step(0, s, *(gates[0](s) if s > 1 else ()))
     for s in range(1, half + 1):
         if s < 3:
             early = step(0, half - 2 + s)
@@ -331,7 +330,7 @@
     pu, pv = panel_basis[0], panel_coeffs[0]
     rows, rank = u.shape
 
-    lefts, rights, grammed = {0: pu}, {0: pv}, []
+    lefts, rights = {0: pu}, {0: pv}
 
     def grow(have, bits):
         for bit in bits:
@@ -341,20 +340,18 @@
 
     high = [n_col >> t for t in range(1, n_col.bit_length() - 1)]
 
-    def columns_grams(lists):
-        grow(lefts, [1])
-        grow(rights, [1])
-        grammed.extend(gram_products(u, v, [lefts[m] for m in range(n_col)]))
-        return (grammed[2], *rights.values())
-
-    gates = {1: lambda _: grow(lefts, high) + grow(rights, high), n_row // 2: columns_grams}
+    gates = {
+        0: lambda s: grow(lefts, high) if s == 2 else (),
+        1: lambda _: grow(rights, high),
+        n_row // 2: lambda _: grow(lefts, [1]) + grow(rights, [1]),
+    }
     us, vs = ring_gathers(pu, pv, "row", n_row, gates)
-    h_high, h_low, core_up = grammed
     ui_parts = [lefts[m] for m in range(n_col)]
 
     ujs = picked_left(us, owner_row, n_row, n_col)
     ujs = [ujs[0]] + [swap(ujs[m], "col", n_col, m) for m in range(1, n_col)]
     kts = coupled(vs, [rights[m] for m in range(n_col)], owner_row, n_row, n_col)
+    h_high, h_low, core_up = gram_products(u, v, [after(ui_parts[0], kts[0]), *ui_parts[1:]])
     kts = [kts[0]] + [swap(kts[m], "col", n_col, m) for m in range(1, n_col)]
 
     out = jax.ShapeDtypeStruct((rows, rank), BF16)

time: 145 us -> 139 us (0.959)
  waiting for transfers between devices: 36.7 us -> 32.8 us
  local copies, waits for them, and re-layouts: 2.64 us -> 0.11 us
  starting transfers between devices: 23.4 us -> 24.9 us
    ppermute x12, waiting for transfers between devices: 6.41 us -> 0.56 us  [swap(): return lax.ppermute(x, axis, [(i, i ^ m) for i in range(n)])]
    unnamed x28 -> x26, local copies, waits for them, and re-layouts: 2.59 us -> 0.06 us
    ppermute x16, waiting for transfers between devices: 30.3 us -> 32.2 us  [step(): fwd, bwd = (lax.ppermute(fwd, axis, ahead), lax.ppermute(bwd, axis, back))]
    ppermute x12, starting transfers between devices: 5.87 us -> 7.42 us  [swap(): return lax.ppermute(x, axis, [(i, i ^ m) for i in range(n)])]
  transfers between devices with their start and end apart: 28 -> 28, of which waited for: 14 -> 16; matrix products, arithmetic and copies ran while one was open for 0% -> 0% of each run, Pallas kernels for 5% -> 5%
where the time goes in v5:
time: 139 us
  Pallas kernels  79.4 us (57%)
  waiting for transfers between devices  32.8 us (24%)
  starting transfers between devices  24.9 us (18%)
  between operations  2.1 us (2%)
    pallas_call x1, Pallas kernels, body(): pl.pallas_call(functools.partial(finish, n_col), out_shape=(out, out), in...  72 us
    ppermute x16, waiting for transfers between devices, step(): fwd, bwd = (lax.ppermute(fwd, axis, ahead), lax.ppermute(bwd, axis, back))  32.2 us
    ppermute x16, starting transfers between devices, step(): fwd, bwd = (lax.ppermute(fwd, axis, ahead), lax.ppermute(bwd, axis, back))  17.5 us
    ppermute x12, starting transfers between devices, swap(): return lax.ppermute(x, axis, [(i, i ^ m) for i in range(n)])  7.42 us
    pallas_call x1, Pallas kernels, gram_products(): pl.pallas_call(functools.partial(grams, len(parts)), out_shape=[jax.Shape...  3.13 us
    pallas_call x1, Pallas kernels, picked_left(): pl.pallas_call(functools.partial(pick_left, n_row, n_col), out_shape=[jax...  2.87 us
  transfers between devices with their start and end apart: 28, of which 16 were waited for; matrix products, arithmetic and copies ran while one was open for 0% of the time, Pallas kernels for 5%

profile of v5, /device:TPU:0, one launch (start us, length us, event | category | flops | bytes accessed | tf_op | source)
XLA Modules:
  0.0 139.3 jit_solution(2239226412157204027)
XLA Ops:
  0.6 3.1 %collective-permute-start.1 = (bf16[64,2304]{1,0:T(8,128)(2,1)}, bf16[64,2304]{1,0:T(8,128)(2,1)S(1)}, u32[]{:S(2)}, u32[]{:S(2)}) collective-permute-start(bf16[64,2304]{1,0:T(8,128)(2,1)} %bitcast.12), channel_id=1, source_target_pairs={{0,8},{8,16},{16,24},{24,28},{28,20},{20,12},{12,4},{4,0},{1,9},{9... | collective-permute-start | bytes 884744 | tf_op jit(solution)/shard_map/ppermute | solution.py:61
  3.7 0.0 collective-permute-start.2
  3.7 1.9 %collective-permute-start.3 = (bf16[64,2304]{1,0:T(8,128)(2,1)}, bf16[64,2304]{1,0:T(8,128)(2,1)S(1)}, u32[]{:S(2)}, u32[]{:S(2)}) collective-permute-start(bf16[64,2304]{1,0:T(8,128)(2,1)} %bitcast.14), channel_id=1, source_target_pairs={{0,2},{1,3},{2,0},{3,1},{4,6},{5,7},{6,4},{7,5},{8,10},{9,11},{10,... | collective-permute-start | bytes 884744 | tf_op jit(solution)/shard_map/ppermute | solution.py:82
  5.6 5.2 %collective-permute-done.1.refs_1_ = bf16[64,2304]{1,0:T(8,128)(2,1)S(1)} collective-permute-done((bf16[64,2304]{1,0:T(8,128)(2,1)}, bf16[64,2304]{1,0:T(8,128)(2,1)S(1)}, u32[]{:S(2)}, u32[]{:S(2)}) %collective-permute-start.1) | collective-permute-done | bytes 294944 | tf_op jit(solution)/shard_map/ppermute | solution.py:61
  10.9 1.5 %collective-permute-done.2.refs_7_ = bf16[64,2304]{1,0:T(8,128)(2,1)S(1)} collective-permute-done((bf16[64,2304]{1,0:T(8,128)(2,1)}, bf16[64,2304]{1,0:T(8,128)(2,1)S(1)}, u32[]{:S(2)}, u32[]{:S(2)}) %collective-permute-start.2) | collective-permute-done | bytes 294944 | tf_op jit(solution)/shard_map/ppermute | solution.py:61
  12.4 0.0 collective-permute-done.3.refs_2_
  12.4 1.7 %collective-permute-start.4 = (bf16[64,2304]{1,0:T(8,128)(2,1)S(1)}, bf16[64,2304]{1,0:T(8,128)(2,1)S(1)}, u32[]{:S(2)}, u32[]{:S(2)}) collective-permute-start(bf16[64,2304]{1,0:T(8,128)(2,1)S(1)} %collective-permute-done.1.refs_1_), channel_id=1, source_target_pairs={{0,8},{8,16},{16,24},{24,28},{28,20},{20,12},{12,4},{4,0},{1,9},{9... | collective-permute-start | bytes 884744 | tf_op jit(solution)/shard_map/ppermute | solution.py:61
  14.1 0.3 collective-permute-start.5
  14.4 1.6 %collective-permute-start = (bf16[64,2304]{1,0:T(8,128)(2,1)}, bf16[64,2304]{1,0:T(8,128)(2,1)S(1)}, u32[]{:S(2)}, u32[]{:S(2)}) collective-permute-start(bf16[64,2304]{1,0:T(8,128)(2,1)} %bitcast.6), channel_id=1, source_target_pairs={{0,2},{1,3},{2,0},{3,1},{4,6},{5,7},{6,4},{7,5},{8,10},{9,11},{10,... | collective-permute-start | bytes 884744 | tf_op jit(solution)/shard_map/ppermute | solution.py:82
  16.1 3.9 %collective-permute-done.4.refs_2_ = bf16[64,2304]{1,0:T(8,128)(2,1)S(1)} collective-permute-done((bf16[64,2304]{1,0:T(8,128)(2,1)S(1)}, bf16[64,2304]{1,0:T(8,128)(2,1)S(1)}, u32[]{:S(2)}, u32[]{:S(2)}) %collective-permute-start.4) | collective-permute-done | bytes 294944 | tf_op jit(solution)/shard_map/ppermute | solution.py:61
  20.0 1.3 collective-permute-done.5.refs_6_
  21.2 1.6 %collective-permute-start.8 = (bf16[64,2304]{1,0:T(8,128)(2,1)S(1)}, bf16[64,2304]{1,0:T(8,128)(2,1)S(1)}, u32[]{:S(2)}, u32[]{:S(2)}) collective-permute-start(bf16[64,2304]{1,0:T(8,128)(2,1)S(1)} %collective-permute-done.4.refs_2_), channel_id=1, source_target_pairs={{0,8},{8,16},{16,24},{24,28},{28,20},{20,12},{12,4},{4,0},{1,9},{9... | collective-permute-start | bytes 884744 | tf_op jit(solution)/shard_map/ppermute | solution.py:61
  22.8 0.4 collective-permute-start.9
  23.3 0.0 collective-permute-done.refs_11_
  23.3 1.6 %collective-permute-start.6 = (bf16[64,2304]{1,0:T(8,128)(2,1)}, bf16[64,2304]{1,0:T(8,128)(2,1)S(1)}, u32[]{:S(2)}, u32[]{:S(2)}) collective-permute-start(bf16[64,2304]{1,0:T(8,128)(2,1)} %bitcast.7), channel_id=1, source_target_pairs={{0,8},{8,16},{16,24},{24,28},{28,20},{20,12},{12,4},{4,0},{1,9},{9... | collective-permute-start | bytes 884744 | tf_op jit(solution)/shard_map/ppermute | solution.py:61
  24.9 0.4 collective-permute-start.7
  25.4 0.0 collective-permute-start.14
  25.4 5.2 %collective-permute-done.8.refs_3_ = bf16[64,2304]{1,0:T(8,128)(2,1)S(1)} collective-permute-done((bf16[64,2304]{1,0:T(8,128)(2,1)S(1)}, bf16[64,2304]{1,0:T(8,128)(2,1)S(1)}, u32[]{:S(2)}, u32[]{:S(2)}) %collective-permute-start.8) | collective-permute-done | bytes 294944 | tf_op jit(solution)/shard_map/ppermute | solution.py:61
  30.6 1.3 collective-permute-done.9.refs_5_
  31.9 1.9 %collective-permute-done.6.refs_1_ = bf16[64,2304]{1,0:T(8,128)(2,1)S(1)} collective-permute-done((bf16[64,2304]{1,0:T(8,128)(2,1)}, bf16[64,2304]{1,0:T(8,128)(2,1)S(1)}, u32[]{:S(2)}, u32[]{:S(2)}) %collective-permute-start.6) | collective-permute-done | bytes 294944 | tf_op jit(solution)/shard_map/ppermute | solution.py:61
  33.8 1.4 %collective-permute-done.7.refs_7_ = bf16[64,2304]{1,0:T(8,128)(2,1)S(1)} collective-permute-done((bf16[64,2304]{1,0:T(8,128)(2,1)}, bf16[64,2304]{1,0:T(8,128)(2,1)S(1)}, u32[]{:S(2)}, u32[]{:S(2)}) %collective-permute-start.7) | collective-permute-done | bytes 294944 | tf_op jit(solution)/shard_map/ppermute | solution.py:61
  35.2 1.6 %collective-permute-start.10 = (bf16[64,2304]{1,0:T(8,128)(2,1)S(1)}, bf16[64,2304]{1,0:T(8,128)(2,1)S(1)}, u32[]{:S(2)}, u32[]{:S(2)}) collective-permute-start(bf16[64,2304]{1,0:T(8,128)(2,1)S(1)} %collective-permute-done.6.refs_1_), channel_id=1, source_target_pairs={{0,8},{8,16},{16,24},{24,28},{28,20},{20,12},{12,4},{4,0},{1,9},{9... | collective-permute-start | bytes 884744 | tf_op jit(solution)/shard_map/ppermute | solution.py:61
  36.8 0.4 collective-permute-start.11
  37.2 0.4 collective-permute-start.21
  37.6 0.0 copy-start
  37.6 0.0 copy-start.2
  37.6 1.8 %collective-permute-start.20 = (bf16[32,2304]{1,0:T(8,128)(2,1)S(1)}, bf16[32,2304]{1,0:T(8,128)(2,1)}, u32[]{:S(2)}, u32[]{:S(2)}) collective-permute-start(bf16[32,2304]{1,0:T(8,128)(2,1)S(1)} %slice.14), channel_id=1, source_target_pairs={{0,8},{8,16},{16,24},{24,28},{28,20},{20,12},{12,4},{4,0},{1,9},{9... | collective-permute-start | bytes 442376 | tf_op jit(solution)/shard_map/ppermute | solution.py:61
  39.4 0.0 collective-permute-done.14.refs_1_
  39.4 0.0 collective-permute-start.16
  39.4 2.5 %collective-permute-done.10.refs_2_ = bf16[64,2304]{1,0:T(8,128)(2,1)S(1)} collective-permute-done((bf16[64,2304]{1,0:T(8,128)(2,1)S(1)}, bf16[64,2304]{1,0:T(8,128)(2,1)S(1)}, u32[]{:S(2)}, u32[]{:S(2)}) %collective-permute-start.10) | collective-permute-done | bytes 294944 | tf_op jit(solution)/shard_map/ppermute | solution.py:61
  41.9 0.0 collective-permute-start.15
  41.9 1.6 %collective-permute-done.11.refs_6_ = bf16[64,2304]{1,0:T(8,128)(2,1)S(1)} collective-permute-done((bf16[64,2304]{1,0:T(8,128)(2,1)S(1)}, bf16[64,2304]{1,0:T(8,128)(2,1)S(1)}, u32[]{:S(2)}, u32[]{:S(2)}) %collective-permute-start.11) | collective-permute-done | bytes 294944 | tf_op jit(solution)/shard_map/ppermute | solution.py:61
  43.6 0.0 collective-permute-start.17
  43.6 1.7 %collective-permute-done.21.refs_8_ = bf16[32,2304]{1,0:T(8,128)(2,1)} collective-permute-done((bf16[32,2304]{1,0:T(8,128)(2,1)S(1)}, bf16[32,2304]{1,0:T(8,128)(2,1)}, u32[]{:S(2)}, u32[]{:S(2)}) %collective-permute-start.21) | collective-permute-done | bytes 147488 | tf_op jit(solution)/shard_map/ppermute | solution.py:61
  45.2 2.0 %collective-permute-start.12 = (bf16[64,2304]{1,0:T(8,128)(2,1)S(1)}, bf16[64,2304]{1,0:T(8,128)(2,1)S(1)}, u32[]{:S(2)}, u32[]{:S(2)}) collective-permute-start(bf16[64,2304]{1,0:T(8,128)(2,1)S(1)} %collective-permute-done.10.refs_2_), channel_id=1, source_target_pairs={{0,8},{8,16},{16,24},{24,28},{28,20},{20,12},{12,4},{4,0},{1,9},{9... | collective-permute-start | bytes 884744 | tf_op jit(solution)/shard_map/ppermute | solution.py:61
  47.2 0.0 collective-permute-done.20.refs_4_
  47.2 0.1 collective-permute-start.13
  47.3 2.9 %pick_left.1 = (bf16[64,2304]{1,0:T(8,128)(2,1)}, bf16[64,2304]{1,0:T(8,128)(2,1)}, bf16[64,2304]{1,0:T(8,128)(2,1)}, bf16[64,2304]{1,0:T(8,128)(2,1)}) custom-call(s32[4]{0:T(128)} %owner.5, bf16[64,2304]{1,0:T(8,128)(2,1)} %bitcast.16, bf16[64,2304]{1,0:T(8,128)(2,1)} %copy-done.9, bf16[64,2304]{1,0:T(8,128)(2,1)} %copy-done.11, ...), custom_call_target="tpu_custom_call" | custom-call | bytes 3145728 | tf_op jit(solution)/shard_map/pick_left/pallas_call | solution.py:118
  50.1 0.0 collective-permute-done.16.refs_10_
  50.1 0.0 collective-permute-start.22
  50.2 1.6 %collective-permute-start.23 = (bf16[64,2304]{1,0:T(8,128)(2,1)}, bf16[64,2304]{1,0:T(8,128)(2,1)S(1)}, u32[]{:S(2)}, u32[]{:S(2)}) collective-permute-start(bf16[64,2304]{1,0:T(8,128)(2,1)} %get-tuple-element.55), channel_id=1, source_target_pairs={{0,2},{1,3},{2,0},{3,1},{4,6},{5,7},{6,4},{7,5},{8,10},{9,11},{10,... | collective-permute-start | bytes 884744 | tf_op jit(solution)/shard_map/ppermute | solution.py:82
  51.8 0.0 collective-permute-done.17.refs_12_
  51.8 0.3 collective-permute-start.24
  52.1 0.9 collective-permute-done.12.refs_3_
  53.0 1.7 %collective-permute-done.13.refs_5_ = bf16[64,2304]{1,0:T(8,128)(2,1)S(1)} collective-permute-done((bf16[64,2304]{1,0:T(8,128)(2,1)S(1)}, bf16[64,2304]{1,0:T(8,128)(2,1)S(1)}, u32[]{:S(2)}, u32[]{:S(2)}) %collective-permute-start.13) | collective-permute-done | bytes 294944 | tf_op jit(solution)/shard_map/ppermute | solution.py:61
  54.7 0.3 collective-permute-start.19
  55.0 1.7 %collective-permute-start.18 = (bf16[32,2304]{1,0:T(8,128)(2,1)S(1)}, bf16[32,2304]{1,0:T(8,128)(2,1)S(1)}, u32[]{:S(2)}, u32[]{:S(2)}) collective-permute-start(bf16[32,2304]{1,0:T(8,128)(2,1)S(1)} %slice.12), channel_id=1, source_target_pairs={{0,8},{8,16},{16,24},{24,28},{28,20},{20,12},{12,4},{4,0},{1,9},{9... | collective-permute-start | bytes 442376 | tf_op jit(solution)/shard_map/ppermute | solution.py:61
  58.1 0.0 copy-start.1
  58.1 0.0 copy-start.3
  58.1 0.0 copy-start.4
  58.1 1.8 %collective-permute-done.19.refs_8_ = bf16[32,2304]{1,0:T(8,128)(2,1)S(1)} collective-permute-done((bf16[32,2304]{1,0:T(8,128)(2,1)S(1)}, bf16[32,2304]{1,0:T(8,128)(2,1)S(1)}, u32[]{:S(2)}, u32[]{:S(2)}) %collective-permute-start.19) | collective-permute-done | bytes 147488 | tf_op jit(solution)/shard_map/ppermute | solution.py:61
  59.9 0.3 collective-permute-done.18.refs_4_
  60.2 1.3 coupling.1
  61.5 0.1 collective-permute-start.25
  61.6 1.6 %collective-permute-start.26 = (bf16[64,256]{1,0:T(8,128)(2,1)S(1)}, bf16[64,256]{1,0:T(8,128)(2,1)S(1)}, u32[]{:S(2)}, u32[]{:S(2)}) collective-permute-start(bf16[64,256]{1,0:T(8,128)(2,1)S(1)} %get-tuple-element.58), channel_id=1, source_target_pairs={{0,2},{1,3},{2,0},{3,1},{4,6},{5,7},{6,4},{7,5},{8,10},{9,11},{10,... | collective-permute-start | bytes 98312 | tf_op jit(solution)/shard_map/ppermute | solution.py:82
  63.2 0.0 collective-permute-done.22.refs_5_
  63.2 0.3 collective-permute-start.27
  63.5 0.0 copy-start.6
  63.5 3.1 %grams.1 = (bf16[512,512]{1,0:T(8,128)(2,1)S(1)}, bf16[512,512]{1,0:T(8,128)(2,1)S(1)}, f32[256,256]{1,0:T(8,128)S(1)}) custom-call(bf16[2304,256]{1,0:T(8,128)(2,1)S(1)} %bitcast.19, bf16[2304,256]{1,0:T(8,128)(2,1)S(1)} %bitcast.21, bf16[64,2304]{1,0:T(8,128)(2,1)S(1)} %bitcast.17, bf16[64,2304]{1,0:T(8,128)(2,1)S(1)} %collective-permute-done.14.refs_1_, ...), custom_call_target="tpu_custom_call" | custom-call | flops 1207959552 | bytes 6291456 | tf_op jit(solution)/shard_map/grams/pallas_call | solution.py:184
  66.6 0.0 collective-permute-done.23.refs_6_
  66.7 0.0 collective-permute-done.25.refs_9_
  66.7 0.5 collective-permute-done.26.refs_10_
  67.2 0.0 collective-permute-done.27.refs_11_
  67.2 72.0 %finish.1 = (bf16[2304,256]{1,0:T(8,128)(2,1)}, bf16[2304,256]{1,0:T(8,128)(2,1)}) custom-call(s32[1,1]{1,0:T(1,128)S(6)} %copy.10.old_ref, s32[1,1]{1,0:T(1,128)S(6)} %copy.11.goal_ref, s32[8]{0:T(128)S(1)} %copy-done.6, s32[4]{0:T(128)S(1)} %copy-done.2, bf16[2304,256]{1,0:T(8,128)(2,1)S(1)} %bitcast.20, bf16[2304,256]{1,0:T(8,128)(2,1)S(1)} %bitcast.22, ...), custom_call_target="tpu_custom_call" | custom-call | flops 8589934592 | bytes 12582912 | tf_op jit(solution)/shard_map/finish/pallas_call | solution.py:361
  (26 shorter events, 0.1 us)
Async XLA Ops:
  0.6 10.2 %collective-permute-start.1 = (bf16[64,2304]{1,0:T(8,128)(2,1)}, bf16[64,2304]{1,0:T(8,128)(2,1)S(1)}, u32[]{:S(2)}, u32[]{:S(2)}) collective-permute-start(bf16[64,2304]{1,0:T(8,128)(2,1)} %bitcast.12), channel_id=1, source_target_pairs={{0,8},{8,16},{16,24},{24,28},{28,20},{20,12},{12,4},{4,0},{1,9},{9... | collective-permute-start | bytes 884744 | tf_op jit(solution)/shard_map/ppermute | solution.py:61
  3.7 8.7 %collective-permute-start.2 = (bf16[64,2304]{1,0:T(8,128)(2,1)}, bf16[64,2304]{1,0:T(8,128)(2,1)S(1)}, u32[]{:S(2)}, u32[]{:S(2)}) collective-permute-start(bf16[64,2304]{1,0:T(8,128)(2,1)} %bitcast.13), channel_id=1, source_target_pairs={{8,0},{16,8},{24,16},{28,24},{20,28},{12,20},{4,12},{0,4},{9,1},{1... | collective-permute-start | bytes 884744 | tf_op jit(solution)/shard_map/ppermute | solution.py:61
  3.7 8.7 %collective-permute-start.3 = (bf16[64,2304]{1,0:T(8,128)(2,1)}, bf16[64,2304]{1,0:T(8,128)(2,1)S(1)}, u32[]{:S(2)}, u32[]{:S(2)}) collective-permute-start(bf16[64,2304]{1,0:T(8,128)(2,1)} %bitcast.14), channel_id=1, source_target_pairs={{0,2},{1,3},{2,0},{3,1},{4,6},{5,7},{6,4},{7,5},{8,10},{9,11},{10,... | collective-permute-start | bytes 884744 | tf_op jit(solution)/shard_map/ppermute | solution.py:82
  10.9 12.4 %copy-start.9 = (bf16[64,2304]{1,0:T(8,128)(2,1)}, bf16[64,2304]{1,0:T(8,128)(2,1)S(1)}, u32[]{:S(2)}) copy-start(bf16[64,2304]{1,0:T(8,128)(2,1)S(1)} %collective-permute-done.1.refs_1_) | copy-start | bytes 884740
  12.4 10.9 %copy-start.10 = (bf16[64,2304]{1,0:T(8,128)(2,1)}, bf16[64,2304]{1,0:T(8,128)(2,1)S(1)}, u32[]{:S(2)}) copy-start(bf16[64,2304]{1,0:T(8,128)(2,1)S(1)} %collective-permute-done.2.refs_7_) | copy-start | bytes 884740
  12.4 7.6 %collective-permute-start.4 = (bf16[64,2304]{1,0:T(8,128)(2,1)S(1)}, bf16[64,2304]{1,0:T(8,128)(2,1)S(1)}, u32[]{:S(2)}, u32[]{:S(2)}) collective-permute-start(bf16[64,2304]{1,0:T(8,128)(2,1)S(1)} %collective-permute-done.1.refs_1_), channel_id=1, source_target_pairs={{0,8},{8,16},{16,24},{24,28},{28,20},{20,12},{12,4},{4,0},{1,9},{9... | collective-permute-start | bytes 884744 | tf_op jit(solution)/shard_map/ppermute | solution.py:61
  14.1 7.1 %collective-permute-start.5 = (bf16[64,2304]{1,0:T(8,128)(2,1)S(1)}, bf16[64,2304]{1,0:T(8,128)(2,1)S(1)}, u32[]{:S(2)}, u32[]{:S(2)}) collective-permute-start(bf16[64,2304]{1,0:T(8,128)(2,1)S(1)} %collective-permute-done.2.refs_7_), channel_id=1, source_target_pairs={{8,0},{16,8},{24,16},{28,24},{20,28},{12,20},{4,12},{0,4},{9,1},{1... | collective-permute-start | bytes 884744 | tf_op jit(solution)/shard_map/ppermute | solution.py:61
  14.4 8.9 %collective-permute-start = (bf16[64,2304]{1,0:T(8,128)(2,1)}, bf16[64,2304]{1,0:T(8,128)(2,1)S(1)}, u32[]{:S(2)}, u32[]{:S(2)}) collective-permute-start(bf16[64,2304]{1,0:T(8,128)(2,1)} %bitcast.6), channel_id=1, source_target_pairs={{0,2},{1,3},{2,0},{3,1},{4,6},{5,7},{6,4},{7,5},{8,10},{9,11},{10,... | collective-permute-start | bytes 884744 | tf_op jit(solution)/shard_map/ppermute | solution.py:82
  20.0 13.8 %copy-start.11 = (bf16[64,2304]{1,0:T(8,128)(2,1)}, bf16[64,2304]{1,0:T(8,128)(2,1)S(1)}, u32[]{:S(2)}) copy-start(bf16[64,2304]{1,0:T(8,128)(2,1)S(1)} %collective-permute-done.4.refs_2_) | copy-start | bytes 884740
  21.2 13.9 %copy-start.12 = (bf16[64,2304]{1,0:T(8,128)(2,1)}, bf16[64,2304]{1,0:T(8,128)(2,1)S(1)}, u32[]{:S(2)}) copy-start(bf16[64,2304]{1,0:T(8,128)(2,1)S(1)} %collective-permute-done.5.refs_6_) | copy-start | bytes 884740
  21.2 9.4 %collective-permute-start.8 = (bf16[64,2304]{1,0:T(8,128)(2,1)S(1)}, bf16[64,2304]{1,0:T(8,128)(2,1)S(1)}, u32[]{:S(2)}, u32[]{:S(2)}) collective-permute-start(bf16[64,2304]{1,0:T(8,128)(2,1)S(1)} %collective-permute-done.4.refs_2_), channel_id=1, source_target_pairs={{0,8},{8,16},{16,24},{24,28},{28,20},{20,12},{12,4},{4,0},{1,9},{9... | collective-permute-start | bytes 884744 | tf_op jit(solution)/shard_map/ppermute | solution.py:61
  22.8 9.1 %collective-permute-start.9 = (bf16[64,2304]{1,0:T(8,128)(2,1)S(1)}, bf16[64,2304]{1,0:T(8,128)(2,1)S(1)}, u32[]{:S(2)}, u32[]{:S(2)}) collective-permute-start(bf16[64,2304]{1,0:T(8,128)(2,1)S(1)} %collective-permute-done.5.refs_6_), channel_id=1, source_target_pairs={{8,0},{16,8},{24,16},{28,24},{20,28},{12,20},{4,12},{0,4},{9,1},{1... | collective-permute-start | bytes 884744 | tf_op jit(solution)/shard_map/ppermute | solution.py:61
  23.3 10.5 %collective-permute-start.6 = (bf16[64,2304]{1,0:T(8,128)(2,1)}, bf16[64,2304]{1,0:T(8,128)(2,1)S(1)}, u32[]{:S(2)}, u32[]{:S(2)}) collective-permute-start(bf16[64,2304]{1,0:T(8,128)(2,1)} %bitcast.7), channel_id=1, source_target_pairs={{0,8},{8,16},{16,24},{24,28},{28,20},{20,12},{12,4},{4,0},{1,9},{9... | collective-permute-start | bytes 884744 | tf_op jit(solution)/shard_map/ppermute | solution.py:61
  24.9 10.3 %collective-permute-start.7 = (bf16[64,2304]{1,0:T(8,128)(2,1)}, bf16[64,2304]{1,0:T(8,128)(2,1)S(1)}, u32[]{:S(2)}, u32[]{:S(2)}) collective-permute-start(bf16[64,2304]{1,0:T(8,128)(2,1)} %bitcast.8), channel_id=1, source_target_pairs={{8,0},{16,8},{24,16},{28,24},{20,28},{12,20},{4,12},{0,4},{9,1},{1... | collective-permute-start | bytes 884744 | tf_op jit(solution)/shard_map/ppermute | solution.py:61
  25.4 14.0 %collective-permute-start.14 = (bf16[64,2304]{1,0:T(8,128)(2,1)}, bf16[64,2304]{1,0:T(8,128)(2,1)S(1)}, u32[]{:S(2)}, u32[]{:S(2)}) collective-permute-start(bf16[64,2304]{1,0:T(8,128)(2,1)} %bitcast.15), channel_id=1, source_target_pairs={{0,1},{1,0},{2,3},{3,2},{4,5},{5,4},{6,7},{7,6},{8,9},{9,8},{10,11... | collective-permute-start | bytes 884744 | tf_op jit(solution)/shard_map/ppermute | solution.py:82
  30.6 8.8 %copy-start.7 = (bf16[64,2304]{1,0:T(8,128)(2,1)}, bf16[64,2304]{1,0:T(8,128)(2,1)S(1)}, u32[]{:S(2)}) copy-start(bf16[64,2304]{1,0:T(8,128)(2,1)S(1)} %collective-permute-done.8.refs_3_) | copy-start | bytes 884740
  31.9 10.0 %copy-start.8 = (bf16[64,2304]{1,0:T(8,128)(2,1)}, bf16[64,2304]{1,0:T(8,128)(2,1)S(1)}, u32[]{:S(2)}) copy-start(bf16[64,2304]{1,0:T(8,128)(2,1)S(1)} %collective-permute-done.9.refs_5_) | copy-start | bytes 884740
  35.2 6.7 %collective-permute-start.10 = (bf16[64,2304]{1,0:T(8,128)(2,1)S(1)}, bf16[64,2304]{1,0:T(8,128)(2,1)S(1)}, u32[]{:S(2)}, u32[]{:S(2)}) collective-permute-start(bf16[64,2304]{1,0:T(8,128)(2,1)S(1)} %collective-permute-done.6.refs_1_), channel_id=1, source_target_pairs={{0,8},{8,16},{16,24},{24,28},{28,20},{20,12},{12,4},{4,0},{1,9},{9... | collective-permute-start | bytes 884744 | tf_op jit(solution)/shard_map/ppermute | solution.py:61
  36.8 6.7 %collective-permute-start.11 = (bf16[64,2304]{1,0:T(8,128)(2,1)S(1)}, bf16[64,2304]{1,0:T(8,128)(2,1)S(1)}, u32[]{:S(2)}, u32[]{:S(2)}) collective-permute-start(bf16[64,2304]{1,0:T(8,128)(2,1)S(1)} %collective-permute-done.7.refs_7_), channel_id=1, source_target_pairs={{8,0},{16,8},{24,16},{28,24},{20,28},{12,20},{4,12},{0,4},{9,1},{1... | collective-permute-start | bytes 884744 | tf_op jit(solution)/shard_map/ppermute | solution.py:61
  37.2 8.0 %collective-permute-start.21 = (bf16[32,2304]{1,0:T(8,128)(2,1)S(1)}, bf16[32,2304]{1,0:T(8,128)(2,1)}, u32[]{:S(2)}, u32[]{:S(2)}) collective-permute-start(bf16[32,2304]{1,0:T(8,128)(2,1)S(1)} %slice.15), channel_id=1, source_target_pairs={{8,0},{16,8},{24,16},{28,24},{20,28},{12,20},{4,12},{0,4},{9,1},{1... | collective-permute-start | bytes 442376 | tf_op jit(solution)/shard_map/ppermute | solution.py:61
  37.6 22.6 %copy-start = (bf16[1,64,2304]{2,1,0:T(8,128)(2,1)S(1)}, bf16[1,64,2304]{2,1,0:T(8,128)(2,1)}, u32[]{:S(2)}) copy-start(bf16[1,64,2304]{2,1,0:T(8,128)(2,1)} %param.11) | copy-start | bytes 884740
  37.6 22.6 %copy-start.2 = (s32[4]{0:T(128)S(1)}, s32[4]{0:T(128)}, u32[]{:S(2)}) copy-start(s32[4]{0:T(128)} %owner.5) | copy-start | bytes 52
  37.6 9.6 %collective-permute-start.20 = (bf16[32,2304]{1,0:T(8,128)(2,1)S(1)}, bf16[32,2304]{1,0:T(8,128)(2,1)}, u32[]{:S(2)}, u32[]{:S(2)}) collective-permute-start(bf16[32,2304]{1,0:T(8,128)(2,1)S(1)} %slice.14), channel_id=1, source_target_pairs={{0,8},{8,16},{16,24},{24,28},{28,20},{20,12},{12,4},{4,0},{1,9},{9... | collective-permute-start | bytes 442376 | tf_op jit(solution)/shard_map/ppermute | solution.py:61
  39.4 10.7 %collective-permute-start.16 = (bf16[64,2304]{1,0:T(8,128)(2,1)}, bf16[64,2304]{1,0:T(8,128)(2,1)S(1)}, u32[]{:S(2)}, u32[]{:S(2)}) collective-permute-start(bf16[64,2304]{1,0:T(8,128)(2,1)} %bitcast.9), channel_id=1, source_target_pairs={{0,1},{1,0},{2,3},{3,2},{4,5},{5,4},{6,7},{7,6},{8,9},{9,8},{10,11... | collective-permute-start | bytes 884744 | tf_op jit(solution)/shard_map/ppermute | solution.py:82
  41.9 8.3 %collective-permute-start.15 = (bf16[64,2304]{1,0:T(8,128)(2,1)S(1)}, bf16[64,2304]{1,0:T(8,128)(2,1)}, u32[]{:S(2)}, u32[]{:S(2)}) collective-permute-start(bf16[64,2304]{1,0:T(8,128)(2,1)S(1)} %collective-permute-done.3.refs_2_), channel_id=1, source_target_pairs={{0,1},{1,0},{2,3},{3,2},{4,5},{5,4},{6,7},{7,6},{8,9},{9,8},{10,11... | collective-permute-start | bytes 884744 | tf_op jit(solution)/shard_map/ppermute | solution.py:82
  43.6 8.2 %collective-permute-start.17 = (bf16[64,2304]{1,0:T(8,128)(2,1)S(1)}, bf16[64,2304]{1,0:T(8,128)(2,1)S(1)}, u32[]{:S(2)}, u32[]{:S(2)}) collective-permute-start(bf16[64,2304]{1,0:T(8,128)(2,1)S(1)} %collective-permute-done.refs_11_), channel_id=1, source_target_pairs={{0,1},{1,0},{2,3},{3,2},{4,5},{5,4},{6,7},{7,6},{8,9},{9,8},{10,11... | collective-permute-start | bytes 884744 | tf_op jit(solution)/shard_map/ppermute | solution.py:82
  45.2 7.7 %collective-permute-start.12 = (bf16[64,2304]{1,0:T(8,128)(2,1)S(1)}, bf16[64,2304]{1,0:T(8,128)(2,1)S(1)}, u32[]{:S(2)}, u32[]{:S(2)}) collective-permute-start(bf16[64,2304]{1,0:T(8,128)(2,1)S(1)} %collective-permute-done.10.refs_2_), channel_id=1, source_target_pairs={{0,8},{8,16},{16,24},{24,28},{28,20},{20,12},{12,4},{4,0},{1,9},{9... | collective-permute-start | bytes 884744 | tf_op jit(solution)/shard_map/ppermute | solution.py:61
  47.2 7.5 %collective-permute-start.13 = (bf16[64,2304]{1,0:T(8,128)(2,1)S(1)}, bf16[64,2304]{1,0:T(8,128)(2,1)S(1)}, u32[]{:S(2)}, u32[]{:S(2)}) collective-permute-start(bf16[64,2304]{1,0:T(8,128)(2,1)S(1)} %collective-permute-done.11.refs_6_), channel_id=1, source_target_pairs={{8,0},{16,8},{24,16},{28,24},{20,28},{12,20},{4,12},{0,4},{9,1},{1... | collective-permute-start | bytes 884744 | tf_op jit(solution)/shard_map/ppermute | solution.py:61
  50.1 13.0 %collective-permute-start.22 = (bf16[64,2304]{1,0:T(8,128)(2,1)}, bf16[64,2304]{1,0:T(8,128)(2,1)S(1)}, u32[]{:S(2)}, u32[]{:S(2)}) collective-permute-start(bf16[64,2304]{1,0:T(8,128)(2,1)} %get-tuple-element.54), channel_id=1, source_target_pairs={{0,1},{1,0},{2,3},{3,2},{4,5},{5,4},{6,7},{7,6},{8,9},{9,8},{10,11... | collective-permute-start | bytes 884744 | tf_op jit(solution)/shard_map/ppermute | solution.py:82
  50.2 16.4 %collective-permute-start.23 = (bf16[64,2304]{1,0:T(8,128)(2,1)}, bf16[64,2304]{1,0:T(8,128)(2,1)S(1)}, u32[]{:S(2)}, u32[]{:S(2)}) collective-permute-start(bf16[64,2304]{1,0:T(8,128)(2,1)} %get-tuple-element.55), channel_id=1, source_target_pairs={{0,2},{1,3},{2,0},{3,1},{4,6},{5,7},{6,4},{7,5},{8,10},{9,11},{10,... | collective-permute-start | bytes 884744 | tf_op jit(solution)/shard_map/ppermute | solution.py:82
  51.8 14.9 %collective-permute-start.24 = (bf16[64,2304]{1,0:T(8,128)(2,1)}, bf16[64,2304]{1,0:T(8,128)(2,1)S(1)}, u32[]{:S(2)}, u32[]{:S(2)}) collective-permute-start(bf16[64,2304]{1,0:T(8,128)(2,1)} %get-tuple-element.56), channel_id=1, source_target_pairs={{0,3},{1,2},{2,1},{3,0},{4,7},{5,6},{6,5},{7,4},{8,11},{9,10},{10,... | collective-permute-start | bytes 884744 | tf_op jit(solution)/shard_map/ppermute | solution.py:82
  54.7 5.2 %collective-permute-start.19 = (bf16[32,2304]{1,0:T(8,128)(2,1)S(1)}, bf16[32,2304]{1,0:T(8,128)(2,1)S(1)}, u32[]{:S(2)}, u32[]{:S(2)}) collective-permute-start(bf16[32,2304]{1,0:T(8,128)(2,1)S(1)} %slice.13), channel_id=1, source_target_pairs={{8,0},{16,8},{24,16},{28,24},{20,28},{12,20},{4,12},{0,4},{9,1},{1... | collective-permute-start | bytes 442376 | tf_op jit(solution)/shard_map/ppermute | solution.py:61
  55.0 5.1 %collective-permute-start.18 = (bf16[32,2304]{1,0:T(8,128)(2,1)S(1)}, bf16[32,2304]{1,0:T(8,128)(2,1)S(1)}, u32[]{:S(2)}, u32[]{:S(2)}) collective-permute-start(bf16[32,2304]{1,0:T(8,128)(2,1)S(1)} %slice.12), channel_id=1, source_target_pairs={{0,8},{8,16},{16,24},{24,28},{28,20},{20,12},{12,4},{4,0},{1,9},{9... | collective-permute-start | bytes 442376 | tf_op jit(solution)/shard_map/ppermute | solution.py:61
  58.1 5.4 %copy-start.1 = (bf16[1,64,2304]{2,1,0:T(8,128)(2,1)S(1)}, bf16[1,64,2304]{2,1,0:T(8,128)(2,1)}, u32[]{:S(2)}) copy-start(bf16[1,64,2304]{2,1,0:T(8,128)(2,1)} %param.10) | copy-start | bytes 884740
  58.1 5.4 %copy-start.3 = (bf16[1,1,2304,256]{3,2,1,0:T(8,128)(2,1)S(1)}, bf16[1,1,2304,256]{3,2,1,0:T(8,128)(2,1)}, u32[]{:S(2)}) copy-start(bf16[1,1,2304,256]{3,2,1,0:T(8,128)(2,1)} %param.8) | copy-start | bytes 3538948
  58.1 5.4 %copy-start.4 = (bf16[1,1,2304,256]{3,2,1,0:T(8,128)(2,1)S(1)}, bf16[1,1,2304,256]{3,2,1,0:T(8,128)(2,1)}, u32[]{:S(2)}) copy-start(bf16[1,1,2304,256]{3,2,1,0:T(8,128)(2,1)} %param.9) | copy-start | bytes 3538948
  61.5 5.1 %collective-permute-start.25 = (bf16[64,256]{1,0:T(8,128)(2,1)S(1)}, bf16[64,256]{1,0:T(8,128)(2,1)S(1)}, u32[]{:S(2)}, u32[]{:S(2)}) collective-permute-start(bf16[64,256]{1,0:T(8,128)(2,1)S(1)} %get-tuple-element.57), channel_id=1, source_target_pairs={{0,1},{1,0},{2,3},{3,2},{4,5},{5,4},{6,7},{7,6},{8,9},{9,8},{10,11... | collective-permute-start | bytes 98312 | tf_op jit(solution)/shard_map/ppermute | solution.py:82
  61.6 5.6 %collective-permute-start.26 = (bf16[64,256]{1,0:T(8,128)(2,1)S(1)}, bf16[64,256]{1,0:T(8,128)(2,1)S(1)}, u32[]{:S(2)}, u32[]{:S(2)}) collective-permute-start(bf16[64,256]{1,0:T(8,128)(2,1)S(1)} %get-tuple-element.58), channel_id=1, source_target_pairs={{0,2},{1,3},{2,0},{3,1},{4,6},{5,7},{6,4},{7,5},{8,10},{9,11},{10,... | collective-permute-start | bytes 98312 | tf_op jit(solution)/shard_map/ppermute | solution.py:82
  63.2 4.0 %collective-permute-start.27 = (bf16[64,256]{1,0:T(8,128)(2,1)S(1)}, bf16[64,256]{1,0:T(8,128)(2,1)S(1)}, u32[]{:S(2)}, u32[]{:S(2)}) collective-permute-start(bf16[64,256]{1,0:T(8,128)(2,1)S(1)} %get-tuple-element.59), channel_id=1, source_target_pairs={{0,3},{1,2},{2,1},{3,0},{4,7},{5,6},{6,5},{7,4},{8,11},{9,10},{10,... | collective-permute-start | bytes 98312 | tf_op jit(solution)/shard_map/ppermute | solution.py:82
  63.5 3.7 %copy-start.5 = (bf16[64,2304]{1,0:T(8,128)(2,1)S(1)}, bf16[64,2304]{1,0:T(8,128)(2,1)}, u32[]{:S(2)}) copy-start(bf16[64,2304]{1,0:T(8,128)(2,1)} %get-tuple-element.53.refs_4_) | copy-start | bytes 884740
  63.5 3.7 %copy-start.6 = (s32[8]{0:T(128)S(1)}, s32[8]{0:T(128)}, u32[]{:S(2)}) copy-start(s32[8]{0:T(128)} %panel.1) | copy-start | bytes 100

commit v6 on v5

--- a/solution.py
+++ b/solution.py
@@ -82,11 +82,11 @@
     return lax.ppermute(x, axis, [(i, i ^ m) for i in range(n)])
 
 
-def part_copies(parts, target, sem):
+def assemble(parts, target):
     shard = target.shape[0] // len(parts)
     col = lax.axis_index("col")
-    spots = [pl.ds(pl.multiple_of((col ^ m) * shard, shard), shard) for m in range(len(parts))]
-    return [pltpu.make_async_copy(part, target.at[spots[m]], sem.at[m]) for m, part in enumerate(parts)]
+    for m, part in enumerate(parts):
+        target[pl.ds(pl.multiple_of((col ^ m) * shard, shard), shard), :] = part[...]
 
 
 def owner_steps(n_row, n_col, owner):
@@ -120,6 +120,7 @@
         out_shape=[jax.ShapeDtypeStruct((shard, width), BF16)] * n_col,
         in_specs=[SMEM] + [VMEM] * (n_row + 1),
         out_specs=[VMEM] * n_col,
+        compiler_params=pltpu.CompilerParams(vmem_limit_bytes=8 << 20),
         cost_estimate=pl.CostEstimate(flops=0, bytes_accessed=3 << 20, transcendentals=0),
         name="pick_left",
     )(owner, *pieces)
@@ -148,30 +149,23 @@
         in_specs=[SMEM] + [VMEM] * (n_row + 1 + n_col),
         out_specs=[VMEM] * n_col,
         scratch_shapes=[pltpu.VMEM((rank, width), BF16), pltpu.VMEM((rank, width), BF16)],
-        compiler_params=pltpu.CompilerParams(vmem_limit_bytes=32 << 20),
+        compiler_params=pltpu.CompilerParams(vmem_limit_bytes=12 << 20),
         cost_estimate=pl.CostEstimate(flops=2 * rank * rank * width, bytes_accessed=3 << 20, transcendentals=0),
         name="coupling",
     )(owner, *pieces, *parts)
 
 
-def grams(n_col, u_hbm, v_hbm, *refs):
-    high, low, cu_ref, u_ref, v_ref, uit, sem, part_sem = refs[n_col:]
+def grams(n_col, u_ref, v_ref, *refs):
+    high, low, cu_ref, uit = refs[n_col:]
     rank = cu_ref.shape[0]
-    loads = [pltpu.make_async_copy(v_hbm, v_ref, sem.at[0]), pltpu.make_async_copy(u_hbm, u_ref, sem.at[1])]
-    parts = part_copies(refs[:n_col], uit, part_sem)
-    for copy in [*loads, *parts]:
-        copy.start()
+    assemble(refs[:n_col], uit)
     top, bottom = pl.ds(0, rank), pl.ds(rank, rank)
 
     def put(at, lanes, value):
         high[at, lanes], low[at, lanes] = halves(value)
 
-    loads[0].wait()
     cu_ref[...] = tn(v_ref[...], v_ref[...])
-    loads[1].wait()
     put(top, top, tn(u_ref[...], u_ref[...]))
-    for copy in parts:
-        copy.wait()
     cross = nn(uit[...], u_ref[...])
     put(bottom, top, cross)
     put(top, bottom, cross.T)
@@ -180,20 +174,13 @@
 
 def gram_products(u, v, parts):
     rows, rank = u.shape
-    tall = pltpu.VMEM((rows, rank), BF16)
     return pl.pallas_call(
         functools.partial(grams, len(parts)),
         out_shape=[jax.ShapeDtypeStruct((2 * rank, 2 * rank), BF16)] * 2 + [jax.ShapeDtypeStruct((rank, rank), F32)],
-        in_specs=[HBM] * (2 + len(parts)),
+        in_specs=[VMEM] * (2 + len(parts)),
         out_specs=[VMEM] * 3,
-        scratch_shapes=[
-            tall,
-            tall,
-            pltpu.VMEM((rank, rows), BF16),
-            pltpu.SemaphoreType.DMA((2,)),
-            pltpu.SemaphoreType.DMA((len(parts),)),
-        ],
-        compiler_params=pltpu.CompilerParams(vmem_limit_bytes=40 << 20),
+        scratch_shapes=[pltpu.VMEM((rank, rows), BF16)],
+        compiler_params=pltpu.CompilerParams(vmem_limit_bytes=24 << 20),
         cost_estimate=pl.CostEstimate(flops=8 * rank * rank * rows, bytes_accessed=6 << 20, transcendentals=0),
         name="grams",
     )(u, v, *parts)
@@ -203,40 +190,21 @@
     return jnp.where(below, e, jnp.where(eye, 0.5 * e, 0.0))
 
 
-def finish(n_col, old_ref, goal_ref, panel, owner, u_hbm, v_hbm, hh_hbm, hl_hbm, cu_hbm, *refs):
-    ui_hbm, ujt_hbm, kt_in = refs[:n_col], refs[n_col : 2 * n_col], refs[2 * n_col : 3 * n_col]
-    (q_hbm, w_hbm, u_ref, v_ref, uit_ref, hh, hl, cu_ref, ujt, q_ref, w_ref, kt, mh, gn, y_ref, a_ref) = refs[
-        3 * n_col : -5
-    ]
-    in_sem, ui_sem, uj_sem, q_sem, w_sem = refs[-5:]
+def finish(n_col, old_ref, goal_ref, panel, owner, u_ref, v_ref, hh, hl, cu_ref, *refs):
+    ui_in, ujt_in, kt_in = refs[:n_col], refs[n_col : 2 * n_col], refs[2 * n_col : 3 * n_col]
+    q_hbm, w_hbm, uit_ref, ujt, q_ref, w_ref, kt, mh, gn, y_ref, a_ref, q_sem, w_sem = refs[3 * n_col :]
     rows, rank = u_ref.shape
-    shard = rank // n_col
     row, col = lax.axis_index("row"), lax.axis_index("col")
-    spots = [pl.ds(pl.multiple_of((col ^ m) * shard, shard), shard) for m in range(n_col)]
-    loads = [
-        pltpu.make_async_copy(src, dst, in_sem.at[t])
-        for t, (src, dst) in enumerate(
-            [(v_hbm, v_ref), (hh_hbm, hh), (hl_hbm, hl), (cu_hbm, cu_ref), (u_hbm, u_ref)]
-        )
-    ]
-    ui_loads = part_copies(ui_hbm, uit_ref, ui_sem)
-    uj_loads = [pltpu.make_async_copy(ujt_hbm[m], ujt.at[spots[m]], uj_sem.at[m]) for m in range(n_col)]
-    for copy in [*uj_loads, *loads, *ui_loads]:
-        copy.start()
     old, goal, here, there = old_ref[0, 0], goal_ref[0, 0], panel[row], panel[owner[col]]
     sub = lax.broadcasted_iota(jnp.int32, (rank, rank), 0)
     lane = lax.broadcasted_iota(jnp.int32, (rank, rank), 1)
     eye, below = sub == lane, sub > lane
     one = jnp.where(eye, 1.0, 0.0).astype(F32)
-    for m in range(n_col):
-        kt[spots[m], :] = kt_in[m][...]
+    assemble(kt_in, kt)
+    assemble(ujt_in, ujt)
     zero = jnp.zeros((rank, rank), F32)
     kt[...] = jnp.where((sub < there) & (lane < here), kt[...].astype(F32), zero).astype(BF16)
-    for copy in [*uj_loads, *loads[:1]]:
-        copy.wait()
     cl = jnp.where(lane < goal, nn(ujt[...], v_ref[...]), zero).astype(BF16)
-    for copy in loads[1:4]:
-        copy.wait()
     cu = jnp.where((sub < old) & (lane < goal), cu_ref[...], zero).astype(BF16)
     m_high, m_low = halves(-tn(kt[...], cl))
     mh[pl.ds(0, rank), :], mh[pl.ds(rank, rank), :] = cu, m_high
@@ -306,8 +274,7 @@
     r_up = jnp.where(sub < old, r[:rank], 0.0).astype(BF16)
     w_high, w_low = halves(r[rank:])
     r_low = (-(nn(kt[...], w_high) + nn(kt[...], w_low))).astype(BF16)
-    for copy in [*loads[4:], *ui_loads]:
-        copy.wait()
+    assemble(ui_in, uit_ref)
     step = rows // q_sem.shape[0]
     stores = []
     for t in range(rows // step):
@@ -361,15 +328,10 @@
     fresh_basis, fresh_coeffs = pl.pallas_call(
         functools.partial(finish, n_col),
         out_shape=(out, out),
-        in_specs=[SMEM] * 4 + [HBM] * (5 + 2 * n_col) + [VMEM] * n_col,
+        in_specs=[SMEM] * 4 + [VMEM] * (5 + 3 * n_col),
         out_specs=(HBM, HBM),
         scratch_shapes=[
-            tall,
-            tall,
             wide,
-            pltpu.VMEM((2 * rank, 2 * rank), BF16),
-            pltpu.VMEM((2 * rank, 2 * rank), BF16),
-            square,
             wide,
             tall,
             tall,
@@ -378,13 +340,10 @@
             square,
             square,
             square,
-            pltpu.SemaphoreType.DMA((5,)),
-            pltpu.SemaphoreType.DMA((n_col,)),
-            pltpu.SemaphoreType.DMA((n_col,)),
             pltpu.SemaphoreType.DMA((tiles,)),
             pltpu.SemaphoreType.DMA((tiles,)),
         ],
-        compiler_params=pltpu.CompilerParams(vmem_limit_bytes=40 << 20),
+        compiler_params=pltpu.CompilerParams(vmem_limit_bytes=24 << 20),
         cost_estimate=pl.CostEstimate(flops=8 << 30, bytes_accessed=12 << 20, transcendentals=0),
         name="finish",
     )(tile_rank, target_rank, panel_rank, owner_row, u, v, h_high, h_low, core_up, *ui_parts, *ujs, *kts)

time: 139 us -> 137 us (0.986)
  Pallas kernels: 79.4 us -> 74.4 us
  local copies, waits for them, and re-layouts: 0.11 us -> 1.69 us
  waiting for transfers between devices: 32.8 us -> 34.3 us
    pallas_call x1, Pallas kernels: 2.87 us -> 0.8 us  [picked_left(): pl.pallas_call(functools.partial(pick_left, n_row, n_col), out_shape=[jax...]
    pallas_call x1, Pallas kernels: 3.13 us -> 1.52 us  [gram_products(): pl.pallas_call(functools.partial(grams, len(parts)), out_shape=[jax.Shape...]
    unnamed x26 -> x16, local copies, waits for them, and re-layouts: 0.06 us -> 1.65 us
  transfers between devices with their start and end apart: 28 -> 28, of which waited for: 16 -> 17; matrix products, arithmetic and copies ran while one was open for 0% -> 0% of each run, Pallas kernels for 5% -> 3%
where the time goes in v6:
time: 137 us
  Pallas kernels  74.4 us (54%)
  waiting for transfers between devices  34.3 us (25%)
  starting transfers between devices  24.9 us (18%)
  between operations  2.1 us (2%)
  local copies, waits for them, and re-layouts  1.69 us (1%)
    pallas_call x1, Pallas kernels, body(): pl.pallas_call(functools.partial(finish, n_col), out_shape=(out, out), in...  70.7 us
    ppermute x16, waiting for transfers between devices, step(): fwd, bwd = (lax.ppermute(fwd, axis, ahead), lax.ppermute(bwd, axis, back))  32.8 us
    ppermute x16, starting transfers between devices, step(): fwd, bwd = (lax.ppermute(fwd, axis, ahead), lax.ppermute(bwd, axis, back))  17.4 us
    ppermute x12, starting transfers between devices, swap(): return lax.ppermute(x, axis, [(i, i ^ m) for i in range(n)])  7.45 us
  transfers between devices with their start and end apart: 28, of which 17 were waited for; matrix products, arithmetic and copies ran while one was open for 0% of the time, Pallas kernels for 3%

profile of v6, /device:TPU:0, one launch (start us, length us, event | category | flops | bytes accessed | tf_op | source)
XLA Modules:
  0.0 137.3 jit_solution(2835020383086806398)
XLA Ops:
  0.6 3.1 %collective-permute-start.1 = (bf16[64,2304]{1,0:T(8,128)(2,1)}, bf16[64,2304]{1,0:T(8,128)(2,1)S(1)}, u32[]{:S(2)}, u32[]{:S(2)}) collective-permute-start(bf16[64,2304]{1,0:T(8,128)(2,1)} %bitcast.12), channel_id=1, source_target_pairs={{0,8},{8,16},{16,24},{24,28},{28,20},{20,12},{12,4},{4,0},{1,9},{9... | collective-permute-start | bytes 884744 | tf_op jit(solution)/shard_map/ppermute | solution.py:61
  3.7 0.0 collective-permute-start.2
  3.7 1.9 %collective-permute-start.3 = (bf16[64,2304]{1,0:T(8,128)(2,1)}, bf16[64,2304]{1,0:T(8,128)(2,1)S(1)}, u32[]{:S(2)}, u32[]{:S(2)}) collective-permute-start(bf16[64,2304]{1,0:T(8,128)(2,1)} %bitcast.14), channel_id=1, source_target_pairs={{0,2},{1,3},{2,0},{3,1},{4,6},{5,7},{6,4},{7,5},{8,10},{9,11},{10,... | collective-permute-start | bytes 884744 | tf_op jit(solution)/shard_map/ppermute | solution.py:82
  5.6 5.2 %collective-permute-done.1.refs_1_ = bf16[64,2304]{1,0:T(8,128)(2,1)S(1)} collective-permute-done((bf16[64,2304]{1,0:T(8,128)(2,1)}, bf16[64,2304]{1,0:T(8,128)(2,1)S(1)}, u32[]{:S(2)}, u32[]{:S(2)}) %collective-permute-start.1) | collective-permute-done | bytes 294944 | tf_op jit(solution)/shard_map/ppermute | solution.py:61
  10.9 1.5 %collective-permute-done.2.refs_7_ = bf16[64,2304]{1,0:T(8,128)(2,1)S(1)} collective-permute-done((bf16[64,2304]{1,0:T(8,128)(2,1)}, bf16[64,2304]{1,0:T(8,128)(2,1)S(1)}, u32[]{:S(2)}, u32[]{:S(2)}) %collective-permute-start.2) | collective-permute-done | bytes 294944 | tf_op jit(solution)/shard_map/ppermute | solution.py:61
  12.4 0.0 collective-permute-done.3.refs_2_
  12.4 1.7 %collective-permute-start.4 = (bf16[64,2304]{1,0:T(8,128)(2,1)S(1)}, bf16[64,2304]{1,0:T(8,128)(2,1)S(1)}, u32[]{:S(2)}, u32[]{:S(2)}) collective-permute-start(bf16[64,2304]{1,0:T(8,128)(2,1)S(1)} %collective-permute-done.1.refs_1_), channel_id=1, source_target_pairs={{0,8},{8,16},{16,24},{24,28},{28,20},{20,12},{12,4},{4,0},{1,9},{9... | collective-permute-start | bytes 884744 | tf_op jit(solution)/shard_map/ppermute | solution.py:61
  14.1 0.3 collective-permute-start.5
  14.4 1.6 %collective-permute-start = (bf16[64,2304]{1,0:T(8,128)(2,1)}, bf16[64,2304]{1,0:T(8,128)(2,1)S(1)}, u32[]{:S(2)}, u32[]{:S(2)}) collective-permute-start(bf16[64,2304]{1,0:T(8,128)(2,1)} %bitcast.6), channel_id=1, source_target_pairs={{0,2},{1,3},{2,0},{3,1},{4,6},{5,7},{6,4},{7,5},{8,10},{9,11},{10,... | collective-permute-start | bytes 884744 | tf_op jit(solution)/shard_map/ppermute | solution.py:82
  16.1 3.9 %collective-permute-done.4.refs_2_ = bf16[64,2304]{1,0:T(8,128)(2,1)S(1)} collective-permute-done((bf16[64,2304]{1,0:T(8,128)(2,1)S(1)}, bf16[64,2304]{1,0:T(8,128)(2,1)S(1)}, u32[]{:S(2)}, u32[]{:S(2)}) %collective-permute-start.4) | collective-permute-done | bytes 294944 | tf_op jit(solution)/shard_map/ppermute | solution.py:61
  20.0 1.3 collective-permute-done.5.refs_6_
  21.2 1.6 %collective-permute-start.8 = (bf16[64,2304]{1,0:T(8,128)(2,1)S(1)}, bf16[64,2304]{1,0:T(8,128)(2,1)S(1)}, u32[]{:S(2)}, u32[]{:S(2)}) collective-permute-start(bf16[64,2304]{1,0:T(8,128)(2,1)S(1)} %collective-permute-done.4.refs_2_), channel_id=1, source_target_pairs={{0,8},{8,16},{16,24},{24,28},{28,20},{20,12},{12,4},{4,0},{1,9},{9... | collective-permute-start | bytes 884744 | tf_op jit(solution)/shard_map/ppermute | solution.py:61
  22.8 0.4 collective-permute-start.9
  23.3 0.0 collective-permute-done.refs_11_
  23.3 1.6 %collective-permute-start.6 = (bf16[64,2304]{1,0:T(8,128)(2,1)}, bf16[64,2304]{1,0:T(8,128)(2,1)S(1)}, u32[]{:S(2)}, u32[]{:S(2)}) collective-permute-start(bf16[64,2304]{1,0:T(8,128)(2,1)} %bitcast.7), channel_id=1, source_target_pairs={{0,8},{8,16},{16,24},{24,28},{28,20},{20,12},{12,4},{4,0},{1,9},{9... | collective-permute-start | bytes 884744 | tf_op jit(solution)/shard_map/ppermute | solution.py:61
  24.9 0.4 collective-permute-start.7
  25.3 0.0 collective-permute-start.14
  25.3 5.3 %collective-permute-done.8.refs_3_ = bf16[64,2304]{1,0:T(8,128)(2,1)S(1)} collective-permute-done((bf16[64,2304]{1,0:T(8,128)(2,1)S(1)}, bf16[64,2304]{1,0:T(8,128)(2,1)S(1)}, u32[]{:S(2)}, u32[]{:S(2)}) %collective-permute-start.8) | collective-permute-done | bytes 294944 | tf_op jit(solution)/shard_map/ppermute | solution.py:61
  30.6 1.3 collective-permute-done.9.refs_5_
  31.9 1.9 %collective-permute-done.6.refs_1_ = bf16[64,2304]{1,0:T(8,128)(2,1)S(1)} collective-permute-done((bf16[64,2304]{1,0:T(8,128)(2,1)}, bf16[64,2304]{1,0:T(8,128)(2,1)S(1)}, u32[]{:S(2)}, u32[]{:S(2)}) %collective-permute-start.6) | collective-permute-done | bytes 294944 | tf_op jit(solution)/shard_map/ppermute | solution.py:61
  33.8 1.4 %collective-permute-done.7.refs_7_ = bf16[64,2304]{1,0:T(8,128)(2,1)S(1)} collective-permute-done((bf16[64,2304]{1,0:T(8,128)(2,1)}, bf16[64,2304]{1,0:T(8,128)(2,1)S(1)}, u32[]{:S(2)}, u32[]{:S(2)}) %collective-permute-start.7) | collective-permute-done | bytes 294944 | tf_op jit(solution)/shard_map/ppermute | solution.py:61
  35.2 1.6 %collective-permute-start.10 = (bf16[64,2304]{1,0:T(8,128)(2,1)S(1)}, bf16[64,2304]{1,0:T(8,128)(2,1)S(1)}, u32[]{:S(2)}, u32[]{:S(2)}) collective-permute-start(bf16[64,2304]{1,0:T(8,128)(2,1)S(1)} %collective-permute-done.6.refs_1_), channel_id=1, source_target_pairs={{0,8},{8,16},{16,24},{24,28},{28,20},{20,12},{12,4},{4,0},{1,9},{9... | collective-permute-start | bytes 884744 | tf_op jit(solution)/shard_map/ppermute | solution.py:61
  36.8 0.4 collective-permute-start.11
  37.2 0.4 collective-permute-start.21
  37.6 0.0 copy-start
  37.6 1.8 %collective-permute-start.20 = (bf16[32,2304]{1,0:T(8,128)(2,1)S(1)}, bf16[32,2304]{1,0:T(8,128)(2,1)S(1)}, u32[]{:S(2)}, u32[]{:S(2)}) collective-permute-start(bf16[32,2304]{1,0:T(8,128)(2,1)S(1)} %slice.14), channel_id=1, source_target_pairs={{0,8},{8,16},{16,24},{24,28},{28,20},{20,12},{12,4},{4,0},{1,9},{9... | collective-permute-start | bytes 442376 | tf_op jit(solution)/shard_map/ppermute | solution.py:61
  39.4 0.0 collective-permute-done.14.refs_1_
  39.4 0.0 collective-permute-start.16
  39.4 2.5 %collective-permute-done.10.refs_2_ = bf16[64,2304]{1,0:T(8,128)(2,1)S(1)} collective-permute-done((bf16[64,2304]{1,0:T(8,128)(2,1)S(1)}, bf16[64,2304]{1,0:T(8,128)(2,1)S(1)}, u32[]{:S(2)}, u32[]{:S(2)}) %collective-permute-start.10) | collective-permute-done | bytes 294944 | tf_op jit(solution)/shard_map/ppermute | solution.py:61
  41.9 0.0 collective-permute-start.15
  41.9 1.7 %collective-permute-done.11.refs_6_ = bf16[64,2304]{1,0:T(8,128)(2,1)S(1)} collective-permute-done((bf16[64,2304]{1,0:T(8,128)(2,1)S(1)}, bf16[64,2304]{1,0:T(8,128)(2,1)S(1)}, u32[]{:S(2)}, u32[]{:S(2)}) %collective-permute-start.11) | collective-permute-done | bytes 294944 | tf_op jit(solution)/shard_map/ppermute | solution.py:61
  43.6 0.0 collective-permute-start.17
  43.6 1.6 %collective-permute-done.21.refs_8_ = bf16[32,2304]{1,0:T(8,128)(2,1)S(1)} collective-permute-done((bf16[32,2304]{1,0:T(8,128)(2,1)S(1)}, bf16[32,2304]{1,0:T(8,128)(2,1)S(1)}, u32[]{:S(2)}, u32[]{:S(2)}) %collective-permute-start.21) | collective-permute-done | bytes 147488 | tf_op jit(solution)/shard_map/ppermute | solution.py:61
  45.2 2.0 %collective-permute-start.12 = (bf16[64,2304]{1,0:T(8,128)(2,1)S(1)}, bf16[64,2304]{1,0:T(8,128)(2,1)S(1)}, u32[]{:S(2)}, u32[]{:S(2)}) collective-permute-start(bf16[64,2304]{1,0:T(8,128)(2,1)S(1)} %collective-permute-done.10.refs_2_), channel_id=1, source_target_pairs={{0,8},{8,16},{16,24},{24,28},{28,20},{20,12},{12,4},{4,0},{1,9},{9... | collective-permute-start | bytes 884744 | tf_op jit(solution)/shard_map/ppermute | solution.py:61
  47.2 0.0 collective-permute-done.20.refs_4_
  47.2 0.0 collective-permute-start.13
  47.2 1.0 copy-done.1
  48.2 0.7 copy-done.3
  48.8 0.8 pick_left.1
  49.6 0.0 collective-permute-done.16.refs_10_
  49.6 0.1 collective-permute-start.22
  49.7 0.0 collective-permute-done.15.refs_3_
  49.7 1.5 %collective-permute-start.23 = (bf16[64,2304]{1,0:T(8,128)(2,1)S(1)}, bf16[64,2304]{1,0:T(8,128)(2,1)S(1)}, u32[]{:S(2)}, u32[]{:S(2)}) collective-permute-start(bf16[64,2304]{1,0:T(8,128)(2,1)S(1)} %get-tuple-element.55), channel_id=1, source_target_pairs={{0,2},{1,3},{2,0},{3,1},{4,6},{5,7},{6,4},{7,5},{8,10},{9,11},{10,... | collective-permute-start | bytes 884744 | tf_op jit(solution)/shard_map/ppermute | solution.py:82
  51.3 0.0 collective-permute-done.17.refs_12_
  51.3 0.3 collective-permute-start.24
  51.6 1.4 %collective-permute-done.12.refs_3_ = bf16[64,2304]{1,0:T(8,128)(2,1)S(1)} collective-permute-done((bf16[64,2304]{1,0:T(8,128)(2,1)S(1)}, bf16[64,2304]{1,0:T(8,128)(2,1)S(1)}, u32[]{:S(2)}, u32[]{:S(2)}) %collective-permute-start.12) | collective-permute-done | bytes 294944 | tf_op jit(solution)/shard_map/ppermute | solution.py:61
  53.0 1.7 %collective-permute-done.13.refs_5_ = bf16[64,2304]{1,0:T(8,128)(2,1)S(1)} collective-permute-done((bf16[64,2304]{1,0:T(8,128)(2,1)S(1)}, bf16[64,2304]{1,0:T(8,128)(2,1)S(1)}, u32[]{:S(2)}, u32[]{:S(2)}) %collective-permute-start.13) | collective-permute-done | bytes 294944 | tf_op jit(solution)/shard_map/ppermute | solution.py:61
  54.8 0.3 collective-permute-start.19
  55.1 1.7 %collective-permute-start.18 = (bf16[32,2304]{1,0:T(8,128)(2,1)S(1)}, bf16[32,2304]{1,0:T(8,128)(2,1)S(1)}, u32[]{:S(2)}, u32[]{:S(2)}) collective-permute-start(bf16[32,2304]{1,0:T(8,128)(2,1)S(1)} %slice.12), channel_id=1, source_target_pairs={{0,8},{8,16},{16,24},{24,28},{28,20},{20,12},{12,4},{4,0},{1,9},{9... | collective-permute-start | bytes 442376 | tf_op jit(solution)/shard_map/ppermute | solution.py:61
  58.2 0.0 copy-start.2
  58.2 0.0 copy-start.5
  58.2 0.0 copy-start.6
  58.2 1.8 %collective-permute-done.19.refs_8_ = bf16[32,2304]{1,0:T(8,128)(2,1)S(1)} collective-permute-done((bf16[32,2304]{1,0:T(8,128)(2,1)S(1)}, bf16[32,2304]{1,0:T(8,128)(2,1)S(1)}, u32[]{:S(2)}, u32[]{:S(2)}) %collective-permute-start.19) | collective-permute-done | bytes 147488 | tf_op jit(solution)/shard_map/ppermute | solution.py:61
  60.0 0.3 collective-permute-done.18.refs_4_
  60.3 1.3 coupling.1
  61.6 0.1 collective-permute-start.25
  61.7 1.5 %collective-permute-start.26 = (bf16[64,256]{1,0:T(8,128)(2,1)S(1)}, bf16[64,256]{1,0:T(8,128)(2,1)S(1)}, u32[]{:S(2)}, u32[]{:S(2)}) collective-permute-start(bf16[64,256]{1,0:T(8,128)(2,1)S(1)} %get-tuple-element.58), channel_id=1, source_target_pairs={{0,2},{1,3},{2,0},{3,1},{4,6},{5,7},{6,4},{7,5},{8,10},{9,11},{10,... | collective-permute-start | bytes 98312 | tf_op jit(solution)/shard_map/ppermute | solution.py:82
  63.3 0.3 collective-permute-start.27
  63.6 1.5 %grams.1 = (bf16[512,512]{1,0:T(8,128)(2,1)S(1)}, bf16[512,512]{1,0:T(8,128)(2,1)S(1)}, f32[256,256]{1,0:T(8,128)S(1)}) custom-call(bf16[2304,256]{1,0:T(8,128)(2,1)S(1)} %bitcast.19, bf16[2304,256]{1,0:T(8,128)(2,1)S(1)} %bitcast.21, bf16[64,2304]{1,0:T(8,128)(2,1)S(1)} %bitcast.17, bf16[64,2304]{1,0:T(8,128)(2,1)S(1)} %collective-permute-done.14.refs_1_, ...), custom_call_target="tpu_custom_call" | custom-call | flops 1207959552 | bytes 6291456 | tf_op jit(solution)/shard_map/grams/pallas_call | solution.py:177
  65.1 0.0 collective-permute-done.23.refs_6_
  65.1 0.0 collective-permute-done.24.refs_7_
  65.2 1.0 collective-permute-done.26.refs_10_
  66.2 0.4 collective-permute-done.27.refs_11_
  66.6 70.7 %finish.1 = (bf16[2304,256]{1,0:T(8,128)(2,1)}, bf16[2304,256]{1,0:T(8,128)(2,1)}) custom-call(s32[1,1]{1,0:T(1,128)S(6)} %copy.10.old_ref, s32[1,1]{1,0:T(1,128)S(6)} %copy.11.goal_ref, s32[8]{0:T(128)S(1)} %copy-done.7, s32[4]{0:T(128)S(1)} %copy-done.4, bf16[2304,256]{1,0:T(8,128)(2,1)S(1)} %bitcast.20, bf16[2304,256]{1,0:T(8,128)(2,1)S(1)} %bitcast.22, ...), custom_call_target="tpu_custom_call" | custom-call | flops 8589934592 | bytes 12582912 | tf_op jit(solution)/shard_map/finish/pallas_call | solution.py:328
  (16 shorter events, 0.1 us)
Async XLA Ops:
  0.6 10.2 %collective-permute-start.1 = (bf16[64,2304]{1,0:T(8,128)(2,1)}, bf16[64,2304]{1,0:T(8,128)(2,1)S(1)}, u32[]{:S(2)}, u32[]{:S(2)}) collective-permute-start(bf16[64,2304]{1,0:T(8,128)(2,1)} %bitcast.12), channel_id=1, source_target_pairs={{0,8},{8,16},{16,24},{24,28},{28,20},{20,12},{12,4},{4,0},{1,9},{9... | collective-permute-start | bytes 884744 | tf_op jit(solution)/shard_map/ppermute | solution.py:61
  3.7 8.7 %collective-permute-start.2 = (bf16[64,2304]{1,0:T(8,128)(2,1)}, bf16[64,2304]{1,0:T(8,128)(2,1)S(1)}, u32[]{:S(2)}, u32[]{:S(2)}) collective-permute-start(bf16[64,2304]{1,0:T(8,128)(2,1)} %bitcast.13), channel_id=1, source_target_pairs={{8,0},{16,8},{24,16},{28,24},{20,28},{12,20},{4,12},{0,4},{9,1},{1... | collective-permute-start | bytes 884744 | tf_op jit(solution)/shard_map/ppermute | solution.py:61
  3.7 8.7 %collective-permute-start.3 = (bf16[64,2304]{1,0:T(8,128)(2,1)}, bf16[64,2304]{1,0:T(8,128)(2,1)S(1)}, u32[]{:S(2)}, u32[]{:S(2)}) collective-permute-start(bf16[64,2304]{1,0:T(8,128)(2,1)} %bitcast.14), channel_id=1, source_target_pairs={{0,2},{1,3},{2,0},{3,1},{4,6},{5,7},{6,4},{7,5},{8,10},{9,11},{10,... | collective-permute-start | bytes 884744 | tf_op jit(solution)/shard_map/ppermute | solution.py:82
  12.4 7.6 %collective-permute-start.4 = (bf16[64,2304]{1,0:T(8,128)(2,1)S(1)}, bf16[64,2304]{1,0:T(8,128)(2,1)S(1)}, u32[]{:S(2)}, u32[]{:S(2)}) collective-permute-start(bf16[64,2304]{1,0:T(8,128)(2,1)S(1)} %collective-permute-done.1.refs_1_), channel_id=1, source_target_pairs={{0,8},{8,16},{16,24},{24,28},{28,20},{20,12},{12,4},{4,0},{1,9},{9... | collective-permute-start | bytes 884744 | tf_op jit(solution)/shard_map/ppermute | solution.py:61
  14.1 7.1 %collective-permute-start.5 = (bf16[64,2304]{1,0:T(8,128)(2,1)S(1)}, bf16[64,2304]{1,0:T(8,128)(2,1)S(1)}, u32[]{:S(2)}, u32[]{:S(2)}) collective-permute-start(bf16[64,2304]{1,0:T(8,128)(2,1)S(1)} %collective-permute-done.2.refs_7_), channel_id=1, source_target_pairs={{8,0},{16,8},{24,16},{28,24},{20,28},{12,20},{4,12},{0,4},{9,1},{1... | collective-permute-start | bytes 884744 | tf_op jit(solution)/shard_map/ppermute | solution.py:61
  14.4 8.9 %collective-permute-start = (bf16[64,2304]{1,0:T(8,128)(2,1)}, bf16[64,2304]{1,0:T(8,128)(2,1)S(1)}, u32[]{:S(2)}, u32[]{:S(2)}) collective-permute-start(bf16[64,2304]{1,0:T(8,128)(2,1)} %bitcast.6), channel_id=1, source_target_pairs={{0,2},{1,3},{2,0},{3,1},{4,6},{5,7},{6,4},{7,5},{8,10},{9,11},{10,... | collective-permute-start | bytes 884744 | tf_op jit(solution)/shard_map/ppermute | solution.py:82
  21.2 9.4 %collective-permute-start.8 = (bf16[64,2304]{1,0:T(8,128)(2,1)S(1)}, bf16[64,2304]{1,0:T(8,128)(2,1)S(1)}, u32[]{:S(2)}, u32[]{:S(2)}) collective-permute-start(bf16[64,2304]{1,0:T(8,128)(2,1)S(1)} %collective-permute-done.4.refs_2_), channel_id=1, source_target_pairs={{0,8},{8,16},{16,24},{24,28},{28,20},{20,12},{12,4},{4,0},{1,9},{9... | collective-permute-start | bytes 884744 | tf_op jit(solution)/shard_map/ppermute | solution.py:61
  22.8 9.1 %collective-permute-start.9 = (bf16[64,2304]{1,0:T(8,128)(2,1)S(1)}, bf16[64,2304]{1,0:T(8,128)(2,1)S(1)}, u32[]{:S(2)}, u32[]{:S(2)}) collective-permute-start(bf16[64,2304]{1,0:T(8,128)(2,1)S(1)} %collective-permute-done.5.refs_6_), channel_id=1, source_target_pairs={{8,0},{16,8},{24,16},{28,24},{20,28},{12,20},{4,12},{0,4},{9,1},{1... | collective-permute-start | bytes 884744 | tf_op jit(solution)/shard_map/ppermute | solution.py:61
  23.3 10.5 %collective-permute-start.6 = (bf16[64,2304]{1,0:T(8,128)(2,1)}, bf16[64,2304]{1,0:T(8,128)(2,1)S(1)}, u32[]{:S(2)}, u32[]{:S(2)}) collective-permute-start(bf16[64,2304]{1,0:T(8,128)(2,1)} %bitcast.7), channel_id=1, source_target_pairs={{0,8},{8,16},{16,24},{24,28},{28,20},{20,12},{12,4},{4,0},{1,9},{9... | collective-permute-start | bytes 884744 | tf_op jit(solution)/shard_map/ppermute | solution.py:61
  24.9 10.3 %collective-permute-start.7 = (bf16[64,2304]{1,0:T(8,128)(2,1)}, bf16[64,2304]{1,0:T(8,128)(2,1)S(1)}, u32[]{:S(2)}, u32[]{:S(2)}) collective-permute-start(bf16[64,2304]{1,0:T(8,128)(2,1)} %bitcast.8), channel_id=1, source_target_pairs={{8,0},{16,8},{24,16},{28,24},{20,28},{12,20},{4,12},{0,4},{9,1},{1... | collective-permute-start | bytes 884744 | tf_op jit(solution)/shard_map/ppermute | solution.py:61
  25.3 14.1 %collective-permute-start.14 = (bf16[64,2304]{1,0:T(8,128)(2,1)}, bf16[64,2304]{1,0:T(8,128)(2,1)S(1)}, u32[]{:S(2)}, u32[]{:S(2)}) collective-permute-start(bf16[64,2304]{1,0:T(8,128)(2,1)} %bitcast.15), channel_id=1, source_target_pairs={{0,1},{1,0},{2,3},{3,2},{4,5},{5,4},{6,7},{7,6},{8,9},{9,8},{10,11... | collective-permute-start | bytes 884744 | tf_op jit(solution)/shard_map/ppermute | solution.py:82
  35.2 6.7 %collective-permute-start.10 = (bf16[64,2304]{1,0:T(8,128)(2,1)S(1)}, bf16[64,2304]{1,0:T(8,128)(2,1)S(1)}, u32[]{:S(2)}, u32[]{:S(2)}) collective-permute-start(bf16[64,2304]{1,0:T(8,128)(2,1)S(1)} %collective-permute-done.6.refs_1_), channel_id=1, source_target_pairs={{0,8},{8,16},{16,24},{24,28},{28,20},{20,12},{12,4},{4,0},{1,9},{9... | collective-permute-start | bytes 884744 | tf_op jit(solution)/shard_map/ppermute | solution.py:61
  36.8 6.8 %collective-permute-start.11 = (bf16[64,2304]{1,0:T(8,128)(2,1)S(1)}, bf16[64,2304]{1,0:T(8,128)(2,1)S(1)}, u32[]{:S(2)}, u32[]{:S(2)}) collective-permute-start(bf16[64,2304]{1,0:T(8,128)(2,1)S(1)} %collective-permute-done.7.refs_7_), channel_id=1, source_target_pairs={{8,0},{16,8},{24,16},{28,24},{20,28},{12,20},{4,12},{0,4},{9,1},{1... | collective-permute-start | bytes 884744 | tf_op jit(solution)/shard_map/ppermute | solution.py:61
  37.2 7.9 %collective-permute-start.21 = (bf16[32,2304]{1,0:T(8,128)(2,1)S(1)}, bf16[32,2304]{1,0:T(8,128)(2,1)S(1)}, u32[]{:S(2)}, u32[]{:S(2)}) collective-permute-start(bf16[32,2304]{1,0:T(8,128)(2,1)S(1)} %slice.15), channel_id=1, source_target_pairs={{8,0},{16,8},{24,16},{28,24},{20,28},{12,20},{4,12},{0,4},{9,1},{1... | collective-permute-start | bytes 442376 | tf_op jit(solution)/shard_map/ppermute | solution.py:61
  37.6 22.7 %copy-start.4 = (s32[4]{0:T(128)S(1)}, s32[4]{0:T(128)}, u32[]{:S(2)}) copy-start(s32[4]{0:T(128)} %owner.5) | copy-start | bytes 52
  37.6 22.7 %copy-start = (bf16[1,64,2304]{2,1,0:T(8,128)(2,1)S(1)}, bf16[1,64,2304]{2,1,0:T(8,128)(2,1)}, u32[]{:S(2)}) copy-start(bf16[1,64,2304]{2,1,0:T(8,128)(2,1)} %param.11) | copy-start | bytes 884740
  37.6 9.6 %collective-permute-start.20 = (bf16[32,2304]{1,0:T(8,128)(2,1)S(1)}, bf16[32,2304]{1,0:T(8,128)(2,1)S(1)}, u32[]{:S(2)}, u32[]{:S(2)}) collective-permute-start(bf16[32,2304]{1,0:T(8,128)(2,1)S(1)} %slice.14), channel_id=1, source_target_pairs={{0,8},{8,16},{16,24},{24,28},{28,20},{20,12},{12,4},{4,0},{1,9},{9... | collective-permute-start | bytes 442376 | tf_op jit(solution)/shard_map/ppermute | solution.py:61
  39.4 10.2 %collective-permute-start.16 = (bf16[64,2304]{1,0:T(8,128)(2,1)}, bf16[64,2304]{1,0:T(8,128)(2,1)S(1)}, u32[]{:S(2)}, u32[]{:S(2)}) collective-permute-start(bf16[64,2304]{1,0:T(8,128)(2,1)} %bitcast.9), channel_id=1, source_target_pairs={{0,1},{1,0},{2,3},{3,2},{4,5},{5,4},{6,7},{7,6},{8,9},{9,8},{10,11... | collective-permute-start | bytes 884744 | tf_op jit(solution)/shard_map/ppermute | solution.py:82
  41.9 7.8 %collective-permute-start.15 = (bf16[64,2304]{1,0:T(8,128)(2,1)S(1)}, bf16[64,2304]{1,0:T(8,128)(2,1)S(1)}, u32[]{:S(2)}, u32[]{:S(2)}) collective-permute-start(bf16[64,2304]{1,0:T(8,128)(2,1)S(1)} %collective-permute-done.3.refs_2_), channel_id=1, source_target_pairs={{0,1},{1,0},{2,3},{3,2},{4,5},{5,4},{6,7},{7,6},{8,9},{9,8},{10,11... | collective-permute-start | bytes 884744 | tf_op jit(solution)/shard_map/ppermute | solution.py:82
  43.6 7.7 %collective-permute-start.17 = (bf16[64,2304]{1,0:T(8,128)(2,1)S(1)}, bf16[64,2304]{1,0:T(8,128)(2,1)S(1)}, u32[]{:S(2)}, u32[]{:S(2)}) collective-permute-start(bf16[64,2304]{1,0:T(8,128)(2,1)S(1)} %collective-permute-done.refs_11_), channel_id=1, source_target_pairs={{0,1},{1,0},{2,3},{3,2},{4,5},{5,4},{6,7},{7,6},{8,9},{9,8},{10,11... | collective-permute-start | bytes 884744 | tf_op jit(solution)/shard_map/ppermute | solution.py:82
  45.2 7.8 %collective-permute-start.12 = (bf16[64,2304]{1,0:T(8,128)(2,1)S(1)}, bf16[64,2304]{1,0:T(8,128)(2,1)S(1)}, u32[]{:S(2)}, u32[]{:S(2)}) collective-permute-start(bf16[64,2304]{1,0:T(8,128)(2,1)S(1)} %collective-permute-done.10.refs_2_), channel_id=1, source_target_pairs={{0,8},{8,16},{16,24},{24,28},{28,20},{20,12},{12,4},{4,0},{1,9},{9... | collective-permute-start | bytes 884744 | tf_op jit(solution)/shard_map/ppermute | solution.py:61
  47.2 7.6 %collective-permute-start.13 = (bf16[64,2304]{1,0:T(8,128)(2,1)S(1)}, bf16[64,2304]{1,0:T(8,128)(2,1)S(1)}, u32[]{:S(2)}, u32[]{:S(2)}) collective-permute-start(bf16[64,2304]{1,0:T(8,128)(2,1)S(1)} %collective-permute-done.11.refs_6_), channel_id=1, source_target_pairs={{8,0},{16,8},{24,16},{28,24},{20,28},{12,20},{4,12},{0,4},{9,1},{1... | collective-permute-start | bytes 884744 | tf_op jit(solution)/shard_map/ppermute | solution.py:61
  47.2 1.0 copy-start.1
  48.2 0.7 copy-start.3
  49.6 13.6 %collective-permute-start.22 = (bf16[64,2304]{1,0:T(8,128)(2,1)S(1)}, bf16[64,2304]{1,0:T(8,128)(2,1)S(1)}, u32[]{:S(2)}, u32[]{:S(2)}) collective-permute-start(bf16[64,2304]{1,0:T(8,128)(2,1)S(1)} %get-tuple-element.54), channel_id=1, source_target_pairs={{0,1},{1,0},{2,3},{3,2},{4,5},{5,4},{6,7},{7,6},{8,9},{9,8},{10,11... | collective-permute-start | bytes 884744 | tf_op jit(solution)/shard_map/ppermute | solution.py:82
  49.7 15.4 %collective-permute-start.23 = (bf16[64,2304]{1,0:T(8,128)(2,1)S(1)}, bf16[64,2304]{1,0:T(8,128)(2,1)S(1)}, u32[]{:S(2)}, u32[]{:S(2)}) collective-permute-start(bf16[64,2304]{1,0:T(8,128)(2,1)S(1)} %get-tuple-element.55), channel_id=1, source_target_pairs={{0,2},{1,3},{2,0},{3,1},{4,6},{5,7},{6,4},{7,5},{8,10},{9,11},{10,... | collective-permute-start | bytes 884744 | tf_op jit(solution)/shard_map/ppermute | solution.py:82
  51.3 13.9 %collective-permute-start.24 = (bf16[64,2304]{1,0:T(8,128)(2,1)S(1)}, bf16[64,2304]{1,0:T(8,128)(2,1)S(1)}, u32[]{:S(2)}, u32[]{:S(2)}) collective-permute-start(bf16[64,2304]{1,0:T(8,128)(2,1)S(1)} %get-tuple-element.56), channel_id=1, source_target_pairs={{0,3},{1,2},{2,1},{3,0},{4,7},{5,6},{6,5},{7,4},{8,11},{9,10},{10,... | collective-permute-start | bytes 884744 | tf_op jit(solution)/shard_map/ppermute | solution.py:82
  54.8 5.2 %collective-permute-start.19 = (bf16[32,2304]{1,0:T(8,128)(2,1)S(1)}, bf16[32,2304]{1,0:T(8,128)(2,1)S(1)}, u32[]{:S(2)}, u32[]{:S(2)}) collective-permute-start(bf16[32,2304]{1,0:T(8,128)(2,1)S(1)} %slice.13), channel_id=1, source_target_pairs={{8,0},{16,8},{24,16},{28,24},{20,28},{12,20},{4,12},{0,4},{9,1},{1... | collective-permute-start | bytes 442376 | tf_op jit(solution)/shard_map/ppermute | solution.py:61
  55.1 5.1 %collective-permute-start.18 = (bf16[32,2304]{1,0:T(8,128)(2,1)S(1)}, bf16[32,2304]{1,0:T(8,128)(2,1)S(1)}, u32[]{:S(2)}, u32[]{:S(2)}) collective-permute-start(bf16[32,2304]{1,0:T(8,128)(2,1)S(1)} %slice.12), channel_id=1, source_target_pairs={{0,8},{8,16},{16,24},{24,28},{28,20},{20,12},{12,4},{4,0},{1,9},{9... | collective-permute-start | bytes 442376 | tf_op jit(solution)/shard_map/ppermute | solution.py:61
  58.2 5.4 %copy-start.2 = (bf16[1,64,2304]{2,1,0:T(8,128)(2,1)S(1)}, bf16[1,64,2304]{2,1,0:T(8,128)(2,1)}, u32[]{:S(2)}) copy-start(bf16[1,64,2304]{2,1,0:T(8,128)(2,1)} %param.10) | copy-start | bytes 884740
  58.2 5.4 %copy-start.5 = (bf16[1,1,2304,256]{3,2,1,0:T(8,128)(2,1)S(1)}, bf16[1,1,2304,256]{3,2,1,0:T(8,128)(2,1)}, u32[]{:S(2)}) copy-start(bf16[1,1,2304,256]{3,2,1,0:T(8,128)(2,1)} %param.8) | copy-start | bytes 3538948
  58.2 5.4 %copy-start.6 = (bf16[1,1,2304,256]{3,2,1,0:T(8,128)(2,1)S(1)}, bf16[1,1,2304,256]{3,2,1,0:T(8,128)(2,1)}, u32[]{:S(2)}) copy-start(bf16[1,1,2304,256]{3,2,1,0:T(8,128)(2,1)} %param.9) | copy-start | bytes 3538948
  61.6 3.5 %collective-permute-start.25 = (bf16[64,256]{1,0:T(8,128)(2,1)S(1)}, bf16[64,256]{1,0:T(8,128)(2,1)S(1)}, u32[]{:S(2)}, u32[]{:S(2)}) collective-permute-start(bf16[64,256]{1,0:T(8,128)(2,1)S(1)} %get-tuple-element.57), channel_id=1, source_target_pairs={{0,1},{1,0},{2,3},{3,2},{4,5},{5,4},{6,7},{7,6},{8,9},{9,8},{10,11... | collective-permute-start | bytes 98312 | tf_op jit(solution)/shard_map/ppermute | solution.py:82
  61.7 4.5 %collective-permute-start.26 = (bf16[64,256]{1,0:T(8,128)(2,1)S(1)}, bf16[64,256]{1,0:T(8,128)(2,1)S(1)}, u32[]{:S(2)}, u32[]{:S(2)}) collective-permute-start(bf16[64,256]{1,0:T(8,128)(2,1)S(1)} %get-tuple-element.58), channel_id=1, source_target_pairs={{0,2},{1,3},{2,0},{3,1},{4,6},{5,7},{6,4},{7,5},{8,10},{9,11},{10,... | collective-permute-start | bytes 98312 | tf_op jit(solution)/shard_map/ppermute | solution.py:82
  63.3 3.3 %collective-permute-start.27 = (bf16[64,256]{1,0:T(8,128)(2,1)S(1)}, bf16[64,256]{1,0:T(8,128)(2,1)S(1)}, u32[]{:S(2)}, u32[]{:S(2)}) collective-permute-start(bf16[64,256]{1,0:T(8,128)(2,1)S(1)} %get-tuple-element.59), channel_id=1, source_target_pairs={{0,3},{1,2},{2,1},{3,0},{4,7},{5,6},{6,5},{7,4},{8,11},{9,10},{10,... | collective-permute-start | bytes 98312 | tf_op jit(solution)/shard_map/ppermute | solution.py:82
  63.6 3.0 %copy-start.7 = (s32[8]{0:T(128)S(1)}, s32[8]{0:T(128)}, u32[]{:S(2)}) copy-start(s32[8]{0:T(128)} %panel.1) | copy-start | bytes 100

commit v7 on v6

--- a/solution.py
+++ b/solution.py
@@ -73,7 +73,7 @@
         if s < 3:
             early = step(0, half - 2 + s)
         gate = gates[s](lists) if s in gates else ()
-        step(1, s, *gate, *(done if s < 3 else ()))
+        step(1, s, *gate, *(done if s < 2 else ()))
         done = early
     return lists
 
@@ -155,44 +155,55 @@
     )(owner, *pieces, *parts)
 
 
-def grams(n_col, u_ref, v_ref, *refs):
-    high, low, cu_ref, uit = refs[n_col:]
+def grams(n_col, old_ref, goal_ref, u_ref, v_ref, *refs):
+    high, low, cu_ref, hm_ref, g_ref, uit = refs[n_col:]
     rank = cu_ref.shape[0]
+    sub = lax.broadcasted_iota(jnp.int32, (rank, rank), 0)
+    lane = lax.broadcasted_iota(jnp.int32, (rank, rank), 1)
     assemble(refs[:n_col], uit)
     top, bottom = pl.ds(0, rank), pl.ds(rank, rank)
-
-    def put(at, lanes, value):
-        high[at, lanes], low[at, lanes] = halves(value)
-
-    cu_ref[...] = tn(v_ref[...], v_ref[...])
-    put(top, top, tn(u_ref[...], u_ref[...]))
+    kept = (sub < old_ref[0, 0]) & (lane < goal_ref[0, 0])
+    cu = jnp.where(kept, tn(v_ref[...], v_ref[...]), 0.0).astype(BF16)
+    cu_ref[...] = cu
+    first_high, first_low = halves(tn(u_ref[...], u_ref[...]))
+    hm = nn(first_high, cu) + nn(first_low, cu)
+    hm_ref[top, :] = hm
+    hm_high, hm_low = halves(hm)
+    g_ref[...] = tn(cu, hm_high) + tn(cu, hm_low)
     cross = nn(uit[...], u_ref[...])
-    put(bottom, top, cross)
-    put(top, bottom, cross.T)
-    put(bottom, bottom, nt(uit[...], uit[...]))
-
-
-def gram_products(u, v, parts):
+    cross_high, cross_low = halves(cross)
+    hm_ref[bottom, :] = nn(cross_high, cu) + nn(cross_low, cu)
+    high[top, :], low[top, :] = halves(cross.T)
+    high[bottom, :], low[bottom, :] = halves(nt(uit[...], uit[...]))
+
+
+def gram_products(old, goal, u, v, parts):
     rows, rank = u.shape
     return pl.pallas_call(
         functools.partial(grams, len(parts)),
-        out_shape=[jax.ShapeDtypeStruct((2 * rank, 2 * rank), BF16)] * 2 + [jax.ShapeDtypeStruct((rank, rank), F32)],
-        in_specs=[VMEM] * (2 + len(parts)),
-        out_specs=[VMEM] * 3,
-        scratch_shapes=[pltpu.VMEM((rank, rows), BF16)],
+        out_shape=[
+            jax.ShapeDtypeStruct((2 * rank, rank), BF16),
+            jax.ShapeDtypeStruct((2 * rank, rank), BF16),
+            jax.ShapeDtypeStruct((rank, rank), BF16),
+            jax.ShapeDtypeStruct((2 * rank, rank), F32),
+            jax.ShapeDtypeStruct((rank, rank), F32),
+            jax.ShapeDtypeStruct((rank, rows), BF16),
+        ],
+        in_specs=[SMEM] * 2 + [VMEM] * (2 + len(parts)),
+        out_specs=[VMEM] * 6,
         compiler_params=pltpu.CompilerParams(vmem_limit_bytes=24 << 20),
         cost_estimate=pl.CostEstimate(flops=8 * rank * rank * rows, bytes_accessed=6 << 20, transcendentals=0),
         name="grams",
-    )(u, v, *parts)
+    )(old, goal, u, v, *parts)
 
 
 def lower_half(e, eye, below):
     return jnp.where(below, e, jnp.where(eye, 0.5 * e, 0.0))
 
 
-def finish(n_col, old_ref, goal_ref, panel, owner, u_ref, v_ref, hh, hl, cu_ref, *refs):
-    ui_in, ujt_in, kt_in = refs[:n_col], refs[n_col : 2 * n_col], refs[2 * n_col : 3 * n_col]
-    q_hbm, w_hbm, uit_ref, ujt, q_ref, w_ref, kt, mh, gn, y_ref, a_ref, q_sem, w_sem = refs[3 * n_col :]
+def finish(n_col, old_ref, goal_ref, panel, owner, u_ref, v_ref, hh, hl, cu_ref, hm_ref, g_ref, uit_ref, *refs):
+    ujt_in, kt_in = refs[:n_col], refs[n_col : 2 * n_col]
+    q_hbm, w_hbm, ujt, q_ref, w_ref, kt, mh, gn, y_ref, a_ref, q_sem, w_sem = refs[2 * n_col :]
     rows, rank = u_ref.shape
     row, col = lax.axis_index("row"), lax.axis_index("col")
     old, goal, here, there = old_ref[0, 0], goal_ref[0, 0], panel[row], panel[owner[col]]
@@ -205,12 +216,15 @@
     zero = jnp.zeros((rank, rank), F32)
     kt[...] = jnp.where((sub < there) & (lane < here), kt[...].astype(F32), zero).astype(BF16)
     cl = jnp.where(lane < goal, nn(ujt[...], v_ref[...]), zero).astype(BF16)
-    cu = jnp.where((sub < old) & (lane < goal), cu_ref[...], zero).astype(BF16)
+    cu = cu_ref[...]
     m_high, m_low = halves(-tn(kt[...], cl))
     mh[pl.ds(0, rank), :], mh[pl.ds(rank, rank), :] = cu, m_high
-    hm = nn(hh[...], mh[...]) + nn(hl[...], mh[...]) + nn(hh[:, rank:], m_low)
-    hm_high, hm_low = halves(hm)
-    g = tn(mh[...], hm_high) + tn(mh[...], hm_low) + tn(m_low, hm_high[rank:])
+    more = nn(hh[...], m_high) + nn(hh[...], m_low) + nn(hl[...], m_high)
+    more_high, more_low = halves(more)
+    mixed = tn(cu, more_high[:rank]) + tn(cu, more_low[:rank])
+    own = tn(m_high, more_high[rank:]) + tn(m_high, more_low[rank:]) + tn(m_low, more_high[rank:])
+    g = g_ref[...] + mixed + mixed.T + own
+    hm_high, hm_low = halves(hm_ref[...] + more)
     g = g + jnp.where(eye & (lane >= goal), 1.0, 0.0)
     dg = jnp.where(eye, g, 0.0)
     d_row = lax.rsqrt(jnp.sum(dg, axis=0, keepdims=True))
@@ -274,7 +288,6 @@
     r_up = jnp.where(sub < old, r[:rank], 0.0).astype(BF16)
     w_high, w_low = halves(r[rank:])
     r_low = (-(nn(kt[...], w_high) + nn(kt[...], w_low))).astype(BF16)
-    assemble(ui_in, uit_ref)
     step = rows // q_sem.shape[0]
     stores = []
     for t in range(rows // step):
@@ -318,7 +331,7 @@
     ujs = picked_left(us, owner_row, n_row, n_col)
     ujs = [ujs[0]] + [swap(ujs[m], "col", n_col, m) for m in range(1, n_col)]
     kts = coupled(vs, [rights[m] for m in range(n_col)], owner_row, n_row, n_col)
-    h_high, h_low, core_up = gram_products(u, v, [after(ui_parts[0], kts[0]), *ui_parts[1:]])
+    early = gram_products(tile_rank, target_rank, u, v, [after(ui_parts[0], kts[0]), *ui_parts[1:]])
     kts = [kts[0]] + [swap(kts[m], "col", n_col, m) for m in range(1, n_col)]
 
     out = jax.ShapeDtypeStruct((rows, rank), BF16)
@@ -328,10 +341,9 @@
     fresh_basis, fresh_coeffs = pl.pallas_call(
         functools.partial(finish, n_col),
         out_shape=(out, out),
-        in_specs=[SMEM] * 4 + [VMEM] * (5 + 3 * n_col),
+        in_specs=[SMEM] * 4 + [VMEM] * (8 + 2 * n_col),
         out_specs=(HBM, HBM),
         scratch_shapes=[
-            wide,
             wide,
             tall,
             tall,
@@ -346,7 +358,7 @@
         compiler_params=pltpu.CompilerParams(vmem_limit_bytes=24 << 20),
         cost_estimate=pl.CostEstimate(flops=8 << 30, bytes_accessed=12 << 20, transcendentals=0),
         name="finish",
-    )(tile_rank, target_rank, panel_rank, owner_row, u, v, h_high, h_low, core_up, *ui_parts, *ujs, *kts)
+    )(tile_rank, target_rank, panel_rank, owner_row, u, v, *early, *ujs, *kts)
     return fresh_basis[None, None], fresh_coeffs[None, None]
 
 

time: 137 us -> 137 us (level)
  starting transfers between devices: 24.9 us -> 23.3 us
    ppermute x12, waiting for transfers between devices: 1.49 us -> 5.2 us  [swap(): return lax.ppermute(x, axis, [(i, i ^ m) for i in range(n)])]
    ppermute x16, waiting for transfers between devices: 32.8 us -> 29.3 us  [step(): fwd, bwd = (lax.ppermute(fwd, axis, ahead), lax.ppermute(bwd, axis, back))]
    ppermute x12, starting transfers between devices: 7.45 us -> 5.9 us  [swap(): return lax.ppermute(x, axis, [(i, i ^ m) for i in range(n)])]
  transfers between devices with their start and end apart: 28 -> 28, of which waited for: 17 -> 19; matrix products, arithmetic and copies ran while one was open for 0% -> 0% of each run, Pallas kernels for 3% -> 3%
where the time goes in v7:
time: 137 us
  Pallas kernels  75.1 us (55%)
  waiting for transfers between devices  34.5 us (25%)
  starting transfers between devices  23.3 us (17%)
  between operations  2.09 us (2%)
  local copies, waits for them, and re-layouts  1.69 us (1%)
    pallas_call x1, Pallas kernels, body(): pl.pallas_call(functools.partial(finish, n_col), out_shape=(out, out), in...  70.5 us
    ppermute x16, waiting for transfers between devices, step(): fwd, bwd = (lax.ppermute(fwd, axis, ahead), lax.ppermute(bwd, axis, back))  29.3 us
    ppermute x16, starting transfers between devices, step(): fwd, bwd = (lax.ppermute(fwd, axis, ahead), lax.ppermute(bwd, axis, back))  17.4 us
    ppermute x12, starting transfers between devices, swap(): return lax.ppermute(x, axis, [(i, i ^ m) for i in range(n)])  5.9 us
    ppermute x12, waiting for transfers between devices, swap(): return lax.ppermute(x, axis, [(i, i ^ m) for i in range(n)])  5.2 us
  transfers between devices with their start and end apart: 28, of which 19 were waited for; matrix products, arithmetic and copies ran while one was open for 0% of the time, Pallas kernels for 3%

profile of v7, /device:TPU:0, one launch (start us, length us, event | category | flops | bytes accessed | tf_op | source)
XLA Modules:
  0.0 136.7 jit_solution(14867024717806067555)
XLA Ops:
  0.6 3.1 %collective-permute-start.1 = (bf16[64,2304]{1,0:T(8,128)(2,1)}, bf16[64,2304]{1,0:T(8,128)(2,1)S(1)}, u32[]{:S(2)}, u32[]{:S(2)}) collective-permute-start(bf16[64,2304]{1,0:T(8,128)(2,1)} %bitcast.12), channel_id=1, source_target_pairs={{0,8},{8,16},{16,24},{24,28},{28,20},{20,12},{12,4},{4,0},{1,9},{9... | collective-permute-start | bytes 884744 | tf_op jit(solution)/shard_map/ppermute | solution.py:61
  3.7 0.0 collective-permute-start.2
  3.7 1.9 %collective-permute-start.3 = (bf16[64,2304]{1,0:T(8,128)(2,1)}, bf16[64,2304]{1,0:T(8,128)(2,1)S(1)}, u32[]{:S(2)}, u32[]{:S(2)}) collective-permute-start(bf16[64,2304]{1,0:T(8,128)(2,1)} %bitcast.14), channel_id=1, source_target_pairs={{0,2},{1,3},{2,0},{3,1},{4,6},{5,7},{6,4},{7,5},{8,10},{9,11},{10,... | collective-permute-start | bytes 884744 | tf_op jit(solution)/shard_map/ppermute | solution.py:82
  5.6 0.1 collective-permute-start
  5.7 5.1 %collective-permute-done.1.refs_1_ = bf16[64,2304]{1,0:T(8,128)(2,1)S(1)} collective-permute-done((bf16[64,2304]{1,0:T(8,128)(2,1)}, bf16[64,2304]{1,0:T(8,128)(2,1)S(1)}, u32[]{:S(2)}, u32[]{:S(2)}) %collective-permute-start.1) | collective-permute-done | bytes 294944 | tf_op jit(solution)/shard_map/ppermute | solution.py:61
  10.9 1.5 %collective-permute-done.2.refs_7_ = bf16[64,2304]{1,0:T(8,128)(2,1)S(1)} collective-permute-done((bf16[64,2304]{1,0:T(8,128)(2,1)}, bf16[64,2304]{1,0:T(8,128)(2,1)S(1)}, u32[]{:S(2)}, u32[]{:S(2)}) %collective-permute-start.2) | collective-permute-done | bytes 294944 | tf_op jit(solution)/shard_map/ppermute | solution.py:61
  12.4 1.5 %collective-permute-done.3.refs_2_ = bf16[64,2304]{1,0:T(8,128)(2,1)S(1)} collective-permute-done((bf16[64,2304]{1,0:T(8,128)(2,1)}, bf16[64,2304]{1,0:T(8,128)(2,1)S(1)}, u32[]{:S(2)}, u32[]{:S(2)}) %collective-permute-start.3) | collective-permute-done | bytes 294944 | tf_op jit(solution)/shard_map/ppermute | solution.py:82
  13.9 2.0 %collective-permute-start.4 = (bf16[64,2304]{1,0:T(8,128)(2,1)S(1)}, bf16[64,2304]{1,0:T(8,128)(2,1)S(1)}, u32[]{:S(2)}, u32[]{:S(2)}) collective-permute-start(bf16[64,2304]{1,0:T(8,128)(2,1)S(1)} %collective-permute-done.1.refs_1_), channel_id=1, source_target_pairs={{0,8},{8,16},{16,24},{24,28},{28,20},{20,12},{12,4},{4,0},{1,9},{9... | collective-permute-start | bytes 884744 | tf_op jit(solution)/shard_map/ppermute | solution.py:61
  15.9 0.0 collective-permute-start.5
  15.9 2.8 %collective-permute-done.refs_11_ = bf16[64,2304]{1,0:T(8,128)(2,1)S(1)} collective-permute-done((bf16[64,2304]{1,0:T(8,128)(2,1)}, bf16[64,2304]{1,0:T(8,128)(2,1)S(1)}, u32[]{:S(2)}, u32[]{:S(2)}) %collective-permute-start) | collective-permute-done | bytes 294944 | tf_op jit(solution)/shard_map/ppermute | solution.py:82
  18.7 1.9 %collective-permute-done.4.refs_2_ = bf16[64,2304]{1,0:T(8,128)(2,1)S(1)} collective-permute-done((bf16[64,2304]{1,0:T(8,128)(2,1)S(1)}, bf16[64,2304]{1,0:T(8,128)(2,1)S(1)}, u32[]{:S(2)}, u32[]{:S(2)}) %collective-permute-start.4) | collective-permute-done | bytes 294944 | tf_op jit(solution)/shard_map/ppermute | solution.py:61
  20.6 2.3 %collective-permute-done.5.refs_6_ = bf16[64,2304]{1,0:T(8,128)(2,1)S(1)} collective-permute-done((bf16[64,2304]{1,0:T(8,128)(2,1)S(1)}, bf16[64,2304]{1,0:T(8,128)(2,1)S(1)}, u32[]{:S(2)}, u32[]{:S(2)}) %collective-permute-start.5) | collective-permute-done | bytes 294944 | tf_op jit(solution)/shard_map/ppermute | solution.py:61
  22.9 1.6 %collective-permute-start.6 = (bf16[64,2304]{1,0:T(8,128)(2,1)}, bf16[64,2304]{1,0:T(8,128)(2,1)S(1)}, u32[]{:S(2)}, u32[]{:S(2)}) collective-permute-start(bf16[64,2304]{1,0:T(8,128)(2,1)} %bitcast.7), channel_id=1, source_target_pairs={{0,8},{8,16},{16,24},{24,28},{28,20},{20,12},{12,4},{4,0},{1,9},{9... | collective-permute-start | bytes 884744 | tf_op jit(solution)/shard_map/ppermute | solution.py:61
  24.5 0.4 collective-permute-start.7
  24.9 1.6 %collective-permute-start.18 = (bf16[64,2304]{1,0:T(8,128)(2,1)S(1)}, bf16[64,2304]{1,0:T(8,128)(2,1)S(1)}, u32[]{:S(2)}, u32[]{:S(2)}) collective-permute-start(bf16[64,2304]{1,0:T(8,128)(2,1)S(1)} %collective-permute-done.4.refs_2_), channel_id=1, source_target_pairs={{0,8},{8,16},{16,24},{24,28},{28,20},{20,12},{12,4},{4,0},{1,9},{9... | collective-permute-start | bytes 884744 | tf_op jit(solution)/shard_map/ppermute | solution.py:61
  26.5 0.4 collective-permute-start.19
  26.9 0.0 collective-permute-start.12
  26.9 4.0 %collective-permute-done.6.refs_1_ = bf16[64,2304]{1,0:T(8,128)(2,1)S(1)} collective-permute-done((bf16[64,2304]{1,0:T(8,128)(2,1)}, bf16[64,2304]{1,0:T(8,128)(2,1)S(1)}, u32[]{:S(2)}, u32[]{:S(2)}) %collective-permute-start.6) | collective-permute-done | bytes 294944 | tf_op jit(solution)/shard_map/ppermute | solution.py:61
  30.9 1.6 %collective-permute-done.7.refs_7_ = bf16[64,2304]{1,0:T(8,128)(2,1)S(1)} collective-permute-done((bf16[64,2304]{1,0:T(8,128)(2,1)}, bf16[64,2304]{1,0:T(8,128)(2,1)S(1)}, u32[]{:S(2)}, u32[]{:S(2)}) %collective-permute-start.7) | collective-permute-done | bytes 294944 | tf_op jit(solution)/shard_map/ppermute | solution.py:61
  32.5 1.2 collective-permute-start.8
  33.7 0.9 collective-permute-start.9
  34.5 2.7 %collective-permute-done.18.refs_3_ = bf16[64,2304]{1,0:T(8,128)(2,1)S(1)} collective-permute-done((bf16[64,2304]{1,0:T(8,128)(2,1)S(1)}, bf16[64,2304]{1,0:T(8,128)(2,1)S(1)}, u32[]{:S(2)}, u32[]{:S(2)}) %collective-permute-start.18) | collective-permute-done | bytes 294944 | tf_op jit(solution)/shard_map/ppermute | solution.py:61
  37.2 1.6 %collective-permute-done.19.refs_5_ = bf16[64,2304]{1,0:T(8,128)(2,1)S(1)} collective-permute-done((bf16[64,2304]{1,0:T(8,128)(2,1)S(1)}, bf16[64,2304]{1,0:T(8,128)(2,1)S(1)}, u32[]{:S(2)}, u32[]{:S(2)}) %collective-permute-start.19) | collective-permute-done | bytes 294944 | tf_op jit(solution)/shard_map/ppermute | solution.py:61
  38.8 0.3 collective-permute-start.21
  39.2 0.0 copy-start
  39.2 1.8 %collective-permute-start.20 = (bf16[32,2304]{1,0:T(8,128)(2,1)S(1)}, bf16[32,2304]{1,0:T(8,128)(2,1)S(1)}, u32[]{:S(2)}, u32[]{:S(2)}) collective-permute-start(bf16[32,2304]{1,0:T(8,128)(2,1)S(1)} %slice.14), channel_id=1, source_target_pairs={{0,8},{8,16},{16,24},{24,28},{28,20},{20,12},{12,4},{4,0},{1,9},{9... | collective-permute-start | bytes 442376 | tf_op jit(solution)/shard_map/ppermute | solution.py:61
  41.0 0.0 collective-permute-done.12.refs_1_
  41.0 0.0 collective-permute-start.14
  41.0 0.5 collective-permute-done.8.refs_2_
  41.5 0.0 collective-permute-start.13
  41.5 1.6 %collective-permute-done.9.refs_6_ = bf16[64,2304]{1,0:T(8,128)(2,1)S(1)} collective-permute-done((bf16[64,2304]{1,0:T(8,128)(2,1)S(1)}, bf16[64,2304]{1,0:T(8,128)(2,1)S(1)}, u32[]{:S(2)}, u32[]{:S(2)}) %collective-permute-start.9) | collective-permute-done | bytes 294944 | tf_op jit(solution)/shard_map/ppermute | solution.py:61
  43.2 0.0 collective-permute-start.15
  43.2 1.6 %collective-permute-done.21.refs_8_ = bf16[32,2304]{1,0:T(8,128)(2,1)S(1)} collective-permute-done((bf16[32,2304]{1,0:T(8,128)(2,1)S(1)}, bf16[32,2304]{1,0:T(8,128)(2,1)S(1)}, u32[]{:S(2)}, u32[]{:S(2)}) %collective-permute-start.21) | collective-permute-done | bytes 147488 | tf_op jit(solution)/shard_map/ppermute | solution.py:61
  44.7 1.6 %collective-permute-start.10 = (bf16[64,2304]{1,0:T(8,128)(2,1)S(1)}, bf16[64,2304]{1,0:T(8,128)(2,1)S(1)}, u32[]{:S(2)}, u32[]{:S(2)}) collective-permute-start(bf16[64,2304]{1,0:T(8,128)(2,1)S(1)} %collective-permute-done.8.refs_2_), channel_id=1, source_target_pairs={{0,8},{8,16},{16,24},{24,28},{28,20},{20,12},{12,4},{4,0},{1,9},{9... | collective-permute-start | bytes 884744 | tf_op jit(solution)/shard_map/ppermute | solution.py:61
  46.3 0.0 collective-permute-done.20.refs_4_
  46.3 0.4 collective-permute-start.11
  46.8 1.0 copy-done.1
  47.7 0.7 copy-done.3
  48.4 0.8 pick_left.1
  49.2 0.0 collective-permute-done.14.refs_10_
  49.2 0.1 collective-permute-start.22
  49.3 0.0 collective-permute-done.13.refs_3_
  49.3 1.6 %collective-permute-start.23 = (bf16[64,2304]{1,0:T(8,128)(2,1)S(1)}, bf16[64,2304]{1,0:T(8,128)(2,1)S(1)}, u32[]{:S(2)}, u32[]{:S(2)}) collective-permute-start(bf16[64,2304]{1,0:T(8,128)(2,1)S(1)} %get-tuple-element.61), channel_id=1, source_target_pairs={{0,2},{1,3},{2,0},{3,1},{4,6},{5,7},{6,4},{7,5},{8,10},{9,11},{10,... | collective-permute-start | bytes 884744 | tf_op jit(solution)/shard_map/ppermute | solution.py:82
  50.9 0.0 collective-permute-done.15.refs_12_
  50.9 0.3 collective-permute-start.24
  51.2 1.4 %collective-permute-done.10.refs_3_ = bf16[64,2304]{1,0:T(8,128)(2,1)S(1)} collective-permute-done((bf16[64,2304]{1,0:T(8,128)(2,1)S(1)}, bf16[64,2304]{1,0:T(8,128)(2,1)S(1)}, u32[]{:S(2)}, u32[]{:S(2)}) %collective-permute-start.10) | collective-permute-done | bytes 294944 | tf_op jit(solution)/shard_map/ppermute | solution.py:61
  52.6 1.3 collective-permute-done.11.refs_5_
  53.9 0.5 collective-permute-start.17
  54.4 1.6 %collective-permute-start.16 = (bf16[32,2304]{1,0:T(8,128)(2,1)S(1)}, bf16[32,2304]{1,0:T(8,128)(2,1)S(1)}, u32[]{:S(2)}, u32[]{:S(2)}) collective-permute-start(bf16[32,2304]{1,0:T(8,128)(2,1)S(1)} %slice.12), channel_id=1, source_target_pairs={{0,8},{8,16},{16,24},{24,28},{28,20},{20,12},{12,4},{4,0},{1,9},{9... | collective-permute-start | bytes 442376 | tf_op jit(solution)/shard_map/ppermute | solution.py:61
  57.3 0.0 copy-start.2
  57.3 0.0 copy-start.5
  57.3 0.0 copy-start.6
  57.4 1.8 %collective-permute-done.17.refs_8_ = bf16[32,2304]{1,0:T(8,128)(2,1)S(1)} collective-permute-done((bf16[32,2304]{1,0:T(8,128)(2,1)S(1)}, bf16[32,2304]{1,0:T(8,128)(2,1)S(1)}, u32[]{:S(2)}, u32[]{:S(2)}) %collective-permute-start.17) | collective-permute-done | bytes 147488 | tf_op jit(solution)/shard_map/ppermute | solution.py:61
  59.1 0.4 collective-permute-done.16.refs_4_
  59.6 1.3 coupling.1
  60.9 0.1 collective-permute-start.25
  61.0 1.6 %collective-permute-start.26 = (bf16[64,256]{1,0:T(8,128)(2,1)S(1)}, bf16[64,256]{1,0:T(8,128)(2,1)S(1)}, u32[]{:S(2)}, u32[]{:S(2)}) collective-permute-start(bf16[64,256]{1,0:T(8,128)(2,1)S(1)} %get-tuple-element.64), channel_id=1, source_target_pairs={{0,2},{1,3},{2,0},{3,1},{4,6},{5,7},{6,4},{7,5},{8,10},{9,11},{10,... | collective-permute-start | bytes 98312 | tf_op jit(solution)/shard_map/ppermute | solution.py:82
  62.6 0.3 collective-permute-start.27
  62.9 2.5 %grams.1 = (bf16[512,256]{1,0:T(8,128)(2,1)S(1)}, bf16[512,256]{1,0:T(8,128)(2,1)S(1)}, bf16[256,256]{1,0:T(8,128)(2,1)S(1)}, f32[512,256]{1,0:T(8,128)S(1)}, f3...) custom-call(s32[1,1]{1,0:T(1,128)S(6)} %copy.10.old_ref, s32[1,1]{1,0:T(1,128)S(6)} %copy.11.goal_ref, ...), custom_call_target="tpu_custom_call" | custom-call | flops 1207959552 | bytes 6291456 | tf_op jit(solution)/shard_map/grams/pallas_call | solution.py:182
  65.4 0.0 collective-permute-done.23.refs_2_
  65.4 0.0 collective-permute-done.25.refs_5_
  65.4 0.5 collective-permute-done.26.refs_6_
  65.9 0.4 collective-permute-done.27.refs_7_
  66.3 70.5 %finish.1 = (bf16[2304,256]{1,0:T(8,128)(2,1)}, bf16[2304,256]{1,0:T(8,128)(2,1)}) custom-call(s32[1,1]{1,0:T(1,128)S(6)} %copy.10.old_ref, s32[1,1]{1,0:T(1,128)S(6)} %copy.11.goal_ref, s32[8]{0:T(128)S(1)} %copy-done.7, s32[4]{0:T(128)S(1)} %copy-done.4, bf16[2304,256]{1,0:T(8,128)(2,1)S(1)} %bitcast.19, bf16[2304,256]{1,0:T(8,128)(2,1)S(1)} %bitcast.21, ...), custom_call_target="tpu_custom_call" | custom-call | flops 8589934592 | bytes 12582912 | tf_op jit(solution)/shard_map/finish/pallas_call | solution.py:341
  (16 shorter events, 0.1 us)
Async XLA Ops:
  0.6 10.2 %collective-permute-start.1 = (bf16[64,2304]{1,0:T(8,128)(2,1)}, bf16[64,2304]{1,0:T(8,128)(2,1)S(1)}, u32[]{:S(2)}, u32[]{:S(2)}) collective-permute-start(bf16[64,2304]{1,0:T(8,128)(2,1)} %bitcast.12), channel_id=1, source_target_pairs={{0,8},{8,16},{16,24},{24,28},{28,20},{20,12},{12,4},{4,0},{1,9},{9... | collective-permute-start | bytes 884744 | tf_op jit(solution)/shard_map/ppermute | solution.py:61
  3.7 8.7 %collective-permute-start.2 = (bf16[64,2304]{1,0:T(8,128)(2,1)}, bf16[64,2304]{1,0:T(8,128)(2,1)S(1)}, u32[]{:S(2)}, u32[]{:S(2)}) collective-permute-start(bf16[64,2304]{1,0:T(8,128)(2,1)} %bitcast.13), channel_id=1, source_target_pairs={{8,0},{16,8},{24,16},{28,24},{20,28},{12,20},{4,12},{0,4},{9,1},{1... | collective-permute-start | bytes 884744 | tf_op jit(solution)/shard_map/ppermute | solution.py:61
  3.7 10.1 %collective-permute-start.3 = (bf16[64,2304]{1,0:T(8,128)(2,1)}, bf16[64,2304]{1,0:T(8,128)(2,1)S(1)}, u32[]{:S(2)}, u32[]{:S(2)}) collective-permute-start(bf16[64,2304]{1,0:T(8,128)(2,1)} %bitcast.14), channel_id=1, source_target_pairs={{0,2},{1,3},{2,0},{3,1},{4,6},{5,7},{6,4},{7,5},{8,10},{9,11},{10,... | collective-permute-start | bytes 884744 | tf_op jit(solution)/shard_map/ppermute | solution.py:82
  5.6 13.1 %collective-permute-start = (bf16[64,2304]{1,0:T(8,128)(2,1)}, bf16[64,2304]{1,0:T(8,128)(2,1)S(1)}, u32[]{:S(2)}, u32[]{:S(2)}) collective-permute-start(bf16[64,2304]{1,0:T(8,128)(2,1)} %bitcast.6), channel_id=1, source_target_pairs={{0,2},{1,3},{2,0},{3,1},{4,6},{5,7},{6,4},{7,5},{8,10},{9,11},{10,... | collective-permute-start | bytes 884744 | tf_op jit(solution)/shard_map/ppermute | solution.py:82
  13.9 6.7 %collective-permute-start.4 = (bf16[64,2304]{1,0:T(8,128)(2,1)S(1)}, bf16[64,2304]{1,0:T(8,128)(2,1)S(1)}, u32[]{:S(2)}, u32[]{:S(2)}) collective-permute-start(bf16[64,2304]{1,0:T(8,128)(2,1)S(1)} %collective-permute-done.1.refs_1_), channel_id=1, source_target_pairs={{0,8},{8,16},{16,24},{24,28},{28,20},{20,12},{12,4},{4,0},{1,9},{9... | collective-permute-start | bytes 884744 | tf_op jit(solution)/shard_map/ppermute | solution.py:61
  15.9 7.0 %collective-permute-start.5 = (bf16[64,2304]{1,0:T(8,128)(2,1)S(1)}, bf16[64,2304]{1,0:T(8,128)(2,1)S(1)}, u32[]{:S(2)}, u32[]{:S(2)}) collective-permute-start(bf16[64,2304]{1,0:T(8,128)(2,1)S(1)} %collective-permute-done.2.refs_7_), channel_id=1, source_target_pairs={{8,0},{16,8},{24,16},{28,24},{20,28},{12,20},{4,12},{0,4},{9,1},{1... | collective-permute-start | bytes 884744 | tf_op jit(solution)/shard_map/ppermute | solution.py:61
  22.9 8.0 %collective-permute-start.6 = (bf16[64,2304]{1,0:T(8,128)(2,1)}, bf16[64,2304]{1,0:T(8,128)(2,1)S(1)}, u32[]{:S(2)}, u32[]{:S(2)}) collective-permute-start(bf16[64,2304]{1,0:T(8,128)(2,1)} %bitcast.7), channel_id=1, source_target_pairs={{0,8},{8,16},{16,24},{24,28},{28,20},{20,12},{12,4},{4,0},{1,9},{9... | collective-permute-start | bytes 884744 | tf_op jit(solution)/shard_map/ppermute | solution.py:61
  24.5 8.0 %collective-permute-start.7 = (bf16[64,2304]{1,0:T(8,128)(2,1)}, bf16[64,2304]{1,0:T(8,128)(2,1)S(1)}, u32[]{:S(2)}, u32[]{:S(2)}) collective-permute-start(bf16[64,2304]{1,0:T(8,128)(2,1)} %bitcast.8), channel_id=1, source_target_pairs={{8,0},{16,8},{24,16},{28,24},{20,28},{12,20},{4,12},{0,4},{9,1},{1... | collective-permute-start | bytes 884744 | tf_op jit(solution)/shard_map/ppermute | solution.py:61
  24.9 12.3 %collective-permute-start.18 = (bf16[64,2304]{1,0:T(8,128)(2,1)S(1)}, bf16[64,2304]{1,0:T(8,128)(2,1)S(1)}, u32[]{:S(2)}, u32[]{:S(2)}) collective-permute-start(bf16[64,2304]{1,0:T(8,128)(2,1)S(1)} %collective-permute-done.4.refs_2_), channel_id=1, source_target_pairs={{0,8},{8,16},{16,24},{24,28},{28,20},{20,12},{12,4},{4,0},{1,9},{9... | collective-permute-start | bytes 884744 | tf_op jit(solution)/shard_map/ppermute | solution.py:61
  26.5 12.3 %collective-permute-start.19 = (bf16[64,2304]{1,0:T(8,128)(2,1)S(1)}, bf16[64,2304]{1,0:T(8,128)(2,1)S(1)}, u32[]{:S(2)}, u32[]{:S(2)}) collective-permute-start(bf16[64,2304]{1,0:T(8,128)(2,1)S(1)} %collective-permute-done.5.refs_6_), channel_id=1, source_target_pairs={{8,0},{16,8},{24,16},{28,24},{20,28},{12,20},{4,12},{0,4},{9,1},{1... | collective-permute-start | bytes 884744 | tf_op jit(solution)/shard_map/ppermute | solution.py:61
  26.9 14.1 %collective-permute-start.12 = (bf16[64,2304]{1,0:T(8,128)(2,1)}, bf16[64,2304]{1,0:T(8,128)(2,1)S(1)}, u32[]{:S(2)}, u32[]{:S(2)}) collective-permute-start(bf16[64,2304]{1,0:T(8,128)(2,1)} %bitcast.15), channel_id=1, source_target_pairs={{0,1},{1,0},{2,3},{3,2},{4,5},{5,4},{6,7},{7,6},{8,9},{9,8},{10,11... | collective-permute-start | bytes 884744 | tf_op jit(solution)/shard_map/ppermute | solution.py:82
  32.5 9.0 %collective-permute-start.8 = (bf16[64,2304]{1,0:T(8,128)(2,1)S(1)}, bf16[64,2304]{1,0:T(8,128)(2,1)S(1)}, u32[]{:S(2)}, u32[]{:S(2)}) collective-permute-start(bf16[64,2304]{1,0:T(8,128)(2,1)S(1)} %collective-permute-done.6.refs_1_), channel_id=1, source_target_pairs={{0,8},{8,16},{16,24},{24,28},{28,20},{20,12},{12,4},{4,0},{1,9},{9... | collective-permute-start | bytes 884744 | tf_op jit(solution)/shard_map/ppermute | solution.py:61
  33.7 9.5 %collective-permute-start.9 = (bf16[64,2304]{1,0:T(8,128)(2,1)S(1)}, bf16[64,2304]{1,0:T(8,128)(2,1)S(1)}, u32[]{:S(2)}, u32[]{:S(2)}) collective-permute-start(bf16[64,2304]{1,0:T(8,128)(2,1)S(1)} %collective-permute-done.7.refs_7_), channel_id=1, source_target_pairs={{8,0},{16,8},{24,16},{28,24},{20,28},{12,20},{4,12},{0,4},{9,1},{1... | collective-permute-start | bytes 884744 | tf_op jit(solution)/shard_map/ppermute | solution.py:61
  38.8 5.9 %collective-permute-start.21 = (bf16[32,2304]{1,0:T(8,128)(2,1)S(1)}, bf16[32,2304]{1,0:T(8,128)(2,1)S(1)}, u32[]{:S(2)}, u32[]{:S(2)}) collective-permute-start(bf16[32,2304]{1,0:T(8,128)(2,1)S(1)} %slice.15), channel_id=1, source_target_pairs={{8,0},{16,8},{24,16},{28,24},{20,28},{12,20},{4,12},{0,4},{9,1},{1... | collective-permute-start | bytes 442376 | tf_op jit(solution)/shard_map/ppermute | solution.py:61
  39.2 20.4 %copy-start.4 = (s32[4]{0:T(128)S(1)}, s32[4]{0:T(128)}, u32[]{:S(2)}) copy-start(s32[4]{0:T(128)} %owner.5) | copy-start | bytes 52
  39.2 20.4 %copy-start = (bf16[1,64,2304]{2,1,0:T(8,128)(2,1)S(1)}, bf16[1,64,2304]{2,1,0:T(8,128)(2,1)}, u32[]{:S(2)}) copy-start(bf16[1,64,2304]{2,1,0:T(8,128)(2,1)} %param.11) | copy-start | bytes 884740
  39.2 7.1 %collective-permute-start.20 = (bf16[32,2304]{1,0:T(8,128)(2,1)S(1)}, bf16[32,2304]{1,0:T(8,128)(2,1)S(1)}, u32[]{:S(2)}, u32[]{:S(2)}) collective-permute-start(bf16[32,2304]{1,0:T(8,128)(2,1)S(1)} %slice.14), channel_id=1, source_target_pairs={{0,8},{8,16},{16,24},{24,28},{28,20},{20,12},{12,4},{4,0},{1,9},{9... | collective-permute-start | bytes 442376 | tf_op jit(solution)/shard_map/ppermute | solution.py:61
  41.0 8.2 %collective-permute-start.14 = (bf16[64,2304]{1,0:T(8,128)(2,1)}, bf16[64,2304]{1,0:T(8,128)(2,1)S(1)}, u32[]{:S(2)}, u32[]{:S(2)}) collective-permute-start(bf16[64,2304]{1,0:T(8,128)(2,1)} %bitcast.9), channel_id=1, source_target_pairs={{0,1},{1,0},{2,3},{3,2},{4,5},{5,4},{6,7},{7,6},{8,9},{9,8},{10,11... | collective-permute-start | bytes 884744 | tf_op jit(solution)/shard_map/ppermute | solution.py:82
  41.5 7.7 %collective-permute-start.13 = (bf16[64,2304]{1,0:T(8,128)(2,1)S(1)}, bf16[64,2304]{1,0:T(8,128)(2,1)S(1)}, u32[]{:S(2)}, u32[]{:S(2)}) collective-permute-start(bf16[64,2304]{1,0:T(8,128)(2,1)S(1)} %collective-permute-done.3.refs_2_), channel_id=1, source_target_pairs={{0,1},{1,0},{2,3},{3,2},{4,5},{5,4},{6,7},{7,6},{8,9},{9,8},{10,11... | collective-permute-start | bytes 884744 | tf_op jit(solution)/shard_map/ppermute | solution.py:82
  43.2 7.7 %collective-permute-start.15 = (bf16[64,2304]{1,0:T(8,128)(2,1)S(1)}, bf16[64,2304]{1,0:T(8,128)(2,1)S(1)}, u32[]{:S(2)}, u32[]{:S(2)}) collective-permute-start(bf16[64,2304]{1,0:T(8,128)(2,1)S(1)} %collective-permute-done.refs_11_), channel_id=1, source_target_pairs={{0,1},{1,0},{2,3},{3,2},{4,5},{5,4},{6,7},{7,6},{8,9},{9,8},{10,11... | collective-permute-start | bytes 884744 | tf_op jit(solution)/shard_map/ppermute | solution.py:82
  44.7 7.8 %collective-permute-start.10 = (bf16[64,2304]{1,0:T(8,128)(2,1)S(1)}, bf16[64,2304]{1,0:T(8,128)(2,1)S(1)}, u32[]{:S(2)}, u32[]{:S(2)}) collective-permute-start(bf16[64,2304]{1,0:T(8,128)(2,1)S(1)} %collective-permute-done.8.refs_2_), channel_id=1, source_target_pairs={{0,8},{8,16},{16,24},{24,28},{28,20},{20,12},{12,4},{4,0},{1,9},{9... | collective-permute-start | bytes 884744 | tf_op jit(solution)/shard_map/ppermute | solution.py:61
  46.3 7.6 %collective-permute-start.11 = (bf16[64,2304]{1,0:T(8,128)(2,1)S(1)}, bf16[64,2304]{1,0:T(8,128)(2,1)S(1)}, u32[]{:S(2)}, u32[]{:S(2)}) collective-permute-start(bf16[64,2304]{1,0:T(8,128)(2,1)S(1)} %collective-permute-done.9.refs_6_), channel_id=1, source_target_pairs={{8,0},{16,8},{24,16},{28,24},{20,28},{12,20},{4,12},{0,4},{9,1},{1... | collective-permute-start | bytes 884744 | tf_op jit(solution)/shard_map/ppermute | solution.py:61
  46.8 1.0 copy-start.1
  47.7 0.7 copy-start.3
  49.2 13.4 %collective-permute-start.22 = (bf16[64,2304]{1,0:T(8,128)(2,1)S(1)}, bf16[64,2304]{1,0:T(8,128)(2,1)S(1)}, u32[]{:S(2)}, u32[]{:S(2)}) collective-permute-start(bf16[64,2304]{1,0:T(8,128)(2,1)S(1)} %get-tuple-element.60), channel_id=1, source_target_pairs={{0,1},{1,0},{2,3},{3,2},{4,5},{5,4},{6,7},{7,6},{8,9},{9,8},{10,11... | collective-permute-start | bytes 884744 | tf_op jit(solution)/shard_map/ppermute | solution.py:82
  49.3 16.1 %collective-permute-start.23 = (bf16[64,2304]{1,0:T(8,128)(2,1)S(1)}, bf16[64,2304]{1,0:T(8,128)(2,1)S(1)}, u32[]{:S(2)}, u32[]{:S(2)}) collective-permute-start(bf16[64,2304]{1,0:T(8,128)(2,1)S(1)} %get-tuple-element.61), channel_id=1, source_target_pairs={{0,2},{1,3},{2,0},{3,1},{4,6},{5,7},{6,4},{7,5},{8,10},{9,11},{10,... | collective-permute-start | bytes 884744 | tf_op jit(solution)/shard_map/ppermute | solution.py:82
  50.9 14.5 %collective-permute-start.24 = (bf16[64,2304]{1,0:T(8,128)(2,1)S(1)}, bf16[64,2304]{1,0:T(8,128)(2,1)S(1)}, u32[]{:S(2)}, u32[]{:S(2)}) collective-permute-start(bf16[64,2304]{1,0:T(8,128)(2,1)S(1)} %get-tuple-element.62), channel_id=1, source_target_pairs={{0,3},{1,2},{2,1},{3,0},{4,7},{5,6},{6,5},{7,4},{8,11},{9,10},{10,... | collective-permute-start | bytes 884744 | tf_op jit(solution)/shard_map/ppermute | solution.py:82
  53.9 5.2 %collective-permute-start.17 = (bf16[32,2304]{1,0:T(8,128)(2,1)S(1)}, bf16[32,2304]{1,0:T(8,128)(2,1)S(1)}, u32[]{:S(2)}, u32[]{:S(2)}) collective-permute-start(bf16[32,2304]{1,0:T(8,128)(2,1)S(1)} %slice.13), channel_id=1, source_target_pairs={{8,0},{16,8},{24,16},{28,24},{20,28},{12,20},{4,12},{0,4},{9,1},{1... | collective-permute-start | bytes 442376 | tf_op jit(solution)/shard_map/ppermute | solution.py:61
  54.4 5.1 %collective-permute-start.16 = (bf16[32,2304]{1,0:T(8,128)(2,1)S(1)}, bf16[32,2304]{1,0:T(8,128)(2,1)S(1)}, u32[]{:S(2)}, u32[]{:S(2)}) collective-permute-start(bf16[32,2304]{1,0:T(8,128)(2,1)S(1)} %slice.12), channel_id=1, source_target_pairs={{0,8},{8,16},{16,24},{24,28},{28,20},{20,12},{12,4},{4,0},{1,9},{9... | collective-permute-start | bytes 442376 | tf_op jit(solution)/shard_map/ppermute | solution.py:61
  57.3 5.6 %copy-start.2 = (bf16[1,64,2304]{2,1,0:T(8,128)(2,1)S(1)}, bf16[1,64,2304]{2,1,0:T(8,128)(2,1)}, u32[]{:S(2)}) copy-start(bf16[1,64,2304]{2,1,0:T(8,128)(2,1)} %param.10) | copy-start | bytes 884740
  57.3 5.5 %copy-start.5 = (bf16[1,1,2304,256]{3,2,1,0:T(8,128)(2,1)S(1)}, bf16[1,1,2304,256]{3,2,1,0:T(8,128)(2,1)}, u32[]{:S(2)}) copy-start(bf16[1,1,2304,256]{3,2,1,0:T(8,128)(2,1)} %param.8) | copy-start | bytes 3538948
  57.3 5.5 %copy-start.6 = (bf16[1,1,2304,256]{3,2,1,0:T(8,128)(2,1)S(1)}, bf16[1,1,2304,256]{3,2,1,0:T(8,128)(2,1)}, u32[]{:S(2)}) copy-start(bf16[1,1,2304,256]{3,2,1,0:T(8,128)(2,1)} %param.9) | copy-start | bytes 3538948
  60.9 4.5 %collective-permute-start.25 = (bf16[64,256]{1,0:T(8,128)(2,1)S(1)}, bf16[64,256]{1,0:T(8,128)(2,1)S(1)}, u32[]{:S(2)}, u32[]{:S(2)}) collective-permute-start(bf16[64,256]{1,0:T(8,128)(2,1)S(1)} %get-tuple-element.63), channel_id=1, source_target_pairs={{0,1},{1,0},{2,3},{3,2},{4,5},{5,4},{6,7},{7,6},{8,9},{9,8},{10,11... | collective-permute-start | bytes 98312 | tf_op jit(solution)/shard_map/ppermute | solution.py:82
  61.0 4.9 %collective-permute-start.26 = (bf16[64,256]{1,0:T(8,128)(2,1)S(1)}, bf16[64,256]{1,0:T(8,128)(2,1)S(1)}, u32[]{:S(2)}, u32[]{:S(2)}) collective-permute-start(bf16[64,256]{1,0:T(8,128)(2,1)S(1)} %get-tuple-element.64), channel_id=1, source_target_pairs={{0,2},{1,3},{2,0},{3,1},{4,6},{5,7},{6,4},{7,5},{8,10},{9,11},{10,... | collective-permute-start | bytes 98312 | tf_op jit(solution)/shard_map/ppermute | solution.py:82
  62.6 3.7 %collective-permute-start.27 = (bf16[64,256]{1,0:T(8,128)(2,1)S(1)}, bf16[64,256]{1,0:T(8,128)(2,1)S(1)}, u32[]{:S(2)}, u32[]{:S(2)}) collective-permute-start(bf16[64,256]{1,0:T(8,128)(2,1)S(1)} %get-tuple-element.65), channel_id=1, source_target_pairs={{0,3},{1,2},{2,1},{3,0},{4,7},{5,6},{6,5},{7,4},{8,11},{9,10},{10,... | collective-permute-start | bytes 98312 | tf_op jit(solution)/shard_map/ppermute | solution.py:82
  62.9 3.4 %copy-start.7 = (s32[8]{0:T(128)S(1)}, s32[8]{0:T(128)}, u32[]{:S(2)}) copy-start(s32[8]{0:T(128)} %panel.1) | copy-start | bytes 100

commit v8 on v7

--- a/solution.py
+++ b/solution.py
@@ -337,7 +337,7 @@
     out = jax.ShapeDtypeStruct((rows, rank), BF16)
     square = pltpu.VMEM((rank, rank), F32)
     tall, wide = pltpu.VMEM((rows, rank), BF16), pltpu.VMEM((rank, rows), BF16)
-    tiles = rows // 256 if rows % 256 == 0 else 1
+    tiles = rows // 384 if rows % 384 == 0 else 1
     fresh_basis, fresh_coeffs = pl.pallas_call(
         functools.partial(finish, n_col),
         out_shape=(out, out),

time: 137 us -> 137 us (level)
  no operation moved by 1% of the time
where the time goes in v8:
time: 137 us
  Pallas kernels  75 us (55%)
  waiting for transfers between devices  34.5 us (25%)
  starting transfers between devices  23.3 us (17%)
  between operations  2.09 us (2%)
  local copies, waits for them, and re-layouts  1.69 us (1%)
    pallas_call x1, Pallas kernels, body(): pl.pallas_call(functools.partial(finish, n_col), out_shape=(out, out), in...  70.4 us
    ppermute x16, waiting for transfers between devices, step(): fwd, bwd = (lax.ppermute(fwd, axis, ahead), lax.ppermute(bwd, axis, back))  29.4 us
    ppermute x16, starting transfers between devices, step(): fwd, bwd = (lax.ppermute(fwd, axis, ahead), lax.ppermute(bwd, axis, back))  17.4 us
    ppermute x12, starting transfers between devices, swap(): return lax.ppermute(x, axis, [(i, i ^ m) for i in range(n)])  5.9 us
    ppermute x12, waiting for transfers between devices, swap(): return lax.ppermute(x, axis, [(i, i ^ m) for i in range(n)])  5.18 us
  transfers between devices with their start and end apart: 28, of which 19 were waited for; matrix products, arithmetic and copies ran while one was open for 0% of the time, Pallas kernels for 3%

profile of v8, /device:TPU:0, one launch (start us, length us, event | category | flops | bytes accessed | tf_op | source)
XLA Modules:
  0.0 136.7 jit_solution(3858477610677675740)
XLA Ops:
  0.6 3.1 %collective-permute-start.1 = (bf16[64,2304]{1,0:T(8,128)(2,1)}, bf16[64,2304]{1,0:T(8,128)(2,1)S(1)}, u32[]{:S(2)}, u32[]{:S(2)}) collective-permute-start(bf16[64,2304]{1,0:T(8,128)(2,1)} %bitcast.12), channel_id=1, source_target_pairs={{0,8},{8,16},{16,24},{24,28},{28,20},{20,12},{12,4},{4,0},{1,9},{9... | collective-permute-start | bytes 884744 | tf_op jit(solution)/shard_map/ppermute | solution.py:61
  3.7 0.0 collective-permute-start.2
  3.7 1.9 %collective-permute-start.3 = (bf16[64,2304]{1,0:T(8,128)(2,1)}, bf16[64,2304]{1,0:T(8,128)(2,1)S(1)}, u32[]{:S(2)}, u32[]{:S(2)}) collective-permute-start(bf16[64,2304]{1,0:T(8,128)(2,1)} %bitcast.14), channel_id=1, source_target_pairs={{0,2},{1,3},{2,0},{3,1},{4,6},{5,7},{6,4},{7,5},{8,10},{9,11},{10,... | collective-permute-start | bytes 884744 | tf_op jit(solution)/shard_map/ppermute | solution.py:82
  5.6 0.1 collective-permute-start
  5.7 5.1 %collective-permute-done.1.refs_1_ = bf16[64,2304]{1,0:T(8,128)(2,1)S(1)} collective-permute-done((bf16[64,2304]{1,0:T(8,128)(2,1)}, bf16[64,2304]{1,0:T(8,128)(2,1)S(1)}, u32[]{:S(2)}, u32[]{:S(2)}) %collective-permute-start.1) | collective-permute-done | bytes 294944 | tf_op jit(solution)/shard_map/ppermute | solution.py:61
  10.9 1.5 %collective-permute-done.2.refs_7_ = bf16[64,2304]{1,0:T(8,128)(2,1)S(1)} collective-permute-done((bf16[64,2304]{1,0:T(8,128)(2,1)}, bf16[64,2304]{1,0:T(8,128)(2,1)S(1)}, u32[]{:S(2)}, u32[]{:S(2)}) %collective-permute-start.2) | collective-permute-done | bytes 294944 | tf_op jit(solution)/shard_map/ppermute | solution.py:61
  12.4 1.5 %collective-permute-done.3.refs_2_ = bf16[64,2304]{1,0:T(8,128)(2,1)S(1)} collective-permute-done((bf16[64,2304]{1,0:T(8,128)(2,1)}, bf16[64,2304]{1,0:T(8,128)(2,1)S(1)}, u32[]{:S(2)}, u32[]{:S(2)}) %collective-permute-start.3) | collective-permute-done | bytes 294944 | tf_op jit(solution)/shard_map/ppermute | solution.py:82
  13.9 2.0 %collective-permute-start.4 = (bf16[64,2304]{1,0:T(8,128)(2,1)S(1)}, bf16[64,2304]{1,0:T(8,128)(2,1)S(1)}, u32[]{:S(2)}, u32[]{:S(2)}) collective-permute-start(bf16[64,2304]{1,0:T(8,128)(2,1)S(1)} %collective-permute-done.1.refs_1_), channel_id=1, source_target_pairs={{0,8},{8,16},{16,24},{24,28},{28,20},{20,12},{12,4},{4,0},{1,9},{9... | collective-permute-start | bytes 884744 | tf_op jit(solution)/shard_map/ppermute | solution.py:61
  15.9 0.0 collective-permute-start.5
  15.9 2.8 %collective-permute-done.refs_11_ = bf16[64,2304]{1,0:T(8,128)(2,1)S(1)} collective-permute-done((bf16[64,2304]{1,0:T(8,128)(2,1)}, bf16[64,2304]{1,0:T(8,128)(2,1)S(1)}, u32[]{:S(2)}, u32[]{:S(2)}) %collective-permute-start) | collective-permute-done | bytes 294944 | tf_op jit(solution)/shard_map/ppermute | solution.py:82
  18.7 1.9 %collective-permute-done.4.refs_2_ = bf16[64,2304]{1,0:T(8,128)(2,1)S(1)} collective-permute-done((bf16[64,2304]{1,0:T(8,128)(2,1)S(1)}, bf16[64,2304]{1,0:T(8,128)(2,1)S(1)}, u32[]{:S(2)}, u32[]{:S(2)}) %collective-permute-start.4) | collective-permute-done | bytes 294944 | tf_op jit(solution)/shard_map/ppermute | solution.py:61
  20.6 2.3 %collective-permute-done.5.refs_6_ = bf16[64,2304]{1,0:T(8,128)(2,1)S(1)} collective-permute-done((bf16[64,2304]{1,0:T(8,128)(2,1)S(1)}, bf16[64,2304]{1,0:T(8,128)(2,1)S(1)}, u32[]{:S(2)}, u32[]{:S(2)}) %collective-permute-start.5) | collective-permute-done | bytes 294944 | tf_op jit(solution)/shard_map/ppermute | solution.py:61
  22.9 1.6 %collective-permute-start.6 = (bf16[64,2304]{1,0:T(8,128)(2,1)}, bf16[64,2304]{1,0:T(8,128)(2,1)S(1)}, u32[]{:S(2)}, u32[]{:S(2)}) collective-permute-start(bf16[64,2304]{1,0:T(8,128)(2,1)} %bitcast.7), channel_id=1, source_target_pairs={{0,8},{8,16},{16,24},{24,28},{28,20},{20,12},{12,4},{4,0},{1,9},{9... | collective-permute-start | bytes 884744 | tf_op jit(solution)/shard_map/ppermute | solution.py:61
  24.5 0.4 collective-permute-start.7
  24.9 1.6 %collective-permute-start.18 = (bf16[64,2304]{1,0:T(8,128)(2,1)S(1)}, bf16[64,2304]{1,0:T(8,128)(2,1)S(1)}, u32[]{:S(2)}, u32[]{:S(2)}) collective-permute-start(bf16[64,2304]{1,0:T(8,128)(2,1)S(1)} %collective-permute-done.4.refs_2_), channel_id=1, source_target_pairs={{0,8},{8,16},{16,24},{24,28},{28,20},{20,12},{12,4},{4,0},{1,9},{9... | collective-permute-start | bytes 884744 | tf_op jit(solution)/shard_map/ppermute | solution.py:61
  26.5 0.4 collective-permute-start.19
  26.9 0.0 collective-permute-start.12
  26.9 4.0 %collective-permute-done.6.refs_1_ = bf16[64,2304]{1,0:T(8,128)(2,1)S(1)} collective-permute-done((bf16[64,2304]{1,0:T(8,128)(2,1)}, bf16[64,2304]{1,0:T(8,128)(2,1)S(1)}, u32[]{:S(2)}, u32[]{:S(2)}) %collective-permute-start.6) | collective-permute-done | bytes 294944 | tf_op jit(solution)/shard_map/ppermute | solution.py:61
  30.9 1.6 %collective-permute-done.7.refs_7_ = bf16[64,2304]{1,0:T(8,128)(2,1)S(1)} collective-permute-done((bf16[64,2304]{1,0:T(8,128)(2,1)}, bf16[64,2304]{1,0:T(8,128)(2,1)S(1)}, u32[]{:S(2)}, u32[]{:S(2)}) %collective-permute-start.7) | collective-permute-done | bytes 294944 | tf_op jit(solution)/shard_map/ppermute | solution.py:61
  32.5 1.2 collective-permute-start.8
  33.7 0.9 collective-permute-start.9
  34.5 2.7 %collective-permute-done.18.refs_3_ = bf16[64,2304]{1,0:T(8,128)(2,1)S(1)} collective-permute-done((bf16[64,2304]{1,0:T(8,128)(2,1)S(1)}, bf16[64,2304]{1,0:T(8,128)(2,1)S(1)}, u32[]{:S(2)}, u32[]{:S(2)}) %collective-permute-start.18) | collective-permute-done | bytes 294944 | tf_op jit(solution)/shard_map/ppermute | solution.py:61
  37.2 1.6 %collective-permute-done.19.refs_5_ = bf16[64,2304]{1,0:T(8,128)(2,1)S(1)} collective-permute-done((bf16[64,2304]{1,0:T(8,128)(2,1)S(1)}, bf16[64,2304]{1,0:T(8,128)(2,1)S(1)}, u32[]{:S(2)}, u32[]{:S(2)}) %collective-permute-start.19) | collective-permute-done | bytes 294944 | tf_op jit(solution)/shard_map/ppermute | solution.py:61
  38.8 0.3 collective-permute-start.21
  39.2 0.0 copy-start
  39.2 1.8 %collective-permute-start.20 = (bf16[32,2304]{1,0:T(8,128)(2,1)S(1)}, bf16[32,2304]{1,0:T(8,128)(2,1)S(1)}, u32[]{:S(2)}, u32[]{:S(2)}) collective-permute-start(bf16[32,2304]{1,0:T(8,128)(2,1)S(1)} %slice.14), channel_id=1, source_target_pairs={{0,8},{8,16},{16,24},{24,28},{28,20},{20,12},{12,4},{4,0},{1,9},{9... | collective-permute-start | bytes 442376 | tf_op jit(solution)/shard_map/ppermute | solution.py:61
  41.0 0.0 collective-permute-done.12.refs_1_
  41.0 0.0 collective-permute-start.14
  41.0 0.5 collective-permute-done.8.refs_2_
  41.5 0.0 collective-permute-start.13
  41.5 1.6 %collective-permute-done.9.refs_6_ = bf16[64,2304]{1,0:T(8,128)(2,1)S(1)} collective-permute-done((bf16[64,2304]{1,0:T(8,128)(2,1)S(1)}, bf16[64,2304]{1,0:T(8,128)(2,1)S(1)}, u32[]{:S(2)}, u32[]{:S(2)}) %collective-permute-start.9) | collective-permute-done | bytes 294944 | tf_op jit(solution)/shard_map/ppermute | solution.py:61
  43.2 0.0 collective-permute-start.15
  43.2 1.6 %collective-permute-done.21.refs_8_ = bf16[32,2304]{1,0:T(8,128)(2,1)S(1)} collective-permute-done((bf16[32,2304]{1,0:T(8,128)(2,1)S(1)}, bf16[32,2304]{1,0:T(8,128)(2,1)S(1)}, u32[]{:S(2)}, u32[]{:S(2)}) %collective-permute-start.21) | collective-permute-done | bytes 147488 | tf_op jit(solution)/shard_map/ppermute | solution.py:61
  44.7 1.6 %collective-permute-start.10 = (bf16[64,2304]{1,0:T(8,128)(2,1)S(1)}, bf16[64,2304]{1,0:T(8,128)(2,1)S(1)}, u32[]{:S(2)}, u32[]{:S(2)}) collective-permute-start(bf16[64,2304]{1,0:T(8,128)(2,1)S(1)} %collective-permute-done.8.refs_2_), channel_id=1, source_target_pairs={{0,8},{8,16},{16,24},{24,28},{28,20},{20,12},{12,4},{4,0},{1,9},{9... | collective-permute-start | bytes 884744 | tf_op jit(solution)/shard_map/ppermute | solution.py:61
  46.3 0.0 collective-permute-done.20.refs_4_
  46.3 0.4 collective-permute-start.11
  46.8 1.0 copy-done.1
  47.7 0.7 copy-done.3
  48.4 0.8 pick_left.1
  49.2 0.0 collective-permute-done.14.refs_10_
  49.2 0.1 collective-permute-start.22
  49.3 0.0 collective-permute-done.13.refs_3_
  49.3 1.6 %collective-permute-start.23 = (bf16[64,2304]{1,0:T(8,128)(2,1)S(1)}, bf16[64,2304]{1,0:T(8,128)(2,1)S(1)}, u32[]{:S(2)}, u32[]{:S(2)}) collective-permute-start(bf16[64,2304]{1,0:T(8,128)(2,1)S(1)} %get-tuple-element.61), channel_id=1, source_target_pairs={{0,2},{1,3},{2,0},{3,1},{4,6},{5,7},{6,4},{7,5},{8,10},{9,11},{10,... | collective-permute-start | bytes 884744 | tf_op jit(solution)/shard_map/ppermute | solution.py:82
  50.9 0.0 collective-permute-done.15.refs_12_
  50.9 0.3 collective-permute-start.24
  51.1 1.4 %collective-permute-done.10.refs_3_ = bf16[64,2304]{1,0:T(8,128)(2,1)S(1)} collective-permute-done((bf16[64,2304]{1,0:T(8,128)(2,1)S(1)}, bf16[64,2304]{1,0:T(8,128)(2,1)S(1)}, u32[]{:S(2)}, u32[]{:S(2)}) %collective-permute-start.10) | collective-permute-done | bytes 294944 | tf_op jit(solution)/shard_map/ppermute | solution.py:61
  52.6 1.3 collective-permute-done.11.refs_5_
  53.9 0.5 collective-permute-start.17
  54.4 1.6 %collective-permute-start.16 = (bf16[32,2304]{1,0:T(8,128)(2,1)S(1)}, bf16[32,2304]{1,0:T(8,128)(2,1)S(1)}, u32[]{:S(2)}, u32[]{:S(2)}) collective-permute-start(bf16[32,2304]{1,0:T(8,128)(2,1)S(1)} %slice.12), channel_id=1, source_target_pairs={{0,8},{8,16},{16,24},{24,28},{28,20},{20,12},{12,4},{4,0},{1,9},{9... | collective-permute-start | bytes 442376 | tf_op jit(solution)/shard_map/ppermute | solution.py:61
  57.3 0.0 copy-start.2
  57.3 0.0 copy-start.5
  57.3 0.0 copy-start.6
  57.4 1.8 %collective-permute-done.17.refs_8_ = bf16[32,2304]{1,0:T(8,128)(2,1)S(1)} collective-permute-done((bf16[32,2304]{1,0:T(8,128)(2,1)S(1)}, bf16[32,2304]{1,0:T(8,128)(2,1)S(1)}, u32[]{:S(2)}, u32[]{:S(2)}) %collective-permute-start.17) | collective-permute-done | bytes 147488 | tf_op jit(solution)/shard_map/ppermute | solution.py:61
  59.1 0.4 collective-permute-done.16.refs_4_
  59.6 1.3 coupling.1
  60.9 0.1 collective-permute-start.25
  61.0 1.6 %collective-permute-start.26 = (bf16[64,256]{1,0:T(8,128)(2,1)S(1)}, bf16[64,256]{1,0:T(8,128)(2,1)S(1)}, u32[]{:S(2)}, u32[]{:S(2)}) collective-permute-start(bf16[64,256]{1,0:T(8,128)(2,1)S(1)} %get-tuple-element.64), channel_id=1, source_target_pairs={{0,2},{1,3},{2,0},{3,1},{4,6},{5,7},{6,4},{7,5},{8,10},{9,11},{10,... | collective-permute-start | bytes 98312 | tf_op jit(solution)/shard_map/ppermute | solution.py:82
  62.6 0.3 collective-permute-start.27
  62.9 2.5 %grams.1 = (bf16[512,256]{1,0:T(8,128)(2,1)S(1)}, bf16[512,256]{1,0:T(8,128)(2,1)S(1)}, bf16[256,256]{1,0:T(8,128)(2,1)S(1)}, f32[512,256]{1,0:T(8,128)S(1)}, f3...) custom-call(s32[1,1]{1,0:T(1,128)S(6)} %copy.10.old_ref, s32[1,1]{1,0:T(1,128)S(6)} %copy.11.goal_ref, ...), custom_call_target="tpu_custom_call" | custom-call | flops 1207959552 | bytes 6291456 | tf_op jit(solution)/shard_map/grams/pallas_call | solution.py:182
  65.4 0.0 collective-permute-done.24.refs_3_
  65.4 0.0 collective-permute-done.25.refs_5_
  65.4 0.4 collective-permute-done.26.refs_6_
  65.8 0.4 collective-permute-done.27.refs_7_
  66.3 70.4 %finish.1 = (bf16[2304,256]{1,0:T(8,128)(2,1)}, bf16[2304,256]{1,0:T(8,128)(2,1)}) custom-call(s32[1,1]{1,0:T(1,128)S(6)} %copy.10.old_ref, s32[1,1]{1,0:T(1,128)S(6)} %copy.11.goal_ref, s32[8]{0:T(128)S(1)} %copy-done.7, s32[4]{0:T(128)S(1)} %copy-done.4, bf16[2304,256]{1,0:T(8,128)(2,1)S(1)} %bitcast.19, bf16[2304,256]{1,0:T(8,128)(2,1)S(1)} %bitcast.21, ...), custom_call_target="tpu_custom_call" | custom-call | flops 8589934592 | bytes 12582912 | tf_op jit(solution)/shard_map/finish/pallas_call | solution.py:341
  (16 shorter events, 0.1 us)
Async XLA Ops:
  0.6 10.2 %collective-permute-start.1 = (bf16[64,2304]{1,0:T(8,128)(2,1)}, bf16[64,2304]{1,0:T(8,128)(2,1)S(1)}, u32[]{:S(2)}, u32[]{:S(2)}) collective-permute-start(bf16[64,2304]{1,0:T(8,128)(2,1)} %bitcast.12), channel_id=1, source_target_pairs={{0,8},{8,16},{16,24},{24,28},{28,20},{20,12},{12,4},{4,0},{1,9},{9... | collective-permute-start | bytes 884744 | tf_op jit(solution)/shard_map/ppermute | solution.py:61
  3.7 8.7 %collective-permute-start.2 = (bf16[64,2304]{1,0:T(8,128)(2,1)}, bf16[64,2304]{1,0:T(8,128)(2,1)S(1)}, u32[]{:S(2)}, u32[]{:S(2)}) collective-permute-start(bf16[64,2304]{1,0:T(8,128)(2,1)} %bitcast.13), channel_id=1, source_target_pairs={{8,0},{16,8},{24,16},{28,24},{20,28},{12,20},{4,12},{0,4},{9,1},{1... | collective-permute-start | bytes 884744 | tf_op jit(solution)/shard_map/ppermute | solution.py:61
  3.7 10.1 %collective-permute-start.3 = (bf16[64,2304]{1,0:T(8,128)(2,1)}, bf16[64,2304]{1,0:T(8,128)(2,1)S(1)}, u32[]{:S(2)}, u32[]{:S(2)}) collective-permute-start(bf16[64,2304]{1,0:T(8,128)(2,1)} %bitcast.14), channel_id=1, source_target_pairs={{0,2},{1,3},{2,0},{3,1},{4,6},{5,7},{6,4},{7,5},{8,10},{9,11},{10,... | collective-permute-start | bytes 884744 | tf_op jit(solution)/shard_map/ppermute | solution.py:82
  5.6 13.1 %collective-permute-start = (bf16[64,2304]{1,0:T(8,128)(2,1)}, bf16[64,2304]{1,0:T(8,128)(2,1)S(1)}, u32[]{:S(2)}, u32[]{:S(2)}) collective-permute-start(bf16[64,2304]{1,0:T(8,128)(2,1)} %bitcast.6), channel_id=1, source_target_pairs={{0,2},{1,3},{2,0},{3,1},{4,6},{5,7},{6,4},{7,5},{8,10},{9,11},{10,... | collective-permute-start | bytes 884744 | tf_op jit(solution)/shard_map/ppermute | solution.py:82
  13.9 6.7 %collective-permute-start.4 = (bf16[64,2304]{1,0:T(8,128)(2,1)S(1)}, bf16[64,2304]{1,0:T(8,128)(2,1)S(1)}, u32[]{:S(2)}, u32[]{:S(2)}) collective-permute-start(bf16[64,2304]{1,0:T(8,128)(2,1)S(1)} %collective-permute-done.1.refs_1_), channel_id=1, source_target_pairs={{0,8},{8,16},{16,24},{24,28},{28,20},{20,12},{12,4},{4,0},{1,9},{9... | collective-permute-start | bytes 884744 | tf_op jit(solution)/shard_map/ppermute | solution.py:61
  15.9 7.0 %collective-permute-start.5 = (bf16[64,2304]{1,0:T(8,128)(2,1)S(1)}, bf16[64,2304]{1,0:T(8,128)(2,1)S(1)}, u32[]{:S(2)}, u32[]{:S(2)}) collective-permute-start(bf16[64,2304]{1,0:T(8,128)(2,1)S(1)} %collective-permute-done.2.refs_7_), channel_id=1, source_target_pairs={{8,0},{16,8},{24,16},{28,24},{20,28},{12,20},{4,12},{0,4},{9,1},{1... | collective-permute-start | bytes 884744 | tf_op jit(solution)/shard_map/ppermute | solution.py:61
  22.9 8.0 %collective-permute-start.6 = (bf16[64,2304]{1,0:T(8,128)(2,1)}, bf16[64,2304]{1,0:T(8,128)(2,1)S(1)}, u32[]{:S(2)}, u32[]{:S(2)}) collective-permute-start(bf16[64,2304]{1,0:T(8,128)(2,1)} %bitcast.7), channel_id=1, source_target_pairs={{0,8},{8,16},{16,24},{24,28},{28,20},{20,12},{12,4},{4,0},{1,9},{9... | collective-permute-start | bytes 884744 | tf_op jit(solution)/shard_map/ppermute | solution.py:61
  24.5 8.0 %collective-permute-start.7 = (bf16[64,2304]{1,0:T(8,128)(2,1)}, bf16[64,2304]{1,0:T(8,128)(2,1)S(1)}, u32[]{:S(2)}, u32[]{:S(2)}) collective-permute-start(bf16[64,2304]{1,0:T(8,128)(2,1)} %bitcast.8), channel_id=1, source_target_pairs={{8,0},{16,8},{24,16},{28,24},{20,28},{12,20},{4,12},{0,4},{9,1},{1... | collective-permute-start | bytes 884744 | tf_op jit(solution)/shard_map/ppermute | solution.py:61
  24.9 12.3 %collective-permute-start.18 = (bf16[64,2304]{1,0:T(8,128)(2,1)S(1)}, bf16[64,2304]{1,0:T(8,128)(2,1)S(1)}, u32[]{:S(2)}, u32[]{:S(2)}) collective-permute-start(bf16[64,2304]{1,0:T(8,128)(2,1)S(1)} %collective-permute-done.4.refs_2_), channel_id=1, source_target_pairs={{0,8},{8,16},{16,24},{24,28},{28,20},{20,12},{12,4},{4,0},{1,9},{9... | collective-permute-start | bytes 884744 | tf_op jit(solution)/shard_map/ppermute | solution.py:61
  26.5 12.3 %collective-permute-start.19 = (bf16[64,2304]{1,0:T(8,128)(2,1)S(1)}, bf16[64,2304]{1,0:T(8,128)(2,1)S(1)}, u32[]{:S(2)}, u32[]{:S(2)}) collective-permute-start(bf16[64,2304]{1,0:T(8,128)(2,1)S(1)} %collective-permute-done.5.refs_6_), channel_id=1, source_target_pairs={{8,0},{16,8},{24,16},{28,24},{20,28},{12,20},{4,12},{0,4},{9,1},{1... | collective-permute-start | bytes 884744 | tf_op jit(solution)/shard_map/ppermute | solution.py:61
  26.9 14.1 %collective-permute-start.12 = (bf16[64,2304]{1,0:T(8,128)(2,1)}, bf16[64,2304]{1,0:T(8,128)(2,1)S(1)}, u32[]{:S(2)}, u32[]{:S(2)}) collective-permute-start(bf16[64,2304]{1,0:T(8,128)(2,1)} %bitcast.15), channel_id=1, source_target_pairs={{0,1},{1,0},{2,3},{3,2},{4,5},{5,4},{6,7},{7,6},{8,9},{9,8},{10,11... | collective-permute-start | bytes 884744 | tf_op jit(solution)/shard_map/ppermute | solution.py:82
  32.5 9.0 %collective-permute-start.8 = (bf16[64,2304]{1,0:T(8,128)(2,1)S(1)}, bf16[64,2304]{1,0:T(8,128)(2,1)S(1)}, u32[]{:S(2)}, u32[]{:S(2)}) collective-permute-start(bf16[64,2304]{1,0:T(8,128)(2,1)S(1)} %collective-permute-done.6.refs_1_), channel_id=1, source_target_pairs={{0,8},{8,16},{16,24},{24,28},{28,20},{20,12},{12,4},{4,0},{1,9},{9... | collective-permute-start | bytes 884744 | tf_op jit(solution)/shard_map/ppermute | solution.py:61
  33.7 9.5 %collective-permute-start.9 = (bf16[64,2304]{1,0:T(8,128)(2,1)S(1)}, bf16[64,2304]{1,0:T(8,128)(2,1)S(1)}, u32[]{:S(2)}, u32[]{:S(2)}) collective-permute-start(bf16[64,2304]{1,0:T(8,128)(2,1)S(1)} %collective-permute-done.7.refs_7_), channel_id=1, source_target_pairs={{8,0},{16,8},{24,16},{28,24},{20,28},{12,20},{4,12},{0,4},{9,1},{1... | collective-permute-start | bytes 884744 | tf_op jit(solution)/shard_map/ppermute | solution.py:61
  38.8 5.9 %collective-permute-start.21 = (bf16[32,2304]{1,0:T(8,128)(2,1)S(1)}, bf16[32,2304]{1,0:T(8,128)(2,1)S(1)}, u32[]{:S(2)}, u32[]{:S(2)}) collective-permute-start(bf16[32,2304]{1,0:T(8,128)(2,1)S(1)} %slice.15), channel_id=1, source_target_pairs={{8,0},{16,8},{24,16},{28,24},{20,28},{12,20},{4,12},{0,4},{9,1},{1... | collective-permute-start | bytes 442376 | tf_op jit(solution)/shard_map/ppermute | solution.py:61
  39.2 20.4 %copy-start.4 = (s32[4]{0:T(128)S(1)}, s32[4]{0:T(128)}, u32[]{:S(2)}) copy-start(s32[4]{0:T(128)} %owner.5) | copy-start | bytes 52
  39.2 20.4 %copy-start = (bf16[1,64,2304]{2,1,0:T(8,128)(2,1)S(1)}, bf16[1,64,2304]{2,1,0:T(8,128)(2,1)}, u32[]{:S(2)}) copy-start(bf16[1,64,2304]{2,1,0:T(8,128)(2,1)} %param.11) | copy-start | bytes 884740
  39.2 7.1 %collective-permute-start.20 = (bf16[32,2304]{1,0:T(8,128)(2,1)S(1)}, bf16[32,2304]{1,0:T(8,128)(2,1)S(1)}, u32[]{:S(2)}, u32[]{:S(2)}) collective-permute-start(bf16[32,2304]{1,0:T(8,128)(2,1)S(1)} %slice.14), channel_id=1, source_target_pairs={{0,8},{8,16},{16,24},{24,28},{28,20},{20,12},{12,4},{4,0},{1,9},{9... | collective-permute-start | bytes 442376 | tf_op jit(solution)/shard_map/ppermute | solution.py:61
  41.0 8.2 %collective-permute-start.14 = (bf16[64,2304]{1,0:T(8,128)(2,1)}, bf16[64,2304]{1,0:T(8,128)(2,1)S(1)}, u32[]{:S(2)}, u32[]{:S(2)}) collective-permute-start(bf16[64,2304]{1,0:T(8,128)(2,1)} %bitcast.9), channel_id=1, source_target_pairs={{0,1},{1,0},{2,3},{3,2},{4,5},{5,4},{6,7},{7,6},{8,9},{9,8},{10,11... | collective-permute-start | bytes 884744 | tf_op jit(solution)/shard_map/ppermute | solution.py:82
  41.5 7.7 %collective-permute-start.13 = (bf16[64,2304]{1,0:T(8,128)(2,1)S(1)}, bf16[64,2304]{1,0:T(8,128)(2,1)S(1)}, u32[]{:S(2)}, u32[]{:S(2)}) collective-permute-start(bf16[64,2304]{1,0:T(8,128)(2,1)S(1)} %collective-permute-done.3.refs_2_), channel_id=1, source_target_pairs={{0,1},{1,0},{2,3},{3,2},{4,5},{5,4},{6,7},{7,6},{8,9},{9,8},{10,11... | collective-permute-start | bytes 884744 | tf_op jit(solution)/shard_map/ppermute | solution.py:82
  43.2 7.7 %collective-permute-start.15 = (bf16[64,2304]{1,0:T(8,128)(2,1)S(1)}, bf16[64,2304]{1,0:T(8,128)(2,1)S(1)}, u32[]{:S(2)}, u32[]{:S(2)}) collective-permute-start(bf16[64,2304]{1,0:T(8,128)(2,1)S(1)} %collective-permute-done.refs_11_), channel_id=1, source_target_pairs={{0,1},{1,0},{2,3},{3,2},{4,5},{5,4},{6,7},{7,6},{8,9},{9,8},{10,11... | collective-permute-start | bytes 884744 | tf_op jit(solution)/shard_map/ppermute | solution.py:82
  44.7 7.8 %collective-permute-start.10 = (bf16[64,2304]{1,0:T(8,128)(2,1)S(1)}, bf16[64,2304]{1,0:T(8,128)(2,1)S(1)}, u32[]{:S(2)}, u32[]{:S(2)}) collective-permute-start(bf16[64,2304]{1,0:T(8,128)(2,1)S(1)} %collective-permute-done.8.refs_2_), channel_id=1, source_target_pairs={{0,8},{8,16},{16,24},{24,28},{28,20},{20,12},{12,4},{4,0},{1,9},{9... | collective-permute-start | bytes 884744 | tf_op jit(solution)/shard_map/ppermute | solution.py:61
  46.3 7.6 %collective-permute-start.11 = (bf16[64,2304]{1,0:T(8,128)(2,1)S(1)}, bf16[64,2304]{1,0:T(8,128)(2,1)S(1)}, u32[]{:S(2)}, u32[]{:S(2)}) collective-permute-start(bf16[64,2304]{1,0:T(8,128)(2,1)S(1)} %collective-permute-done.9.refs_6_), channel_id=1, source_target_pairs={{8,0},{16,8},{24,16},{28,24},{20,28},{12,20},{4,12},{0,4},{9,1},{1... | collective-permute-start | bytes 884744 | tf_op jit(solution)/shard_map/ppermute | solution.py:61
  46.8 1.0 copy-start.1
  47.7 0.7 copy-start.3
  49.2 13.4 %collective-permute-start.22 = (bf16[64,2304]{1,0:T(8,128)(2,1)S(1)}, bf16[64,2304]{1,0:T(8,128)(2,1)S(1)}, u32[]{:S(2)}, u32[]{:S(2)}) collective-permute-start(bf16[64,2304]{1,0:T(8,128)(2,1)S(1)} %get-tuple-element.60), channel_id=1, source_target_pairs={{0,1},{1,0},{2,3},{3,2},{4,5},{5,4},{6,7},{7,6},{8,9},{9,8},{10,11... | collective-permute-start | bytes 884744 | tf_op jit(solution)/shard_map/ppermute | solution.py:82
  49.3 16.1 %collective-permute-start.23 = (bf16[64,2304]{1,0:T(8,128)(2,1)S(1)}, bf16[64,2304]{1,0:T(8,128)(2,1)S(1)}, u32[]{:S(2)}, u32[]{:S(2)}) collective-permute-start(bf16[64,2304]{1,0:T(8,128)(2,1)S(1)} %get-tuple-element.61), channel_id=1, source_target_pairs={{0,2},{1,3},{2,0},{3,1},{4,6},{5,7},{6,4},{7,5},{8,10},{9,11},{10,... | collective-permute-start | bytes 884744 | tf_op jit(solution)/shard_map/ppermute | solution.py:82
  50.9 14.5 %collective-permute-start.24 = (bf16[64,2304]{1,0:T(8,128)(2,1)S(1)}, bf16[64,2304]{1,0:T(8,128)(2,1)S(1)}, u32[]{:S(2)}, u32[]{:S(2)}) collective-permute-start(bf16[64,2304]{1,0:T(8,128)(2,1)S(1)} %get-tuple-element.62), channel_id=1, source_target_pairs={{0,3},{1,2},{2,1},{3,0},{4,7},{5,6},{6,5},{7,4},{8,11},{9,10},{10,... | collective-permute-start | bytes 884744 | tf_op jit(solution)/shard_map/ppermute | solution.py:82
  53.9 5.2 %collective-permute-start.17 = (bf16[32,2304]{1,0:T(8,128)(2,1)S(1)}, bf16[32,2304]{1,0:T(8,128)(2,1)S(1)}, u32[]{:S(2)}, u32[]{:S(2)}) collective-permute-start(bf16[32,2304]{1,0:T(8,128)(2,1)S(1)} %slice.13), channel_id=1, source_target_pairs={{8,0},{16,8},{24,16},{28,24},{20,28},{12,20},{4,12},{0,4},{9,1},{1... | collective-permute-start | bytes 442376 | tf_op jit(solution)/shard_map/ppermute | solution.py:61
  54.4 5.1 %collective-permute-start.16 = (bf16[32,2304]{1,0:T(8,128)(2,1)S(1)}, bf16[32,2304]{1,0:T(8,128)(2,1)S(1)}, u32[]{:S(2)}, u32[]{:S(2)}) collective-permute-start(bf16[32,2304]{1,0:T(8,128)(2,1)S(1)} %slice.12), channel_id=1, source_target_pairs={{0,8},{8,16},{16,24},{24,28},{28,20},{20,12},{12,4},{4,0},{1,9},{9... | collective-permute-start | bytes 442376 | tf_op jit(solution)/shard_map/ppermute | solution.py:61
  57.3 5.6 %copy-start.2 = (bf16[1,64,2304]{2,1,0:T(8,128)(2,1)S(1)}, bf16[1,64,2304]{2,1,0:T(8,128)(2,1)}, u32[]{:S(2)}) copy-start(bf16[1,64,2304]{2,1,0:T(8,128)(2,1)} %param.10) | copy-start | bytes 884740
  57.3 5.5 %copy-start.5 = (bf16[1,1,2304,256]{3,2,1,0:T(8,128)(2,1)S(1)}, bf16[1,1,2304,256]{3,2,1,0:T(8,128)(2,1)}, u32[]{:S(2)}) copy-start(bf16[1,1,2304,256]{3,2,1,0:T(8,128)(2,1)} %param.8) | copy-start | bytes 3538948
  57.3 5.5 %copy-start.6 = (bf16[1,1,2304,256]{3,2,1,0:T(8,128)(2,1)S(1)}, bf16[1,1,2304,256]{3,2,1,0:T(8,128)(2,1)}, u32[]{:S(2)}) copy-start(bf16[1,1,2304,256]{3,2,1,0:T(8,128)(2,1)} %param.9) | copy-start | bytes 3538948
  60.9 4.5 %collective-permute-start.25 = (bf16[64,256]{1,0:T(8,128)(2,1)S(1)}, bf16[64,256]{1,0:T(8,128)(2,1)S(1)}, u32[]{:S(2)}, u32[]{:S(2)}) collective-permute-start(bf16[64,256]{1,0:T(8,128)(2,1)S(1)} %get-tuple-element.63), channel_id=1, source_target_pairs={{0,1},{1,0},{2,3},{3,2},{4,5},{5,4},{6,7},{7,6},{8,9},{9,8},{10,11... | collective-permute-start | bytes 98312 | tf_op jit(solution)/shard_map/ppermute | solution.py:82
  61.0 4.8 %collective-permute-start.26 = (bf16[64,256]{1,0:T(8,128)(2,1)S(1)}, bf16[64,256]{1,0:T(8,128)(2,1)S(1)}, u32[]{:S(2)}, u32[]{:S(2)}) collective-permute-start(bf16[64,256]{1,0:T(8,128)(2,1)S(1)} %get-tuple-element.64), channel_id=1, source_target_pairs={{0,2},{1,3},{2,0},{3,1},{4,6},{5,7},{6,4},{7,5},{8,10},{9,11},{10,... | collective-permute-start | bytes 98312 | tf_op jit(solution)/shard_map/ppermute | solution.py:82
  62.6 3.7 %collective-permute-start.27 = (bf16[64,256]{1,0:T(8,128)(2,1)S(1)}, bf16[64,256]{1,0:T(8,128)(2,1)S(1)}, u32[]{:S(2)}, u32[]{:S(2)}) collective-permute-start(bf16[64,256]{1,0:T(8,128)(2,1)S(1)} %get-tuple-element.65), channel_id=1, source_target_pairs={{0,3},{1,2},{2,1},{3,0},{4,7},{5,6},{6,5},{7,4},{8,11},{9,10},{10,... | collective-permute-start | bytes 98312 | tf_op jit(solution)/shard_map/ppermute | solution.py:82
  62.9 3.4 %copy-start.7 = (s32[8]{0:T(128)S(1)}, s32[8]{0:T(128)}, u32[]{:S(2)}) copy-start(s32[8]{0:T(128)} %panel.1) | copy-start | bytes 100
